TPU v7x, 128 devices: a whole 4x4x4 slice. The times are simulated.
128 devices in a mesh: gy: 16 (over x_lo, z, core), gx: 8 (over x_hi, y).
Axes of the slice: x: 4 (x_hi: 2, x_lo: 2; x = x_hi * 2 + x_lo), y: 4, z: 4, core: 2. Of those that a mesh axis runs over, the one named last changes fastest.
Arguments:
- e_field: float32 [3, 4, 1024, 1024], P(None, None, 'gy', 'gx'), may hold values from -6 to 6
- h_field: float32 [3, 4, 1024, 1024], P(None, None, 'gy', 'gx'), may hold values from -6 to 6
- j_field: float32 [3, 4, 1024, 1024], P(None, None, 'gy', 'gx'), may hold values from -3 to 3
- material: int32 [4, 1024, 1024], P(None, 'gy', 'gx'), may hold values from 0 to 31
- material_table: float32 [4, 32], replicated, may hold values from 0.05 to 1
- dft_e: float32 [3, 2, 3, 4, 1024, 1024], P(None, None, None, None, 'gy', 'gx'), may hold values from -5 to 7
- dft_h: float32 [3, 2, 3, 4, 1024, 1024], P(None, None, None, None, 'gy', 'gx'), may hold values from -5 to 7
- skin_cell: int32 [128, 128, 128], P(('gy', 'gx')), may hold values from 0 to 32767, as said below
- counts: int32 [128, 128], P(('gy', 'gx')), may hold values from 0 to 128, as said below
- patch_slot: int32 [128, 128, 128], P(('gy', 'gx')), may hold values from 0 to 65535
- area: float32 [3, 4096, 2048], P(None, 'gy', 'gx'), may hold values from -0.5 to 1.5
Outputs:
- e_next: float32 [3, 4, 1024, 1024], P(None, None, 'gy', 'gx')
- j_next: float32 [3, 4, 1024, 1024], P(None, None, 'gy', 'gx')
- dft_e_next: float32 [3, 2, 3, 4, 1024, 1024], P(None, None, None, None, 'gy', 'gx')
- dft_h_next: float32 [3, 2, 3, 4, 1024, 1024], P(None, None, None, None, 'gy', 'gx')
- point_density: float32 [3, 4096, 2048], P(None, 'gy', 'gx')
- avg_density: float32 [3, 4096, 2048], P(None, 'gy', 'gx')
Inputs may be any that keep to these rules, and one draw needn't show every extreme that they name: Within one source block s the entries skin_cell[s, :, :] are distinct. Some owner block d has counts[s, d] = 128 for every source block s.
All inputs are finite; a program needn't handle non-finite values.
Results may differ from a plain program's by a relative error of at most 0.0003.
Values sent between devices are 32-bit elements; how exact they have to be, the bound alone decides.
No kernel may reach another device: no remote copies, remote signals or barrier semaphores. Data moves between devices by JAX's collectives and lax.ppermute only.
A program may use at most 192 MiB of HBM per device.

v0:
```python
import math

import jax
import jax.numpy as jnp
from jax import lax
from jax.sharding import PartitionSpec as P

STEP = 1000
HALF = 100


FREQ_LIST = (28000000000.0, 39000000000.0, 60000000000.0)
TIME_STEP = 1.9e-13


def shifted(value, axis, steps):
    count = lax.axis_size(axis)
    leading, last = (max(0, -steps), min(count, count - steps))
    return lax.ppermute(value, axis, [(source, source + steps) for source in range(leading, last)])


def with_halo(cells, sides, width):
    for axis, dim in sides:
        count = lax.axis_size(axis)
        ends = count - 1
        head = lax.slice_in_dim(cells, 0, width, axis=dim)
        tail = lax.slice_in_dim(cells, cells.shape[dim] - width, cells.shape[dim], axis=dim)
        cells = jnp.concatenate(
            [
                lax.ppermute(tail, axis, [(i, (i + 1) % count) for i in range(ends)]),
                cells,
                lax.ppermute(head, axis, [((i + 1) % count, i) for i in range(ends)]),
            ],
            axis=dim,
        )
    return cells


def phase_list(offset):
    return [2.0 * math.pi * freq_hz * (STEP + offset) * TIME_STEP for freq_hz in FREQ_LIST]


def accumulate(running, field_in, offset):
    pieces = []
    for phase_angle in phase_list(offset):
        pieces.append(
            jnp.stack([field_in * math.cos(phase_angle), field_in * -math.sin(phase_angle)])
        )
    return running + jnp.stack(pieces)


def curl_field(h_field, rows_below, cols_left):
    magnet_x, magnet_y, magnet_z = (h_field[0], h_field[1], h_field[2])
    zero_plane = jnp.zeros_like(magnet_x[:1])
    x_below_z = jnp.concatenate([zero_plane, magnet_x[:-1]], 0)
    y_below_z = jnp.concatenate([zero_plane, magnet_y[:-1]], 0)
    y_below_x = jnp.concatenate([rows_below[0][:, None, :], magnet_y[:, :-1, :]], 1)
    z_below_x = jnp.concatenate([rows_below[1][:, None, :], magnet_z[:, :-1, :]], 1)
    x_below_y = jnp.concatenate([cols_left[0][:, :, None], magnet_x[:, :, :-1]], 2)
    z_below_y = jnp.concatenate([cols_left[1][:, :, None], magnet_z[:, :, :-1]], 2)
    curl_x = magnet_z - z_below_y - (magnet_y - y_below_z)
    curl_y = magnet_x - x_below_z - (magnet_z - z_below_x)
    curl_z = magnet_y - y_below_x - (magnet_x - x_below_y)
    return jnp.stack([curl_x, curl_y, curl_z])


def cross_product(left_vec, right_vec):
    return jnp.stack(
        [
            left_vec[:, 1] * right_vec[:, 2] - left_vec[:, 2] * right_vec[:, 1],
            left_vec[:, 2] * right_vec[:, 0] - left_vec[:, 0] * right_vec[:, 2],
            left_vec[:, 0] * right_vec[:, 1] - left_vec[:, 1] * right_vec[:, 0],
        ],
        1,
    )


def cross_flux(e_rows, h_rows):
    return 0.5 * (
        cross_product(e_rows[:, 0], h_rows[:, 0]) + cross_product(e_rows[:, 1], h_rows[:, 1])
    )


def lookup(material, material_table):
    kind_count = material_table.shape[1]
    flat_ids = material.reshape(1, -1)
    onehot = (
        lax.broadcasted_iota(jnp.int32, (kind_count, flat_ids.shape[1]), 0) == flat_ids
    ).astype(jnp.float32)
    coeffs = jnp.dot(
        material_table, onehot, precision=lax.Precision.HIGHEST, preferred_element_type=jnp.float32
    )
    return coeffs.reshape((4,) + material.shape)


def band_matrix(count, half_width):
    row_ids = lax.broadcasted_iota(jnp.int32, (count, count + 2 * half_width), 0)
    col_ids = lax.broadcasted_iota(jnp.int32, (count, count + 2 * half_width), 1)
    return ((col_ids >= row_ids) & (col_ids < row_ids + 2 * half_width)).astype(jnp.float32)


def pick_rows(values, index, lo_width):
    row_count = values.shape[0]
    hi_count = values.shape[1] // lo_width
    table = (
        values.reshape(row_count, hi_count, lo_width)
        .transpose(1, 0, 2)
        .reshape(hi_count, row_count * lo_width)
    )
    total = index.shape[0]
    block_len = math.gcd(total, 1024)
    hi_ids = (index // lo_width).reshape(-1, block_len)
    lo_ids = (index % lo_width).reshape(-1, block_len)
    lanes = lax.broadcasted_iota(jnp.int32, (1, 1, lo_width), 2)

    def one_block(pair):
        hi_block, lo_block = pair
        rows = jnp.take(table, hi_block, axis=0).reshape(block_len, row_count, lo_width)
        chosen = lo_block[:, None, None] == lanes
        return jnp.sum(jnp.where(chosen, rows, 0.0), axis=2)

    picked = lax.map(one_block, (hi_ids, lo_ids))
    return picked.reshape(total, row_count).T


def spread_rows(density, index, hi_count, lo_width):
    freq_count = density.shape[0]
    total = index.shape[0]
    first = density.astype(jnp.bfloat16)
    rest = density - lax.optimization_barrier(first).astype(jnp.float32)
    second = rest.astype(jnp.bfloat16)
    rest = rest - lax.optimization_barrier(second).astype(jnp.float32)
    third = rest.astype(jnp.bfloat16)
    split_parts = jnp.stack([first, second, third]).transpose(2, 0, 1)
    block_len = math.gcd(total, 2048)
    block_count = total // block_len
    part_blocks = split_parts.reshape(block_count, block_len, 3, freq_count)
    hi_blocks = (index // lo_width).reshape(block_count, block_len)
    lo_blocks = (index % lo_width).reshape(block_count, block_len)

    def add_block(carry, inputs):
        part_block, hi_block, lo_block = inputs
        hi_table = (
            lax.broadcasted_iota(jnp.int32, (hi_count, block_len), 0) == hi_block[None, :]
        ).astype(jnp.bfloat16)
        lo_table = (
            lo_block[:, None] == lax.broadcasted_iota(jnp.int32, (block_len, lo_width), 1)
        ).astype(jnp.bfloat16)
        spread = (part_block[:, :, :, None] * lo_table[:, None, None, :]).reshape(
            block_len, 3 * freq_count * lo_width
        )
        return (carry + jnp.dot(hi_table, spread, preferred_element_type=jnp.float32), None)

    start = jnp.zeros((hi_count, 3 * freq_count * lo_width), jnp.float32)
    summed, unused = lax.scan(add_block, start, (part_blocks, hi_blocks, lo_blocks))
    summed = summed.reshape(hi_count, 3, freq_count, lo_width)
    joined = summed[:, 0] + summed[:, 1] + summed[:, 2]
    return joined.transpose(1, 0, 2)


def send_rows(payload):
    return lax.all_to_all(payload, ("gy", "gx"), split_axis=1, concat_axis=1, tiled=True)


def shards(
    e_field,
    h_field,
    j_field,
    material,
    material_table,
    dft_e,
    dft_h,
    skin_cell,
    counts,
    patch_slot,
    area,
):
    magnet_x, magnet_y, magnet_z = (h_field[0], h_field[1], h_field[2])
    rows_below = shifted(jnp.stack([magnet_y[:, -1, :], magnet_z[:, -1, :]]), "gy", 1)
    cols_left = shifted(jnp.stack([magnet_x[:, :, -1], magnet_z[:, :, -1]]), "gx", 1)
    coeffs = lookup(material, material_table)
    curl_h = curl_field(h_field, rows_below, cols_left)
    e_next = coeffs[0] * e_field + coeffs[1] * (curl_h - j_field)
    j_next = coeffs[2] * j_field + coeffs[3] * (e_next - e_field)
    dft_e_next = accumulate(dft_e, e_next, 0.0)
    dft_h_next = accumulate(dft_h, h_field, 0.5)
    freq_count = dft_e.shape[0]
    blocks = skin_cell.shape[1]
    slot_count = skin_cell.shape[2]
    col_width = e_field.shape[3]
    skin_index = skin_cell.reshape(-1)
    live_mask = (
        lax.broadcasted_iota(jnp.int32, (blocks, slot_count), 1) < counts.reshape(blocks, 1)
    ).astype(jnp.float32)
    both_spectra = jnp.concatenate(
        [dft_e_next.reshape(6 * freq_count, -1), dft_h_next.reshape(6 * freq_count, -1)], 0
    )
    both_rows = (
        pick_rows(both_spectra, skin_index, col_width).reshape(12 * freq_count, blocks, slot_count)
        * live_mask
    )
    spectral_shape = (freq_count, 2, 3, blocks, slot_count)
    arrived = send_rows(both_rows)
    flux_rows = cross_flux(
        arrived[: 6 * freq_count].reshape(spectral_shape),
        arrived[6 * freq_count :].reshape(spectral_shape),
    )
    flux_rows = flux_rows.reshape(freq_count, 3, blocks * slot_count)
    rows_u = area.shape[1]
    cols_v = area.shape[2]
    patch_index = patch_slot.reshape(-1)
    area_rows = pick_rows(area.reshape(3, -1), patch_index, cols_v)
    density = (
        area_rows[0] * flux_rows[:, 0]
        + area_rows[1] * flux_rows[:, 1]
        + area_rows[2] * flux_rows[:, 2]
    )
    point_density = spread_rows(density, patch_index, rows_u, cols_v)
    padded = with_halo(point_density, (("gy", 1),), HALF)
    strip_sum = jnp.einsum(
        "ij,fjv->fiv",
        band_matrix(rows_u, HALF),
        padded,
        precision=lax.Precision.HIGHEST,
        preferred_element_type=jnp.float32,
    )
    padded_cols = with_halo(strip_sum, (("gx", 2),), HALF)
    square_sum = jnp.einsum(
        "fuj,ij->fui",
        padded_cols,
        band_matrix(cols_v, HALF),
        precision=lax.Precision.HIGHEST,
        preferred_element_type=jnp.float32,
    )
    avg_density = square_sum / (4.0 * HALF * HALF)
    return (e_next, j_next, dft_e_next, dft_h_next, point_density, avg_density)


def solution(mesh):
    placed = (
        P(None, None, "gy", "gx"),
        P(None, None, "gy", "gx"),
        P(None, None, "gy", "gx"),
        P(None, "gy", "gx"),
        P(),
        P(None, None, None, None, "gy", "gx"),
        P(None, None, None, None, "gy", "gx"),
        P(("gy", "gx"), None, None),
        P(("gy", "gx"), None),
        P(("gy", "gx"), None, None),
        P(None, "gy", "gx"),
    )
    return jax.shard_map(
        shards,
        mesh=mesh,
        in_specs=placed,
        out_specs=(
            P(None, None, "gy", "gx"),
            P(None, None, "gy", "gx"),
            P(None, None, None, None, "gy", "gx"),
            P(None, None, None, None, "gy", "gx"),
            P(None, "gy", "gx"),
            P(None, "gy", "gx"),
        ),
        check_vma=False,
    )
```

profile of v0, /device:TPU:26, one launch (start us, length us, event | category | flops | bytes accessed | tf_op | source)
XLA Modules:
  0.0 1289.0 jit_solution(4209805642646674367)
XLA Ops:
  17.8 216.5 %while.33 = (s32[]{:T(128)}, f32[16,1024,3]{1,2,0:T(4,128)}, s32[16,1024]{1,0:T(8,128)}, s32[16,1024]{1,0:T(8,128)}, f32[256,768]{1,0:T(8,128)S(1)}, /*index=5*/s32[]{:T(128)}) while((s32[]{:T(128)}, f32[16,1024,3]{1,2,0:T(4,128)}, s32[16,1024]{1,0:T(8,128)}, s32[16,1024]{1,0:T(8,128)}, f32[256,768]{1,0:T(8,128)S(1)}, ...), condition=%wide.region_2.3_spmd.clone, body=%wide.region_0.2_spmd.clone.sunk | while | flops 2628610 | bytes 16337485 | solution.py:122
  294.6 794.7 %while.34 = (s32[]{:T(128)}, f32[16,1024,36]{1,0,2:T(8,128)S(1)}, s32[16,1024]{1,0:T(8,128)}, s32[16,1024]{1,0:T(8,128)}, f32[256,4608]{1,0:T(8,128)}, /*index=5*/s32[]{:T(128)}, s32[]{:T(128)}) while((s32[]{:T(128)}, f32[16,1024,36]{1,0,2:T(8,128)S(1)}, s32[16,1024]{1,0:T(8,128)}, s32[16,1024]{1,0:T(8,128)}, ...), condition=%wide.region_5.6_spmd.clone, body=%wide.region_3.5_spmd.clone.sunk | while | flops 14260226 | bytes 95414352 | solution.py:122
  295.9 18.9 %gather_fusion.1 = f32[1024,4608]{1,0:T(8,128)} fusion(f32[256,4608]{1,0:T(8,128)} %get-tuple-element.530, s32[1024]{0:T(1024)S(1)} %broadcast_clamp_fusion.5), kind=kCustom, calls=%fused_computation.1.clone.clone.1 | custom fusion | bytes 37752832 | tf_op jit(solution)/shard_map/while/body/eval_jaxpr/jit(_take)/gather | solution.py:118
  314.8 18.7 %copy.396 = f32[1024,4608]{0,1:T(8,128)} copy(f32[1024,4608]{1,0:T(8,128)} %gather_fusion.1) | data formatting | bytes 37748736 | tf_op jit(solution)/shard_map/while/body/eval_jaxpr/jit(_take)/gather | solution.py:118
  345.5 18.9 %gather_fusion.1 = f32[1024,4608]{1,0:T(8,128)} fusion(f32[256,4608]{1,0:T(8,128)} %get-tuple-element.530, s32[1024]{0:T(1024)S(1)} %broadcast_clamp_fusion.5), kind=kCustom, calls=%fused_computation.1.clone.clone.1 | custom fusion | bytes 37752832 | tf_op jit(solution)/shard_map/while/body/eval_jaxpr/jit(_take)/gather | solution.py:118
  364.4 18.7 %copy.396 = f32[1024,4608]{0,1:T(8,128)} copy(f32[1024,4608]{1,0:T(8,128)} %gather_fusion.1) | data formatting | bytes 37748736 | tf_op jit(solution)/shard_map/while/body/eval_jaxpr/jit(_take)/gather | solution.py:118
  395.2 18.9 %gather_fusion.1 = f32[1024,4608]{1,0:T(8,128)} fusion(f32[256,4608]{1,0:T(8,128)} %get-tuple-element.530, s32[1024]{0:T(1024)S(1)} %broadcast_clamp_fusion.5), kind=kCustom, calls=%fused_computation.1.clone.clone.1 | custom fusion | bytes 37752832 | tf_op jit(solution)/shard_map/while/body/eval_jaxpr/jit(_take)/gather | solution.py:118
  414.0 18.7 %copy.396 = f32[1024,4608]{0,1:T(8,128)} copy(f32[1024,4608]{1,0:T(8,128)} %gather_fusion.1) | data formatting | bytes 37748736 | tf_op jit(solution)/shard_map/while/body/eval_jaxpr/jit(_take)/gather | solution.py:118
  444.8 18.9 %gather_fusion.1 = f32[1024,4608]{1,0:T(8,128)} fusion(f32[256,4608]{1,0:T(8,128)} %get-tuple-element.530, s32[1024]{0:T(1024)S(1)} %broadcast_clamp_fusion.5), kind=kCustom, calls=%fused_computation.1.clone.clone.1 | custom fusion | bytes 37752832 | tf_op jit(solution)/shard_map/while/body/eval_jaxpr/jit(_take)/gather | solution.py:118
  463.7 18.7 %copy.396 = f32[1024,4608]{0,1:T(8,128)} copy(f32[1024,4608]{1,0:T(8,128)} %gather_fusion.1) | data formatting | bytes 37748736 | tf_op jit(solution)/shard_map/while/body/eval_jaxpr/jit(_take)/gather | solution.py:118
  494.4 18.9 %gather_fusion.1 = f32[1024,4608]{1,0:T(8,128)} fusion(f32[256,4608]{1,0:T(8,128)} %get-tuple-element.530, s32[1024]{0:T(1024)S(1)} %broadcast_clamp_fusion.5), kind=kCustom, calls=%fused_computation.1.clone.clone.1 | custom fusion | bytes 37752832 | tf_op jit(solution)/shard_map/while/body/eval_jaxpr/jit(_take)/gather | solution.py:118
  544.1 18.9 %gather_fusion.1 = f32[1024,4608]{1,0:T(8,128)} fusion(f32[256,4608]{1,0:T(8,128)} %get-tuple-element.530, s32[1024]{0:T(1024)S(1)} %broadcast_clamp_fusion.5), kind=kCustom, calls=%fused_computation.1.clone.clone.1 | custom fusion | bytes 37752832 | tf_op jit(solution)/shard_map/while/body/eval_jaxpr/jit(_take)/gather | solution.py:118
  593.7 18.9 %gather_fusion.1 = f32[1024,4608]{1,0:T(8,128)} fusion(f32[256,4608]{1,0:T(8,128)} %get-tuple-element.530, s32[1024]{0:T(1024)S(1)} %broadcast_clamp_fusion.5), kind=kCustom, calls=%fused_computation.1.clone.clone.1 | custom fusion | bytes 37752832 | tf_op jit(solution)/shard_map/while/body/eval_jaxpr/jit(_take)/gather | solution.py:118
  643.4 18.9 %gather_fusion.1 = f32[1024,4608]{1,0:T(8,128)} fusion(f32[256,4608]{1,0:T(8,128)} %get-tuple-element.530, s32[1024]{0:T(1024)S(1)} %broadcast_clamp_fusion.5), kind=kCustom, calls=%fused_computation.1.clone.clone.1 | custom fusion | bytes 37752832 | tf_op jit(solution)/shard_map/while/body/eval_jaxpr/jit(_take)/gather | solution.py:118
  693.0 18.9 %gather_fusion.1 = f32[1024,4608]{1,0:T(8,128)} fusion(f32[256,4608]{1,0:T(8,128)} %get-tuple-element.530, s32[1024]{0:T(1024)S(1)} %broadcast_clamp_fusion.5), kind=kCustom, calls=%fused_computation.1.clone.clone.1 | custom fusion | bytes 37752832 | tf_op jit(solution)/shard_map/while/body/eval_jaxpr/jit(_take)/gather | solution.py:118
  742.6 18.9 %gather_fusion.1 = f32[1024,4608]{1,0:T(8,128)} fusion(f32[256,4608]{1,0:T(8,128)} %get-tuple-element.530, s32[1024]{0:T(1024)S(1)} %broadcast_clamp_fusion.5), kind=kCustom, calls=%fused_computation.1.clone.clone.1 | custom fusion | bytes 37752832 | tf_op jit(solution)/shard_map/while/body/eval_jaxpr/jit(_take)/gather | solution.py:118
  792.3 18.9 %gather_fusion.1 = f32[1024,4608]{1,0:T(8,128)} fusion(f32[256,4608]{1,0:T(8,128)} %get-tuple-element.530, s32[1024]{0:T(1024)S(1)} %broadcast_clamp_fusion.5), kind=kCustom, calls=%fused_computation.1.clone.clone.1 | custom fusion | bytes 37752832 | tf_op jit(solution)/shard_map/while/body/eval_jaxpr/jit(_take)/gather | solution.py:118
  841.9 18.9 %gather_fusion.1 = f32[1024,4608]{1,0:T(8,128)} fusion(f32[256,4608]{1,0:T(8,128)} %get-tuple-element.530, s32[1024]{0:T(1024)S(1)} %broadcast_clamp_fusion.5), kind=kCustom, calls=%fused_computation.1.clone.clone.1 | custom fusion | bytes 37752832 | tf_op jit(solution)/shard_map/while/body/eval_jaxpr/jit(_take)/gather | solution.py:118
  891.5 18.9 %gather_fusion.1 = f32[1024,4608]{1,0:T(8,128)} fusion(f32[256,4608]{1,0:T(8,128)} %get-tuple-element.530, s32[1024]{0:T(1024)S(1)} %broadcast_clamp_fusion.5), kind=kCustom, calls=%fused_computation.1.clone.clone.1 | custom fusion | bytes 37752832 | tf_op jit(solution)/shard_map/while/body/eval_jaxpr/jit(_take)/gather | solution.py:118
  941.2 18.9 %gather_fusion.1 = f32[1024,4608]{1,0:T(8,128)} fusion(f32[256,4608]{1,0:T(8,128)} %get-tuple-element.530, s32[1024]{0:T(1024)S(1)} %broadcast_clamp_fusion.5), kind=kCustom, calls=%fused_computation.1.clone.clone.1 | custom fusion | bytes 37752832 | tf_op jit(solution)/shard_map/while/body/eval_jaxpr/jit(_take)/gather | solution.py:118
  990.8 18.9 %gather_fusion.1 = f32[1024,4608]{1,0:T(8,128)} fusion(f32[256,4608]{1,0:T(8,128)} %get-tuple-element.530, s32[1024]{0:T(1024)S(1)} %broadcast_clamp_fusion.5), kind=kCustom, calls=%fused_computation.1.clone.clone.1 | custom fusion | bytes 37752832 | tf_op jit(solution)/shard_map/while/body/eval_jaxpr/jit(_take)/gather | solution.py:118
  1040.5 18.9 %gather_fusion.1 = f32[1024,4608]{1,0:T(8,128)} fusion(f32[256,4608]{1,0:T(8,128)} %get-tuple-element.530, s32[1024]{0:T(1024)S(1)} %broadcast_clamp_fusion.5), kind=kCustom, calls=%fused_computation.1.clone.clone.1 | custom fusion | bytes 37752832 | tf_op jit(solution)/shard_map/while/body/eval_jaxpr/jit(_take)/gather | solution.py:118
  1106.5 32.2 %all-to-all-done = f32[36,128,128]{2,0,1:T(8,128)S(1)} async-done(((f32[36,128,128]{2,0,1:T(8,128)}), f32[36,128,128]{2,0,1:T(8,128)S(1)}, u32[]{:S(2)}, u32[]{:S(2)}) %all-to-all-start) | async-done | bytes 2359328 | tf_op jit(solution)/shard_map/all_to_all | solution.py:162
  1143.4 100.5 %while.35 = (s32[]{:T(128)}, f32[256,2304]{1,0:T(8,128)S(1)}, s32[8,2048]{1,0:T(8,128)}, bf16[8,2048,3,3]{1,3,2,0:T(4,128)(2,1)S(1)}, s32[8,2048]{1,0:T(8,128)}, /*index=5*/s32[]{:T(128)}, s32[]{:T(128)}) while((s32[]{:T(128)}, f32[256,2304]{1,0:T(8,128)S(1)}, s32[8,2048]{1,0:T(8,128)}, bf16[8,2048,3,3]{1,3,2,0:T(4,128)(2,1)S(1)}, ...), condition=%wide.region_7.8_spmd.clone, body=%wide.region_6.7_spmd.clone.sunk | while | flops 2423390208 | bytes 25849952 | solution.py:155
  (491 shorter events, 876.2 us)
Async XLA Ops:
  0.6 12.6 copy-start
  0.6 8.5 copy-start.10
  2.1 10.5 copy-start.7
  2.1 256.7 %collective-permute-start = (f32[2,4,64]{2,1,0:T(4,128)S(1)}, f32[2,4,64]{2,1,0:T(4,128)S(1)}, u32[]{:S(2)}, u32[]{:S(2)}) collective-permute-start(f32[2,4,64]{2,1,0:T(4,128)S(1)} %pad_maximum_fusion), channel_id=1, source_target_pairs={{0,1},{1,2},{2,3},{3,4},{4,5},{5,6},{6,7},{8,9},{9,10},{10,11},{11... | collective-permute-start | bytes 6152 | tf_op jit(solution)/shard_map/ppermute | solution.py:19
  6.3 6.3 copy-start.6
  6.5 6.1 copy-start.23
  6.5 6.7 copy-start.27
  7.3 251.5 %collective-permute-start.1 = (f32[2,4,128]{2,1,0:T(4,128)}, f32[2,4,128]{2,1,0:T(4,128)S(1)}, u32[]{:S(2)}, u32[]{:S(2)}) collective-permute-start(f32[2,4,128]{2,1,0:T(4,128)} %pad_maximum_fusion.1), channel_id=1, source_target_pairs={{0,8},{8,16},{16,24},{24,32},{32,40},{40,48},{48,56},{56,64},{64,7... | collective-permute-start | bytes 12296 | tf_op jit(solution)/shard_map/ppermute | solution.py:19
  11.3 4.4 copy-start.25
  11.3 5.9 copy-start.20
  17.7 216.5 %copy-start.22 = (s32[8,2048]{1,0:T(8,128)S(1)}, s32[8,2048]{1,0:T(8,128)}, u32[]{:S(2)}) copy-start(s32[8,2048]{1,0:T(8,128)} %reshape.398) | copy-start | bytes 196612
  17.8 218.5 %copy-start.15 = (f32[1,3,4,64,128]{4,3,2,1,0:T(8,128)S(1)}, f32[1,3,4,64,128]{4,3,2,1,0:T(8,128)}, u32[]{:S(2)}) copy-start(f32[1,3,4,64,128]{4,3,2,1,0:T(8,128)} %get-tuple-element.379) | copy-start | bytes 1179652
  238.0 39.7 %copy-start.2 = (f32[3,2,3,4,64,128]{5,4,3,2,1,0:T(8,128)}, f32[3,2,3,4,64,128]{5,4,3,2,1,0:T(8,128)S(1)}, u32[]{:S(2)}) copy-start(f32[3,2,3,4,64,128]{5,4,3,2,1,0:T(8,128)S(1)} %maximum_add_fusion.1) | copy-start | bytes 7077892
  288.4 6.2 copy-start.12
  1095.1 11.2 copy-start.24
  1095.1 43.5 %all-to-all-start = ((f32[36,128,128]{2,0,1:T(8,128)}), f32[36,128,128]{2,0,1:T(8,128)S(1)}, u32[]{:S(2)}, u32[]{:S(2)}) async-start(f32[36,128,128]{2,0,1:T(8,128)} %copy.322), calls=%async_computation | async-start | bytes 5242880 | tf_op jit(solution)/shard_map/all_to_all | solution.py:162
  1252.0 14.6 %copy-start.9 = (f32[3,256,256]{2,1,0:T(8,128)}, f32[3,256,256]{2,1,0:T(8,128)S(1)}, u32[]{:S(2)}) copy-start(f32[3,256,256]{2,1,0:T(8,128)S(1)} %add_bitcast_fusion) | copy-start | bytes 2359300
  1252.0 22.4 %copy-start.4 = (f32[3,4,64,128]{2,1,3,0:T(4,128)S(1)}, f32[3,4,64,128]{2,1,3,0:T(4,128)}, u32[]{:S(2)}) copy-start(f32[3,4,64,128]{2,1,3,0:T(4,128)} %copy-done.3) | copy-start | bytes 1179652
  1252.1 10.5 collective-permute-start.2
  1254.2 10.2 collective-permute-start.3
  1260.2 15.3 %copy-start.8 = (f32[3,4,64,128]{2,1,3,0:T(4,128)S(1)}, f32[3,4,64,128]{2,1,3,0:T(4,128)}, u32[]{:S(2)}) copy-start(f32[3,4,64,128]{2,1,3,0:T(4,128)} %get-tuple-element.372) | copy-start | bytes 1179652
  1266.7 12.4 collective-permute-start.4
  1272.5 16.3 %copy-start.1 = (f32[4,32]{1,0:T(4,128)S(1)}, f32[4,32]{1,0:T(4,128)}, u32[]{:S(2)}) copy-start(f32[4,32]{1,0:T(4,128)} %param.21) | copy-start | bytes 1540
  1272.5 13.9 %collective-permute-start.5 = (f32[3,256,100]{1,2,0:T(8,128)S(1)}, f32[3,256,100]{1,2,0:T(8,128)S(1)}, u32[]{:S(2)}, u32[]{:S(2)}) collective-permute-start(f32[3,256,100]{1,2,0:T(8,128)S(1)} %get-tuple-element.360), channel_id=1, source_target_pairs={{1,0},{2,1},{3,2},{4,3},{5,4},{6,5},{7,6},{9,8},{10,9},{11,10},{12... | collective-permute-start | bytes 921608 | tf_op jit(solution)/shard_map/ppermute | solution.py:32
  (13 other events, 26.8 us)
where the time goes:
time: 1300 us; the launch traced here: 1290 us
  local copies, waits for them, and re-layouts  872 us (67%)
  other arithmetic  273 us (21%)
  matrix products  61.9 us (5%)
  waiting for transfers between devices  46.4 us (4%)
  starting transfers between devices  32.6 us (3%)
    gather x64, local copies, waits for them, and re-layouts, one_block(): jnp.take(table, hi_block, axis=0).reshape(block_len, row_count, lo_width)  742 us
    reduce_sum x32, other arithmetic, one_block(): return jnp.sum(jnp.where(chosen, rows, 0.0), axis=2)  182 us
    dot_general x8, matrix products, add_block(): jnp.dot(hi_table, spread, preferred_element_type=jnp.float32)  56.8 us
    unnamed x83, local copies, waits for them, and re-layouts  36.6 us
    mul x8, other arithmetic, add_block(): part_block[:, :, :, None] * lo_table[:, None, None, :]  34.4 us
    dynamic_update_slice x48, local copies, waits for them, and re-layouts, pick_rows(): picked = lax.map(one_block, (hi_ids, lo_ids))  32.2 us
    all_to_all x1, waiting for transfers between devices, send_rows(): lax.all_to_all(payload, ('gy', 'gx'), split_axis=1, concat_axis=1, tiled=...  32.2 us
  transfers between devices with their start and end apart: 7, of which 5 were waited for; matrix products, arithmetic and copies ran while one was open for 20% of the time, Pallas kernels for 0%

commit v1 on v0

v1 whole, which is shorter than its diff:
```python
import functools
import math

import jax
import jax.numpy as jnp
from jax import lax
from jax.experimental import pallas as pl
from jax.experimental.pallas import tpu as pltpu
from jax.sharding import PartitionSpec as P

STEP = 1000
HALF = 100
FREQ_LIST = (28000000000.0, 39000000000.0, 60000000000.0)
TIME_STEP = 1.9e-13

f32 = jnp.float32
bf16 = jnp.bfloat16
VMEM = pl.BlockSpec(memory_space=pltpu.VMEM)
SMEM = pl.BlockSpec(memory_space=pltpu.SMEM)


def phase_list(offset):
    return [2.0 * math.pi * freq_hz * (STEP + offset) * TIME_STEP for freq_hz in FREQ_LIST]


def iota(shape, dim):
    return lax.broadcasted_iota(jnp.int32, shape, dim)


def shifted(value, axis, steps):
    count = lax.axis_size(axis)
    leading, last = (max(0, -steps), min(count, count - steps))
    return lax.ppermute(value, axis, [(source, source + steps) for source in range(leading, last)])


def with_halo(cells, sides, width):
    for axis, dim in sides:
        count = lax.axis_size(axis)
        ends = count - 1
        head = lax.slice_in_dim(cells, 0, width, axis=dim)
        tail = lax.slice_in_dim(cells, cells.shape[dim] - width, cells.shape[dim], axis=dim)
        cells = jnp.concatenate(
            [
                lax.ppermute(tail, axis, [(i, (i + 1) % count) for i in range(ends)]),
                cells,
                lax.ppermute(head, axis, [((i + 1) % count, i) for i in range(ends)]),
            ],
            axis=dim,
        )
    return cells


def band_matrix(count, half_width):
    row_ids = iota((count, count + 2 * half_width), 0)
    col_ids = iota((count, count + 2 * half_width), 1)
    return ((col_ids >= row_ids) & (col_ids < row_ids + 2 * half_width)).astype(f32)


def field_kernel(
    e_ref, h_ref, j_ref, kind_ref, table_ref, dft_e_ref, dft_h_ref, row_ref, col_ref,
    e_out, j_out, dft_e_out, dft_h_out, flux_out, below_ref, wide_ref,
):
    z = pl.program_id(0)

    @pl.when(z == 0)
    def _():
        below_ref[...] = jnp.zeros_like(below_ref)
        wide_ref[...] = jnp.zeros_like(wide_ref)
        wide_ref[0:4, 0:32] = table_ref[...]

    rows, cols = kind_ref.shape[1:]
    hx, hy, hz = h_ref[0, 0], h_ref[1, 0], h_ref[2, 0]
    first_row = iota((rows, cols), 0) == 0
    first_col = iota((rows, cols), 1) == 0
    diagonal = iota((rows, rows), 0) == iota((rows, rows), 1)

    def below_x(field, part):
        halo = row_ref[part, pl.ds(z, 1), :]
        return jnp.where(first_row, halo, pltpu.roll(field, 1, 0))

    def below_y(field, part):
        halo = col_ref[part, pl.ds(z, 1), :]
        halo = jnp.sum(jnp.where(diagonal, halo, 0.0), axis=1, keepdims=True)
        return jnp.where(first_col, halo, pltpu.roll(field, 1, 1))

    curl = (
        (hz - below_y(hz, 1)) - (hy - below_ref[1]),
        (hx - below_ref[0]) - (hz - below_x(hz, 1)),
        (hy - below_x(hy, 0)) - (hx - below_y(hx, 0)),
    )
    kinds = kind_ref[0]
    coeffs = [
        jnp.take_along_axis(
            jnp.broadcast_to(wide_ref[r : r + 1, :], (rows, cols)), kinds, axis=1
        )
        for r in range(4)
    ]
    e_next = []
    for c in range(3):
        old_e, old_j = e_ref[c, 0], j_ref[c, 0]
        new_e = coeffs[0] * old_e + coeffs[1] * (curl[c] - old_j)
        e_out[c, 0] = new_e
        j_out[c, 0] = coeffs[2] * old_j + coeffs[3] * (new_e - old_e)
        e_next.append(new_e)
    field_h = (hx, hy, hz)
    phase_e, phase_h = phase_list(0.0), phase_list(0.5)
    half_plane = pl.ds(pl.multiple_of((z // 2) * cols, cols), cols)
    rest_plane = pl.ds(pl.multiple_of((z // 2) * cols + 2 * cols, cols), cols)
    for f in range(3):
        spec_e, spec_h = [], []
        for part in range(2):
            factor_e = math.cos(phase_e[f]) if part == 0 else -math.sin(phase_e[f])
            factor_h = math.cos(phase_h[f]) if part == 0 else -math.sin(phase_h[f])
            now_e = [dft_e_ref[f, part, c, 0] + e_next[c] * factor_e for c in range(3)]
            now_h = [dft_h_ref[f, part, c, 0] + field_h[c] * factor_h for c in range(3)]
            for c in range(3):
                dft_e_out[f, part, c, 0] = now_e[c]
                dft_h_out[f, part, c, 0] = now_h[c]
            spec_e.append(now_e)
            spec_h.append(now_h)
        for c in range(3):
            a, b = (c + 1) % 3, (c + 2) % 3
            flux = 0.5 * (
                (spec_e[0][a] * spec_h[0][b] - spec_e[0][b] * spec_h[0][a])
                + (spec_e[1][a] * spec_h[1][b] - spec_e[1][b] * spec_h[1][a])
            )
            head = flux.astype(bf16)
            flux_out[3 * f + c, z % 2, :, half_plane] = head
            flux_out[3 * f + c, z % 2, :, rest_plane] = (flux - head.astype(f32)).astype(bf16)
    below_ref[0] = hx
    below_ref[1] = hy


def field_step(e, h, j, kinds, table, dft_e, dft_h, rows_below, cols_left):
    planes, rows, cols = kinds.shape
    plane3 = pl.BlockSpec((3, 1, rows, cols), lambda z: (0, z, 0, 0))
    spectra = pl.BlockSpec((3, 2, 3, 1, rows, cols), lambda z: (0, 0, 0, z, 0, 0))

    def whole(shape):
        return pl.BlockSpec(shape, lambda z: (0,) * len(shape))

    flux_shape = (9, 2, rows, 4 * cols)
    return pl.pallas_call(
        field_kernel,
        grid=(planes,),
        out_shape=(
            jax.ShapeDtypeStruct(e.shape, f32),
            jax.ShapeDtypeStruct(e.shape, f32),
            jax.ShapeDtypeStruct(dft_e.shape, f32),
            jax.ShapeDtypeStruct(dft_h.shape, f32),
            jax.ShapeDtypeStruct(flux_shape, bf16),
        ),
        in_specs=[
            plane3, plane3, plane3,
            pl.BlockSpec((1, rows, cols), lambda z: (z, 0, 0)),
            whole(table.shape), spectra, spectra,
            whole(rows_below.shape), whole(cols_left.shape),
        ],
        out_specs=(plane3, plane3, spectra, spectra, whole(flux_shape)),
        scratch_shapes=[pltpu.VMEM((2, rows, cols), f32), pltpu.VMEM((8, cols), f32)],
        name="field_step",
    )(e, h, j, kinds, table, dft_e, dft_h, rows_below, cols_left)


def gather_kernel(count_ref, cell_ref, table_ref, out_ref, packed, found):
    lane = iota((1, 128), 1)

    def pack(d, carry):
        offset, current = carry
        row, start = lax.shift_right_logical(offset, 7), lax.bitwise_and(offset, 127)
        live = count_ref[0, d]
        rolled = pltpu.roll(cell_ref[0, pl.ds(d, 1), :], start, 1)
        merged = jnp.where(lane >= start, rolled, current)
        packed[pl.ds(row, 1), :] = merged
        return offset + live, jnp.where(start + live >= 128, rolled, merged)

    offset, current = lax.fori_loop(
        0, 128, pack, (jnp.int32(0), jnp.zeros((1, 128), jnp.int32)), unroll=8
    )
    packed[pl.ds(lax.shift_right_logical(offset, 7), 1), :] = current

    def chunk(c, _):
        cell = jnp.concatenate([packed[pl.ds(2 * c, 1), :], packed[pl.ds(2 * c + 1, 1), :]], 1)
        high = lax.bitwise_and(lax.shift_right_logical(cell, 14), 1)
        inner = lax.bitwise_or(lax.shift_left(high, 7), lax.bitwise_and(cell, 127))
        outer = lax.bitwise_and(lax.shift_right_logical(cell, 7), 127)
        onehot = jnp.where(iota((256, 256), 0) == inner, 1.0, 0.0).astype(bf16)
        result = jnp.dot(
            table_ref[...].reshape(1152, 512),
            jnp.concatenate([onehot, onehot], 0),
            preferred_element_type=f32,
        ).reshape(9, 128, 256)
        mine = iota((128, 256), 0) == outer
        for q in range(9):
            value = jnp.sum(jnp.where(mine, result[q], 0.0), axis=0, keepdims=True)
            found[2 * c, q : q + 1, :] = value[:, :128]
            found[2 * c + 1, q : q + 1, :] = value[:, 128:]
        return 0

    lax.fori_loop(0, lax.shift_right_logical(offset + 255, 8), chunk, 0)
    lanes = iota((16, 128), 1)

    def unpack(d, offset):
        row, start = lax.shift_right_logical(offset, 7), lax.bitwise_and(offset, 127)
        live = count_ref[0, d]
        back = lax.bitwise_and(128 - start, 127)
        value = jnp.where(
            lanes < 128 - start, pltpu.roll(found[row], back, 1), pltpu.roll(found[row + 1], back, 1)
        )
        value = jnp.where(lanes < live, value, 0.0)
        for q in range(9):
            out_ref[d, q] = value[q : q + 1, :]
        return offset + live

    lax.fori_loop(0, 128, unpack, jnp.int32(0), unroll=4)


def gather_flux(counts, cells, table):
    return pl.pallas_call(
        gather_kernel,
        out_shape=jax.ShapeDtypeStruct((128, 9, 1, 128), f32),
        in_specs=[SMEM, VMEM, VMEM],
        out_specs=VMEM,
        scratch_shapes=[pltpu.VMEM((136, 128), jnp.int32), pltpu.VMEM((136, 16, 128), f32)],
        name="gather_flux",
    )(counts, cells, table)


def slot_row(ref, c):
    return jnp.concatenate([ref[0, pl.ds(2 * c, 1), :], ref[0, pl.ds(2 * c + 1, 1), :]], 1)


def area_kernel(patch_ref, area_ref, out_ref, table):
    area = area_ref[...].reshape(768, 256)
    head = area.astype(bf16)
    table[:, :256] = head
    table[:, 256:] = (area - head.astype(f32)).astype(bf16)

    def chunk(c, _):
        patch = slot_row(patch_ref, c)
        u, v = lax.shift_right_logical(patch, 8), lax.bitwise_and(patch, 255)
        onehot = jnp.where(iota((256, 256), 0) == v, 1.0, 0.0).astype(bf16)
        result = jnp.dot(
            table[...], jnp.concatenate([onehot, onehot], 0), preferred_element_type=f32
        ).reshape(3, 256, 256)
        mine = iota((256, 256), 0) == u
        for q in range(3):
            out_ref[c, q : q + 1, :] = jnp.sum(
                jnp.where(mine, result[q], 0.0), axis=0, keepdims=True
            )
        return 0

    lax.fori_loop(0, 64, chunk, 0)


def gather_area(patch, area):
    return pl.pallas_call(
        area_kernel,
        out_shape=jax.ShapeDtypeStruct((64, 8, 256), f32),
        in_specs=[VMEM, VMEM],
        out_specs=VMEM,
        scratch_shapes=[pltpu.VMEM((768, 512), bf16)],
        cost_estimate=pl.CostEstimate(
            flops=2 * 768 * 512 * 16384, bytes_accessed=2000000, transcendentals=0
        ),
        name="gather_area",
    )(patch, area)


def scatter_kernel(patch_ref, area_ref, flux_ref, out_ref):
    out_ref[...] = jnp.zeros_like(out_ref)

    def chunk(c, _):
        patch = slot_row(patch_ref, c)
        u, v = lax.shift_right_logical(patch, 8), lax.bitwise_and(patch, 255)
        onehot = jnp.where(iota((256, 256), 0) == v, 1.0, 0.0).astype(bf16)
        mine = iota((256, 256), 0) == u
        area = area_ref[c]
        heads, rests = [], []
        for f in range(3):
            density = jnp.zeros((1, 256), f32)
            for q in range(3):
                flux = jnp.concatenate(
                    [flux_ref[2 * c, 3 * f + q], flux_ref[2 * c + 1, 3 * f + q]], 1
                )
                density = density + area[q : q + 1, :] * flux
            head = density.astype(bf16).astype(f32)
            heads.append(jnp.where(mine, head, 0.0).astype(bf16))
            rests.append(jnp.where(mine, density - head, 0.0).astype(bf16))
        left = jnp.concatenate([jnp.concatenate(heads, 0), jnp.concatenate(rests, 0)], 1)
        right = jnp.concatenate([onehot, onehot], 1)
        out_ref[...] += lax.dot_general(
            left, right, (((1,), (1,)), ((), ())), preferred_element_type=f32
        ).reshape(3, 256, 256)
        return 0

    lax.fori_loop(0, 64, chunk, 0)


def scatter_density(patch, area_rows, flux):
    return pl.pallas_call(
        scatter_kernel,
        out_shape=jax.ShapeDtypeStruct((3, 256, 256), f32),
        in_specs=[VMEM, VMEM, VMEM],
        out_specs=VMEM,
        name="scatter_density",
    )(patch, area_rows, flux)


def shards(
    e_field, h_field, j_field, material, material_table, dft_e, dft_h, skin_cell, counts,
    patch_slot, area,
):
    magnet_x, magnet_y, magnet_z = (h_field[0], h_field[1], h_field[2])
    rows_below = shifted(jnp.stack([magnet_y[:, -1, :], magnet_z[:, -1, :]]), "gy", 1)
    cols_left = shifted(jnp.stack([magnet_x[:, :, -1], magnet_z[:, :, -1]]), "gx", 1)
    e_next, j_next, dft_e_next, dft_h_next, table = field_step(
        e_field, h_field, j_field, material, material_table, dft_e, dft_h, rows_below, cols_left
    )
    rows = gather_flux(counts, skin_cell, table.reshape(9, 128, 512))
    arrived = lax.all_to_all(rows, ("gy", "gx"), split_axis=0, concat_axis=0, tiled=True)
    area_rows = gather_area(patch_slot, area)
    point_density = scatter_density(patch_slot, area_rows, arrived)
    padded = with_halo(point_density, (("gy", 1),), HALF)
    strip_sum = jnp.einsum(
        "ij,fjv->fiv",
        band_matrix(256, HALF),
        padded,
        precision=lax.Precision.HIGHEST,
        preferred_element_type=f32,
    )
    padded_cols = with_halo(strip_sum, (("gx", 2),), HALF)
    square_sum = jnp.einsum(
        "fuj,ij->fui",
        padded_cols,
        band_matrix(256, HALF),
        precision=lax.Precision.HIGHEST,
        preferred_element_type=f32,
    )
    avg_density = square_sum / (4.0 * HALF * HALF)
    return (e_next, j_next, dft_e_next, dft_h_next, point_density, avg_density)


def solution(mesh):
    placed = (
        P(None, None, "gy", "gx"),
        P(None, None, "gy", "gx"),
        P(None, None, "gy", "gx"),
        P(None, "gy", "gx"),
        P(),
        P(None, None, None, None, "gy", "gx"),
        P(None, None, None, None, "gy", "gx"),
        P(("gy", "gx"), None, None),
        P(("gy", "gx"), None),
        P(("gy", "gx"), None, None),
        P(None, "gy", "gx"),
    )
    return jax.shard_map(
        shards,
        mesh=mesh,
        in_specs=placed,
        out_specs=(
            P(None, None, "gy", "gx"),
            P(None, None, "gy", "gx"),
            P(None, None, None, None, "gy", "gx"),
            P(None, None, None, None, "gy", "gx"),
            P(None, "gy", "gx"),
            P(None, "gy", "gx"),
        ),
        check_vma=False,
    )
```

time: 1300 us -> 138 us (0.11)
  local copies, waits for them, and re-layouts: 872 us -> 4.91 us
  other arithmetic: 273 us -> 0.02 us
  Pallas kernels: 0 us -> 77.4 us
  matrix products: 61.9 us -> 4.85 us
  waiting for transfers between devices: 46.4 us -> 18.6 us
    gather x64 -> x0, local copies, waits for them, and re-layouts: 742 us -> none  [one_block(): jnp.take(table, hi_block, axis=0).reshape(block_len, row_count, lo_width)]
    reduce_sum x32 -> x0, other arithmetic: 182 us -> none  [one_block(): return jnp.sum(jnp.where(chosen, rows, 0.0), axis=2)]
    pallas_call x0 -> x4, Pallas kernels: none -> 77.4 us  [the longest x1 28 us: scatter_density(): pl.pallas_call(scatter_kernel, out_shape=jax.ShapeDtypeStruct((3, 256, 25...]
    dot_general x11 -> x2, matrix products: 61.9 us -> 4.85 us  [the longest x1 2.55 us: shards(): jnp.einsum('ij,fjv->fiv', band_matrix(256, HALF), padded, precision=lax.P...]
    mul x10 -> x0, other arithmetic: 35.7 us -> none  [the longest x8 34.4 us: add_block(): part_block[:, :, :, None] * lo_table[:, None, None, :]]
    unnamed x83 -> x9, local copies, waits for them, and re-layouts: 36.6 us -> 2.38 us
    dynamic_update_slice x48 -> x0, local copies, waits for them, and re-layouts: 32.2 us -> none  [pick_rows(): picked = lax.map(one_block, (hi_ids, lo_ids))]
    all_to_all x1, waiting for transfers between devices: 32.2 us -> 0.01 us  [shards(): lax.all_to_all(rows, ('gy', 'gx'), split_axis=0, concat_axis=0, tiled=True)]
  transfers between devices with their start and end apart: 7 -> 7, of which waited for: 5 -> 5; matrix products, arithmetic and copies ran while one was open for 20% -> 0% of each run, Pallas kernels for 0% -> 19%
where the time goes in v1:
time: 138 us
  Pallas kernels  77.4 us (56%)
  starting transfers between devices  31.1 us (23%)
  waiting for transfers between devices  18.6 us (13%)
  local copies, waits for them, and re-layouts  4.91 us (4%)
  matrix products  4.85 us (4%)
    pallas_call x1, Pallas kernels, scatter_density(): pl.pallas_call(scatter_kernel, out_shape=jax.ShapeDtypeStruct((3, 256, 25...  28 us
    pallas_call x1, Pallas kernels, gather_area(): pl.pallas_call(area_kernel, out_shape=jax.ShapeDtypeStruct((64, 8, 256),...  26.6 us
    pallas_call x1, Pallas kernels, gather_flux(): pl.pallas_call(gather_kernel, out_shape=jax.ShapeDtypeStruct((128, 9, 1,...  15.9 us
    all_to_all x1, starting transfers between devices, shards(): lax.all_to_all(rows, ('gy', 'gx'), split_axis=0, concat_axis=0, tiled=True)  11.7 us
    ppermute x2, waiting for transfers between devices, with_halo(): lax.ppermute(head, axis, [((i + 1) % count, i) for i in range(ends)])  8.73 us
    ppermute x2, waiting for transfers between devices, with_halo(): lax.ppermute(tail, axis, [(i, (i + 1) % count) for i in range(ends)])  8.1 us
    ppermute x2, starting transfers between devices, with_halo(): lax.ppermute(head, axis, [((i + 1) % count, i) for i in range(ends)])  7.58 us
    pallas_call x1, Pallas kernels, field_step(): pl.pallas_call(field_kernel, grid=(planes,), out_shape=(jax.ShapeDtypeStr...  6.84 us
  transfers between devices with their start and end apart: 7, of which 5 were waited for; matrix products, arithmetic and copies ran while one was open for 0% of the time, Pallas kernels for 19%

profile of v1, /device:TPU:26, one launch (start us, length us, event | category | flops | bytes accessed | tf_op | source)
XLA Modules:
  0.0 137.6 jit_solution(4602660948390939907)
XLA Ops:
  0.6 1.1 fusion.28
  2.0 0.2 slice.45
  2.3 1.9 %collective-permute-start = (f32[2,4,128]{2,1,0:T(4,128)S(1)}, f32[2,4,128]{2,1,0:T(4,128)S(1)}, u32[]{:S(2)}, u32[]{:S(2)}) collective-permute-start(f32[2,4,128]{2,1,0:T(4,128)S(1)} %pad_maximum_fusion), channel_id=1, source_target_pairs={{0,8},{8,16},{16,24},{24,32},{32,40},{40,48},{48,56},{56,64},{64,7... | collective-permute-start | bytes 12296 | tf_op jit(solution)/shard_map/ppermute | solution.py:33
  4.4 3.7 %collective-permute-start.1 = (f32[2,4,64]{2,1,0:T(4,128)S(1)}, f32[2,4,64]{2,1,0:T(4,128)S(1)}, u32[]{:S(2)}, u32[]{:S(2)}) collective-permute-start(f32[2,4,64]{2,1,0:T(4,128)S(1)} %pad_maximum_fusion.1), channel_id=1, source_target_pairs={{0,1},{1,2},{2,3},{3,4},{4,5},{5,6},{6,7},{8,9},{9,10},{10,11},{11... | collective-permute-start | bytes 6152 | tf_op jit(solution)/shard_map/ppermute | solution.py:33
  8.1 1.8 %collective-permute-done.1.col_ref = f32[2,4,64]{2,1,0:T(4,128)S(1)} collective-permute-done((f32[2,4,64]{2,1,0:T(4,128)S(1)}, f32[2,4,64]{2,1,0:T(4,128)S(1)}, u32[]{:S(2)}, u32[]{:S(2)}) %collective-permute-start.1) | collective-permute-done | bytes 2080 | tf_op jit(solution)/shard_map/ppermute | solution.py:33
  9.9 0.6 copy-done.2
  10.5 0.6 copy-done.1
  11.1 6.8 %field_step.1 = (f32[3,4,64,128]{3,2,1,0:T(8,128)}, f32[3,4,64,128]{3,2,1,0:T(8,128)}, f32[3,2,3,4,64,128]{5,4,3,2,1,0:T(8,128)}, f32[3,2,3,4,64,128]{5,4,3,2,1,0:T(8,128)}, bf16[9,2,64,512]{3,2,1,0:T(8,128)(2,1)}) custom-call(f32[3,4,64,128]{3,2,1,0:T(8,128)} %e_ref.1, f32[3,4,64,128]{3,2,1,0:T(8,128)} %h_ref.1, f32[3,4,64,128]{3,2,1,0:T(8,128)} %j_ref.1, ...), custom_call_target="tpu_custom_call" | custom-call | tf_op jit(solution)/shard_map/field_step/pallas_call | solution.py:143
  17.9 15.9 %gather_flux.1 = f32[128,9,1,128]{3,2,1,0:T(1,128)} custom-call(s32[1,128]{1,0:T(1,128)} %count_ref.1, s32[1,128,128]{2,1,0:T(8,128)} %cell_ref.1, bf16[9,128,512]{2,1,0:T(8,128)(2,1)} %bitcast.19), custom_call_target="tpu_custom_call" | custom-call | tf_op jit(solution)/shard_map/gather_flux/pallas_call | solution.py:219
  33.9 11.7 %all-to-all-start = ((f32[128,9,1,128]{3,2,1,0:T(1,128)}), f32[128,9,1,128]{3,2,1,0:T(1,128)S(1)}, u32[]{:S(2)}, u32[]{:S(2)}) async-start(f32[128,9,1,128]{3,2,1,0:T(1,128)} %gather_flux.1), calls=%async_computation | async-start | bytes 1179648 | tf_op jit(solution)/shard_map/all_to_all | solution.py:321
  45.6 26.6 %gather_area.1.area_ref = f32[64,8,256]{2,1,0:T(8,128)} custom-call(s32[1,128,128]{2,1,0:T(8,128)} %patch_ref.3, f32[3,256,256]{2,1,0:T(8,128)} %area_ref.1), custom_call_target="tpu_custom_call" | custom-call | flops 12884901888 | bytes 2000000 | tf_op jit(solution)/shard_map/gather_area/pallas_call | solution.py:257
  72.2 0.8 copy-done
  73.0 28.0 %scatter_density.1 = f32[3,256,256]{2,1,0:T(8,128)} custom-call(s32[1,128,128]{2,1,0:T(8,128)} %patch_ref.3, f32[64,8,256]{2,1,0:T(8,128)} %gather_area.1.area_ref, f32[128,9,1,128]{3,2,1,0:T(1,128)} %copy-done), custom_call_target="tpu_custom_call" | custom-call | tf_op jit(solution)/shard_map/scatter_density/pallas_call | solution.py:301
  101.0 1.1 fusion.27
  102.2 2.0 %collective-permute-start.2 = (f32[3,100,256]{2,1,0:T(8,128)S(1)}, f32[3,100,256]{2,1,0:T(8,128)S(1)}, u32[]{:S(2)}, u32[]{:S(2)}) collective-permute-start(f32[3,100,256]{2,1,0:T(8,128)S(1)} %get-tuple-element.18), channel_id=1, source_target_pairs={{0,8},{8,16},{16,24},{24,32},{32,40},{40,48},{48,56},{56,64},{64,7... | collective-permute-start | bytes 921608 | tf_op jit(solution)/shard_map/ppermute | solution.py:44
  104.2 5.7 %collective-permute-start.3 = (f32[3,100,256]{2,1,0:T(8,128)S(1)}, f32[3,100,256]{2,1,0:T(8,128)S(1)}, u32[]{:S(2)}, u32[]{:S(2)}) collective-permute-start(f32[3,100,256]{2,1,0:T(8,128)S(1)} %get-tuple-element.19), channel_id=1, source_target_pairs={{8,0},{16,8},{24,16},{32,24},{40,32},{48,40},{56,48},{64,56},{72,6... | collective-permute-start | bytes 921608 | tf_op jit(solution)/shard_map/ppermute | solution.py:46
  109.9 2.7 %collective-permute-done.2 = f32[3,100,256]{2,1,0:T(8,128)S(1)} collective-permute-done((f32[3,100,256]{2,1,0:T(8,128)S(1)}, f32[3,100,256]{2,1,0:T(8,128)S(1)}, u32[]{:S(2)}, u32[]{:S(2)}) %collective-permute-start.2) | collective-permute-done | bytes 307232 | tf_op jit(solution)/shard_map/ppermute | solution.py:44
  112.6 1.8 %collective-permute-done.3 = f32[3,100,256]{2,1,0:T(8,128)S(1)} collective-permute-done((f32[3,100,256]{2,1,0:T(8,128)S(1)}, f32[3,100,256]{2,1,0:T(8,128)S(1)}, u32[]{:S(2)}, u32[]{:S(2)}) %collective-permute-start.3) | collective-permute-done | bytes 307232 | tf_op jit(solution)/shard_map/ppermute | solution.py:46
  114.3 2.6 %fusion.12 = f32[3,256,256]{1,2,0:T(8,128)S(1)} fusion(f32[3,100,256]{2,1,0:T(8,128)S(1)} %collective-permute-done.3, f32[3,256,256]{2,1,0:T(8,128)} %scatter_density.1, f32[3,100,256]{2,1,0:T(8,128)S(1)} %collective-permute-done.2, s32[256]{0:T(256)S(1)} %iota_add_fusion), kind=kOutput, calls=%fused_computation.12 | convolution fusion | flops 1076889600 | bytes 2188288 | tf_op jit(solution)/shard_map/ij,fjv->fiv/dot_general | solution.py:325
  116.9 4.1 %collective-permute-start.4 = (f32[3,256,100]{1,2,0:T(8,128)S(1)}, f32[3,256,100]{1,2,0:T(8,128)S(1)}, u32[]{:S(2)}, u32[]{:S(2)}) collective-permute-start(f32[3,256,100]{1,2,0:T(8,128)S(1)} %get-tuple-element.16), channel_id=1, source_target_pairs={{0,1},{1,2},{2,3},{3,4},{4,5},{5,6},{6,7},{8,9},{9,10},{10,11},{11... | collective-permute-start | bytes 921608 | tf_op jit(solution)/shard_map/ppermute | solution.py:44
  121.0 1.9 %collective-permute-start.5 = (f32[3,256,100]{1,2,0:T(8,128)S(1)}, f32[3,256,100]{1,2,0:T(8,128)S(1)}, u32[]{:S(2)}, u32[]{:S(2)}) collective-permute-start(f32[3,256,100]{1,2,0:T(8,128)S(1)} %get-tuple-element.17), channel_id=1, source_target_pairs={{1,0},{2,1},{3,2},{4,3},{5,4},{6,5},{7,6},{9,8},{10,9},{11,10},{12... | collective-permute-start | bytes 921608 | tf_op jit(solution)/shard_map/ppermute | solution.py:46
  123.0 5.4 %collective-permute-done.4 = f32[3,256,100]{1,2,0:T(8,128)S(1)} collective-permute-done((f32[3,256,100]{1,2,0:T(8,128)S(1)}, f32[3,256,100]{1,2,0:T(8,128)S(1)}, u32[]{:S(2)}, u32[]{:S(2)}) %collective-permute-start.4) | collective-permute-done | bytes 307232 | tf_op jit(solution)/shard_map/ppermute | solution.py:44
  128.4 7.0 %collective-permute-done.5 = f32[3,256,100]{1,2,0:T(8,128)S(1)} collective-permute-done((f32[3,256,100]{1,2,0:T(8,128)S(1)}, f32[3,256,100]{1,2,0:T(8,128)S(1)}, u32[]{:S(2)}, u32[]{:S(2)}) %collective-permute-start.5) | collective-permute-done | bytes 307232 | tf_op jit(solution)/shard_map/ppermute | solution.py:46
  135.3 2.3 %fusion.15 = f32[3,256,256]{2,1,0:T(8,128)} fusion(f32[3,256,100]{1,2,0:T(8,128)S(1)} %collective-permute-done.5, f32[3,256,256]{1,2,0:T(8,128)S(1)} %fusion.12, f32[3,256,100]{1,2,0:T(8,128)S(1)} %collective-permute-done.4, s32[256]{0:T(256)S(1)} %iota_add_fusion), kind=kOutput, calls=%fused_computation.13 | convolution fusion | flops 1077086208 | bytes 2188288 | tf_op jit(solution)/shard_map/fuj,ij->fui/dot_general | solution.py:333
  (15 shorter events, 0.6 us)
Async XLA Ops:
  2.3 7.6 %collective-permute-start = (f32[2,4,128]{2,1,0:T(4,128)S(1)}, f32[2,4,128]{2,1,0:T(4,128)S(1)}, u32[]{:S(2)}, u32[]{:S(2)}) collective-permute-start(f32[2,4,128]{2,1,0:T(4,128)S(1)} %pad_maximum_fusion), channel_id=1, source_target_pairs={{0,8},{8,16},{16,24},{24,32},{32,40},{40,48},{48,56},{56,64},{64,7... | collective-permute-start | bytes 12296 | tf_op jit(solution)/shard_map/ppermute | solution.py:33
  4.4 5.5 %collective-permute-start.1 = (f32[2,4,64]{2,1,0:T(4,128)S(1)}, f32[2,4,64]{2,1,0:T(4,128)S(1)}, u32[]{:S(2)}, u32[]{:S(2)}) collective-permute-start(f32[2,4,64]{2,1,0:T(4,128)S(1)} %pad_maximum_fusion.1), channel_id=1, source_target_pairs={{0,1},{1,2},{2,3},{3,4},{4,5},{5,6},{6,7},{8,9},{9,10},{10,11},{11... | collective-permute-start | bytes 6152 | tf_op jit(solution)/shard_map/ppermute | solution.py:33
  9.9 0.6 copy-start.2
  10.5 0.6 copy-start.1
  33.9 38.3 %all-to-all-start = ((f32[128,9,1,128]{3,2,1,0:T(1,128)}), f32[128,9,1,128]{3,2,1,0:T(1,128)S(1)}, u32[]{:S(2)}, u32[]{:S(2)}) async-start(f32[128,9,1,128]{3,2,1,0:T(1,128)} %gather_flux.1), calls=%async_computation | async-start | bytes 1179648 | tf_op jit(solution)/shard_map/all_to_all | solution.py:321
  72.2 0.8 copy-start
  102.2 10.4 %collective-permute-start.2 = (f32[3,100,256]{2,1,0:T(8,128)S(1)}, f32[3,100,256]{2,1,0:T(8,128)S(1)}, u32[]{:S(2)}, u32[]{:S(2)}) collective-permute-start(f32[3,100,256]{2,1,0:T(8,128)S(1)} %get-tuple-element.18), channel_id=1, source_target_pairs={{0,8},{8,16},{16,24},{24,32},{32,40},{40,48},{48,56},{56,64},{64,7... | collective-permute-start | bytes 921608 | tf_op jit(solution)/shard_map/ppermute | solution.py:44
  104.2 10.2 %collective-permute-start.3 = (f32[3,100,256]{2,1,0:T(8,128)S(1)}, f32[3,100,256]{2,1,0:T(8,128)S(1)}, u32[]{:S(2)}, u32[]{:S(2)}) collective-permute-start(f32[3,100,256]{2,1,0:T(8,128)S(1)} %get-tuple-element.19), channel_id=1, source_target_pairs={{8,0},{16,8},{24,16},{32,24},{40,32},{48,40},{56,48},{64,56},{72,6... | collective-permute-start | bytes 921608 | tf_op jit(solution)/shard_map/ppermute | solution.py:46
  116.9 11.4 %collective-permute-start.4 = (f32[3,256,100]{1,2,0:T(8,128)S(1)}, f32[3,256,100]{1,2,0:T(8,128)S(1)}, u32[]{:S(2)}, u32[]{:S(2)}) collective-permute-start(f32[3,256,100]{1,2,0:T(8,128)S(1)} %get-tuple-element.16), channel_id=1, source_target_pairs={{0,1},{1,2},{2,3},{3,4},{4,5},{5,6},{6,7},{8,9},{9,10},{10,11},{11... | collective-permute-start | bytes 921608 | tf_op jit(solution)/shard_map/ppermute | solution.py:44
  121.0 14.3 %collective-permute-start.5 = (f32[3,256,100]{1,2,0:T(8,128)S(1)}, f32[3,256,100]{1,2,0:T(8,128)S(1)}, u32[]{:S(2)}, u32[]{:S(2)}) collective-permute-start(f32[3,256,100]{1,2,0:T(8,128)S(1)} %get-tuple-element.17), channel_id=1, source_target_pairs={{1,0},{2,1},{3,2},{4,3},{5,4},{6,5},{7,6},{9,8},{10,9},{11,10},{12... | collective-permute-start | bytes 921608 | tf_op jit(solution)/shard_map/ppermute | solution.py:46

commit v2 on v1

--- a/solution.py
+++ b/solution.py
@@ -33,27 +33,9 @@
     return lax.ppermute(value, axis, [(source, source + steps) for source in range(leading, last)])
 
 
-def with_halo(cells, sides, width):
-    for axis, dim in sides:
-        count = lax.axis_size(axis)
-        ends = count - 1
-        head = lax.slice_in_dim(cells, 0, width, axis=dim)
-        tail = lax.slice_in_dim(cells, cells.shape[dim] - width, cells.shape[dim], axis=dim)
-        cells = jnp.concatenate(
-            [
-                lax.ppermute(tail, axis, [(i, (i + 1) % count) for i in range(ends)]),
-                cells,
-                lax.ppermute(head, axis, [((i + 1) % count, i) for i in range(ends)]),
-            ],
-            axis=dim,
-        )
-    return cells
-
-
-def band_matrix(count, half_width):
-    row_ids = iota((count, count + 2 * half_width), 0)
-    col_ids = iota((count, count + 2 * half_width), 1)
-    return ((col_ids >= row_ids) & (col_ids < row_ids + 2 * half_width)).astype(f32)
+def onehot(count, index):
+    places = iota((count, index.shape[1]), 0).astype(bf16)
+    return jnp.where(places == index.astype(bf16), jnp.ones((), bf16), jnp.zeros((), bf16))
 
 
 def field_kernel(
@@ -175,19 +157,19 @@
         return offset + live, jnp.where(start + live >= 128, rolled, merged)
 
     offset, current = lax.fori_loop(
-        0, 128, pack, (jnp.int32(0), jnp.zeros((1, 128), jnp.int32)), unroll=8
+        0, 128, pack, (jnp.int32(0), jnp.zeros((1, 128), jnp.int32)), unroll=32
     )
     packed[pl.ds(lax.shift_right_logical(offset, 7), 1), :] = current
 
-    def chunk(c, _):
+    def lookup(c):
         cell = jnp.concatenate([packed[pl.ds(2 * c, 1), :], packed[pl.ds(2 * c + 1, 1), :]], 1)
         high = lax.bitwise_and(lax.shift_right_logical(cell, 14), 1)
         inner = lax.bitwise_or(lax.shift_left(high, 7), lax.bitwise_and(cell, 127))
         outer = lax.bitwise_and(lax.shift_right_logical(cell, 7), 127)
-        onehot = jnp.where(iota((256, 256), 0) == inner, 1.0, 0.0).astype(bf16)
+        hot = onehot(256, inner)
         result = jnp.dot(
             table_ref[...].reshape(1152, 512),
-            jnp.concatenate([onehot, onehot], 0),
+            jnp.concatenate([hot, hot], 0),
             preferred_element_type=f32,
         ).reshape(9, 128, 256)
         mine = iota((128, 256), 0) == outer
@@ -195,9 +177,13 @@
             value = jnp.sum(jnp.where(mine, result[q], 0.0), axis=0, keepdims=True)
             found[2 * c, q : q + 1, :] = value[:, :128]
             found[2 * c + 1, q : q + 1, :] = value[:, 128:]
+
+    def chunk(c, _):
+        for part in range(4):
+            lookup(4 * c + part)
         return 0
 
-    lax.fori_loop(0, lax.shift_right_logical(offset + 255, 8), chunk, 0)
+    lax.fori_loop(0, lax.shift_right_logical(offset + 1023, 10), chunk, 0)
     lanes = iota((16, 128), 1)
 
     def unpack(d, offset):
@@ -212,7 +198,7 @@
             out_ref[d, q] = value[q : q + 1, :]
         return offset + live
 
-    lax.fori_loop(0, 128, unpack, jnp.int32(0), unroll=4)
+    lax.fori_loop(0, 128, unpack, jnp.int32(0), unroll=16)
 
 
 def gather_flux(counts, cells, table):
@@ -226,85 +212,144 @@
     )(counts, cells, table)
 
 
+GROUP = 8
+
+
 def slot_row(ref, c):
-    return jnp.concatenate([ref[0, pl.ds(2 * c, 1), :], ref[0, pl.ds(2 * c + 1, 1), :]], 1)
-
-
-def area_kernel(patch_ref, area_ref, out_ref, table):
+    return jnp.concatenate([ref[0, pl.ds(GROUP * c + i, 1), :] for i in range(GROUP)], 1)
+
+
+def area_kernel(patch_ref, area_ref, out_ref, table, *, first):
     area = area_ref[...].reshape(768, 256)
     head = area.astype(bf16)
     table[:, :256] = head
     table[:, 256:] = (area - head.astype(f32)).astype(bf16)
 
     def chunk(c, _):
-        patch = slot_row(patch_ref, c)
+        patch = slot_row(patch_ref, c + first)
         u, v = lax.shift_right_logical(patch, 8), lax.bitwise_and(patch, 255)
-        onehot = jnp.where(iota((256, 256), 0) == v, 1.0, 0.0).astype(bf16)
+        hot = onehot(256, v)
         result = jnp.dot(
-            table[...], jnp.concatenate([onehot, onehot], 0), preferred_element_type=f32
-        ).reshape(3, 256, 256)
-        mine = iota((256, 256), 0) == u
+            table[...], jnp.concatenate([hot, hot], 0), preferred_element_type=f32
+        ).reshape(3, 256, GROUP * 128)
+        mine = iota((256, GROUP * 128), 0) == u
         for q in range(3):
             out_ref[c, q : q + 1, :] = jnp.sum(
                 jnp.where(mine, result[q], 0.0), axis=0, keepdims=True
             )
         return 0
 
-    lax.fori_loop(0, 64, chunk, 0)
-
-
-def gather_area(patch, area):
+    lax.fori_loop(0, out_ref.shape[0], chunk, 0, unroll=4)
+
+
+def gather_area(patch, area, first, groups):
     return pl.pallas_call(
-        area_kernel,
-        out_shape=jax.ShapeDtypeStruct((64, 8, 256), f32),
+        functools.partial(area_kernel, first=first),
+        out_shape=jax.ShapeDtypeStruct((groups, 8, GROUP * 128), f32),
         in_specs=[VMEM, VMEM],
         out_specs=VMEM,
         scratch_shapes=[pltpu.VMEM((768, 512), bf16)],
         cost_estimate=pl.CostEstimate(
-            flops=2 * 768 * 512 * 16384, bytes_accessed=2000000, transcendentals=0
+            flops=2 * 768 * 512 * GROUP * 128 * groups, bytes_accessed=2000000, transcendentals=0
         ),
         name="gather_area",
     )(patch, area)
 
 
-def scatter_kernel(patch_ref, area_ref, flux_ref, out_ref):
+EDGE = 104
+
+
+def scatter_kernel(patch_ref, area_a_ref, area_b_ref, flux_ref, out_ref, head_ref, tail_ref):
     out_ref[...] = jnp.zeros_like(out_ref)
 
-    def chunk(c, _):
+    def add_group(c, area):
         patch = slot_row(patch_ref, c)
         u, v = lax.shift_right_logical(patch, 8), lax.bitwise_and(patch, 255)
-        onehot = jnp.where(iota((256, 256), 0) == v, 1.0, 0.0).astype(bf16)
-        mine = iota((256, 256), 0) == u
-        area = area_ref[c]
+        hot = onehot(256, v)
+        mine = iota((256, GROUP * 128), 0).astype(bf16) == u.astype(bf16)
         heads, rests = [], []
         for f in range(3):
-            density = jnp.zeros((1, 256), f32)
+            density = jnp.zeros((1, GROUP * 128), f32)
             for q in range(3):
                 flux = jnp.concatenate(
-                    [flux_ref[2 * c, 3 * f + q], flux_ref[2 * c + 1, 3 * f + q]], 1
+                    [flux_ref[GROUP * c + i, 3 * f + q] for i in range(GROUP)], 1
                 )
                 density = density + area[q : q + 1, :] * flux
-            head = density.astype(bf16).astype(f32)
-            heads.append(jnp.where(mine, head, 0.0).astype(bf16))
-            rests.append(jnp.where(mine, density - head, 0.0).astype(bf16))
+            head = density.astype(bf16)
+            rest = (density - head.astype(f32)).astype(bf16)
+            heads.append(jnp.where(mine, head, jnp.zeros((), bf16)))
+            rests.append(jnp.where(mine, rest, jnp.zeros((), bf16)))
         left = jnp.concatenate([jnp.concatenate(heads, 0), jnp.concatenate(rests, 0)], 1)
-        right = jnp.concatenate([onehot, onehot], 1)
+        right = jnp.concatenate([hot, hot], 1)
         out_ref[...] += lax.dot_general(
             left, right, (((1,), (1,)), ((), ())), preferred_element_type=f32
         ).reshape(3, 256, 256)
+
+    half = area_a_ref.shape[0]
+
+    def first_half(c, _):
+        add_group(c, area_a_ref[c])
         return 0
 
-    lax.fori_loop(0, 64, chunk, 0)
-
-
-def scatter_density(patch, area_rows, flux):
+    def second_half(c, _):
+        add_group(c + half, area_b_ref[c])
+        return 0
+
+    lax.fori_loop(0, half, first_half, 0, unroll=4)
+    lax.fori_loop(0, area_b_ref.shape[0], second_half, 0, unroll=4)
+    head_ref[...] = out_ref[:, :EDGE, :]
+    tail_ref[...] = out_ref[:, 256 - EDGE :, :]
+
+
+BLOCK_AND_EDGES = (
+    jax.ShapeDtypeStruct((3, 256, 256), f32),
+    jax.ShapeDtypeStruct((3, EDGE, 256), f32),
+    jax.ShapeDtypeStruct((3, EDGE, 256), f32),
+)
+
+
+def scatter_density(patch, area_a, area_b, flux):
     return pl.pallas_call(
         scatter_kernel,
-        out_shape=jax.ShapeDtypeStruct((3, 256, 256), f32),
-        in_specs=[VMEM, VMEM, VMEM],
-        out_specs=VMEM,
+        out_shape=BLOCK_AND_EDGES,
+        in_specs=[VMEM] * 4,
+        out_specs=(VMEM,) * 3,
         name="scatter_density",
-    )(patch, area_rows, flux)
+    )(patch, area_a, area_b, flux)
+
+
+def window_kernel(block_ref, before_ref, after_ref, out_ref, *edges, scale):
+    cells = jnp.concatenate([before_ref[0], block_ref[0], after_ref[0]], 0)
+    length = cells.shape[0]
+    place = iota((length, 256), 0) - EDGE - iota((length, 256), 1)
+    band = jnp.where((place >= -HALF) & (place < HALF), 1.0, 0.0).astype(bf16)
+    head = cells.astype(bf16)
+    rest = (cells - head.astype(f32)).astype(bf16)
+    total = lax.dot_general(
+        jnp.concatenate([head, rest], 0),
+        jnp.concatenate([band, band], 0),
+        (((0,), (0,)), ((), ())),
+        preferred_element_type=f32,
+    )
+    if scale != 1.0:
+        total = total * scale
+    out_ref[0] = total
+    if edges:
+        edges[0][0] = total[:EDGE]
+        edges[1][0] = total[256 - EDGE :]
+
+
+def window_sum(block, before, after, scale, with_edges):
+    whole = pl.BlockSpec((1, 256, 256), lambda f: (f, 0, 0))
+    edge = pl.BlockSpec((1, EDGE, 256), lambda f: (f, 0, 0))
+    return pl.pallas_call(
+        functools.partial(window_kernel, scale=scale),
+        grid=(3,),
+        out_shape=BLOCK_AND_EDGES if with_edges else BLOCK_AND_EDGES[:1],
+        in_specs=[whole, edge, edge],
+        out_specs=(whole, edge, edge) if with_edges else (whole,),
+        name="window_sum",
+    )(block, before, after)
 
 
 def shards(
@@ -314,30 +359,19 @@
     magnet_x, magnet_y, magnet_z = (h_field[0], h_field[1], h_field[2])
     rows_below = shifted(jnp.stack([magnet_y[:, -1, :], magnet_z[:, -1, :]]), "gy", 1)
     cols_left = shifted(jnp.stack([magnet_x[:, :, -1], magnet_z[:, :, -1]]), "gx", 1)
+    area_a = gather_area(patch_slot, area, 0, 8)
+    rows_below, cols_left, area_a = lax.optimization_barrier((rows_below, cols_left, area_a))
     e_next, j_next, dft_e_next, dft_h_next, table = field_step(
         e_field, h_field, j_field, material, material_table, dft_e, dft_h, rows_below, cols_left
     )
     rows = gather_flux(counts, skin_cell, table.reshape(9, 128, 512))
     arrived = lax.all_to_all(rows, ("gy", "gx"), split_axis=0, concat_axis=0, tiled=True)
-    area_rows = gather_area(patch_slot, area)
-    point_density = scatter_density(patch_slot, area_rows, arrived)
-    padded = with_halo(point_density, (("gy", 1),), HALF)
-    strip_sum = jnp.einsum(
-        "ij,fjv->fiv",
-        band_matrix(256, HALF),
-        padded,
-        precision=lax.Precision.HIGHEST,
-        preferred_element_type=f32,
-    )
-    padded_cols = with_halo(strip_sum, (("gx", 2),), HALF)
-    square_sum = jnp.einsum(
-        "fuj,ij->fui",
-        padded_cols,
-        band_matrix(256, HALF),
-        precision=lax.Precision.HIGHEST,
-        preferred_element_type=f32,
-    )
-    avg_density = square_sum / (4.0 * HALF * HALF)
+    area_b = gather_area(patch_slot, area, 8, 8)
+    point_density, head, tail = scatter_density(patch_slot, area_a, area_b, arrived)
+    before, after = shifted(tail, "gy", 1), shifted(head, "gy", -1)
+    strip_sum, head, tail = window_sum(point_density, before, after, 1.0, True)
+    before, after = shifted(tail, "gx", 1), shifted(head, "gx", -1)
+    (avg_density,) = window_sum(strip_sum, before, after, 1.0 / (4.0 * HALF * HALF), False)
     return (e_next, j_next, dft_e_next, dft_h_next, point_density, avg_density)
 
 

time: 138 us -> 118 us (0.86)
  Pallas kernels: 77.4 us -> 61.6 us
  matrix products: 4.85 us -> 0 us
    ppermute x4 -> x0, waiting for transfers between devices: 16.8 us -> none  [the longest x2 8.73 us: with_halo(): lax.ppermute(head, axis, [((i + 1) % count, i) for i in range(ends)])]
    ppermute x2 -> x6, waiting for transfers between devices: 1.8 us -> 16.7 us  [shifted(): lax.ppermute(value, axis, [(source, source + steps) for source in range(l...]
    ppermute x2 -> x6, starting transfers between devices: 5.63 us -> 20 us  [shifted(): lax.ppermute(value, axis, [(source, source + steps) for source in range(l...]
    ppermute x4 -> x0, starting transfers between devices: 13.7 us -> none  [the longest x2 7.58 us: with_halo(): lax.ppermute(head, axis, [((i + 1) % count, i) for i in range(ends)])]
    pallas_call x2 -> x5, Pallas kernels: 54.6 us -> 42.3 us  [the longest x2 18.9 us: gather_area(): pl.pallas_call(functools.partial(area_kernel, first=first), out_shape=jax...]
    dot_general x2 -> x0, matrix products: 4.85 us -> none  [the longest x1 2.55 us: shards(): jnp.einsum('ij,fjv->fiv', band_matrix(256, HALF), padded, precision=lax.P...]
    pallas_call x1, Pallas kernels: 15.9 us -> 12.5 us  [gather_flux(): pl.pallas_call(gather_kernel, out_shape=jax.ShapeDtypeStruct((128, 9, 1,...]
    all_to_all x1, waiting for transfers between devices: 0.01 us -> 2.28 us  [shards(): lax.all_to_all(rows, ('gy', 'gx'), split_axis=0, concat_axis=0, tiled=True)]
  transfers between devices with their start and end apart: 7 -> 7, of which waited for: 5 -> 5; matrix products, arithmetic and copies ran while one was open for 0% -> 0% of each run, Pallas kernels for 19% -> 16%
where the time goes in v2:
time: 118 us; the launch traced here: 117 us
  Pallas kernels  61.6 us (52%)
  starting transfers between devices  30.9 us (26%)
  waiting for transfers between devices  19 us (16%)
  local copies, waits for them, and re-layouts  5.19 us (4%)
    ppermute x6, starting transfers between devices, shifted(): lax.ppermute(value, axis, [(source, source + steps) for source in range(l...  20 us
    pallas_call x2, Pallas kernels, gather_area(): pl.pallas_call(functools.partial(area_kernel, first=first), out_shape=jax...  18.9 us
    ppermute x6, waiting for transfers between devices, shifted(): lax.ppermute(value, axis, [(source, source + steps) for source in range(l...  16.7 us
    pallas_call x1, Pallas kernels, scatter_density(): pl.pallas_call(scatter_kernel, out_shape=BLOCK_AND_EDGES, in_specs=[VMEM]...  16.2 us
    pallas_call x1, Pallas kernels, gather_flux(): pl.pallas_call(gather_kernel, out_shape=jax.ShapeDtypeStruct((128, 9, 1,...  12.5 us
    all_to_all x1, starting transfers between devices, shards(): lax.all_to_all(rows, ('gy', 'gx'), split_axis=0, concat_axis=0, tiled=True)  10.9 us
    pallas_call x2, Pallas kernels, window_sum(): pl.pallas_call(functools.partial(window_kernel, scale=scale), grid=(3,),...  7.24 us
    pallas_call x1, Pallas kernels, field_step(): pl.pallas_call(field_kernel, grid=(planes,), out_shape=(jax.ShapeDtypeStr...  6.86 us
  transfers between devices with their start and end apart: 7, of which 5 were waited for; matrix products, arithmetic and copies ran while one was open for 0% of the time, Pallas kernels for 16%

profile of v2, /device:TPU:26, one launch (start us, length us, event | category | flops | bytes accessed | tf_op | source)
XLA Modules:
  0.0 117.5 jit_solution(4059478245763327562)
XLA Ops:
  0.6 1.1 fusion
  2.0 3.7 %collective-permute-start.1 = (f32[2,4,64]{2,1,0:T(4,128)S(1)}, f32[2,4,64]{2,1,0:T(4,128)S(1)}, u32[]{:S(2)}, u32[]{:S(2)}) collective-permute-start(f32[2,4,64]{2,1,0:T(4,128)S(1)} %pad_maximum_fusion.1), channel_id=1, source_target_pairs={{0,1},{1,2},{2,3},{3,4},{4,5},{5,6},{6,7},{8,9},{9,10},{10,11},{11... | collective-permute-start | bytes 6152 | tf_op jit(solution)/shard_map/ppermute | solution.py:33
  6.1 1.9 %collective-permute-start = (f32[2,4,128]{2,1,0:T(4,128)S(1)}, f32[2,4,128]{2,1,0:T(4,128)S(1)}, u32[]{:S(2)}, u32[]{:S(2)}) collective-permute-start(f32[2,4,128]{2,1,0:T(4,128)S(1)} %pad_maximum_fusion), channel_id=1, source_target_pairs={{0,8},{8,16},{16,24},{24,32},{32,40},{40,48},{48,56},{56,64},{64,7... | collective-permute-start | bytes 12296 | tf_op jit(solution)/shard_map/ppermute | solution.py:33
  8.1 9.4 %gather_area.2.area_a_ref = f32[8,8,1024]{2,1,0:T(8,128)} custom-call(s32[1,128,128]{2,1,0:T(8,128)} %patch_ref.5, f32[3,256,256]{2,1,0:T(8,128)} %area_ref.3), custom_call_target="tpu_custom_call" | custom-call | flops 6442450944 | bytes 2000000 | tf_op jit(solution)/shard_map/gather_area/pallas_call | solution.py:246
  18.1 0.6 copy-done.6
  18.7 6.9 %field_step.1 = (f32[3,4,64,128]{3,2,1,0:T(8,128)}, f32[3,4,64,128]{3,2,1,0:T(8,128)}, f32[3,2,3,4,64,128]{5,4,3,2,1,0:T(8,128)}, f32[3,2,3,4,64,128]{5,4,3,2,1,0:T(8,128)}, bf16[9,2,64,512]{3,2,1,0:T(8,128)(2,1)}) custom-call(f32[3,4,64,128]{3,2,1,0:T(8,128)} %e_ref.1, f32[3,4,64,128]{3,2,1,0:T(8,128)} %h_ref.1, f32[3,4,64,128]{3,2,1,0:T(8,128)} %j_ref.1, ...), custom_call_target="tpu_custom_call" | custom-call | tf_op jit(solution)/shard_map/field_step/pallas_call | solution.py:125
  25.6 12.5 %gather_flux.1 = f32[128,9,1,128]{3,2,1,0:T(1,128)} custom-call(s32[1,128]{1,0:T(1,128)} %count_ref.1, s32[1,128,128]{2,1,0:T(8,128)} %cell_ref.1, bf16[9,128,512]{2,1,0:T(8,128)(2,1)} %bitcast.13), custom_call_target="tpu_custom_call" | custom-call | tf_op jit(solution)/shard_map/gather_flux/pallas_call | solution.py:205
  38.1 10.9 %all-to-all-start = ((f32[128,9,1,128]{3,2,1,0:T(1,128)}), f32[128,9,1,128]{3,2,1,0:T(1,128)S(1)}, u32[]{:S(2)}, u32[]{:S(2)}) async-start(f32[128,9,1,128]{3,2,1,0:T(1,128)} %gather_flux.1), calls=%async_computation | async-start | bytes 1179648 | tf_op jit(solution)/shard_map/all_to_all | solution.py:368
  49.0 9.4 %gather_area.3.area_b_ref = f32[8,8,1024]{2,1,0:T(8,128)} custom-call(s32[1,128,128]{2,1,0:T(8,128)} %patch_ref.5, f32[3,256,256]{2,1,0:T(8,128)} %area_ref.3), custom_call_target="tpu_custom_call" | custom-call | flops 6442450944 | bytes 2000000 | tf_op jit(solution)/shard_map/gather_area/pallas_call | solution.py:246
  58.5 2.3 %all-to-all-done.flux_ref = f32[128,9,1,128]{3,2,1,0:T(1,128)S(1)} async-done(((f32[128,9,1,128]{3,2,1,0:T(1,128)}), f32[128,9,1,128]{3,2,1,0:T(1,128)S(1)}, u32[]{:S(2)}, u32[]{:S(2)}) %all-to-all-start) | async-done | bytes 589856 | tf_op jit(solution)/shard_map/all_to_all | solution.py:368
  60.7 0.8 copy-done
  61.5 16.2 %scatter_density.1 = (f32[3,256,256]{2,1,0:T(8,128)}, f32[3,104,256]{2,1,0:T(8,128)}, f32[3,104,256]{2,1,0:T(8,128)}) custom-call(s32[1,128,128]{2,1,0:T(8,128)} %patch_ref.5, f32[8,8,1024]{2,1,0:T(8,128)} %gather_area.2.area_a_ref, f32[8,8,1024]{2,1,0:T(8,128)} %gather_area.3.area_b_ref, f32[128,9,1,128]{3,2,1,0:T(1,128)} %copy-done), custom_call_target="tpu_custom_call" | custom-call | tf_op jit(solution)/shard_map/scatter_density/pallas_call | solution.py:312
  77.7 1.9 %collective-permute-start.2 = (f32[3,104,256]{2,1,0:T(8,128)}, f32[3,104,256]{2,1,0:T(8,128)S(1)}, u32[]{:S(2)}, u32[]{:S(2)}) collective-permute-start(f32[3,104,256]{2,1,0:T(8,128)} %get-tuple-element.29), channel_id=1, source_target_pairs={{0,8},{8,16},{16,24},{24,32},{32,40},{40,48},{48,56},{56,64},{64,7... | collective-permute-start | bytes 958472 | tf_op jit(solution)/shard_map/ppermute | solution.py:33
  79.6 5.8 %collective-permute-start.3 = (f32[3,104,256]{2,1,0:T(8,128)}, f32[3,104,256]{2,1,0:T(8,128)S(1)}, u32[]{:S(2)}, u32[]{:S(2)}) collective-permute-start(f32[3,104,256]{2,1,0:T(8,128)} %get-tuple-element.30), channel_id=1, source_target_pairs={{8,0},{16,8},{24,16},{32,24},{40,32},{48,40},{56,48},{64,56},{72,6... | collective-permute-start | bytes 958472 | tf_op jit(solution)/shard_map/ppermute | solution.py:33
  85.4 2.9 %collective-permute-done.2.before_ref = f32[3,104,256]{2,1,0:T(8,128)S(1)} collective-permute-done((f32[3,104,256]{2,1,0:T(8,128)}, f32[3,104,256]{2,1,0:T(8,128)S(1)}, u32[]{:S(2)}, u32[]{:S(2)}) %collective-permute-start.2) | collective-permute-done | bytes 319520 | tf_op jit(solution)/shard_map/ppermute | solution.py:33
  88.3 1.9 %collective-permute-done.3.after_ref = f32[3,104,256]{2,1,0:T(8,128)S(1)} collective-permute-done((f32[3,104,256]{2,1,0:T(8,128)}, f32[3,104,256]{2,1,0:T(8,128)S(1)}, u32[]{:S(2)}, u32[]{:S(2)}) %collective-permute-start.3) | collective-permute-done | bytes 319520 | tf_op jit(solution)/shard_map/ppermute | solution.py:33
  90.2 0.7 copy-done.3
  90.9 3.7 %window_sum.2 = (f32[3,256,256]{2,1,0:T(8,128)}, f32[3,104,256]{2,1,0:T(8,128)}, f32[3,104,256]{2,1,0:T(8,128)}) custom-call(f32[3,256,256]{2,1,0:T(8,128)} %get-tuple-element.18.block_ref, f32[3,104,256]{2,1,0:T(8,128)} %copy-done.1, f32[3,104,256]{2,1,0:T(8,128)} %copy-done.3), custom_call_target="tpu_custom_call" | custom-call | tf_op jit(solution)/shard_map/window_sum/pallas_call | solution.py:345
  94.6 4.8 %collective-permute-start.4 = (f32[3,104,256]{2,1,0:T(8,128)}, f32[3,104,256]{2,1,0:T(8,128)S(1)}, u32[]{:S(2)}, u32[]{:S(2)}) collective-permute-start(f32[3,104,256]{2,1,0:T(8,128)} %get-tuple-element.32), channel_id=1, source_target_pairs={{0,1},{1,2},{2,3},{3,4},{4,5},{5,6},{6,7},{8,9},{9,10},{10,11},{11... | collective-permute-start | bytes 958472 | tf_op jit(solution)/shard_map/ppermute | solution.py:33
  99.4 1.9 %collective-permute-start.5 = (f32[3,104,256]{2,1,0:T(8,128)}, f32[3,104,256]{2,1,0:T(8,128)S(1)}, u32[]{:S(2)}, u32[]{:S(2)}) collective-permute-start(f32[3,104,256]{2,1,0:T(8,128)} %get-tuple-element.33), channel_id=1, source_target_pairs={{1,0},{2,1},{3,2},{4,3},{5,4},{6,5},{7,6},{9,8},{10,9},{11,10},{12... | collective-permute-start | bytes 958472 | tf_op jit(solution)/shard_map/ppermute | solution.py:33
  101.3 4.3 %collective-permute-done.4.before_ref = f32[3,104,256]{2,1,0:T(8,128)S(1)} collective-permute-done((f32[3,104,256]{2,1,0:T(8,128)}, f32[3,104,256]{2,1,0:T(8,128)S(1)}, u32[]{:S(2)}, u32[]{:S(2)}) %collective-permute-start.4) | collective-permute-done | bytes 319520 | tf_op jit(solution)/shard_map/ppermute | solution.py:33
  105.6 7.6 %collective-permute-done.5.after_ref = f32[3,104,256]{2,1,0:T(8,128)S(1)} collective-permute-done((f32[3,104,256]{2,1,0:T(8,128)}, f32[3,104,256]{2,1,0:T(8,128)S(1)}, u32[]{:S(2)}, u32[]{:S(2)}) %collective-permute-start.5) | collective-permute-done | bytes 319520 | tf_op jit(solution)/shard_map/ppermute | solution.py:33
  113.2 0.7 copy-done.4
  113.9 3.6 %window_sum.3 = f32[3,256,256]{2,1,0:T(8,128)} custom-call(f32[3,256,256]{2,1,0:T(8,128)} %get-tuple-element.31.block_ref, f32[3,104,256]{2,1,0:T(8,128)} %copy-done.2, f32[3,104,256]{2,1,0:T(8,128)} %copy-done.4), custom_call_target="tpu_custom_call" | custom-call | tf_op jit(solution)/shard_map/window_sum/pallas_call | solution.py:345
  (21 shorter events, 1.3 us)
Async XLA Ops:
  2.0 15.5 %collective-permute-start.1 = (f32[2,4,64]{2,1,0:T(4,128)S(1)}, f32[2,4,64]{2,1,0:T(4,128)S(1)}, u32[]{:S(2)}, u32[]{:S(2)}) collective-permute-start(f32[2,4,64]{2,1,0:T(4,128)S(1)} %pad_maximum_fusion.1), channel_id=1, source_target_pairs={{0,1},{1,2},{2,3},{3,4},{4,5},{5,6},{6,7},{8,9},{9,10},{10,11},{11... | collective-permute-start | bytes 6152 | tf_op jit(solution)/shard_map/ppermute | solution.py:33
  6.1 11.4 %collective-permute-start = (f32[2,4,128]{2,1,0:T(4,128)S(1)}, f32[2,4,128]{2,1,0:T(4,128)S(1)}, u32[]{:S(2)}, u32[]{:S(2)}) collective-permute-start(f32[2,4,128]{2,1,0:T(4,128)S(1)} %pad_maximum_fusion), channel_id=1, source_target_pairs={{0,8},{8,16},{16,24},{24,32},{32,40},{40,48},{48,56},{56,64},{64,7... | collective-permute-start | bytes 12296 | tf_op jit(solution)/shard_map/ppermute | solution.py:33
  17.5 0.6 copy-start.5
  18.1 0.6 copy-start.6
  38.1 22.7 %all-to-all-start = ((f32[128,9,1,128]{3,2,1,0:T(1,128)}), f32[128,9,1,128]{3,2,1,0:T(1,128)S(1)}, u32[]{:S(2)}, u32[]{:S(2)}) async-start(f32[128,9,1,128]{3,2,1,0:T(1,128)} %gather_flux.1), calls=%async_computation | async-start | bytes 1179648 | tf_op jit(solution)/shard_map/all_to_all | solution.py:368
  60.7 0.8 copy-start
  77.7 10.6 %collective-permute-start.2 = (f32[3,104,256]{2,1,0:T(8,128)}, f32[3,104,256]{2,1,0:T(8,128)S(1)}, u32[]{:S(2)}, u32[]{:S(2)}) collective-permute-start(f32[3,104,256]{2,1,0:T(8,128)} %get-tuple-element.29), channel_id=1, source_target_pairs={{0,8},{8,16},{16,24},{24,32},{32,40},{40,48},{48,56},{56,64},{64,7... | collective-permute-start | bytes 958472 | tf_op jit(solution)/shard_map/ppermute | solution.py:33
  79.6 10.6 %collective-permute-start.3 = (f32[3,104,256]{2,1,0:T(8,128)}, f32[3,104,256]{2,1,0:T(8,128)S(1)}, u32[]{:S(2)}, u32[]{:S(2)}) collective-permute-start(f32[3,104,256]{2,1,0:T(8,128)} %get-tuple-element.30), channel_id=1, source_target_pairs={{8,0},{16,8},{24,16},{32,24},{40,32},{48,40},{56,48},{64,56},{72,6... | collective-permute-start | bytes 958472 | tf_op jit(solution)/shard_map/ppermute | solution.py:33
  88.3 1.9 %copy-start.1 = (f32[3,104,256]{2,1,0:T(8,128)}, f32[3,104,256]{2,1,0:T(8,128)S(1)}, u32[]{:S(2)}) copy-start(f32[3,104,256]{2,1,0:T(8,128)S(1)} %collective-permute-done.2.before_ref) | copy-start | bytes 958468
  90.2 0.7 copy-start.3
  94.6 11.0 %collective-permute-start.4 = (f32[3,104,256]{2,1,0:T(8,128)}, f32[3,104,256]{2,1,0:T(8,128)S(1)}, u32[]{:S(2)}, u32[]{:S(2)}) collective-permute-start(f32[3,104,256]{2,1,0:T(8,128)} %get-tuple-element.32), channel_id=1, source_target_pairs={{0,1},{1,2},{2,3},{3,4},{4,5},{5,6},{6,7},{8,9},{9,10},{10,11},{11... | collective-permute-start | bytes 958472 | tf_op jit(solution)/shard_map/ppermute | solution.py:33
  99.4 13.8 %collective-permute-start.5 = (f32[3,104,256]{2,1,0:T(8,128)}, f32[3,104,256]{2,1,0:T(8,128)S(1)}, u32[]{:S(2)}, u32[]{:S(2)}) collective-permute-start(f32[3,104,256]{2,1,0:T(8,128)} %get-tuple-element.33), channel_id=1, source_target_pairs={{1,0},{2,1},{3,2},{4,3},{5,4},{6,5},{7,6},{9,8},{10,9},{11,10},{12... | collective-permute-start | bytes 958472 | tf_op jit(solution)/shard_map/ppermute | solution.py:33
  105.6 7.6 %copy-start.2 = (f32[3,104,256]{2,1,0:T(8,128)}, f32[3,104,256]{2,1,0:T(8,128)S(1)}, u32[]{:S(2)}) copy-start(f32[3,104,256]{2,1,0:T(8,128)S(1)} %collective-permute-done.4.before_ref) | copy-start | bytes 958468
  113.2 0.7 copy-start.4

commit v3 on v2

--- a/solution.py
+++ b/solution.py
@@ -140,6 +140,7 @@
         ],
         out_specs=(plane3, plane3, spectra, spectra, whole(flux_shape)),
         scratch_shapes=[pltpu.VMEM((2, rows, cols), f32), pltpu.VMEM((8, cols), f32)],
+        compiler_params=pltpu.CompilerParams(vmem_limit_bytes=20 << 20),
         name="field_step",
     )(e, h, j, kinds, table, dft_e, dft_h, rows_below, cols_left)
 
@@ -208,6 +209,7 @@
         in_specs=[SMEM, VMEM, VMEM],
         out_specs=VMEM,
         scratch_shapes=[pltpu.VMEM((136, 128), jnp.int32), pltpu.VMEM((136, 16, 128), f32)],
+        compiler_params=pltpu.CompilerParams(vmem_limit_bytes=24 << 20),
         name="gather_flux",
     )(counts, cells, table)
 
@@ -249,6 +251,7 @@
         in_specs=[VMEM, VMEM],
         out_specs=VMEM,
         scratch_shapes=[pltpu.VMEM((768, 512), bf16)],
+        compiler_params=pltpu.CompilerParams(vmem_limit_bytes=32 << 20),
         cost_estimate=pl.CostEstimate(
             flops=2 * 768 * 512 * GROUP * 128 * groups, bytes_accessed=2000000, transcendentals=0
         ),
@@ -259,7 +262,9 @@
 EDGE = 104
 
 
-def scatter_kernel(patch_ref, area_a_ref, area_b_ref, flux_ref, out_ref, head_ref, tail_ref):
+def scatter_kernel(
+    patch_ref, area_a_ref, area_b_ref, flux_ref, out_ref, copy_ref, head_ref, tail_ref
+):
     out_ref[...] = jnp.zeros_like(out_ref)
 
     def add_group(c, area):
@@ -297,6 +302,7 @@
 
     lax.fori_loop(0, half, first_half, 0, unroll=4)
     lax.fori_loop(0, area_b_ref.shape[0], second_half, 0, unroll=4)
+    copy_ref[...] = out_ref[...]
     head_ref[...] = out_ref[:, :EDGE, :]
     tail_ref[...] = out_ref[:, 256 - EDGE :, :]
 
@@ -311,43 +317,44 @@
 def scatter_density(patch, area_a, area_b, flux):
     return pl.pallas_call(
         scatter_kernel,
-        out_shape=BLOCK_AND_EDGES,
+        out_shape=BLOCK_AND_EDGES[:1] + BLOCK_AND_EDGES,
         in_specs=[VMEM] * 4,
-        out_specs=(VMEM,) * 3,
+        out_specs=(VMEM,) * 4,
+        compiler_params=pltpu.CompilerParams(vmem_limit_bytes=40 << 20),
         name="scatter_density",
     )(patch, area_a, area_b, flux)
 
 
 def window_kernel(block_ref, before_ref, after_ref, out_ref, *edges, scale):
-    cells = jnp.concatenate([before_ref[0], block_ref[0], after_ref[0]], 0)
-    length = cells.shape[0]
+    length = 256 + 2 * EDGE
     place = iota((length, 256), 0) - EDGE - iota((length, 256), 1)
     band = jnp.where((place >= -HALF) & (place < HALF), 1.0, 0.0).astype(bf16)
-    head = cells.astype(bf16)
-    rest = (cells - head.astype(f32)).astype(bf16)
-    total = lax.dot_general(
-        jnp.concatenate([head, rest], 0),
-        jnp.concatenate([band, band], 0),
-        (((0,), (0,)), ((), ())),
-        preferred_element_type=f32,
-    )
-    if scale != 1.0:
-        total = total * scale
-    out_ref[0] = total
-    if edges:
-        edges[0][0] = total[:EDGE]
-        edges[1][0] = total[256 - EDGE :]
+    for f in range(3):
+        cells = jnp.concatenate([before_ref[f], block_ref[f], after_ref[f]], 0)
+        head = cells.astype(bf16)
+        rest = (cells - head.astype(f32)).astype(bf16)
+        total = lax.dot_general(
+            jnp.concatenate([head, rest], 0),
+            jnp.concatenate([band, band], 0),
+            (((0,), (0,)), ((), ())),
+            preferred_element_type=f32,
+        )
+        if scale != 1.0:
+            total = total * scale
+        out_ref[f] = total
+        if edges:
+            edges[0][f] = total[:EDGE]
+            edges[1][f] = total[256 - EDGE :]
 
 
 def window_sum(block, before, after, scale, with_edges):
-    whole = pl.BlockSpec((1, 256, 256), lambda f: (f, 0, 0))
-    edge = pl.BlockSpec((1, EDGE, 256), lambda f: (f, 0, 0))
+    count = 3 if with_edges else 1
     return pl.pallas_call(
         functools.partial(window_kernel, scale=scale),
-        grid=(3,),
-        out_shape=BLOCK_AND_EDGES if with_edges else BLOCK_AND_EDGES[:1],
-        in_specs=[whole, edge, edge],
-        out_specs=(whole, edge, edge) if with_edges else (whole,),
+        out_shape=BLOCK_AND_EDGES[:count],
+        in_specs=[VMEM] * 3,
+        out_specs=(VMEM,) * count,
+        compiler_params=pltpu.CompilerParams(vmem_limit_bytes=16 << 20),
         name="window_sum",
     )(block, before, after)
 
@@ -359,17 +366,17 @@
     magnet_x, magnet_y, magnet_z = (h_field[0], h_field[1], h_field[2])
     rows_below = shifted(jnp.stack([magnet_y[:, -1, :], magnet_z[:, -1, :]]), "gy", 1)
     cols_left = shifted(jnp.stack([magnet_x[:, :, -1], magnet_z[:, :, -1]]), "gx", 1)
-    area_a = gather_area(patch_slot, area, 0, 8)
+    area_a = gather_area(patch_slot, area, 0, 6)
     rows_below, cols_left, area_a = lax.optimization_barrier((rows_below, cols_left, area_a))
     e_next, j_next, dft_e_next, dft_h_next, table = field_step(
         e_field, h_field, j_field, material, material_table, dft_e, dft_h, rows_below, cols_left
     )
     rows = gather_flux(counts, skin_cell, table.reshape(9, 128, 512))
     arrived = lax.all_to_all(rows, ("gy", "gx"), split_axis=0, concat_axis=0, tiled=True)
-    area_b = gather_area(patch_slot, area, 8, 8)
-    point_density, head, tail = scatter_density(patch_slot, area_a, area_b, arrived)
+    area_b = gather_area(patch_slot, area, 6, 10)
+    point_density, block, head, tail = scatter_density(patch_slot, area_a, area_b, arrived)
     before, after = shifted(tail, "gy", 1), shifted(head, "gy", -1)
-    strip_sum, head, tail = window_sum(point_density, before, after, 1.0, True)
+    strip_sum, head, tail = window_sum(block, before, after, 1.0, True)
     before, after = shifted(tail, "gx", 1), shifted(head, "gx", -1)
     (avg_density,) = window_sum(strip_sum, before, after, 1.0 / (4.0 * HALF * HALF), False)
     return (e_next, j_next, dft_e_next, dft_h_next, point_density, avg_density)

time: 118 us -> 101 us (0.86)
  Pallas kernels: 61.6 us -> 48.9 us
  local copies, waits for them, and re-layouts: 5.19 us -> 1.9 us
    pallas_call x3, Pallas kernels: 23.4 us -> 17.4 us  [the longest x1 15.3 us: scatter_density(): pl.pallas_call(scatter_kernel, out_shape=BLOCK_AND_EDGES[:1] + BLOCK_AND_...]
    unnamed x17 -> x25, local copies, waits for them, and re-layouts: 3.83 us -> 0.46 us
    pallas_call x2, Pallas kernels: 18.9 us -> 15.6 us  [gather_area(): pl.pallas_call(functools.partial(area_kernel, first=first), out_shape=jax...]
    pallas_call x1, Pallas kernels: 6.86 us -> 4.12 us  [field_step(): pl.pallas_call(field_kernel, grid=(planes,), out_shape=(jax.ShapeDtypeStr...]
  transfers between devices with their start and end apart: 7 -> 7, of which waited for: 5 -> 5; matrix products, arithmetic and copies ran while one was open for 0% -> 0% of each run, Pallas kernels for 16% -> 15%
where the time goes in v3:
time: 101 us
  Pallas kernels  48.9 us (48%)
  starting transfers between devices  31.1 us (31%)
  waiting for transfers between devices  18.3 us (18%)
  local copies, waits for them, and re-layouts  1.9 us (2%)
    ppermute x6, starting transfers between devices, shifted(): lax.ppermute(value, axis, [(source, source + steps) for source in range(l...  20.3 us
    ppermute x6, waiting for transfers between devices, shifted(): lax.ppermute(value, axis, [(source, source + steps) for source in range(l...  16.3 us
    pallas_call x2, Pallas kernels, gather_area(): pl.pallas_call(functools.partial(area_kernel, first=first), out_shape=jax...  15.6 us
    pallas_call x1, Pallas kernels, scatter_density(): pl.pallas_call(scatter_kernel, out_shape=BLOCK_AND_EDGES[:1] + BLOCK_AND_...  15.3 us
    pallas_call x1, Pallas kernels, gather_flux(): pl.pallas_call(gather_kernel, out_shape=jax.ShapeDtypeStruct((128, 9, 1,...  11.7 us
    all_to_all x1, starting transfers between devices, shards(): lax.all_to_all(rows, ('gy', 'gx'), split_axis=0, concat_axis=0, tiled=True)  10.8 us
    pallas_call x1, Pallas kernels, field_step(): pl.pallas_call(field_kernel, grid=(planes,), out_shape=(jax.ShapeDtypeStr...  4.12 us
    pallas_call x2, Pallas kernels, window_sum(): pl.pallas_call(functools.partial(window_kernel, scale=scale), out_shape=B...  2.14 us
  transfers between devices with their start and end apart: 7, of which 5 were waited for; matrix products, arithmetic and copies ran while one was open for 0% of the time, Pallas kernels for 15%

profile of v3, /device:TPU:26, one launch (start us, length us, event | category | flops | bytes accessed | tf_op | source)
XLA Modules:
  0.0 101.1 jit_solution(9092774563406525919)
XLA Ops:
  0.7 1.1 %fusion = (f32[1,4,64,128]{3,2,1,0:T(8,128)S(1)}, f32[1,4,64,128]{3,2,1,0:T(8,128)S(1)}, f32[1,4,64,128]{3,2,1,0:T(8,128)S(1)}) fusion(f32[3,4,64,128]{3,2,1,0:T(8,128)} %h_ref.1), kind=kLoop, calls=%fused_computation.6 | loop fusion | bytes 786432 | tf_op jit(solution)/shard_map/slice | solution.py:366
  1.8 0.1 copy.27
  1.9 0.1 copy.26
  2.1 3.7 %collective-permute-start.1 = (f32[2,4,64]{2,1,0:T(4,128)S(1)}, f32[2,4,64]{2,1,0:T(4,128)S(1)}, u32[]{:S(2)}, u32[]{:S(2)}) collective-permute-start(f32[2,4,64]{2,1,0:T(4,128)S(1)} %pad_maximum_fusion.1), channel_id=1, source_target_pairs={{0,1},{1,2},{2,3},{3,4},{4,5},{5,6},{6,7},{8,9},{9,10},{10,11},{11... | collective-permute-start | bytes 6152 | tf_op jit(solution)/shard_map/ppermute | solution.py:33
  5.8 0.2 slice.29
  6.1 0.1 copy.23
  6.3 2.3 %collective-permute-start = (f32[2,4,128]{2,1,0:T(4,128)S(1)}, f32[2,4,128]{2,1,0:T(4,128)S(1)}, u32[]{:S(2)}, u32[]{:S(2)}) collective-permute-start(f32[2,4,128]{2,1,0:T(4,128)S(1)} %pad_maximum_fusion), channel_id=1, source_target_pairs={{0,8},{8,16},{16,24},{24,32},{32,40},{40,48},{48,56},{56,64},{64,7... | collective-permute-start | bytes 12296 | tf_op jit(solution)/shard_map/ppermute | solution.py:33
  8.7 5.9 %gather_area.2.area_a_ref = f32[6,8,1024]{2,1,0:T(8,128)S(1)} custom-call(s32[1,128,128]{2,1,0:T(8,128)S(1)} %copy-done.7, f32[3,256,256]{2,1,0:T(8,128)S(1)} %copy-done.10), custom_call_target="tpu_custom_call" | custom-call | flops 4831838208 | bytes 2000000 | tf_op jit(solution)/shard_map/gather_area/pallas_call | solution.py:248
  14.7 4.1 %field_step.1 = (f32[3,4,64,128]{3,2,1,0:T(8,128)}, f32[3,4,64,128]{3,2,1,0:T(8,128)}, f32[3,2,3,4,64,128]{5,4,3,2,1,0:T(8,128)}, f32[3,2,3,4,64,128]{5,4,3,2,1,0:T(8,128)}, bf16[9,2,64,512]{3,2,1,0:T(8,128)(2,1)S(1)}) custom-call(f32[3,4,64,128]{3,2,1,0:T(8,128)S(1)} %copy-done.3, f32[3,4,64,128]{3,2,1,0:T(8,128)S(1)} %copy-done.2, ...), custom_call_target="tpu_custom_call" | custom-call | tf_op jit(solution)/shard_map/field_step/pallas_call | solution.py:125
  18.8 11.7 %gather_flux.1 = f32[128,9,1,128]{3,2,1,0:T(1,128)} custom-call(s32[1,128]{1,0:T(1,128)S(1)} %copy-done.9, s32[1,128,128]{2,1,0:T(8,128)S(1)} %copy-done.6, bf16[9,128,512]{2,1,0:T(8,128)(2,1)S(1)} %bitcast.13), custom_call_target="tpu_custom_call" | custom-call | tf_op jit(solution)/shard_map/gather_flux/pallas_call | solution.py:206
  30.5 10.8 %all-to-all-start = ((f32[128,9,1,128]{3,2,1,0:T(1,128)}), f32[128,9,1,128]{3,2,1,0:T(1,128)S(1)}, u32[]{:S(2)}, u32[]{:S(2)}) async-start(f32[128,9,1,128]{3,2,1,0:T(1,128)} %gather_flux.1), calls=%async_computation | async-start | bytes 1179648 | tf_op jit(solution)/shard_map/all_to_all | solution.py:375
  41.3 9.7 %gather_area.3.area_b_ref = f32[10,8,1024]{2,1,0:T(8,128)S(1)} custom-call(s32[1,128,128]{2,1,0:T(8,128)S(1)} %copy-done.7, f32[3,256,256]{2,1,0:T(8,128)S(1)} %copy-done.10), custom_call_target="tpu_custom_call" | custom-call | flops 8053063680 | bytes 2000000 | tf_op jit(solution)/shard_map/gather_area/pallas_call | solution.py:248
  51.0 2.0 %all-to-all-done.flux_ref = f32[128,9,1,128]{3,2,1,0:T(1,128)S(1)} async-done(((f32[128,9,1,128]{3,2,1,0:T(1,128)}), f32[128,9,1,128]{3,2,1,0:T(1,128)S(1)}, u32[]{:S(2)}, u32[]{:S(2)}) %all-to-all-start) | async-done | bytes 589856 | tf_op jit(solution)/shard_map/all_to_all | solution.py:375
  53.1 15.3 %scatter_density.1 = (f32[3,256,256]{2,1,0:T(8,128)}, f32[3,256,256]{2,1,0:T(8,128)S(1)}, f32[3,104,256]{2,1,0:T(8,128)S(1)}, f32[3,104,256]{2,1,0:T(8,128)S(1)}) custom-call(s32[1,128,128]{2,1,0:T(8,128)S(1)} %copy-done.7, f32[6,8,1024]{2,1,0:T(8,128)S(1)} %gather_area.2.area_a_ref, f32[10,8,1024]{2,1,0:T(8,128)S(1)} %gather_area.3.area_b_ref, ...), custom_call_target="tpu_custom_call" | custom-call | tf_op jit(solution)/shard_map/scatter_density/pallas_call | solution.py:318
  68.4 1.9 %collective-permute-start.2 = (f32[3,104,256]{2,1,0:T(8,128)S(1)}, f32[3,104,256]{2,1,0:T(8,128)S(1)}, u32[]{:S(2)}, u32[]{:S(2)}) collective-permute-start(f32[3,104,256]{2,1,0:T(8,128)S(1)} %get-tuple-element.31), channel_id=1, source_target_pairs={{0,8},{8,16},{16,24},{24,32},{32,40},{40,48},{48,56},{56,64},{64,7... | collective-permute-start | bytes 958472 | tf_op jit(solution)/shard_map/ppermute | solution.py:33
  70.3 5.8 %collective-permute-start.3 = (f32[3,104,256]{2,1,0:T(8,128)S(1)}, f32[3,104,256]{2,1,0:T(8,128)S(1)}, u32[]{:S(2)}, u32[]{:S(2)}) collective-permute-start(f32[3,104,256]{2,1,0:T(8,128)S(1)} %get-tuple-element.32), channel_id=1, source_target_pairs={{8,0},{16,8},{24,16},{32,24},{40,32},{48,40},{56,48},{64,56},{72,6... | collective-permute-start | bytes 958472 | tf_op jit(solution)/shard_map/ppermute | solution.py:33
  76.0 2.7 %collective-permute-done.2.before_ref = f32[3,104,256]{2,1,0:T(8,128)S(1)} collective-permute-done((f32[3,104,256]{2,1,0:T(8,128)S(1)}, f32[3,104,256]{2,1,0:T(8,128)S(1)}, u32[]{:S(2)}, u32[]{:S(2)}) %collective-permute-start.2) | collective-permute-done | bytes 319520 | tf_op jit(solution)/shard_map/ppermute | solution.py:33
  78.8 1.8 %collective-permute-done.3.after_ref = f32[3,104,256]{2,1,0:T(8,128)S(1)} collective-permute-done((f32[3,104,256]{2,1,0:T(8,128)S(1)}, f32[3,104,256]{2,1,0:T(8,128)S(1)}, u32[]{:S(2)}, u32[]{:S(2)}) %collective-permute-start.3) | collective-permute-done | bytes 319520 | tf_op jit(solution)/shard_map/ppermute | solution.py:33
  80.5 0.6 window_sum.2
  81.2 4.7 %collective-permute-start.4 = (f32[3,104,256]{2,1,0:T(8,128)S(1)}, f32[3,104,256]{2,1,0:T(8,128)S(1)}, u32[]{:S(2)}, u32[]{:S(2)}) collective-permute-start(f32[3,104,256]{2,1,0:T(8,128)S(1)} %get-tuple-element.34), channel_id=1, source_target_pairs={{0,1},{1,2},{2,3},{3,4},{4,5},{5,6},{6,7},{8,9},{9,10},{10,11},{11... | collective-permute-start | bytes 958472 | tf_op jit(solution)/shard_map/ppermute | solution.py:33
  85.9 1.9 %collective-permute-start.5 = (f32[3,104,256]{2,1,0:T(8,128)S(1)}, f32[3,104,256]{2,1,0:T(8,128)S(1)}, u32[]{:S(2)}, u32[]{:S(2)}) collective-permute-start(f32[3,104,256]{2,1,0:T(8,128)S(1)} %get-tuple-element.35), channel_id=1, source_target_pairs={{1,0},{2,1},{3,2},{4,3},{5,4},{6,5},{7,6},{9,8},{10,9},{11,10},{12... | collective-permute-start | bytes 958472 | tf_op jit(solution)/shard_map/ppermute | solution.py:33
  87.8 4.1 %collective-permute-done.4.before_ref = f32[3,104,256]{2,1,0:T(8,128)S(1)} collective-permute-done((f32[3,104,256]{2,1,0:T(8,128)S(1)}, f32[3,104,256]{2,1,0:T(8,128)S(1)}, u32[]{:S(2)}, u32[]{:S(2)}) %collective-permute-start.4) | collective-permute-done | bytes 319520 | tf_op jit(solution)/shard_map/ppermute | solution.py:33
  91.9 7.7 %collective-permute-done.5.after_ref = f32[3,104,256]{2,1,0:T(8,128)S(1)} collective-permute-done((f32[3,104,256]{2,1,0:T(8,128)S(1)}, f32[3,104,256]{2,1,0:T(8,128)S(1)}, u32[]{:S(2)}, u32[]{:S(2)}) %collective-permute-start.5) | collective-permute-done | bytes 319520 | tf_op jit(solution)/shard_map/ppermute | solution.py:33
  99.6 1.5 %window_sum.3 = f32[3,256,256]{2,1,0:T(8,128)} custom-call(f32[3,256,256]{2,1,0:T(8,128)S(1)} %get-tuple-element.33.block_ref, f32[3,104,256]{2,1,0:T(8,128)S(1)} %collective-permute-done.4.before_ref, f32[3,104,256]{2,1,0:T(8,128)S(1)} %collective-permute-done.5.after_ref), custom_call_target="tpu_custom_call" | custom-call | tf_op jit(solution)/shard_map/window_sum/pallas_call | solution.py:352
  (29 shorter events, 0.2 us)
Async XLA Ops:
  0.6 8.0 %copy-start.7 = (s32[1,128,128]{2,1,0:T(8,128)S(1)}, s32[1,128,128]{2,1,0:T(8,128)}, u32[]{:S(2)}) copy-start(s32[1,128,128]{2,1,0:T(8,128)} %patch_ref.5) | copy-start | bytes 196612
  0.6 8.0 %copy-start.10 = (f32[3,256,256]{2,1,0:T(8,128)S(1)}, f32[3,256,256]{2,1,0:T(8,128)}, u32[]{:S(2)}) copy-start(f32[3,256,256]{2,1,0:T(8,128)} %area_ref.3) | copy-start | bytes 2359300
  2.1 12.5 %collective-permute-start.1 = (f32[2,4,64]{2,1,0:T(4,128)S(1)}, f32[2,4,64]{2,1,0:T(4,128)S(1)}, u32[]{:S(2)}, u32[]{:S(2)}) collective-permute-start(f32[2,4,64]{2,1,0:T(4,128)S(1)} %pad_maximum_fusion.1), channel_id=1, source_target_pairs={{0,1},{1,2},{2,3},{3,4},{4,5},{5,6},{6,7},{8,9},{9,10},{10,11},{11... | collective-permute-start | bytes 6152 | tf_op jit(solution)/shard_map/ppermute | solution.py:33
  6.2 8.4 %copy-start = (f32[3,2,3,4,64,128]{5,4,3,2,1,0:T(8,128)S(1)}, f32[3,2,3,4,64,128]{5,4,3,2,1,0:T(8,128)}, u32[]{:S(2)}) copy-start(f32[3,2,3,4,64,128]{5,4,3,2,1,0:T(8,128)} %dft_e_ref.1) | copy-start | bytes 7077892
  6.3 8.3 %copy-start.1 = (f32[3,2,3,4,64,128]{5,4,3,2,1,0:T(8,128)S(1)}, f32[3,2,3,4,64,128]{5,4,3,2,1,0:T(8,128)}, u32[]{:S(2)}) copy-start(f32[3,2,3,4,64,128]{5,4,3,2,1,0:T(8,128)} %dft_h_ref.1) | copy-start | bytes 7077892
  6.3 8.3 %copy-start.2 = (f32[3,4,64,128]{3,2,1,0:T(8,128)S(1)}, f32[3,4,64,128]{3,2,1,0:T(8,128)}, u32[]{:S(2)}) copy-start(f32[3,4,64,128]{3,2,1,0:T(8,128)} %h_ref.1) | copy-start | bytes 1179652
  6.3 8.3 %copy-start.3 = (f32[3,4,64,128]{3,2,1,0:T(8,128)S(1)}, f32[3,4,64,128]{3,2,1,0:T(8,128)}, u32[]{:S(2)}) copy-start(f32[3,4,64,128]{3,2,1,0:T(8,128)} %e_ref.1) | copy-start | bytes 1179652
  6.3 8.3 %copy-start.4 = (f32[3,4,64,128]{3,2,1,0:T(8,128)S(1)}, f32[3,4,64,128]{3,2,1,0:T(8,128)}, u32[]{:S(2)}) copy-start(f32[3,4,64,128]{3,2,1,0:T(8,128)} %j_ref.1) | copy-start | bytes 1179652
  6.3 8.3 %copy-start.5 = (s32[4,64,128]{2,1,0:T(8,128)S(1)}, s32[4,64,128]{2,1,0:T(8,128)}, u32[]{:S(2)}) copy-start(s32[4,64,128]{2,1,0:T(8,128)} %kind_ref.1) | copy-start | bytes 393220
  6.3 8.3 %copy-start.8 = (f32[4,32]{1,0:T(4,128)S(1)}, f32[4,32]{1,0:T(4,128)}, u32[]{:S(2)}) copy-start(f32[4,32]{1,0:T(4,128)} %table_ref.1) | copy-start | bytes 1540
  6.3 8.3 %collective-permute-start = (f32[2,4,128]{2,1,0:T(4,128)S(1)}, f32[2,4,128]{2,1,0:T(4,128)S(1)}, u32[]{:S(2)}, u32[]{:S(2)}) collective-permute-start(f32[2,4,128]{2,1,0:T(4,128)S(1)} %pad_maximum_fusion), channel_id=1, source_target_pairs={{0,8},{8,16},{16,24},{24,32},{32,40},{40,48},{48,56},{56,64},{64,7... | collective-permute-start | bytes 12296 | tf_op jit(solution)/shard_map/ppermute | solution.py:33
  14.6 4.2 %copy-start.6 = (s32[1,128,128]{2,1,0:T(8,128)S(1)}, s32[1,128,128]{2,1,0:T(8,128)}, u32[]{:S(2)}) copy-start(s32[1,128,128]{2,1,0:T(8,128)} %cell_ref.1) | copy-start | bytes 196612
  14.6 4.2 %copy-start.9 = (s32[1,128]{1,0:T(1,128)S(1)}, s32[1,128]{1,0:T(1,128)}, u32[]{:S(2)}) copy-start(s32[1,128]{1,0:T(1,128)} %count_ref.1) | copy-start | bytes 1540
  30.5 22.5 %all-to-all-start = ((f32[128,9,1,128]{3,2,1,0:T(1,128)}), f32[128,9,1,128]{3,2,1,0:T(1,128)S(1)}, u32[]{:S(2)}, u32[]{:S(2)}) async-start(f32[128,9,1,128]{3,2,1,0:T(1,128)} %gather_flux.1), calls=%async_computation | async-start | bytes 1179648 | tf_op jit(solution)/shard_map/all_to_all | solution.py:375
  68.4 10.4 %collective-permute-start.2 = (f32[3,104,256]{2,1,0:T(8,128)S(1)}, f32[3,104,256]{2,1,0:T(8,128)S(1)}, u32[]{:S(2)}, u32[]{:S(2)}) collective-permute-start(f32[3,104,256]{2,1,0:T(8,128)S(1)} %get-tuple-element.31), channel_id=1, source_target_pairs={{0,8},{8,16},{16,24},{24,32},{32,40},{40,48},{48,56},{56,64},{64,7... | collective-permute-start | bytes 958472 | tf_op jit(solution)/shard_map/ppermute | solution.py:33
  70.3 10.2 %collective-permute-start.3 = (f32[3,104,256]{2,1,0:T(8,128)S(1)}, f32[3,104,256]{2,1,0:T(8,128)S(1)}, u32[]{:S(2)}, u32[]{:S(2)}) collective-permute-start(f32[3,104,256]{2,1,0:T(8,128)S(1)} %get-tuple-element.32), channel_id=1, source_target_pairs={{8,0},{16,8},{24,16},{32,24},{40,32},{48,40},{56,48},{64,56},{72,6... | collective-permute-start | bytes 958472 | tf_op jit(solution)/shard_map/ppermute | solution.py:33
  81.2 10.7 %collective-permute-start.4 = (f32[3,104,256]{2,1,0:T(8,128)S(1)}, f32[3,104,256]{2,1,0:T(8,128)S(1)}, u32[]{:S(2)}, u32[]{:S(2)}) collective-permute-start(f32[3,104,256]{2,1,0:T(8,128)S(1)} %get-tuple-element.34), channel_id=1, source_target_pairs={{0,1},{1,2},{2,3},{3,4},{4,5},{5,6},{6,7},{8,9},{9,10},{10,11},{11... | collective-permute-start | bytes 958472 | tf_op jit(solution)/shard_map/ppermute | solution.py:33
  85.9 13.7 %collective-permute-start.5 = (f32[3,104,256]{2,1,0:T(8,128)S(1)}, f32[3,104,256]{2,1,0:T(8,128)S(1)}, u32[]{:S(2)}, u32[]{:S(2)}) collective-permute-start(f32[3,104,256]{2,1,0:T(8,128)S(1)} %get-tuple-element.35), channel_id=1, source_target_pairs={{1,0},{2,1},{3,2},{4,3},{5,4},{6,5},{7,6},{9,8},{10,9},{11,10},{12... | collective-permute-start | bytes 958472 | tf_op jit(solution)/shard_map/ppermute | solution.py:33

commit v4 on v3

--- a/solution.py
+++ b/solution.py
@@ -145,23 +145,7 @@
     )(e, h, j, kinds, table, dft_e, dft_h, rows_below, cols_left)
 
 
-def gather_kernel(count_ref, cell_ref, table_ref, out_ref, packed, found):
-    lane = iota((1, 128), 1)
-
-    def pack(d, carry):
-        offset, current = carry
-        row, start = lax.shift_right_logical(offset, 7), lax.bitwise_and(offset, 127)
-        live = count_ref[0, d]
-        rolled = pltpu.roll(cell_ref[0, pl.ds(d, 1), :], start, 1)
-        merged = jnp.where(lane >= start, rolled, current)
-        packed[pl.ds(row, 1), :] = merged
-        return offset + live, jnp.where(start + live >= 128, rolled, merged)
-
-    offset, current = lax.fori_loop(
-        0, 128, pack, (jnp.int32(0), jnp.zeros((1, 128), jnp.int32)), unroll=32
-    )
-    packed[pl.ds(lax.shift_right_logical(offset, 7), 1), :] = current
-
+def gather_kernel(count_ref, offset_ref, packed, table_ref, out_ref, found):
     def lookup(c):
         cell = jnp.concatenate([packed[pl.ds(2 * c, 1), :], packed[pl.ds(2 * c + 1, 1), :]], 1)
         high = lax.bitwise_and(lax.shift_right_logical(cell, 14), 1)
@@ -184,10 +168,11 @@
             lookup(4 * c + part)
         return 0
 
-    lax.fori_loop(0, lax.shift_right_logical(offset + 1023, 10), chunk, 0)
+    lax.fori_loop(0, lax.shift_right_logical(offset_ref[0, 128] + 1023, 10), chunk, 0)
     lanes = iota((16, 128), 1)
 
-    def unpack(d, offset):
+    def unpack(d, _):
+        offset = offset_ref[0, d]
         row, start = lax.shift_right_logical(offset, 7), lax.bitwise_and(offset, 127)
         live = count_ref[0, d]
         back = lax.bitwise_and(128 - start, 127)
@@ -197,21 +182,21 @@
         value = jnp.where(lanes < live, value, 0.0)
         for q in range(9):
             out_ref[d, q] = value[q : q + 1, :]
-        return offset + live
-
-    lax.fori_loop(0, 128, unpack, jnp.int32(0), unroll=16)
-
-
-def gather_flux(counts, cells, table):
+        return 0
+
+    lax.fori_loop(0, 128, unpack, 0, unroll=16)
+
+
+def gather_flux(counts, offsets, packed, table):
     return pl.pallas_call(
         gather_kernel,
         out_shape=jax.ShapeDtypeStruct((128, 9, 1, 128), f32),
-        in_specs=[SMEM, VMEM, VMEM],
+        in_specs=[SMEM, SMEM, VMEM, VMEM],
         out_specs=VMEM,
-        scratch_shapes=[pltpu.VMEM((136, 128), jnp.int32), pltpu.VMEM((136, 16, 128), f32)],
+        scratch_shapes=[pltpu.VMEM((136, 16, 128), f32)],
         compiler_params=pltpu.CompilerParams(vmem_limit_bytes=24 << 20),
         name="gather_flux",
-    )(counts, cells, table)
+    )(counts, offsets, packed, table)
 
 
 GROUP = 8
@@ -221,27 +206,85 @@
     return jnp.concatenate([ref[0, pl.ds(GROUP * c + i, 1), :] for i in range(GROUP)], 1)
 
 
-def area_kernel(patch_ref, area_ref, out_ref, table, *, first):
+def split_area(area_ref, table):
     area = area_ref[...].reshape(768, 256)
     head = area.astype(bf16)
     table[:, :256] = head
     table[:, 256:] = (area - head.astype(f32)).astype(bf16)
 
+
+def area_group(patch_ref, table, out_ref, c, first):
+    patch = slot_row(patch_ref, c + first)
+    u, v = lax.shift_right_logical(patch, 8), lax.bitwise_and(patch, 255)
+    hot = onehot(256, v)
+    result = jnp.dot(
+        table[...], jnp.concatenate([hot, hot], 0), preferred_element_type=f32
+    ).reshape(3, 256, GROUP * 128)
+    mine = iota((256, GROUP * 128), 0) == u
+    for q in range(3):
+        out_ref[c, q : q + 1, :] = jnp.sum(jnp.where(mine, result[q], 0.0), axis=0, keepdims=True)
+
+
+def first_area_kernel(
+    count_ref, cell_ref, patch_ref, area_ref, out_ref, packed, offset_ref, table, *, groups
+):
+    split_area(area_ref, table)
+    lane = iota((1, 128), 1)
+    share = 128 // groups
+
+    def chunk(c, carry):
+        offset, current = carry
+        for i in range(share):
+            d = c * share + i
+            row, start = lax.shift_right_logical(offset, 7), lax.bitwise_and(offset, 127)
+            live = count_ref[0, d]
+            offset_ref[0, d] = offset
+            rolled = pltpu.roll(cell_ref[0, pl.ds(d, 1), :], start, 1)
+            merged = jnp.where(lane >= start, rolled, current)
+            packed[pl.ds(row, 1), :] = merged
+            current = jnp.where(start + live >= 128, rolled, merged)
+            offset = offset + live
+        area_group(patch_ref, table, out_ref, c, 0)
+        return offset, current
+
+    offset, current = lax.fori_loop(
+        0, groups, chunk, (jnp.int32(0), jnp.zeros((1, 128), jnp.int32)), unroll=2
+    )
+    packed[pl.ds(lax.shift_right_logical(offset, 7), 1), :] = current
+    offset_ref[0, 128] = offset
+
+
+def area_kernel(patch_ref, area_ref, out_ref, table, *, first):
+    split_area(area_ref, table)
+
     def chunk(c, _):
-        patch = slot_row(patch_ref, c + first)
-        u, v = lax.shift_right_logical(patch, 8), lax.bitwise_and(patch, 255)
-        hot = onehot(256, v)
-        result = jnp.dot(
-            table[...], jnp.concatenate([hot, hot], 0), preferred_element_type=f32
-        ).reshape(3, 256, GROUP * 128)
-        mine = iota((256, GROUP * 128), 0) == u
-        for q in range(3):
-            out_ref[c, q : q + 1, :] = jnp.sum(
-                jnp.where(mine, result[q], 0.0), axis=0, keepdims=True
-            )
+        area_group(patch_ref, table, out_ref, c, first)
         return 0
 
     lax.fori_loop(0, out_ref.shape[0], chunk, 0, unroll=4)
+
+
+def area_cost(groups):
+    return pl.CostEstimate(
+        flops=2 * 768 * 512 * GROUP * 128 * groups, bytes_accessed=2000000, transcendentals=0
+    )
+
+
+def gather_area_and_pack(counts, cells, patch, area, groups):
+    return pl.pallas_call(
+        functools.partial(first_area_kernel, groups=groups),
+        out_shape=(
+            jax.ShapeDtypeStruct((groups, 8, GROUP * 128), f32),
+            jax.ShapeDtypeStruct((136, 128), jnp.int32),
+            jax.ShapeDtypeStruct((1, 136), jnp.int32),
+        ),
+        in_specs=[SMEM, VMEM, VMEM, VMEM],
+        out_specs=(VMEM, VMEM, SMEM),
+        scratch_shapes=[pltpu.VMEM((768, 512), bf16)],
+        compiler_params=pltpu.CompilerParams(vmem_limit_bytes=32 << 20),
+        cost_estimate=area_cost(groups),
+        name="area_and_pack",
+    )(counts, cells, patch, area)
 
 
 def gather_area(patch, area, first, groups):
@@ -252,9 +295,7 @@
         out_specs=VMEM,
         scratch_shapes=[pltpu.VMEM((768, 512), bf16)],
         compiler_params=pltpu.CompilerParams(vmem_limit_bytes=32 << 20),
-        cost_estimate=pl.CostEstimate(
-            flops=2 * 768 * 512 * GROUP * 128 * groups, bytes_accessed=2000000, transcendentals=0
-        ),
+        cost_estimate=area_cost(groups),
         name="gather_area",
     )(patch, area)
 
@@ -263,8 +304,9 @@
 
 
 def scatter_kernel(
-    patch_ref, area_a_ref, area_b_ref, flux_ref, out_ref, copy_ref, head_ref, tail_ref
+    patch_ref, area_a_ref, area_b_ref, flux_ref, out_ref, head_ref, tail_ref, *, first
 ):
+    freqs = out_ref.shape[0]
     out_ref[...] = jnp.zeros_like(out_ref)
 
     def add_group(c, area):
@@ -273,7 +315,7 @@
         hot = onehot(256, v)
         mine = iota((256, GROUP * 128), 0).astype(bf16) == u.astype(bf16)
         heads, rests = [], []
-        for f in range(3):
+        for f in range(first, first + freqs):
             density = jnp.zeros((1, GROUP * 128), f32)
             for q in range(3):
                 flux = jnp.concatenate(
@@ -288,75 +330,117 @@
         right = jnp.concatenate([hot, hot], 1)
         out_ref[...] += lax.dot_general(
             left, right, (((1,), (1,)), ((), ())), preferred_element_type=f32
-        ).reshape(3, 256, 256)
+        ).reshape(freqs, 256, 256)
 
     half = area_a_ref.shape[0]
 
-    def first_half(c, _):
+    def first_part(c, _):
         add_group(c, area_a_ref[c])
         return 0
 
-    def second_half(c, _):
+    def second_part(c, _):
         add_group(c + half, area_b_ref[c])
         return 0
 
-    lax.fori_loop(0, half, first_half, 0, unroll=4)
-    lax.fori_loop(0, area_b_ref.shape[0], second_half, 0, unroll=4)
-    copy_ref[...] = out_ref[...]
-    head_ref[...] = out_ref[:, :EDGE, :]
-    tail_ref[...] = out_ref[:, 256 - EDGE :, :]
-
-
-BLOCK_AND_EDGES = (
-    jax.ShapeDtypeStruct((3, 256, 256), f32),
-    jax.ShapeDtypeStruct((3, EDGE, 256), f32),
-    jax.ShapeDtypeStruct((3, EDGE, 256), f32),
-)
-
-
-def scatter_density(patch, area_a, area_b, flux):
-    return pl.pallas_call(
-        scatter_kernel,
-        out_shape=BLOCK_AND_EDGES[:1] + BLOCK_AND_EDGES,
+    lax.fori_loop(0, half, first_part, 0, unroll=4)
+    lax.fori_loop(0, area_b_ref.shape[0], second_part, 0, unroll=4)
+    for f in range(freqs):
+        head_ref[f] = jnp.transpose(out_ref[f, :, :128])[:EDGE]
+        tail_ref[f] = jnp.transpose(out_ref[f, :, 128:])[128 - EDGE :]
+
+
+def block_and_edges(freqs):
+    return (
+        jax.ShapeDtypeStruct((freqs, 256, 256), f32),
+        jax.ShapeDtypeStruct((freqs, EDGE, 256), f32),
+        jax.ShapeDtypeStruct((freqs, EDGE, 256), f32),
+    )
+
+
+def scatter_density(patch, area_a, area_b, flux, first, freqs):
+    return pl.pallas_call(
+        functools.partial(scatter_kernel, first=first),
+        out_shape=block_and_edges(freqs),
         in_specs=[VMEM] * 4,
-        out_specs=(VMEM,) * 4,
-        compiler_params=pltpu.CompilerParams(vmem_limit_bytes=40 << 20),
+        out_specs=(VMEM,) * 3,
+        compiler_params=pltpu.CompilerParams(vmem_limit_bytes=36 << 20),
+        cost_estimate=pl.CostEstimate(
+            flops=2 * freqs * 65536 * 2 * 16384, bytes_accessed=2000000, transcendentals=0
+        ),
         name="scatter_density",
     )(patch, area_a, area_b, flux)
 
 
-def window_kernel(block_ref, before_ref, after_ref, out_ref, *edges, scale):
-    length = 256 + 2 * EDGE
-    place = iota((length, 256), 0) - EDGE - iota((length, 256), 1)
-    band = jnp.where((place >= -HALF) & (place < HALF), 1.0, 0.0).astype(bf16)
-    for f in range(3):
-        cells = jnp.concatenate([before_ref[f], block_ref[f], after_ref[f]], 0)
-        head = cells.astype(bf16)
-        rest = (cells - head.astype(f32)).astype(bf16)
-        total = lax.dot_general(
-            jnp.concatenate([head, rest], 0),
-            jnp.concatenate([band, band], 0),
+def in_window(place):
+    return jnp.where((place >= -HALF) & (place < HALF), 1.0, 0.0).astype(bf16)
+
+
+def two_parts(cells):
+    head = cells.astype(bf16)
+    return head, (cells - head.astype(f32)).astype(bf16)
+
+
+def column_kernel(block_ref, before_ref, after_ref, out_ref, head_ref, tail_ref):
+    inner = in_window(iota((256, 256), 0) - iota((256, 256), 1))
+    place, column = iota((EDGE, 256), 0), iota((EDGE, 256), 1)
+    outer = jnp.concatenate(
+        [in_window(place - EDGE - column), in_window(place + 256 - column)], 0
+    )
+    inner = jnp.concatenate([inner, inner], 0)
+    outer = jnp.concatenate([outer, outer], 0)
+    for f in range(out_ref.shape[0]):
+        total = jnp.dot(
+            jnp.concatenate(two_parts(block_ref[f]), 1), inner, preferred_element_type=f32
+        )
+        edges = jnp.concatenate([before_ref[f], after_ref[f]], 0)
+        total = total + lax.dot_general(
+            jnp.concatenate(two_parts(edges), 0),
+            outer,
             (((0,), (0,)), ((), ())),
             preferred_element_type=f32,
         )
-        if scale != 1.0:
-            total = total * scale
         out_ref[f] = total
-        if edges:
-            edges[0][f] = total[:EDGE]
-            edges[1][f] = total[256 - EDGE :]
-
-
-def window_sum(block, before, after, scale, with_edges):
-    count = 3 if with_edges else 1
-    return pl.pallas_call(
-        functools.partial(window_kernel, scale=scale),
-        out_shape=BLOCK_AND_EDGES[:count],
+        head_ref[f] = total[:EDGE]
+        tail_ref[f] = total[256 - EDGE :]
+
+
+def column_sum(block, before, after):
+    freqs = block.shape[0]
+    return pl.pallas_call(
+        column_kernel,
+        out_shape=block_and_edges(freqs),
         in_specs=[VMEM] * 3,
-        out_specs=(VMEM,) * count,
+        out_specs=(VMEM,) * 3,
         compiler_params=pltpu.CompilerParams(vmem_limit_bytes=16 << 20),
-        name="window_sum",
+        name="column_sum",
     )(block, before, after)
+
+
+def row_kernel(*refs):
+    out_ref = refs[-1]
+    length = 256 + 2 * EDGE
+    band = in_window(iota((256, length), 1) - EDGE - iota((256, length), 0))
+    band = jnp.concatenate([band, band], 1)
+    done = 0
+    for block_ref, before_ref, after_ref in zip(refs[0:-1:3], refs[1:-1:3], refs[2:-1:3]):
+        for f in range(block_ref.shape[0]):
+            cells = jnp.concatenate([before_ref[f], block_ref[f], after_ref[f]], 0)
+            total = jnp.dot(
+                band, jnp.concatenate(two_parts(cells), 0), preferred_element_type=f32
+            )
+            out_ref[done] = total * (1.0 / (4.0 * HALF * HALF))
+            done += 1
+
+
+def row_sum(*pieces):
+    return pl.pallas_call(
+        row_kernel,
+        out_shape=jax.ShapeDtypeStruct((3, 256, 256), f32),
+        in_specs=[VMEM] * len(pieces),
+        out_specs=VMEM,
+        compiler_params=pltpu.CompilerParams(vmem_limit_bytes=16 << 20),
+        name="row_sum",
+    )(*pieces)
 
 
 def shards(
@@ -366,19 +450,26 @@
     magnet_x, magnet_y, magnet_z = (h_field[0], h_field[1], h_field[2])
     rows_below = shifted(jnp.stack([magnet_y[:, -1, :], magnet_z[:, -1, :]]), "gy", 1)
     cols_left = shifted(jnp.stack([magnet_x[:, :, -1], magnet_z[:, :, -1]]), "gx", 1)
-    area_a = gather_area(patch_slot, area, 0, 6)
+    area_a, packed, offsets = gather_area_and_pack(counts, skin_cell, patch_slot, area, 4)
     rows_below, cols_left, area_a = lax.optimization_barrier((rows_below, cols_left, area_a))
     e_next, j_next, dft_e_next, dft_h_next, table = field_step(
         e_field, h_field, j_field, material, material_table, dft_e, dft_h, rows_below, cols_left
     )
-    rows = gather_flux(counts, skin_cell, table.reshape(9, 128, 512))
+    rows = gather_flux(counts, offsets, packed, table.reshape(9, 128, 512))
     arrived = lax.all_to_all(rows, ("gy", "gx"), split_axis=0, concat_axis=0, tiled=True)
-    area_b = gather_area(patch_slot, area, 6, 10)
-    point_density, block, head, tail = scatter_density(patch_slot, area_a, area_b, arrived)
-    before, after = shifted(tail, "gy", 1), shifted(head, "gy", -1)
-    strip_sum, head, tail = window_sum(block, before, after, 1.0, True)
-    before, after = shifted(tail, "gx", 1), shifted(head, "gx", -1)
-    (avg_density,) = window_sum(strip_sum, before, after, 1.0 / (4.0 * HALF * HALF), False)
+    area_b = gather_area(patch_slot, area, 4, 12)
+
+    blocks, pieces = [], []
+    edges = []
+    for first, freqs in ((0, 2), (2, 1)):
+        block, head, tail = scatter_density(patch_slot, area_a, area_b, arrived, first, freqs)
+        blocks.append(block)
+        edges.append((shifted(tail, "gx", 1), shifted(head, "gx", -1)))
+    for block, (before, after) in zip(blocks, edges):
+        strip, head, tail = column_sum(block, before, after)
+        pieces += [strip, shifted(tail, "gy", 1), shifted(head, "gy", -1)]
+    point_density = jnp.concatenate(blocks, 0)
+    avg_density = row_sum(*pieces)
     return (e_next, j_next, dft_e_next, dft_h_next, point_density, avg_density)
 
 

time: 101 us -> 108 us (1.069)
  the two profiles are of different devices: /device:TPU:26 before, /device:TPU:101 now
where the time goes in v4:
time: 108 us; the launch traced here: 107 us
  Pallas kernels  49.1 us (45%)
  starting transfers between devices  49 us (45%)
  waiting for transfers between devices  5.3 us (5%)
  local copies, waits for them, and re-layouts  1.92 us (2%)
    ppermute x10, starting transfers between devices, shifted(): lax.ppermute(value, axis, [(source, source + steps) for source in range(l...  38.1 us
    pallas_call x2, Pallas kernels, scatter_density(): pl.pallas_call(functools.partial(scatter_kernel, first=first), out_shape=...  15 us
    pallas_call x1, Pallas kernels, gather_area(): pl.pallas_call(functools.partial(area_kernel, first=first), out_shape=jax...  11.3 us
    pallas_call x1, Pallas kernels, gather_flux(): pl.pallas_call(gather_kernel, out_shape=jax.ShapeDtypeStruct((128, 9, 1,...  11.1 us
    all_to_all x1, starting transfers between devices, shards(): lax.all_to_all(rows, ('gy', 'gx'), split_axis=0, concat_axis=0, tiled=True)  10.9 us
    pallas_call x1, Pallas kernels, gather_area_and_pack(): pl.pallas_call(functools.partial(first_area_kernel, groups=groups), out_s...  5.37 us
    ppermute x10, waiting for transfers between devices, shifted(): lax.ppermute(value, axis, [(source, source + steps) for source in range(l...  5.29 us
    pallas_call x1, Pallas kernels, field_step(): pl.pallas_call(field_kernel, grid=(planes,), out_shape=(jax.ShapeDtypeStr...  4.13 us
  transfers between devices with their start and end apart: 11, of which 1 were waited for; matrix products, arithmetic and copies ran while one was open for 1% of the time, Pallas kernels for 21%

profile of v4, /device:TPU:101, one launch (start us, length us, event | category | flops | bytes accessed | tf_op | source)
XLA Modules:
  0.0 107.3 jit_solution(12921527880101929211)
XLA Ops:
  0.7 1.1 %fusion = (f32[1,4,64,128]{3,2,1,0:T(8,128)S(1)}, f32[1,4,64,128]{3,2,1,0:T(8,128)S(1)}, f32[1,4,64,128]{3,2,1,0:T(8,128)S(1)}) fusion(f32[3,4,64,128]{3,2,1,0:T(8,128)} %h_ref.1), kind=kLoop, calls=%fused_computation.7 | loop fusion | bytes 786432 | tf_op jit(solution)/shard_map/slice | solution.py:450
  2.1 3.2 %collective-permute-start.1 = (f32[2,4,64]{2,1,0:T(4,128)S(1)}, f32[2,4,64]{2,1,0:T(4,128)S(1)}, u32[]{:S(2)}, u32[]{:S(2)}) collective-permute-start(f32[2,4,64]{2,1,0:T(4,128)S(1)} %pad_maximum_fusion.2), channel_id=1, source_target_pairs={{0,1},{1,2},{2,3},{3,4},{4,5},{5,6},{6,7},{8,9},{9,10},{10,11},{11... | collective-permute-start | bytes 6152 | tf_op jit(solution)/shard_map/ppermute | solution.py:33
  5.4 0.2 slice.29
  5.9 2.6 %collective-permute-start = (f32[2,4,128]{2,1,0:T(4,128)S(1)}, f32[2,4,128]{2,1,0:T(4,128)S(1)}, u32[]{:S(2)}, u32[]{:S(2)}) collective-permute-start(f32[2,4,128]{2,1,0:T(4,128)S(1)} %pad_maximum_fusion.1), channel_id=1, source_target_pairs={{0,8},{8,16},{16,24},{24,32},{32,40},{40,48},{48,56},{56,64},{64,7... | collective-permute-start | bytes 12296 | tf_op jit(solution)/shard_map/ppermute | solution.py:33
  8.5 5.4 %area_and_pack.1 = (f32[4,8,1024]{2,1,0:T(8,128)S(1)}, s32[136,128]{1,0:T(8,128)S(1)}, s32[1,136]{1,0:T(1,128)S(1)}) custom-call(s32[1,128]{1,0:T(1,128)S(1)} %copy-done.7, s32[1,128,128]{2,1,0:T(8,128)S(1)} %copy-done.9, s32[1,128,128]{2,1,0:T(8,128)S(1)} %copy-done.10, f32[3,256,256]{2,1,0:T(8,128)S(1)} %copy-done.8), custom_call_target="tpu_custom_call" | custom-call | flops 3221225472 | bytes 2000000 | tf_op jit(solution)/shard_map/area_and_pack/pallas_call | solution.py:274
  14.0 4.1 %field_step.1 = (f32[3,4,64,128]{3,2,1,0:T(8,128)}, f32[3,4,64,128]{3,2,1,0:T(8,128)}, f32[3,2,3,4,64,128]{5,4,3,2,1,0:T(8,128)}, f32[3,2,3,4,64,128]{5,4,3,2,1,0:T(8,128)}, bf16[9,2,64,512]{3,2,1,0:T(8,128)(2,1)S(1)}) custom-call(f32[3,4,64,128]{3,2,1,0:T(8,128)S(1)} %copy-done.3, f32[3,4,64,128]{3,2,1,0:T(8,128)S(1)} %copy-done.2, ...), custom_call_target="tpu_custom_call" | custom-call | tf_op jit(solution)/shard_map/field_step/pallas_call | solution.py:125
  18.1 11.1 %gather_flux.1 = f32[128,9,1,128]{3,2,1,0:T(1,128)} custom-call(s32[1,128]{1,0:T(1,128)S(1)} %copy-done.7, s32[1,136]{1,0:T(1,128)S(1)} %get-tuple-element.37.offset_ref, s32[136,128]{1,0:T(8,128)S(1)} %get-tuple-element.38.packed, bf16[9,128,512]{2,1,0:T(8,128)(2,1)S(1)} %bitcast.13), custom_call_target="tpu_custom_call" | custom-call | tf_op jit(solution)/shard_map/gather_flux/pallas_call | solution.py:191
  29.2 10.9 %all-to-all-start = ((f32[128,9,1,128]{3,2,1,0:T(1,128)}), f32[128,9,1,128]{3,2,1,0:T(1,128)S(1)}, u32[]{:S(2)}, u32[]{:S(2)}) async-start(f32[128,9,1,128]{3,2,1,0:T(1,128)} %gather_flux.1), calls=%async_computation | async-start | bytes 1179648 | tf_op jit(solution)/shard_map/all_to_all | solution.py:459
  40.1 11.3 %gather_area.1.area_b_ref = f32[12,8,1024]{2,1,0:T(8,128)S(1)} custom-call(s32[1,128,128]{2,1,0:T(8,128)S(1)} %copy-done.10, f32[3,256,256]{2,1,0:T(8,128)S(1)} %copy-done.8), custom_call_target="tpu_custom_call" | custom-call | flops 9663676416 | bytes 2000000 | tf_op jit(solution)/shard_map/gather_area/pallas_call | solution.py:291
  51.4 9.7 %scatter_density.2 = (f32[2,256,256]{2,1,0:T(8,128)S(1)}, f32[2,104,256]{2,1,0:T(8,128)S(1)}, f32[2,104,256]{2,1,0:T(8,128)S(1)}) custom-call(s32[1,128,128]{2,1,0:T(8,128)S(1)} %copy-done.10, f32[4,8,1024]{2,1,0:T(8,128)S(1)} %get-tuple-element.36.area_a_ref, f32[12,8,1024]{2,1,0:T(8,128)S(1)} %gather_area.1.area_b_ref, ...), custom_call_target="tpu_custom_call" | custom-call | flops 8589934592 | bytes 2000000 | tf_op jit(solution)/shard_map/scatter_density/pallas_call | solution.py:361
  61.1 3.1 %collective-permute-start.2 = (f32[2,104,256]{2,1,0:T(8,128)S(1)}, f32[2,104,256]{2,1,0:T(8,128)S(1)}, u32[]{:S(2)}, u32[]{:S(2)}) collective-permute-start(f32[2,104,256]{2,1,0:T(8,128)S(1)} %get-tuple-element.42), channel_id=1, source_target_pairs={{0,1},{1,2},{2,3},{3,4},{4,5},{5,6},{6,7},{8,9},{9,10},{10,11},{11... | collective-permute-start | bytes 638984 | tf_op jit(solution)/shard_map/ppermute | solution.py:33
  64.3 5.9 %collective-permute-start.3 = (f32[2,104,256]{2,1,0:T(8,128)S(1)}, f32[2,104,256]{2,1,0:T(8,128)S(1)}, u32[]{:S(2)}, u32[]{:S(2)}) collective-permute-start(f32[2,104,256]{2,1,0:T(8,128)S(1)} %get-tuple-element.43), channel_id=1, source_target_pairs={{1,0},{2,1},{3,2},{4,3},{5,4},{6,5},{7,6},{9,8},{10,9},{11,10},{12... | collective-permute-start | bytes 638984 | tf_op jit(solution)/shard_map/ppermute | solution.py:33
  70.2 5.3 %scatter_density.3 = (f32[1,256,256]{2,1,0:T(8,128)S(1)}, f32[1,104,256]{2,1,0:T(8,128)S(1)}, f32[1,104,256]{2,1,0:T(8,128)S(1)}) custom-call(s32[1,128,128]{2,1,0:T(8,128)S(1)} %copy-done.10, f32[4,8,1024]{2,1,0:T(8,128)S(1)} %get-tuple-element.36.area_a_ref, f32[12,8,1024]{2,1,0:T(8,128)S(1)} %gather_area.1.area_b_ref, ...), custom_call_target="tpu_custom_call" | custom-call | flops 4294967296 | bytes 2000000 | tf_op jit(solution)/shard_map/scatter_density/pallas_call | solution.py:361
  75.5 1.9 %collective-permute-start.6 = (f32[1,104,256]{2,1,0:T(8,128)S(1)}, f32[1,104,256]{2,1,0:T(8,128)S(1)}, u32[]{:S(2)}, u32[]{:S(2)}) collective-permute-start(f32[1,104,256]{2,1,0:T(8,128)S(1)} %get-tuple-element.47), channel_id=1, source_target_pairs={{0,1},{1,2},{2,3},{3,4},{4,5},{5,6},{6,7},{8,9},{9,10},{10,11},{11... | collective-permute-start | bytes 319496 | tf_op jit(solution)/shard_map/ppermute | solution.py:33
  77.4 7.0 %collective-permute-start.7 = (f32[1,104,256]{2,1,0:T(8,128)S(1)}, f32[1,104,256]{2,1,0:T(8,128)S(1)}, u32[]{:S(2)}, u32[]{:S(2)}) collective-permute-start(f32[1,104,256]{2,1,0:T(8,128)S(1)} %get-tuple-element.48), channel_id=1, source_target_pairs={{1,0},{2,1},{3,2},{4,3},{5,4},{6,5},{7,6},{9,8},{10,9},{11,10},{12... | collective-permute-start | bytes 319496 | tf_op jit(solution)/shard_map/ppermute | solution.py:33
  84.4 0.5 column_sum.2
  84.9 4.7 %collective-permute-start.4 = (f32[2,104,256]{2,1,0:T(8,128)S(1)}, f32[2,104,256]{2,1,0:T(8,128)S(1)}, u32[]{:S(2)}, u32[]{:S(2)}) collective-permute-start(f32[2,104,256]{2,1,0:T(8,128)S(1)} %get-tuple-element.45), channel_id=1, source_target_pairs={{0,8},{8,16},{16,24},{24,32},{32,40},{40,48},{48,56},{56,64},{64,7... | collective-permute-start | bytes 638984 | tf_op jit(solution)/shard_map/ppermute | solution.py:33
  89.7 1.9 %collective-permute-start.5 = (f32[2,104,256]{2,1,0:T(8,128)S(1)}, f32[2,104,256]{2,1,0:T(8,128)S(1)}, u32[]{:S(2)}, u32[]{:S(2)}) collective-permute-start(f32[2,104,256]{2,1,0:T(8,128)S(1)} %get-tuple-element.46), channel_id=1, source_target_pairs={{8,0},{16,8},{24,16},{32,24},{40,32},{48,40},{56,48},{64,56},{72,6... | collective-permute-start | bytes 638984 | tf_op jit(solution)/shard_map/ppermute | solution.py:33
  91.6 0.3 column_sum.3
  91.9 5.8 %collective-permute-start.8 = (f32[1,104,256]{2,1,0:T(8,128)S(1)}, f32[1,104,256]{2,1,0:T(8,128)S(1)}, u32[]{:S(2)}, u32[]{:S(2)}) collective-permute-start(f32[1,104,256]{2,1,0:T(8,128)S(1)} %get-tuple-element.50), channel_id=1, source_target_pairs={{0,8},{8,16},{16,24},{24,32},{32,40},{40,48},{48,56},{56,64},{64,7... | collective-permute-start | bytes 319496 | tf_op jit(solution)/shard_map/ppermute | solution.py:33
  97.7 1.9 %collective-permute-start.9 = (f32[1,104,256]{2,1,0:T(8,128)S(1)}, f32[1,104,256]{2,1,0:T(8,128)S(1)}, u32[]{:S(2)}, u32[]{:S(2)}) collective-permute-start(f32[1,104,256]{2,1,0:T(8,128)S(1)} %get-tuple-element.51), channel_id=1, source_target_pairs={{8,0},{16,8},{24,16},{32,24},{40,32},{48,40},{56,48},{64,56},{72,6... | collective-permute-start | bytes 319496 | tf_op jit(solution)/shard_map/ppermute | solution.py:33
  99.6 0.9 pad_maximum_fusion
  100.6 5.3 %collective-permute-done.9.refs_5_ = f32[1,104,256]{2,1,0:T(8,128)S(1)} collective-permute-done((f32[1,104,256]{2,1,0:T(8,128)S(1)}, f32[1,104,256]{2,1,0:T(8,128)S(1)}, u32[]{:S(2)}, u32[]{:S(2)}) %collective-permute-start.9) | collective-permute-done | bytes 106528 | tf_op jit(solution)/shard_map/ppermute | solution.py:33
  105.8 1.5 %row_sum.1 = f32[3,256,256]{2,1,0:T(8,128)} custom-call(f32[2,256,256]{2,1,0:T(8,128)S(1)} %get-tuple-element.44.refs_0_, f32[2,104,256]{2,1,0:T(8,128)S(1)} %collective-permute-done.4.refs_1_, f32[2,104,256]{2,1,0:T(8,128)S(1)} %collective-permute-done.5.refs_2_, f32[1,256,256]{2,1,0:T(8,128)S(1)} %get-tuple-element.49.refs_3_, ...), custom_call_target="tpu_custom_call" | custom-call | tf_op jit(solution)/shard_map/row_sum/pallas_call | solution.py:436
  (40 shorter events, 0.6 us)
Async XLA Ops:
  0.6 7.8 %copy-start.9 = (s32[1,128,128]{2,1,0:T(8,128)S(1)}, s32[1,128,128]{2,1,0:T(8,128)}, u32[]{:S(2)}) copy-start(s32[1,128,128]{2,1,0:T(8,128)} %cell_ref.1) | copy-start | bytes 196612
  0.6 7.8 %copy-start.7 = (s32[1,128]{1,0:T(1,128)S(1)}, s32[1,128]{1,0:T(1,128)}, u32[]{:S(2)}) copy-start(s32[1,128]{1,0:T(1,128)} %count_ref.3) | copy-start | bytes 1540
  0.7 7.8 %copy-start.10 = (s32[1,128,128]{2,1,0:T(8,128)S(1)}, s32[1,128,128]{2,1,0:T(8,128)}, u32[]{:S(2)}) copy-start(s32[1,128,128]{2,1,0:T(8,128)} %patch_ref.7) | copy-start | bytes 196612
  0.7 7.8 %copy-start.8 = (f32[3,256,256]{2,1,0:T(8,128)S(1)}, f32[3,256,256]{2,1,0:T(8,128)}, u32[]{:S(2)}) copy-start(f32[3,256,256]{2,1,0:T(8,128)} %area_ref.3) | copy-start | bytes 2359300
  2.1 11.7 %collective-permute-start.1 = (f32[2,4,64]{2,1,0:T(4,128)S(1)}, f32[2,4,64]{2,1,0:T(4,128)S(1)}, u32[]{:S(2)}, u32[]{:S(2)}) collective-permute-start(f32[2,4,64]{2,1,0:T(4,128)S(1)} %pad_maximum_fusion.2), channel_id=1, source_target_pairs={{0,1},{1,2},{2,3},{3,4},{4,5},{5,6},{6,7},{8,9},{9,10},{10,11},{11... | collective-permute-start | bytes 6152 | tf_op jit(solution)/shard_map/ppermute | solution.py:33
  5.8 8.1 %copy-start = (f32[3,2,3,4,64,128]{5,4,3,2,1,0:T(8,128)S(1)}, f32[3,2,3,4,64,128]{5,4,3,2,1,0:T(8,128)}, u32[]{:S(2)}) copy-start(f32[3,2,3,4,64,128]{5,4,3,2,1,0:T(8,128)} %dft_e_ref.1) | copy-start | bytes 7077892
  5.8 8.1 %copy-start.1 = (f32[3,2,3,4,64,128]{5,4,3,2,1,0:T(8,128)S(1)}, f32[3,2,3,4,64,128]{5,4,3,2,1,0:T(8,128)}, u32[]{:S(2)}) copy-start(f32[3,2,3,4,64,128]{5,4,3,2,1,0:T(8,128)} %dft_h_ref.1) | copy-start | bytes 7077892
  5.8 8.1 %copy-start.2 = (f32[3,4,64,128]{3,2,1,0:T(8,128)S(1)}, f32[3,4,64,128]{3,2,1,0:T(8,128)}, u32[]{:S(2)}) copy-start(f32[3,4,64,128]{3,2,1,0:T(8,128)} %h_ref.1) | copy-start | bytes 1179652
  5.8 8.1 %copy-start.3 = (f32[3,4,64,128]{3,2,1,0:T(8,128)S(1)}, f32[3,4,64,128]{3,2,1,0:T(8,128)}, u32[]{:S(2)}) copy-start(f32[3,4,64,128]{3,2,1,0:T(8,128)} %e_ref.1) | copy-start | bytes 1179652
  5.9 8.1 %copy-start.4 = (f32[3,4,64,128]{3,2,1,0:T(8,128)S(1)}, f32[3,4,64,128]{3,2,1,0:T(8,128)}, u32[]{:S(2)}) copy-start(f32[3,4,64,128]{3,2,1,0:T(8,128)} %j_ref.1) | copy-start | bytes 1179652
  5.9 8.1 %copy-start.5 = (s32[4,64,128]{2,1,0:T(8,128)S(1)}, s32[4,64,128]{2,1,0:T(8,128)}, u32[]{:S(2)}) copy-start(s32[4,64,128]{2,1,0:T(8,128)} %kind_ref.1) | copy-start | bytes 393220
  5.9 8.1 %copy-start.6 = (f32[4,32]{1,0:T(4,128)S(1)}, f32[4,32]{1,0:T(4,128)}, u32[]{:S(2)}) copy-start(f32[4,32]{1,0:T(4,128)} %table_ref.1) | copy-start | bytes 1540
  5.9 8.0 %collective-permute-start = (f32[2,4,128]{2,1,0:T(4,128)S(1)}, f32[2,4,128]{2,1,0:T(4,128)S(1)}, u32[]{:S(2)}, u32[]{:S(2)}) collective-permute-start(f32[2,4,128]{2,1,0:T(4,128)S(1)} %pad_maximum_fusion.1), channel_id=1, source_target_pairs={{0,8},{8,16},{16,24},{24,32},{32,40},{40,48},{48,56},{56,64},{64,7... | collective-permute-start | bytes 12296 | tf_op jit(solution)/shard_map/ppermute | solution.py:33
  29.2 22.2 %all-to-all-start = ((f32[128,9,1,128]{3,2,1,0:T(1,128)}), f32[128,9,1,128]{3,2,1,0:T(1,128)S(1)}, u32[]{:S(2)}, u32[]{:S(2)}) async-start(f32[128,9,1,128]{3,2,1,0:T(1,128)} %gather_flux.1), calls=%async_computation | async-start | bytes 1179648 | tf_op jit(solution)/shard_map/all_to_all | solution.py:459
  61.1 23.3 %collective-permute-start.2 = (f32[2,104,256]{2,1,0:T(8,128)S(1)}, f32[2,104,256]{2,1,0:T(8,128)S(1)}, u32[]{:S(2)}, u32[]{:S(2)}) collective-permute-start(f32[2,104,256]{2,1,0:T(8,128)S(1)} %get-tuple-element.42), channel_id=1, source_target_pairs={{0,1},{1,2},{2,3},{3,4},{4,5},{5,6},{6,7},{8,9},{9,10},{10,11},{11... | collective-permute-start | bytes 638984 | tf_op jit(solution)/shard_map/ppermute | solution.py:33
  64.3 20.2 %collective-permute-start.3 = (f32[2,104,256]{2,1,0:T(8,128)S(1)}, f32[2,104,256]{2,1,0:T(8,128)S(1)}, u32[]{:S(2)}, u32[]{:S(2)}) collective-permute-start(f32[2,104,256]{2,1,0:T(8,128)S(1)} %get-tuple-element.43), channel_id=1, source_target_pairs={{1,0},{2,1},{3,2},{4,3},{5,4},{6,5},{7,6},{9,8},{10,9},{11,10},{12... | collective-permute-start | bytes 638984 | tf_op jit(solution)/shard_map/ppermute | solution.py:33
  75.5 16.1 %collective-permute-start.6 = (f32[1,104,256]{2,1,0:T(8,128)S(1)}, f32[1,104,256]{2,1,0:T(8,128)S(1)}, u32[]{:S(2)}, u32[]{:S(2)}) collective-permute-start(f32[1,104,256]{2,1,0:T(8,128)S(1)} %get-tuple-element.47), channel_id=1, source_target_pairs={{0,1},{1,2},{2,3},{3,4},{4,5},{5,6},{6,7},{8,9},{9,10},{10,11},{11... | collective-permute-start | bytes 319496 | tf_op jit(solution)/shard_map/ppermute | solution.py:33
  77.4 14.2 %collective-permute-start.7 = (f32[1,104,256]{2,1,0:T(8,128)S(1)}, f32[1,104,256]{2,1,0:T(8,128)S(1)}, u32[]{:S(2)}, u32[]{:S(2)}) collective-permute-start(f32[1,104,256]{2,1,0:T(8,128)S(1)} %get-tuple-element.48), channel_id=1, source_target_pairs={{1,0},{2,1},{3,2},{4,3},{5,4},{6,5},{7,6},{9,8},{10,9},{11,10},{12... | collective-permute-start | bytes 319496 | tf_op jit(solution)/shard_map/ppermute | solution.py:33
  84.9 20.9 %collective-permute-start.4 = (f32[2,104,256]{2,1,0:T(8,128)S(1)}, f32[2,104,256]{2,1,0:T(8,128)S(1)}, u32[]{:S(2)}, u32[]{:S(2)}) collective-permute-start(f32[2,104,256]{2,1,0:T(8,128)S(1)} %get-tuple-element.45), channel_id=1, source_target_pairs={{0,8},{8,16},{16,24},{24,32},{32,40},{40,48},{48,56},{56,64},{64,7... | collective-permute-start | bytes 638984 | tf_op jit(solution)/shard_map/ppermute | solution.py:33
  89.7 16.2 %collective-permute-start.5 = (f32[2,104,256]{2,1,0:T(8,128)S(1)}, f32[2,104,256]{2,1,0:T(8,128)S(1)}, u32[]{:S(2)}, u32[]{:S(2)}) collective-permute-start(f32[2,104,256]{2,1,0:T(8,128)S(1)} %get-tuple-element.46), channel_id=1, source_target_pairs={{8,0},{16,8},{24,16},{32,24},{40,32},{48,40},{56,48},{64,56},{72,6... | collective-permute-start | bytes 638984 | tf_op jit(solution)/shard_map/ppermute | solution.py:33
  91.9 8.6 %collective-permute-start.8 = (f32[1,104,256]{2,1,0:T(8,128)S(1)}, f32[1,104,256]{2,1,0:T(8,128)S(1)}, u32[]{:S(2)}, u32[]{:S(2)}) collective-permute-start(f32[1,104,256]{2,1,0:T(8,128)S(1)} %get-tuple-element.50), channel_id=1, source_target_pairs={{0,8},{8,16},{16,24},{24,32},{32,40},{40,48},{48,56},{56,64},{64,7... | collective-permute-start | bytes 319496 | tf_op jit(solution)/shard_map/ppermute | solution.py:33
  97.7 8.1 %collective-permute-start.9 = (f32[1,104,256]{2,1,0:T(8,128)S(1)}, f32[1,104,256]{2,1,0:T(8,128)S(1)}, u32[]{:S(2)}, u32[]{:S(2)}) collective-permute-start(f32[1,104,256]{2,1,0:T(8,128)S(1)} %get-tuple-element.51), channel_id=1, source_target_pairs={{8,0},{16,8},{24,16},{32,24},{40,32},{48,40},{56,48},{64,56},{72,6... | collective-permute-start | bytes 319496 | tf_op jit(solution)/shard_map/ppermute | solution.py:33

commit v5 on v4

--- a/solution.py
+++ b/solution.py
@@ -31,6 +31,33 @@
     count = lax.axis_size(axis)
     leading, last = (max(0, -steps), min(count, count - steps))
     return lax.ppermute(value, axis, [(source, source + steps) for source in range(leading, last)])
+
+
+def exchange(first, second, axis):
+    count = lax.axis_size(axis)
+    swaps = []
+    for start, value in ((0, first), (1, second)):
+        lower = range(start, count - 1, 2)
+        pairs = [(i, i + 1) for i in lower] + [(i + 1, i) for i in lower]
+        swaps.append(lax.ppermute(value, axis, pairs))
+    return swaps
+
+
+def put_edges(odd, head, tail, first_ref, second_ref, f):
+    @pl.when(odd == 0)
+    def _():
+        first_ref[f] = tail
+        second_ref[f] = head
+
+    @pl.when(odd != 0)
+    def _():
+        first_ref[f] = head
+        second_ref[f] = tail
+
+
+def got_edges(odd, first_ref, second_ref, f):
+    first, second = first_ref[f], second_ref[f]
+    return jnp.where(odd == 0, second, first), jnp.where(odd == 0, first, second)
 
 
 def onehot(count, index):
@@ -301,10 +328,11 @@
 
 
 EDGE = 104
+PIECES = ((0, 2), (2, 1))
 
 
 def scatter_kernel(
-    patch_ref, area_a_ref, area_b_ref, flux_ref, out_ref, head_ref, tail_ref, *, first
+    odd_ref, patch_ref, area_a_ref, area_b_ref, flux_ref, out_ref, first_ref, second_ref, *, first
 ):
     freqs = out_ref.shape[0]
     out_ref[...] = jnp.zeros_like(out_ref)
@@ -345,8 +373,9 @@
     lax.fori_loop(0, half, first_part, 0, unroll=4)
     lax.fori_loop(0, area_b_ref.shape[0], second_part, 0, unroll=4)
     for f in range(freqs):
-        head_ref[f] = jnp.transpose(out_ref[f, :, :128])[:EDGE]
-        tail_ref[f] = jnp.transpose(out_ref[f, :, 128:])[128 - EDGE :]
+        head = jnp.transpose(out_ref[f, :, :128])[:EDGE]
+        tail = jnp.transpose(out_ref[f, :, 128:])[128 - EDGE :]
+        put_edges(odd_ref[0, 0], head, tail, first_ref, second_ref, f)
 
 
 def block_and_edges(freqs):
@@ -357,18 +386,18 @@
     )
 
 
-def scatter_density(patch, area_a, area_b, flux, first, freqs):
+def scatter_density(odd, patch, area_a, area_b, flux, first, freqs):
     return pl.pallas_call(
         functools.partial(scatter_kernel, first=first),
         out_shape=block_and_edges(freqs),
-        in_specs=[VMEM] * 4,
+        in_specs=[SMEM] + [VMEM] * 4,
         out_specs=(VMEM,) * 3,
         compiler_params=pltpu.CompilerParams(vmem_limit_bytes=36 << 20),
         cost_estimate=pl.CostEstimate(
             flops=2 * freqs * 65536 * 2 * 16384, bytes_accessed=2000000, transcendentals=0
         ),
         name="scatter_density",
-    )(patch, area_a, area_b, flux)
+    )(odd, patch, area_a, area_b, flux)
 
 
 def in_window(place):
@@ -380,7 +409,7 @@
     return head, (cells - head.astype(f32)).astype(bf16)
 
 
-def column_kernel(block_ref, before_ref, after_ref, out_ref, head_ref, tail_ref):
+def column_kernel(odd_ref, block_ref, one_ref, two_ref, out_ref, first_ref, second_ref):
     inner = in_window(iota((256, 256), 0) - iota((256, 256), 1))
     place, column = iota((EDGE, 256), 0), iota((EDGE, 256), 1)
     outer = jnp.concatenate(
@@ -392,7 +421,7 @@
         total = jnp.dot(
             jnp.concatenate(two_parts(block_ref[f]), 1), inner, preferred_element_type=f32
         )
-        edges = jnp.concatenate([before_ref[f], after_ref[f]], 0)
+        edges = jnp.concatenate(got_edges(odd_ref[0, 0], one_ref, two_ref, f), 0)
         total = total + lax.dot_general(
             jnp.concatenate(two_parts(edges), 0),
             outer,
@@ -400,31 +429,31 @@
             preferred_element_type=f32,
         )
         out_ref[f] = total
-        head_ref[f] = total[:EDGE]
-        tail_ref[f] = total[256 - EDGE :]
-
-
-def column_sum(block, before, after):
+        put_edges(odd_ref[0, 1], total[:EDGE], total[256 - EDGE :], first_ref, second_ref, f)
+
+
+def column_sum(odd, block, first, second):
     freqs = block.shape[0]
     return pl.pallas_call(
         column_kernel,
         out_shape=block_and_edges(freqs),
-        in_specs=[VMEM] * 3,
+        in_specs=[SMEM] + [VMEM] * 3,
         out_specs=(VMEM,) * 3,
         compiler_params=pltpu.CompilerParams(vmem_limit_bytes=16 << 20),
         name="column_sum",
-    )(block, before, after)
-
-
-def row_kernel(*refs):
+    )(odd, block, first, second)
+
+
+def row_kernel(odd_ref, *refs):
     out_ref = refs[-1]
     length = 256 + 2 * EDGE
     band = in_window(iota((256, length), 1) - EDGE - iota((256, length), 0))
     band = jnp.concatenate([band, band], 1)
     done = 0
-    for block_ref, before_ref, after_ref in zip(refs[0:-1:3], refs[1:-1:3], refs[2:-1:3]):
+    for block_ref, one_ref, two_ref in zip(refs[0:-1:3], refs[1:-1:3], refs[2:-1:3]):
         for f in range(block_ref.shape[0]):
-            cells = jnp.concatenate([before_ref[f], block_ref[f], after_ref[f]], 0)
+            before, after = got_edges(odd_ref[0, 1], one_ref, two_ref, f)
+            cells = jnp.concatenate([before, block_ref[f], after], 0)
             total = jnp.dot(
                 band, jnp.concatenate(two_parts(cells), 0), preferred_element_type=f32
             )
@@ -432,15 +461,15 @@
             done += 1
 
 
-def row_sum(*pieces):
+def row_sum(odd, *pieces):
     return pl.pallas_call(
         row_kernel,
         out_shape=jax.ShapeDtypeStruct((3, 256, 256), f32),
-        in_specs=[VMEM] * len(pieces),
+        in_specs=[SMEM] + [VMEM] * len(pieces),
         out_specs=VMEM,
         compiler_params=pltpu.CompilerParams(vmem_limit_bytes=16 << 20),
         name="row_sum",
-    )(*pieces)
+    )(odd, *pieces)
 
 
 def shards(
@@ -450,6 +479,7 @@
     magnet_x, magnet_y, magnet_z = (h_field[0], h_field[1], h_field[2])
     rows_below = shifted(jnp.stack([magnet_y[:, -1, :], magnet_z[:, -1, :]]), "gy", 1)
     cols_left = shifted(jnp.stack([magnet_x[:, :, -1], magnet_z[:, :, -1]]), "gx", 1)
+    odd = jnp.stack([lax.axis_index("gx") % 2, lax.axis_index("gy") % 2]).reshape(1, 2)
     area_a, packed, offsets = gather_area_and_pack(counts, skin_cell, patch_slot, area, 4)
     rows_below, cols_left, area_a = lax.optimization_barrier((rows_below, cols_left, area_a))
     e_next, j_next, dft_e_next, dft_h_next, table = field_step(
@@ -459,17 +489,16 @@
     arrived = lax.all_to_all(rows, ("gy", "gx"), split_axis=0, concat_axis=0, tiled=True)
     area_b = gather_area(patch_slot, area, 4, 12)
 
-    blocks, pieces = [], []
-    edges = []
-    for first, freqs in ((0, 2), (2, 1)):
-        block, head, tail = scatter_density(patch_slot, area_a, area_b, arrived, first, freqs)
+    blocks, pieces, swaps = [], [], []
+    for first, freqs in PIECES:
+        block, *edges = scatter_density(odd, patch_slot, area_a, area_b, arrived, first, freqs)
         blocks.append(block)
-        edges.append((shifted(tail, "gx", 1), shifted(head, "gx", -1)))
-    for block, (before, after) in zip(blocks, edges):
-        strip, head, tail = column_sum(block, before, after)
-        pieces += [strip, shifted(tail, "gy", 1), shifted(head, "gy", -1)]
+        swaps.append(exchange(*edges, "gx"))
+    for block, swap in zip(blocks, swaps):
+        strip, *edges = column_sum(odd, block, *swap)
+        pieces += [strip, *exchange(*edges, "gy")]
     point_density = jnp.concatenate(blocks, 0)
-    avg_density = row_sum(*pieces)
+    avg_density = row_sum(odd, *pieces)
     return (e_next, j_next, dft_e_next, dft_h_next, point_density, avg_density)
 
 

time: 108 us -> 97.3 us (0.901)
  the two profiles are of different devices: /device:TPU:101 before, /device:TPU:26 now
where the time goes in v5:
time: 97.3 us; the launch traced here: 97.1 us
  Pallas kernels  51 us (52%)
  starting transfers between devices  38.4 us (39%)
  waiting for transfers between devices  3.66 us (4%)
  local copies, waits for them, and re-layouts  1.92 us (2%)
  between operations  1.03 us (1%)
  other arithmetic  1.02 us (1%)
    ppermute x8, starting transfers between devices, exchange(): swaps.append(lax.ppermute(value, axis, pairs))  20.4 us
    pallas_call x2, Pallas kernels, scatter_density(): pl.pallas_call(functools.partial(scatter_kernel, first=first), out_shape=...  16.2 us
    all_to_all x1, starting transfers between devices, shards(): lax.all_to_all(rows, ('gy', 'gx'), split_axis=0, concat_axis=0, tiled=True)  12.4 us
    pallas_call x1, Pallas kernels, gather_area(): pl.pallas_call(functools.partial(area_kernel, first=first), out_shape=jax...  11.3 us
    pallas_call x1, Pallas kernels, gather_flux(): pl.pallas_call(gather_kernel, out_shape=jax.ShapeDtypeStruct((128, 9, 1,...  9.66 us
    ppermute x2, starting transfers between devices, shifted(): lax.ppermute(value, axis, [(source, source + steps) for source in range(l...  5.61 us
    pallas_call x1, Pallas kernels, gather_area_and_pack(): pl.pallas_call(functools.partial(first_area_kernel, groups=groups), out_s...  5.37 us
    pallas_call x1, Pallas kernels, field_step(): pl.pallas_call(field_kernel, grid=(planes,), out_shape=(jax.ShapeDtypeStr...  4.13 us
  transfers between devices with their start and end apart: 11, of which 2 were waited for; matrix products, arithmetic and copies ran while one was open for 1% of the time, Pallas kernels for 26%

profile of v5, /device:TPU:26, one launch (start us, length us, event | category | flops | bytes accessed | tf_op | source)
XLA Modules:
  0.0 97.1 jit_solution(18436478545383363686)
XLA Ops:
  0.7 1.1 %fusion = (f32[1,4,64,128]{3,2,1,0:T(8,128)S(1)}, f32[1,4,64,128]{3,2,1,0:T(8,128)S(1)}, f32[1,4,64,128]{3,2,1,0:T(8,128)S(1)}) fusion(f32[3,4,64,128]{3,2,1,0:T(8,128)} %h_ref.1), kind=kLoop, calls=%fused_computation.8 | loop fusion | bytes 786432 | tf_op jit(solution)/shard_map/slice | solution.py:479
  1.8 0.1 copy.26
  2.1 3.7 %collective-permute-start.1 = (f32[2,4,64]{2,1,0:T(4,128)S(1)}, f32[2,4,64]{2,1,0:T(4,128)S(1)}, u32[]{:S(2)}, u32[]{:S(2)}) collective-permute-start(f32[2,4,64]{2,1,0:T(4,128)S(1)} %pad_maximum_fusion.2), channel_id=1, source_target_pairs={{0,1},{1,2},{2,3},{3,4},{4,5},{5,6},{6,7},{8,9},{9,10},{10,11},{11... | collective-permute-start | bytes 6152 | tf_op jit(solution)/shard_map/ppermute | solution.py:33
  5.8 0.2 slice.29
  6.3 1.9 %collective-permute-start = (f32[2,4,128]{2,1,0:T(4,128)S(1)}, f32[2,4,128]{2,1,0:T(4,128)S(1)}, u32[]{:S(2)}, u32[]{:S(2)}) collective-permute-start(f32[2,4,128]{2,1,0:T(4,128)S(1)} %pad_maximum_fusion.1), channel_id=1, source_target_pairs={{0,8},{8,16},{16,24},{24,32},{32,40},{40,48},{48,56},{56,64},{64,7... | collective-permute-start | bytes 12296 | tf_op jit(solution)/shard_map/ppermute | solution.py:33
  8.4 5.4 %area_and_pack.1 = (f32[4,8,1024]{2,1,0:T(8,128)S(1)}, s32[136,128]{1,0:T(8,128)S(1)}, s32[1,136]{1,0:T(1,128)S(1)}) custom-call(s32[1,128]{1,0:T(1,128)S(1)} %copy-done.7, s32[1,128,128]{2,1,0:T(8,128)S(1)} %copy-done.9, s32[1,128,128]{2,1,0:T(8,128)S(1)} %copy-done.10, f32[3,256,256]{2,1,0:T(8,128)S(1)} %copy-done.8), custom_call_target="tpu_custom_call" | custom-call | flops 3221225472 | bytes 2000000 | tf_op jit(solution)/shard_map/area_and_pack/pallas_call | solution.py:301
  13.9 4.1 %field_step.1 = (f32[3,4,64,128]{3,2,1,0:T(8,128)}, f32[3,4,64,128]{3,2,1,0:T(8,128)}, f32[3,2,3,4,64,128]{5,4,3,2,1,0:T(8,128)}, f32[3,2,3,4,64,128]{5,4,3,2,1,0:T(8,128)}, bf16[9,2,64,512]{3,2,1,0:T(8,128)(2,1)S(1)}) custom-call(f32[3,4,64,128]{3,2,1,0:T(8,128)S(1)} %copy-done.3, f32[3,4,64,128]{3,2,1,0:T(8,128)S(1)} %copy-done.2, ...), custom_call_target="tpu_custom_call" | custom-call | tf_op jit(solution)/shard_map/field_step/pallas_call | solution.py:152
  18.0 9.7 %gather_flux.1 = f32[128,9,1,128]{3,2,1,0:T(1,128)} custom-call(s32[1,128]{1,0:T(1,128)S(1)} %copy-done.7, s32[1,136]{1,0:T(1,128)S(1)} %get-tuple-element.37.offset_ref, s32[136,128]{1,0:T(8,128)S(1)} %get-tuple-element.38.packed, bf16[9,128,512]{2,1,0:T(8,128)(2,1)S(1)} %bitcast.17), custom_call_target="tpu_custom_call" | custom-call | tf_op jit(solution)/shard_map/gather_flux/pallas_call | solution.py:218
  27.7 12.4 %all-to-all-start = ((f32[128,9,1,128]{3,2,1,0:T(1,128)}), f32[128,9,1,128]{3,2,1,0:T(1,128)S(1)}, u32[]{:S(2)}, u32[]{:S(2)}) async-start(f32[128,9,1,128]{3,2,1,0:T(1,128)} %gather_flux.1), calls=%async_computation | async-start | bytes 1179648 | tf_op jit(solution)/shard_map/all_to_all | solution.py:489
  40.1 11.3 %gather_area.1.area_b_ref = f32[12,8,1024]{2,1,0:T(8,128)S(1)} custom-call(s32[1,128,128]{2,1,0:T(8,128)S(1)} %copy-done.10, f32[3,256,256]{2,1,0:T(8,128)S(1)} %copy-done.8), custom_call_target="tpu_custom_call" | custom-call | flops 9663676416 | bytes 2000000 | tf_op jit(solution)/shard_map/gather_area/pallas_call | solution.py:318
  51.4 0.4 all-to-all-done.flux_ref
  51.8 10.3 %scatter_density.2 = (f32[2,256,256]{2,1,0:T(8,128)S(1)}, f32[2,104,256]{2,1,0:T(8,128)S(1)}, f32[2,104,256]{2,1,0:T(8,128)S(1)}) custom-call(s32[1,2]{1,0:T(1,128)S(1)} %add_bitcast_fusion.odd_ref, s32[1,128,128]{2,1,0:T(8,128)S(1)} %copy-done.10, f32[4,8,1024]{2,1,0:T(8,128)S(1)} %get-tuple-element.36.area_a_ref, ...), custom_call_target="tpu_custom_call" | custom-call | flops 8589934592 | bytes 2000000 | tf_op jit(solution)/shard_map/scatter_density/pallas_call | solution.py:390
  62.1 1.0 %collective-permute-start.2 = (f32[2,104,256]{2,1,0:T(8,128)S(1)}, f32[2,104,256]{2,1,0:T(8,128)S(1)}, u32[]{:S(2)}, u32[]{:S(2)}) collective-permute-start(f32[2,104,256]{2,1,0:T(8,128)S(1)} %get-tuple-element.42), channel_id=1, source_target_pairs={{0,1},{2,3},{4,5},{6,7},{1,0},{3,2},{5,4},{7,6},{8,9},{10,11},{12,... | collective-permute-start | bytes 638984 | tf_op jit(solution)/shard_map/ppermute | solution.py:42
  63.2 4.2 %collective-permute-start.3 = (f32[2,104,256]{2,1,0:T(8,128)S(1)}, f32[2,104,256]{2,1,0:T(8,128)S(1)}, u32[]{:S(2)}, u32[]{:S(2)}) collective-permute-start(f32[2,104,256]{2,1,0:T(8,128)S(1)} %get-tuple-element.43), channel_id=1, source_target_pairs={{1,2},{3,4},{5,6},{2,1},{4,3},{6,5},{9,10},{11,12},{13,14},{10,9},... | collective-permute-start | bytes 638984 | tf_op jit(solution)/shard_map/ppermute | solution.py:42
  67.3 5.9 %scatter_density.3 = (f32[1,256,256]{2,1,0:T(8,128)S(1)}, f32[1,104,256]{2,1,0:T(8,128)S(1)}, f32[1,104,256]{2,1,0:T(8,128)S(1)}) custom-call(s32[1,2]{1,0:T(1,128)S(1)} %add_bitcast_fusion.odd_ref, s32[1,128,128]{2,1,0:T(8,128)S(1)} %copy-done.10, f32[4,8,1024]{2,1,0:T(8,128)S(1)} %get-tuple-element.36.area_a_ref, ...), custom_call_target="tpu_custom_call" | custom-call | flops 4294967296 | bytes 2000000 | tf_op jit(solution)/shard_map/scatter_density/pallas_call | solution.py:390
  73.2 0.4 collective-permute-start.6
  73.6 5.2 %collective-permute-start.7 = (f32[1,104,256]{2,1,0:T(8,128)S(1)}, f32[1,104,256]{2,1,0:T(8,128)S(1)}, u32[]{:S(2)}, u32[]{:S(2)}) collective-permute-start(f32[1,104,256]{2,1,0:T(8,128)S(1)} %get-tuple-element.48), channel_id=1, source_target_pairs={{1,2},{3,4},{5,6},{2,1},{4,3},{6,5},{9,10},{11,12},{13,14},{10,9},... | collective-permute-start | bytes 319496 | tf_op jit(solution)/shard_map/ppermute | solution.py:42
  78.8 1.4 %column_sum.2 = (f32[2,256,256]{2,1,0:T(8,128)S(1)}, f32[2,104,256]{2,1,0:T(8,128)S(1)}, f32[2,104,256]{2,1,0:T(8,128)S(1)}) custom-call(s32[1,2]{1,0:T(1,128)S(1)} %add_bitcast_fusion.odd_ref, f32[2,256,256]{2,1,0:T(8,128)S(1)} %get-tuple-element.40.block_ref, f32[2,104,256]{2,1,0:T(8,128)S(1)} %collective-permute-done.2.one_ref, ...), custom_call_target="tpu_custom_call" | custom-call | tf_op jit(solution)/shard_map/column_sum/pallas_call | solution.py:437
  80.3 5.5 %collective-permute-start.5 = (f32[2,104,256]{2,1,0:T(8,128)S(1)}, f32[2,104,256]{2,1,0:T(8,128)S(1)}, u32[]{:S(2)}, u32[]{:S(2)}) collective-permute-start(f32[2,104,256]{2,1,0:T(8,128)S(1)} %get-tuple-element.46), channel_id=1, source_target_pairs={{8,16},{24,32},{40,48},{56,64},{72,80},{88,96},{104,112},{16,8},{3... | collective-permute-start | bytes 638984 | tf_op jit(solution)/shard_map/ppermute | solution.py:42
  85.9 0.9 column_sum.3
  86.9 4.0 %collective-permute-start.9 = (f32[1,104,256]{2,1,0:T(8,128)S(1)}, f32[1,104,256]{2,1,0:T(8,128)S(1)}, u32[]{:S(2)}, u32[]{:S(2)}) collective-permute-start(f32[1,104,256]{2,1,0:T(8,128)S(1)} %get-tuple-element.51), channel_id=1, source_target_pairs={{8,16},{24,32},{40,48},{56,64},{72,80},{88,96},{104,112},{16,8},{3... | collective-permute-start | bytes 319496 | tf_op jit(solution)/shard_map/ppermute | solution.py:42
  90.8 0.9 pad_maximum_fusion
  91.8 3.2 %collective-permute-done.9.refs_5_ = f32[1,104,256]{2,1,0:T(8,128)S(1)} collective-permute-done((f32[1,104,256]{2,1,0:T(8,128)S(1)}, f32[1,104,256]{2,1,0:T(8,128)S(1)}, u32[]{:S(2)}, u32[]{:S(2)}) %collective-permute-start.9) | collective-permute-done | bytes 106528 | tf_op jit(solution)/shard_map/ppermute | solution.py:42
  95.0 2.1 %row_sum.1 = f32[3,256,256]{2,1,0:T(8,128)} custom-call(s32[1,2]{1,0:T(1,128)S(1)} %add_bitcast_fusion.odd_ref, f32[2,256,256]{2,1,0:T(8,128)S(1)} %get-tuple-element.44.refs_0_, f32[2,104,256]{2,1,0:T(8,128)S(1)} %collective-permute-done.4.refs_1_, f32[2,104,256]{2,1,0:T(8,128)S(1)} %collective-permute-done.5.refs_2_, ...), custom_call_target="tpu_custom_call" | custom-call | tf_op jit(solution)/shard_map/row_sum/pallas_call | solution.py:465
  (41 shorter events, 0.7 us)
Async XLA Ops:
  0.6 7.6 %copy-start.9 = (s32[1,128,128]{2,1,0:T(8,128)S(1)}, s32[1,128,128]{2,1,0:T(8,128)}, u32[]{:S(2)}) copy-start(s32[1,128,128]{2,1,0:T(8,128)} %cell_ref.1) | copy-start | bytes 196612
  0.6 7.6 %copy-start.7 = (s32[1,128]{1,0:T(1,128)S(1)}, s32[1,128]{1,0:T(1,128)}, u32[]{:S(2)}) copy-start(s32[1,128]{1,0:T(1,128)} %count_ref.3) | copy-start | bytes 1540
  0.7 7.6 %copy-start.10 = (s32[1,128,128]{2,1,0:T(8,128)S(1)}, s32[1,128,128]{2,1,0:T(8,128)}, u32[]{:S(2)}) copy-start(s32[1,128,128]{2,1,0:T(8,128)} %patch_ref.7) | copy-start | bytes 196612
  0.7 7.6 %copy-start.8 = (f32[3,256,256]{2,1,0:T(8,128)S(1)}, f32[3,256,256]{2,1,0:T(8,128)}, u32[]{:S(2)}) copy-start(f32[3,256,256]{2,1,0:T(8,128)} %area_ref.3) | copy-start | bytes 2359300
  2.1 11.7 %collective-permute-start.1 = (f32[2,4,64]{2,1,0:T(4,128)S(1)}, f32[2,4,64]{2,1,0:T(4,128)S(1)}, u32[]{:S(2)}, u32[]{:S(2)}) collective-permute-start(f32[2,4,64]{2,1,0:T(4,128)S(1)} %pad_maximum_fusion.2), channel_id=1, source_target_pairs={{0,1},{1,2},{2,3},{3,4},{4,5},{5,6},{6,7},{8,9},{9,10},{10,11},{11... | collective-permute-start | bytes 6152 | tf_op jit(solution)/shard_map/ppermute | solution.py:33
  6.3 7.5 %collective-permute-start = (f32[2,4,128]{2,1,0:T(4,128)S(1)}, f32[2,4,128]{2,1,0:T(4,128)S(1)}, u32[]{:S(2)}, u32[]{:S(2)}) collective-permute-start(f32[2,4,128]{2,1,0:T(4,128)S(1)} %pad_maximum_fusion.1), channel_id=1, source_target_pairs={{0,8},{8,16},{16,24},{24,32},{32,40},{40,48},{48,56},{56,64},{64,7... | collective-permute-start | bytes 12296 | tf_op jit(solution)/shard_map/ppermute | solution.py:33
  8.3 5.5 %copy-start = (f32[3,2,3,4,64,128]{5,4,3,2,1,0:T(8,128)S(1)}, f32[3,2,3,4,64,128]{5,4,3,2,1,0:T(8,128)}, u32[]{:S(2)}) copy-start(f32[3,2,3,4,64,128]{5,4,3,2,1,0:T(8,128)} %dft_e_ref.1) | copy-start | bytes 7077892
  8.3 5.5 %copy-start.1 = (f32[3,2,3,4,64,128]{5,4,3,2,1,0:T(8,128)S(1)}, f32[3,2,3,4,64,128]{5,4,3,2,1,0:T(8,128)}, u32[]{:S(2)}) copy-start(f32[3,2,3,4,64,128]{5,4,3,2,1,0:T(8,128)} %dft_h_ref.1) | copy-start | bytes 7077892
  8.3 5.5 %copy-start.2 = (f32[3,4,64,128]{3,2,1,0:T(8,128)S(1)}, f32[3,4,64,128]{3,2,1,0:T(8,128)}, u32[]{:S(2)}) copy-start(f32[3,4,64,128]{3,2,1,0:T(8,128)} %h_ref.1) | copy-start | bytes 1179652
  8.3 5.5 %copy-start.3 = (f32[3,4,64,128]{3,2,1,0:T(8,128)S(1)}, f32[3,4,64,128]{3,2,1,0:T(8,128)}, u32[]{:S(2)}) copy-start(f32[3,4,64,128]{3,2,1,0:T(8,128)} %e_ref.1) | copy-start | bytes 1179652
  8.3 5.5 %copy-start.4 = (f32[3,4,64,128]{3,2,1,0:T(8,128)S(1)}, f32[3,4,64,128]{3,2,1,0:T(8,128)}, u32[]{:S(2)}) copy-start(f32[3,4,64,128]{3,2,1,0:T(8,128)} %j_ref.1) | copy-start | bytes 1179652
  8.3 5.5 %copy-start.5 = (s32[4,64,128]{2,1,0:T(8,128)S(1)}, s32[4,64,128]{2,1,0:T(8,128)}, u32[]{:S(2)}) copy-start(s32[4,64,128]{2,1,0:T(8,128)} %kind_ref.1) | copy-start | bytes 393220
  8.4 5.5 %copy-start.6 = (f32[4,32]{1,0:T(4,128)S(1)}, f32[4,32]{1,0:T(4,128)}, u32[]{:S(2)}) copy-start(f32[4,32]{1,0:T(4,128)} %table_ref.1) | copy-start | bytes 1540
  27.7 24.1 %all-to-all-start = ((f32[128,9,1,128]{3,2,1,0:T(1,128)}), f32[128,9,1,128]{3,2,1,0:T(1,128)S(1)}, u32[]{:S(2)}, u32[]{:S(2)}) async-start(f32[128,9,1,128]{3,2,1,0:T(1,128)} %gather_flux.1), calls=%async_computation | async-start | bytes 1179648 | tf_op jit(solution)/shard_map/all_to_all | solution.py:489
  62.1 16.6 %collective-permute-start.2 = (f32[2,104,256]{2,1,0:T(8,128)S(1)}, f32[2,104,256]{2,1,0:T(8,128)S(1)}, u32[]{:S(2)}, u32[]{:S(2)}) collective-permute-start(f32[2,104,256]{2,1,0:T(8,128)S(1)} %get-tuple-element.42), channel_id=1, source_target_pairs={{0,1},{2,3},{4,5},{6,7},{1,0},{3,2},{5,4},{7,6},{8,9},{10,11},{12,... | collective-permute-start | bytes 638984 | tf_op jit(solution)/shard_map/ppermute | solution.py:42
  63.2 15.6 %collective-permute-start.3 = (f32[2,104,256]{2,1,0:T(8,128)S(1)}, f32[2,104,256]{2,1,0:T(8,128)S(1)}, u32[]{:S(2)}, u32[]{:S(2)}) collective-permute-start(f32[2,104,256]{2,1,0:T(8,128)S(1)} %get-tuple-element.43), channel_id=1, source_target_pairs={{1,2},{3,4},{5,6},{2,1},{4,3},{6,5},{9,10},{11,12},{13,14},{10,9},... | collective-permute-start | bytes 638984 | tf_op jit(solution)/shard_map/ppermute | solution.py:42
  73.2 12.6 %collective-permute-start.6 = (f32[1,104,256]{2,1,0:T(8,128)S(1)}, f32[1,104,256]{2,1,0:T(8,128)S(1)}, u32[]{:S(2)}, u32[]{:S(2)}) collective-permute-start(f32[1,104,256]{2,1,0:T(8,128)S(1)} %get-tuple-element.47), channel_id=1, source_target_pairs={{0,1},{2,3},{4,5},{6,7},{1,0},{3,2},{5,4},{7,6},{8,9},{10,11},{12,... | collective-permute-start | bytes 319496 | tf_op jit(solution)/shard_map/ppermute | solution.py:42
  73.6 12.3 %collective-permute-start.7 = (f32[1,104,256]{2,1,0:T(8,128)S(1)}, f32[1,104,256]{2,1,0:T(8,128)S(1)}, u32[]{:S(2)}, u32[]{:S(2)}) collective-permute-start(f32[1,104,256]{2,1,0:T(8,128)S(1)} %get-tuple-element.48), channel_id=1, source_target_pairs={{1,2},{3,4},{5,6},{2,1},{4,3},{6,5},{9,10},{11,12},{13,14},{10,9},... | collective-permute-start | bytes 319496 | tf_op jit(solution)/shard_map/ppermute | solution.py:42
  80.2 14.8 %collective-permute-start.4 = (f32[2,104,256]{2,1,0:T(8,128)S(1)}, f32[2,104,256]{2,1,0:T(8,128)S(1)}, u32[]{:S(2)}, u32[]{:S(2)}) collective-permute-start(f32[2,104,256]{2,1,0:T(8,128)S(1)} %get-tuple-element.45), channel_id=1, source_target_pairs={{0,8},{16,24},{32,40},{48,56},{64,72},{80,88},{96,104},{112,120},{... | collective-permute-start | bytes 638984 | tf_op jit(solution)/shard_map/ppermute | solution.py:42
  80.3 14.7 %collective-permute-start.5 = (f32[2,104,256]{2,1,0:T(8,128)S(1)}, f32[2,104,256]{2,1,0:T(8,128)S(1)}, u32[]{:S(2)}, u32[]{:S(2)}) collective-permute-start(f32[2,104,256]{2,1,0:T(8,128)S(1)} %get-tuple-element.46), channel_id=1, source_target_pairs={{8,16},{24,32},{40,48},{56,64},{72,80},{88,96},{104,112},{16,8},{3... | collective-permute-start | bytes 638984 | tf_op jit(solution)/shard_map/ppermute | solution.py:42
  86.8 5.0 %collective-permute-start.8 = (f32[1,104,256]{2,1,0:T(8,128)S(1)}, f32[1,104,256]{2,1,0:T(8,128)S(1)}, u32[]{:S(2)}, u32[]{:S(2)}) collective-permute-start(f32[1,104,256]{2,1,0:T(8,128)S(1)} %get-tuple-element.50), channel_id=1, source_target_pairs={{0,8},{16,24},{32,40},{48,56},{64,72},{80,88},{96,104},{112,120},{... | collective-permute-start | bytes 319496 | tf_op jit(solution)/shard_map/ppermute | solution.py:42
  86.9 8.1 %collective-permute-start.9 = (f32[1,104,256]{2,1,0:T(8,128)S(1)}, f32[1,104,256]{2,1,0:T(8,128)S(1)}, u32[]{:S(2)}, u32[]{:S(2)}) collective-permute-start(f32[1,104,256]{2,1,0:T(8,128)S(1)} %get-tuple-element.51), channel_id=1, source_target_pairs={{8,16},{24,32},{40,48},{56,64},{72,80},{88,96},{104,112},{16,8},{3... | collective-permute-start | bytes 319496 | tf_op jit(solution)/shard_map/ppermute | solution.py:42

commit v6 on v5

--- a/solution.py
+++ b/solution.py
@@ -36,28 +36,26 @@
 def exchange(first, second, axis):
     count = lax.axis_size(axis)
     swaps = []
-    for start, value in ((0, first), (1, second)):
+    for start, value in ((1, first), (0, second)):
         lower = range(start, count - 1, 2)
         pairs = [(i, i + 1) for i in lower] + [(i + 1, i) for i in lower]
         swaps.append(lax.ppermute(value, axis, pairs))
     return swaps
 
 
+def is_odd(odd_ref, axis):
+    row = odd_ref[axis : axis + 1, :]
+    return jnp.concatenate([row, row], 1) != 0
+
+
 def put_edges(odd, head, tail, first_ref, second_ref, f):
-    @pl.when(odd == 0)
-    def _():
-        first_ref[f] = tail
-        second_ref[f] = head
-
-    @pl.when(odd != 0)
-    def _():
-        first_ref[f] = head
-        second_ref[f] = tail
+    first_ref[f] = jnp.where(odd, tail, head)
+    second_ref[f] = jnp.where(odd, head, tail)
 
 
 def got_edges(odd, first_ref, second_ref, f):
     first, second = first_ref[f], second_ref[f]
-    return jnp.where(odd == 0, second, first), jnp.where(odd == 0, first, second)
+    return jnp.where(odd, second, first), jnp.where(odd, first, second)
 
 
 def onehot(count, index):
@@ -375,7 +373,7 @@
     for f in range(freqs):
         head = jnp.transpose(out_ref[f, :, :128])[:EDGE]
         tail = jnp.transpose(out_ref[f, :, 128:])[128 - EDGE :]
-        put_edges(odd_ref[0, 0], head, tail, first_ref, second_ref, f)
+        put_edges(is_odd(odd_ref, 0), head, tail, first_ref, second_ref, f)
 
 
 def block_and_edges(freqs):
@@ -390,7 +388,7 @@
     return pl.pallas_call(
         functools.partial(scatter_kernel, first=first),
         out_shape=block_and_edges(freqs),
-        in_specs=[SMEM] + [VMEM] * 4,
+        in_specs=[VMEM] * 5,
         out_specs=(VMEM,) * 3,
         compiler_params=pltpu.CompilerParams(vmem_limit_bytes=36 << 20),
         cost_estimate=pl.CostEstimate(
@@ -409,7 +407,8 @@
     return head, (cells - head.astype(f32)).astype(bf16)
 
 
-def column_kernel(odd_ref, block_ref, one_ref, two_ref, out_ref, first_ref, second_ref):
+def column_kernel(odd_ref, *refs):
+    refs, (out_ref, first_ref, second_ref) = refs[:-3], refs[-3:]
     inner = in_window(iota((256, 256), 0) - iota((256, 256), 1))
     place, column = iota((EDGE, 256), 0), iota((EDGE, 256), 1)
     outer = jnp.concatenate(
@@ -417,59 +416,57 @@
     )
     inner = jnp.concatenate([inner, inner], 0)
     outer = jnp.concatenate([outer, outer], 0)
-    for f in range(out_ref.shape[0]):
-        total = jnp.dot(
-            jnp.concatenate(two_parts(block_ref[f]), 1), inner, preferred_element_type=f32
-        )
-        edges = jnp.concatenate(got_edges(odd_ref[0, 0], one_ref, two_ref, f), 0)
-        total = total + lax.dot_general(
-            jnp.concatenate(two_parts(edges), 0),
-            outer,
-            (((0,), (0,)), ((), ())),
-            preferred_element_type=f32,
-        )
-        out_ref[f] = total
-        put_edges(odd_ref[0, 1], total[:EDGE], total[256 - EDGE :], first_ref, second_ref, f)
-
-
-def column_sum(odd, block, first, second):
-    freqs = block.shape[0]
+    done = 0
+    for block_ref, one_ref, two_ref in zip(refs[0::3], refs[1::3], refs[2::3]):
+        for f in range(block_ref.shape[0]):
+            total = jnp.dot(
+                jnp.concatenate(two_parts(block_ref[f]), 1), inner, preferred_element_type=f32
+            )
+            edges = jnp.concatenate(got_edges(is_odd(odd_ref, 0), one_ref, two_ref, f), 0)
+            total = total + lax.dot_general(
+                jnp.concatenate(two_parts(edges), 0),
+                outer,
+                (((0,), (0,)), ((), ())),
+                preferred_element_type=f32,
+            )
+            out_ref[done] = total
+            put_edges(
+                is_odd(odd_ref, 1), total[:EDGE], total[256 - EDGE :], first_ref, second_ref, done
+            )
+            done += 1
+
+
+def column_sum(odd, *pieces):
     return pl.pallas_call(
         column_kernel,
-        out_shape=block_and_edges(freqs),
-        in_specs=[SMEM] + [VMEM] * 3,
+        out_shape=block_and_edges(3),
+        in_specs=[VMEM] * (1 + len(pieces)),
         out_specs=(VMEM,) * 3,
         compiler_params=pltpu.CompilerParams(vmem_limit_bytes=16 << 20),
         name="column_sum",
-    )(odd, block, first, second)
-
-
-def row_kernel(odd_ref, *refs):
-    out_ref = refs[-1]
+    )(odd, *pieces)
+
+
+def row_kernel(odd_ref, block_ref, one_ref, two_ref, out_ref):
     length = 256 + 2 * EDGE
     band = in_window(iota((256, length), 1) - EDGE - iota((256, length), 0))
     band = jnp.concatenate([band, band], 1)
-    done = 0
-    for block_ref, one_ref, two_ref in zip(refs[0:-1:3], refs[1:-1:3], refs[2:-1:3]):
-        for f in range(block_ref.shape[0]):
-            before, after = got_edges(odd_ref[0, 1], one_ref, two_ref, f)
-            cells = jnp.concatenate([before, block_ref[f], after], 0)
-            total = jnp.dot(
-                band, jnp.concatenate(two_parts(cells), 0), preferred_element_type=f32
-            )
-            out_ref[done] = total * (1.0 / (4.0 * HALF * HALF))
-            done += 1
-
-
-def row_sum(odd, *pieces):
+    for f in range(3):
+        before, after = got_edges(is_odd(odd_ref, 1), one_ref, two_ref, f)
+        cells = jnp.concatenate([before, block_ref[f], after], 0)
+        total = jnp.dot(band, jnp.concatenate(two_parts(cells), 0), preferred_element_type=f32)
+        out_ref[f] = total * (1.0 / (4.0 * HALF * HALF))
+
+
+def row_sum(odd, block, first, second):
     return pl.pallas_call(
         row_kernel,
         out_shape=jax.ShapeDtypeStruct((3, 256, 256), f32),
-        in_specs=[SMEM] + [VMEM] * len(pieces),
+        in_specs=[VMEM] * 4,
         out_specs=VMEM,
         compiler_params=pltpu.CompilerParams(vmem_limit_bytes=16 << 20),
         name="row_sum",
-    )(odd, *pieces)
+    )(odd, block, first, second)
 
 
 def shards(
@@ -479,7 +476,8 @@
     magnet_x, magnet_y, magnet_z = (h_field[0], h_field[1], h_field[2])
     rows_below = shifted(jnp.stack([magnet_y[:, -1, :], magnet_z[:, -1, :]]), "gy", 1)
     cols_left = shifted(jnp.stack([magnet_x[:, :, -1], magnet_z[:, :, -1]]), "gx", 1)
-    odd = jnp.stack([lax.axis_index("gx") % 2, lax.axis_index("gy") % 2]).reshape(1, 2)
+    odd = jnp.stack([lax.axis_index("gx") % 2, lax.axis_index("gy") % 2])
+    odd = jnp.broadcast_to(odd[:, None], (2, 128))
     area_a, packed, offsets = gather_area_and_pack(counts, skin_cell, patch_slot, area, 4)
     rows_below, cols_left, area_a = lax.optimization_barrier((rows_below, cols_left, area_a))
     e_next, j_next, dft_e_next, dft_h_next, table = field_step(
@@ -489,16 +487,15 @@
     arrived = lax.all_to_all(rows, ("gy", "gx"), split_axis=0, concat_axis=0, tiled=True)
     area_b = gather_area(patch_slot, area, 4, 12)
 
-    blocks, pieces, swaps = [], [], []
+    blocks, pieces = [], []
     for first, freqs in PIECES:
         block, *edges = scatter_density(odd, patch_slot, area_a, area_b, arrived, first, freqs)
         blocks.append(block)
-        swaps.append(exchange(*edges, "gx"))
-    for block, swap in zip(blocks, swaps):
-        strip, *edges = column_sum(odd, block, *swap)
-        pieces += [strip, *exchange(*edges, "gy")]
+        pieces += [block, *exchange(*edges, "gx")]
+    strip, *edges = column_sum(odd, *pieces)
+    edges = exchange(*edges, "gy")
     point_density = jnp.concatenate(blocks, 0)
-    avg_density = row_sum(odd, *pieces)
+    avg_density = row_sum(odd, strip, *edges)
     return (e_next, j_next, dft_e_next, dft_h_next, point_density, avg_density)
 
 

time: 97.3 us -> 95.4 us (0.980); the launches traced: 97.1 us -> 93.7 us
  waiting for transfers between devices: 3.66 us -> 12.2 us
  starting transfers between devices: 38.4 us -> 29.9 us
  Pallas kernels: 51 us -> 47.6 us
    ppermute x8 -> x6, waiting for transfers between devices: 3.23 us -> 11.7 us  [exchange(): swaps.append(lax.ppermute(value, axis, pairs))]
    ppermute x8 -> x6, starting transfers between devices: 20.4 us -> 13.2 us  [exchange(): swaps.append(lax.ppermute(value, axis, pairs))]
    pallas_call x2 -> x1, Pallas kernels: 2.33 us -> 0.63 us  [column_sum(): pl.pallas_call(column_kernel, out_shape=block_and_edges(3), in_specs=[VME...]
    all_to_all x1, starting transfers between devices: 12.4 us -> 11.1 us  [shards(): lax.all_to_all(rows, ('gy', 'gx'), split_axis=0, concat_axis=0, tiled=True)]
    pallas_call x2, Pallas kernels: 16.2 us -> 15 us  [scatter_density(): pl.pallas_call(functools.partial(scatter_kernel, first=first), out_shape=...]
  transfers between devices with their start and end apart: 11 -> 9, of which waited for: 2 -> 3; matrix products, arithmetic and copies ran while one was open for 1% -> 2% of each run, Pallas kernels for 26% -> 23%
where the time goes in v6:
time: 95.4 us; the launch traced here: 93.7 us
  Pallas kernels  47.6 us (50%)
  starting transfers between devices  29.9 us (31%)
  waiting for transfers between devices  12.2 us (13%)
  local copies, waits for them, and re-layouts  1.99 us (2%)
  other arithmetic  1.02 us (1%)
  between operations  1 us (1%)
    pallas_call x2, Pallas kernels, scatter_density(): pl.pallas_call(functools.partial(scatter_kernel, first=first), out_shape=...  15 us
    ppermute x6, starting transfers between devices, exchange(): swaps.append(lax.ppermute(value, axis, pairs))  13.2 us
    ppermute x6, waiting for transfers between devices, exchange(): swaps.append(lax.ppermute(value, axis, pairs))  11.7 us
    pallas_call x1, Pallas kernels, gather_area(): pl.pallas_call(functools.partial(area_kernel, first=first), out_shape=jax...  11.3 us
    all_to_all x1, starting transfers between devices, shards(): lax.all_to_all(rows, ('gy', 'gx'), split_axis=0, concat_axis=0, tiled=True)  11.1 us
    pallas_call x1, Pallas kernels, gather_flux(): pl.pallas_call(gather_kernel, out_shape=jax.ShapeDtypeStruct((128, 9, 1,...  9.66 us
    ppermute x2, starting transfers between devices, shifted(): lax.ppermute(value, axis, [(source, source + steps) for source in range(l...  5.61 us
    pallas_call x1, Pallas kernels, gather_area_and_pack(): pl.pallas_call(functools.partial(first_area_kernel, groups=groups), out_s...  5.37 us
  transfers between devices with their start and end apart: 9, of which 3 were waited for; matrix products, arithmetic and copies ran while one was open for 2% of the time, Pallas kernels for 23%

profile of v6, /device:TPU:26, one launch (start us, length us, event | category | flops | bytes accessed | tf_op | source)
XLA Modules:
  0.0 93.7 jit_solution(3767667208861924032)
XLA Ops:
  0.7 1.1 %fusion = (f32[1,4,64,128]{3,2,1,0:T(8,128)S(1)}, f32[1,4,64,128]{3,2,1,0:T(8,128)S(1)}, f32[1,4,64,128]{3,2,1,0:T(8,128)S(1)}) fusion(f32[3,4,64,128]{3,2,1,0:T(8,128)} %h_ref.1), kind=kLoop, calls=%fused_computation.8 | loop fusion | bytes 786432 | tf_op jit(solution)/shard_map/slice | solution.py:476
  1.8 0.1 copy.26
  2.0 0.1 copy.27
  2.1 3.7 %collective-permute-start.1 = (f32[2,4,64]{2,1,0:T(4,128)S(1)}, f32[2,4,64]{2,1,0:T(4,128)S(1)}, u32[]{:S(2)}, u32[]{:S(2)}) collective-permute-start(f32[2,4,64]{2,1,0:T(4,128)S(1)} %pad_maximum_fusion.2), channel_id=1, source_target_pairs={{0,1},{1,2},{2,3},{3,4},{4,5},{5,6},{6,7},{8,9},{9,10},{10,11},{11... | collective-permute-start | bytes 6152 | tf_op jit(solution)/shard_map/ppermute | solution.py:33
  5.8 0.2 slice.29
  6.2 0.1 copy.29
  6.3 1.9 %collective-permute-start = (f32[2,4,128]{2,1,0:T(4,128)S(1)}, f32[2,4,128]{2,1,0:T(4,128)S(1)}, u32[]{:S(2)}, u32[]{:S(2)}) collective-permute-start(f32[2,4,128]{2,1,0:T(4,128)S(1)} %pad_maximum_fusion.1), channel_id=1, source_target_pairs={{0,8},{8,16},{16,24},{24,32},{32,40},{40,48},{48,56},{56,64},{64,7... | collective-permute-start | bytes 12296 | tf_op jit(solution)/shard_map/ppermute | solution.py:33
  8.4 5.4 %area_and_pack.1 = (f32[4,8,1024]{2,1,0:T(8,128)S(1)}, s32[136,128]{1,0:T(8,128)S(1)}, s32[1,136]{1,0:T(1,128)S(1)}) custom-call(s32[1,128]{1,0:T(1,128)S(1)} %copy-done.7, s32[1,128,128]{2,1,0:T(8,128)S(1)} %copy-done.9, s32[1,128,128]{2,1,0:T(8,128)S(1)} %copy-done.10, f32[3,256,256]{2,1,0:T(8,128)S(1)} %copy-done.8), custom_call_target="tpu_custom_call" | custom-call | flops 3221225472 | bytes 2000000 | tf_op jit(solution)/shard_map/area_and_pack/pallas_call | solution.py:299
  13.9 4.1 %field_step.1 = (f32[3,4,64,128]{3,2,1,0:T(8,128)}, f32[3,4,64,128]{3,2,1,0:T(8,128)}, f32[3,2,3,4,64,128]{5,4,3,2,1,0:T(8,128)}, f32[3,2,3,4,64,128]{5,4,3,2,1,0:T(8,128)}, bf16[9,2,64,512]{3,2,1,0:T(8,128)(2,1)S(1)}) custom-call(f32[3,4,64,128]{3,2,1,0:T(8,128)S(1)} %copy-done.3, f32[3,4,64,128]{3,2,1,0:T(8,128)S(1)} %copy-done.2, ...), custom_call_target="tpu_custom_call" | custom-call | tf_op jit(solution)/shard_map/field_step/pallas_call | solution.py:150
  18.0 9.7 %gather_flux.1 = f32[128,9,1,128]{3,2,1,0:T(1,128)} custom-call(s32[1,128]{1,0:T(1,128)S(1)} %copy-done.7, s32[1,136]{1,0:T(1,128)S(1)} %get-tuple-element.34.offset_ref, s32[136,128]{1,0:T(8,128)S(1)} %get-tuple-element.35.packed, bf16[9,128,512]{2,1,0:T(8,128)(2,1)S(1)} %bitcast.15), custom_call_target="tpu_custom_call" | custom-call | tf_op jit(solution)/shard_map/gather_flux/pallas_call | solution.py:216
  27.7 11.1 %all-to-all-start = ((f32[128,9,1,128]{3,2,1,0:T(1,128)}), f32[128,9,1,128]{3,2,1,0:T(1,128)S(1)}, u32[]{:S(2)}, u32[]{:S(2)}) async-start(f32[128,9,1,128]{3,2,1,0:T(1,128)} %gather_flux.1), calls=%async_computation | async-start | bytes 1179648 | tf_op jit(solution)/shard_map/all_to_all | solution.py:487
  38.8 11.3 %gather_area.1.area_b_ref = f32[12,8,1024]{2,1,0:T(8,128)S(1)} custom-call(s32[1,128,128]{2,1,0:T(8,128)S(1)} %copy-done.10, f32[3,256,256]{2,1,0:T(8,128)S(1)} %copy-done.8), custom_call_target="tpu_custom_call" | custom-call | flops 9663676416 | bytes 2000000 | tf_op jit(solution)/shard_map/gather_area/pallas_call | solution.py:316
  50.1 0.4 all-to-all-done.flux_ref
  50.6 9.7 %scatter_density.2 = (f32[2,256,256]{2,1,0:T(8,128)S(1)}, f32[2,104,256]{2,1,0:T(8,128)S(1)}, f32[2,104,256]{2,1,0:T(8,128)S(1)}) custom-call(s32[2,128]{1,0:T(2,128)S(1)} %broadcast_in_dim.2.odd_ref, s32[1,128,128]{2,1,0:T(8,128)S(1)} %copy-done.10, f32[4,8,1024]{2,1,0:T(8,128)S(1)} %get-tuple-element.33.area_a_ref, ...), custom_call_target="tpu_custom_call" | custom-call | flops 8589934592 | bytes 2000000 | tf_op jit(solution)/shard_map/scatter_density/pallas_call | solution.py:388
  60.3 4.7 %collective-permute-start.2 = (f32[2,104,256]{2,1,0:T(8,128)S(1)}, f32[2,104,256]{2,1,0:T(8,128)S(1)}, u32[]{:S(2)}, u32[]{:S(2)}) collective-permute-start(f32[2,104,256]{2,1,0:T(8,128)S(1)} %get-tuple-element.39), channel_id=1, source_target_pairs={{1,2},{3,4},{5,6},{2,1},{4,3},{6,5},{9,10},{11,12},{13,14},{10,9},... | collective-permute-start | bytes 638984 | tf_op jit(solution)/shard_map/ppermute | solution.py:42
  65.0 0.3 collective-permute-start.3
  65.3 5.3 %scatter_density.3 = (f32[1,256,256]{2,1,0:T(8,128)S(1)}, f32[1,104,256]{2,1,0:T(8,128)S(1)}, f32[1,104,256]{2,1,0:T(8,128)S(1)}) custom-call(s32[2,128]{1,0:T(2,128)S(1)} %broadcast_in_dim.2.odd_ref, s32[1,128,128]{2,1,0:T(8,128)S(1)} %copy-done.10, f32[4,8,1024]{2,1,0:T(8,128)S(1)} %get-tuple-element.33.area_a_ref, ...), custom_call_target="tpu_custom_call" | custom-call | flops 4294967296 | bytes 2000000 | tf_op jit(solution)/shard_map/scatter_density/pallas_call | solution.py:388
  70.6 4.7 %collective-permute-start.4 = (f32[1,104,256]{2,1,0:T(8,128)S(1)}, f32[1,104,256]{2,1,0:T(8,128)S(1)}, u32[]{:S(2)}, u32[]{:S(2)}) collective-permute-start(f32[1,104,256]{2,1,0:T(8,128)S(1)} %get-tuple-element.41), channel_id=1, source_target_pairs={{1,2},{3,4},{5,6},{2,1},{4,3},{6,5},{9,10},{11,12},{13,14},{10,9},... | collective-permute-start | bytes 319496 | tf_op jit(solution)/shard_map/ppermute | solution.py:42
  75.4 5.6 %collective-permute-done.4.refs_4_ = f32[1,104,256]{2,1,0:T(8,128)S(1)} collective-permute-done((f32[1,104,256]{2,1,0:T(8,128)S(1)}, f32[1,104,256]{2,1,0:T(8,128)S(1)}, u32[]{:S(2)}, u32[]{:S(2)}) %collective-permute-start.4) | collective-permute-done | bytes 106528 | tf_op jit(solution)/shard_map/ppermute | solution.py:42
  81.1 0.6 column_sum.1
  81.7 3.3 %collective-permute-start.6 = (f32[3,104,256]{2,1,0:T(8,128)S(1)}, f32[3,104,256]{2,1,0:T(8,128)S(1)}, u32[]{:S(2)}, u32[]{:S(2)}) collective-permute-start(f32[3,104,256]{2,1,0:T(8,128)S(1)} %get-tuple-element.44), channel_id=1, source_target_pairs={{8,16},{24,32},{40,48},{56,64},{72,80},{88,96},{104,112},{16,8},{3... | collective-permute-start | bytes 958472 | tf_op jit(solution)/shard_map/ppermute | solution.py:42
  85.1 0.9 pad_maximum_fusion
  86.1 6.1 %collective-permute-done.6.one_ref = f32[3,104,256]{2,1,0:T(8,128)S(1)} collective-permute-done((f32[3,104,256]{2,1,0:T(8,128)S(1)}, f32[3,104,256]{2,1,0:T(8,128)S(1)}, u32[]{:S(2)}, u32[]{:S(2)}) %collective-permute-start.6) | collective-permute-done | bytes 319520 | tf_op jit(solution)/shard_map/ppermute | solution.py:42
  92.1 1.5 %row_sum.1 = f32[3,256,256]{2,1,0:T(8,128)} custom-call(s32[2,128]{1,0:T(2,128)S(1)} %broadcast_in_dim.2.odd_ref, f32[3,256,256]{2,1,0:T(8,128)S(1)} %get-tuple-element.43.block_ref, f32[3,104,256]{2,1,0:T(8,128)S(1)} %collective-permute-done.6.one_ref, f32[3,104,256]{2,1,0:T(8,128)S(1)} %collective-permute-done.7.two_ref), custom_call_target="tpu_custom_call" | custom-call | tf_op jit(solution)/shard_map/row_sum/pallas_call | solution.py:462
  (37 shorter events, 0.5 us)
Async XLA Ops:
  0.6 7.6 %copy-start.9 = (s32[1,128,128]{2,1,0:T(8,128)S(1)}, s32[1,128,128]{2,1,0:T(8,128)}, u32[]{:S(2)}) copy-start(s32[1,128,128]{2,1,0:T(8,128)} %cell_ref.1) | copy-start | bytes 196612
  0.6 7.6 %copy-start.7 = (s32[1,128]{1,0:T(1,128)S(1)}, s32[1,128]{1,0:T(1,128)}, u32[]{:S(2)}) copy-start(s32[1,128]{1,0:T(1,128)} %count_ref.3) | copy-start | bytes 1540
  0.7 7.6 %copy-start.10 = (s32[1,128,128]{2,1,0:T(8,128)S(1)}, s32[1,128,128]{2,1,0:T(8,128)}, u32[]{:S(2)}) copy-start(s32[1,128,128]{2,1,0:T(8,128)} %patch_ref.7) | copy-start | bytes 196612
  0.7 7.6 %copy-start.8 = (f32[3,256,256]{2,1,0:T(8,128)S(1)}, f32[3,256,256]{2,1,0:T(8,128)}, u32[]{:S(2)}) copy-start(f32[3,256,256]{2,1,0:T(8,128)} %area_ref.3) | copy-start | bytes 2359300
  2.1 11.7 %collective-permute-start.1 = (f32[2,4,64]{2,1,0:T(4,128)S(1)}, f32[2,4,64]{2,1,0:T(4,128)S(1)}, u32[]{:S(2)}, u32[]{:S(2)}) collective-permute-start(f32[2,4,64]{2,1,0:T(4,128)S(1)} %pad_maximum_fusion.2), channel_id=1, source_target_pairs={{0,1},{1,2},{2,3},{3,4},{4,5},{5,6},{6,7},{8,9},{9,10},{10,11},{11... | collective-permute-start | bytes 6152 | tf_op jit(solution)/shard_map/ppermute | solution.py:33
  6.3 7.5 %collective-permute-start = (f32[2,4,128]{2,1,0:T(4,128)S(1)}, f32[2,4,128]{2,1,0:T(4,128)S(1)}, u32[]{:S(2)}, u32[]{:S(2)}) collective-permute-start(f32[2,4,128]{2,1,0:T(4,128)S(1)} %pad_maximum_fusion.1), channel_id=1, source_target_pairs={{0,8},{8,16},{16,24},{24,32},{32,40},{40,48},{48,56},{56,64},{64,7... | collective-permute-start | bytes 12296 | tf_op jit(solution)/shard_map/ppermute | solution.py:33
  8.3 5.5 %copy-start = (f32[3,2,3,4,64,128]{5,4,3,2,1,0:T(8,128)S(1)}, f32[3,2,3,4,64,128]{5,4,3,2,1,0:T(8,128)}, u32[]{:S(2)}) copy-start(f32[3,2,3,4,64,128]{5,4,3,2,1,0:T(8,128)} %dft_e_ref.1) | copy-start | bytes 7077892
  8.3 5.5 %copy-start.1 = (f32[3,2,3,4,64,128]{5,4,3,2,1,0:T(8,128)S(1)}, f32[3,2,3,4,64,128]{5,4,3,2,1,0:T(8,128)}, u32[]{:S(2)}) copy-start(f32[3,2,3,4,64,128]{5,4,3,2,1,0:T(8,128)} %dft_h_ref.1) | copy-start | bytes 7077892
  8.3 5.5 %copy-start.2 = (f32[3,4,64,128]{3,2,1,0:T(8,128)S(1)}, f32[3,4,64,128]{3,2,1,0:T(8,128)}, u32[]{:S(2)}) copy-start(f32[3,4,64,128]{3,2,1,0:T(8,128)} %h_ref.1) | copy-start | bytes 1179652
  8.3 5.5 %copy-start.3 = (f32[3,4,64,128]{3,2,1,0:T(8,128)S(1)}, f32[3,4,64,128]{3,2,1,0:T(8,128)}, u32[]{:S(2)}) copy-start(f32[3,4,64,128]{3,2,1,0:T(8,128)} %e_ref.1) | copy-start | bytes 1179652
  8.3 5.5 %copy-start.4 = (f32[3,4,64,128]{3,2,1,0:T(8,128)S(1)}, f32[3,4,64,128]{3,2,1,0:T(8,128)}, u32[]{:S(2)}) copy-start(f32[3,4,64,128]{3,2,1,0:T(8,128)} %j_ref.1) | copy-start | bytes 1179652
  8.3 5.5 %copy-start.5 = (s32[4,64,128]{2,1,0:T(8,128)S(1)}, s32[4,64,128]{2,1,0:T(8,128)}, u32[]{:S(2)}) copy-start(s32[4,64,128]{2,1,0:T(8,128)} %kind_ref.1) | copy-start | bytes 393220
  8.4 5.5 %copy-start.6 = (f32[4,32]{1,0:T(4,128)S(1)}, f32[4,32]{1,0:T(4,128)}, u32[]{:S(2)}) copy-start(f32[4,32]{1,0:T(4,128)} %table_ref.1) | copy-start | bytes 1540
  27.7 22.9 %all-to-all-start = ((f32[128,9,1,128]{3,2,1,0:T(1,128)}), f32[128,9,1,128]{3,2,1,0:T(1,128)S(1)}, u32[]{:S(2)}, u32[]{:S(2)}) async-start(f32[128,9,1,128]{3,2,1,0:T(1,128)} %gather_flux.1), calls=%async_computation | async-start | bytes 1179648 | tf_op jit(solution)/shard_map/all_to_all | solution.py:487
  60.3 20.8 %collective-permute-start.2 = (f32[2,104,256]{2,1,0:T(8,128)S(1)}, f32[2,104,256]{2,1,0:T(8,128)S(1)}, u32[]{:S(2)}, u32[]{:S(2)}) collective-permute-start(f32[2,104,256]{2,1,0:T(8,128)S(1)} %get-tuple-element.39), channel_id=1, source_target_pairs={{1,2},{3,4},{5,6},{2,1},{4,3},{6,5},{9,10},{11,12},{13,14},{10,9},... | collective-permute-start | bytes 638984 | tf_op jit(solution)/shard_map/ppermute | solution.py:42
  65.0 16.0 %collective-permute-start.3 = (f32[2,104,256]{2,1,0:T(8,128)S(1)}, f32[2,104,256]{2,1,0:T(8,128)S(1)}, u32[]{:S(2)}, u32[]{:S(2)}) collective-permute-start(f32[2,104,256]{2,1,0:T(8,128)S(1)} %get-tuple-element.40), channel_id=1, source_target_pairs={{0,1},{2,3},{4,5},{6,7},{1,0},{3,2},{5,4},{7,6},{8,9},{10,11},{12,... | collective-permute-start | bytes 638984 | tf_op jit(solution)/shard_map/ppermute | solution.py:42
  70.6 10.4 %collective-permute-start.4 = (f32[1,104,256]{2,1,0:T(8,128)S(1)}, f32[1,104,256]{2,1,0:T(8,128)S(1)}, u32[]{:S(2)}, u32[]{:S(2)}) collective-permute-start(f32[1,104,256]{2,1,0:T(8,128)S(1)} %get-tuple-element.41), channel_id=1, source_target_pairs={{1,2},{3,4},{5,6},{2,1},{4,3},{6,5},{9,10},{11,12},{13,14},{10,9},... | collective-permute-start | bytes 319496 | tf_op jit(solution)/shard_map/ppermute | solution.py:42
  75.3 5.7 %collective-permute-start.5 = (f32[1,104,256]{2,1,0:T(8,128)S(1)}, f32[1,104,256]{2,1,0:T(8,128)S(1)}, u32[]{:S(2)}, u32[]{:S(2)}) collective-permute-start(f32[1,104,256]{2,1,0:T(8,128)S(1)} %get-tuple-element.42), channel_id=1, source_target_pairs={{0,1},{2,3},{4,5},{6,7},{1,0},{3,2},{5,4},{7,6},{8,9},{10,11},{12,... | collective-permute-start | bytes 319496 | tf_op jit(solution)/shard_map/ppermute | solution.py:42
  81.7 10.4 %collective-permute-start.6 = (f32[3,104,256]{2,1,0:T(8,128)S(1)}, f32[3,104,256]{2,1,0:T(8,128)S(1)}, u32[]{:S(2)}, u32[]{:S(2)}) collective-permute-start(f32[3,104,256]{2,1,0:T(8,128)S(1)} %get-tuple-element.44), channel_id=1, source_target_pairs={{8,16},{24,32},{40,48},{56,64},{72,80},{88,96},{104,112},{16,8},{3... | collective-permute-start | bytes 958472 | tf_op jit(solution)/shard_map/ppermute | solution.py:42
  85.0 7.1 %collective-permute-start.7 = (f32[3,104,256]{2,1,0:T(8,128)S(1)}, f32[3,104,256]{2,1,0:T(8,128)S(1)}, u32[]{:S(2)}, u32[]{:S(2)}) collective-permute-start(f32[3,104,256]{2,1,0:T(8,128)S(1)} %get-tuple-element.45), channel_id=1, source_target_pairs={{0,8},{16,24},{32,40},{48,56},{64,72},{80,88},{96,104},{112,120},{... | collective-permute-start | bytes 958472 | tf_op jit(solution)/shard_map/ppermute | solution.py:42

commit v7 on v6

--- a/solution.py
+++ b/solution.py
@@ -15,6 +15,8 @@
 
 f32 = jnp.float32
 bf16 = jnp.bfloat16
+f8 = jnp.float8_e4m3fn
+TOP = 100000.0
 VMEM = pl.BlockSpec(memory_space=pltpu.VMEM)
 SMEM = pl.BlockSpec(memory_space=pltpu.SMEM)
 
@@ -61,6 +63,20 @@
 def onehot(count, index):
     places = iota((count, index.shape[1]), 0).astype(bf16)
     return jnp.where(places == index.astype(bf16), jnp.ones((), bf16), jnp.zeros((), bf16))
+
+
+def largest(values):
+    top = jnp.max(jnp.max(jnp.abs(values), axis=0, keepdims=True), axis=1, keepdims=True)
+    return jnp.maximum(top, 1e-30)
+
+
+def split_scaled(values, head_ref, rest_ref):
+    top = largest(values)
+    values = values * (TOP / top)
+    head = values.astype(bf16)
+    head_ref[...] = head
+    rest_ref[...] = (values - head.astype(f32)).astype(f8)
+    return top * (1.0 / TOP)
 
 
 def field_kernel(
@@ -111,8 +127,6 @@
         e_next.append(new_e)
     field_h = (hx, hy, hz)
     phase_e, phase_h = phase_list(0.0), phase_list(0.5)
-    half_plane = pl.ds(pl.multiple_of((z // 2) * cols, cols), cols)
-    rest_plane = pl.ds(pl.multiple_of((z // 2) * cols + 2 * cols, cols), cols)
     for f in range(3):
         spec_e, spec_h = [], []
         for part in range(2):
@@ -131,9 +145,7 @@
                 (spec_e[0][a] * spec_h[0][b] - spec_e[0][b] * spec_h[0][a])
                 + (spec_e[1][a] * spec_h[1][b] - spec_e[1][b] * spec_h[1][a])
             )
-            head = flux.astype(bf16)
-            flux_out[3 * f + c, z % 2, :, half_plane] = head
-            flux_out[3 * f + c, z % 2, :, rest_plane] = (flux - head.astype(f32)).astype(bf16)
+            flux_out[3 * f + c, 0] = flux
     below_ref[0] = hx
     below_ref[1] = hy
 
@@ -143,10 +155,11 @@
     plane3 = pl.BlockSpec((3, 1, rows, cols), lambda z: (0, z, 0, 0))
     spectra = pl.BlockSpec((3, 2, 3, 1, rows, cols), lambda z: (0, 0, 0, z, 0, 0))
 
+    flux = pl.BlockSpec((9, 1, rows, cols), lambda z: (0, z, 0, 0))
+
     def whole(shape):
         return pl.BlockSpec(shape, lambda z: (0,) * len(shape))
 
-    flux_shape = (9, 2, rows, 4 * cols)
     return pl.pallas_call(
         field_kernel,
         grid=(planes,),
@@ -155,7 +168,7 @@
             jax.ShapeDtypeStruct(e.shape, f32),
             jax.ShapeDtypeStruct(dft_e.shape, f32),
             jax.ShapeDtypeStruct(dft_h.shape, f32),
-            jax.ShapeDtypeStruct(flux_shape, bf16),
+            jax.ShapeDtypeStruct((9, planes, rows, cols), f32),
         ),
         in_specs=[
             plane3, plane3, plane3,
@@ -163,28 +176,31 @@
             whole(table.shape), spectra, spectra,
             whole(rows_below.shape), whole(cols_left.shape),
         ],
-        out_specs=(plane3, plane3, spectra, spectra, whole(flux_shape)),
+        out_specs=(plane3, plane3, spectra, spectra, flux),
         scratch_shapes=[pltpu.VMEM((2, rows, cols), f32), pltpu.VMEM((8, cols), f32)],
         compiler_params=pltpu.CompilerParams(vmem_limit_bytes=20 << 20),
         name="field_step",
     )(e, h, j, kinds, table, dft_e, dft_h, rows_below, cols_left)
 
 
-def gather_kernel(count_ref, offset_ref, packed, table_ref, out_ref, found):
+def gather_kernel(offset_ref, packed, flux_ref, out_ref, found, head_ref, rest_ref):
+    planes = [flux_ref[:, z].reshape(576, 128) for z in range(4)]
+    back = split_scaled(jnp.concatenate(planes, 1), head_ref, rest_ref)
+
     def lookup(c):
         cell = jnp.concatenate([packed[pl.ds(2 * c, 1), :], packed[pl.ds(2 * c + 1, 1), :]], 1)
-        high = lax.bitwise_and(lax.shift_right_logical(cell, 14), 1)
-        inner = lax.bitwise_or(lax.shift_left(high, 7), lax.bitwise_and(cell, 127))
-        outer = lax.bitwise_and(lax.shift_right_logical(cell, 7), 127)
-        hot = onehot(256, inner)
-        result = jnp.dot(
-            table_ref[...].reshape(1152, 512),
-            jnp.concatenate([hot, hot], 0),
-            preferred_element_type=f32,
-        ).reshape(9, 128, 256)
-        mine = iota((128, 256), 0) == outer
+        plane = lax.bitwise_and(lax.shift_right_logical(cell, 13), 3)
+        row = lax.bitwise_and(lax.shift_right_logical(cell, 7), 63)
+        inner = lax.bitwise_or(lax.shift_left(plane, 7), lax.bitwise_and(cell, 127))
+        hot = jnp.concatenate(
+            [onehot(256, inner), onehot(256, jnp.where(inner >= 256, inner - 256, 512))], 0
+        )
+        result = jnp.dot(head_ref[...], hot, preferred_element_type=f32)
+        result = result + jnp.dot(rest_ref[...], hot.astype(f8), preferred_element_type=f32)
+        result = result.reshape(9, 64, 256)
+        mine = iota((64, 256), 0) == row
         for q in range(9):
-            value = jnp.sum(jnp.where(mine, result[q], 0.0), axis=0, keepdims=True)
+            value = jnp.sum(jnp.where(mine, result[q], 0.0), axis=0, keepdims=True) * back
             found[2 * c, q : q + 1, :] = value[:, :128]
             found[2 * c + 1, q : q + 1, :] = value[:, 128:]
 
@@ -199,7 +215,7 @@
     def unpack(d, _):
         offset = offset_ref[0, d]
         row, start = lax.shift_right_logical(offset, 7), lax.bitwise_and(offset, 127)
-        live = count_ref[0, d]
+        live = offset_ref[0, d + 1] - offset
         back = lax.bitwise_and(128 - start, 127)
         value = jnp.where(
             lanes < 128 - start, pltpu.roll(found[row], back, 1), pltpu.roll(found[row + 1], back, 1)
@@ -212,16 +228,20 @@
     lax.fori_loop(0, 128, unpack, 0, unroll=16)
 
 
-def gather_flux(counts, offsets, packed, table):
+def gather_flux(offsets, packed, flux):
     return pl.pallas_call(
         gather_kernel,
         out_shape=jax.ShapeDtypeStruct((128, 9, 1, 128), f32),
-        in_specs=[SMEM, SMEM, VMEM, VMEM],
+        in_specs=[SMEM, VMEM, VMEM],
         out_specs=VMEM,
-        scratch_shapes=[pltpu.VMEM((136, 16, 128), f32)],
-        compiler_params=pltpu.CompilerParams(vmem_limit_bytes=24 << 20),
+        scratch_shapes=[
+            pltpu.VMEM((136, 16, 128), f32),
+            pltpu.VMEM((576, 512), bf16),
+            pltpu.VMEM((576, 512), f8),
+        ],
+        compiler_params=pltpu.CompilerParams(vmem_limit_bytes=28 << 20),
         name="gather_flux",
-    )(counts, offsets, packed, table)
+    )(offsets, packed, flux)
 
 
 GROUP = 8
@@ -231,29 +251,34 @@
     return jnp.concatenate([ref[0, pl.ds(GROUP * c + i, 1), :] for i in range(GROUP)], 1)
 
 
-def split_area(area_ref, table):
-    area = area_ref[...].reshape(768, 256)
-    head = area.astype(bf16)
-    table[:, :256] = head
-    table[:, 256:] = (area - head.astype(f32)).astype(bf16)
-
-
-def area_group(patch_ref, table, out_ref, c, first):
+AREA_SCRATCH = [pltpu.VMEM((384, 512), bf16), pltpu.VMEM((384, 512), f8)]
+
+
+def split_area(area_ref, head_ref, rest_ref):
+    halves = [area_ref[:, :128, :].reshape(384, 256), area_ref[:, 128:, :].reshape(384, 256)]
+    return split_scaled(jnp.concatenate(halves, 1), head_ref, rest_ref)
+
+
+def area_group(patch_ref, head_ref, rest_ref, back, out_ref, c, first):
     patch = slot_row(patch_ref, c + first)
     u, v = lax.shift_right_logical(patch, 8), lax.bitwise_and(patch, 255)
-    hot = onehot(256, v)
-    result = jnp.dot(
-        table[...], jnp.concatenate([hot, hot], 0), preferred_element_type=f32
-    ).reshape(3, 256, GROUP * 128)
-    mine = iota((256, GROUP * 128), 0) == u
+    hot = jnp.concatenate(
+        [onehot(256, jnp.where(u < 128, v, 512)), onehot(256, jnp.where(u < 128, 512, v))], 0
+    )
+    result = jnp.dot(head_ref[...], hot, preferred_element_type=f32)
+    result = result + jnp.dot(rest_ref[...], hot.astype(f8), preferred_element_type=f32)
+    result = result.reshape(3, 128, GROUP * 128)
+    mine = iota((128, GROUP * 128), 0) == lax.bitwise_and(u, 127)
     for q in range(3):
-        out_ref[c, q : q + 1, :] = jnp.sum(jnp.where(mine, result[q], 0.0), axis=0, keepdims=True)
+        found = jnp.sum(jnp.where(mine, result[q], 0.0), axis=0, keepdims=True)
+        out_ref[c, q : q + 1, :] = found * back
 
 
 def first_area_kernel(
-    count_ref, cell_ref, patch_ref, area_ref, out_ref, packed, offset_ref, table, *, groups
+    count_ref, cell_ref, patch_ref, area_ref, out_ref, packed, offset_ref, head_ref, rest_ref,
+    *, groups
 ):
-    split_area(area_ref, table)
+    back = split_area(area_ref, head_ref, rest_ref)
     lane = iota((1, 128), 1)
     share = 128 // groups
 
@@ -269,7 +294,7 @@
             packed[pl.ds(row, 1), :] = merged
             current = jnp.where(start + live >= 128, rolled, merged)
             offset = offset + live
-        area_group(patch_ref, table, out_ref, c, 0)
+        area_group(patch_ref, head_ref, rest_ref, back, out_ref, c, 0)
         return offset, current
 
     offset, current = lax.fori_loop(
@@ -279,14 +304,14 @@
     offset_ref[0, 128] = offset
 
 
-def area_kernel(patch_ref, area_ref, out_ref, table, *, first):
-    split_area(area_ref, table)
+def area_kernel(patch_ref, area_ref, out_ref, head_ref, rest_ref, *, first):
+    back = split_area(area_ref, head_ref, rest_ref)
 
     def chunk(c, _):
-        area_group(patch_ref, table, out_ref, c, first)
+        area_group(patch_ref, head_ref, rest_ref, back, out_ref, c, first)
         return 0
 
-    lax.fori_loop(0, out_ref.shape[0], chunk, 0, unroll=4)
+    lax.fori_loop(0, out_ref.shape[0], chunk, 0, unroll=7)
 
 
 def area_cost(groups):
@@ -305,7 +330,7 @@
         ),
         in_specs=[SMEM, VMEM, VMEM, VMEM],
         out_specs=(VMEM, VMEM, SMEM),
-        scratch_shapes=[pltpu.VMEM((768, 512), bf16)],
+        scratch_shapes=AREA_SCRATCH,
         compiler_params=pltpu.CompilerParams(vmem_limit_bytes=32 << 20),
         cost_estimate=area_cost(groups),
         name="area_and_pack",
@@ -318,7 +343,7 @@
         out_shape=jax.ShapeDtypeStruct((groups, 8, GROUP * 128), f32),
         in_specs=[VMEM, VMEM],
         out_specs=VMEM,
-        scratch_shapes=[pltpu.VMEM((768, 512), bf16)],
+        scratch_shapes=AREA_SCRATCH,
         compiler_params=pltpu.CompilerParams(vmem_limit_bytes=32 << 20),
         cost_estimate=area_cost(groups),
         name="gather_area",
@@ -330,46 +355,49 @@
 
 
 def scatter_kernel(
-    odd_ref, patch_ref, area_a_ref, area_b_ref, flux_ref, out_ref, first_ref, second_ref, *, first
+    odd_ref, patch_ref, area_a_ref, area_b_ref, flux_ref, out_ref, first_ref, second_ref, dense,
+    *, first
 ):
     freqs = out_ref.shape[0]
+    half, groups = area_a_ref.shape[0], dense.shape[0]
     out_ref[...] = jnp.zeros_like(out_ref)
-
-    def add_group(c, area):
+    top = jnp.zeros((1, GROUP * 128), f32)
+    for c in range(groups):
+        area = area_a_ref[c] if c < half else area_b_ref[c - half]
+        for f in range(freqs):
+            density = jnp.zeros((1, GROUP * 128), f32)
+            for q in range(3):
+                flux = jnp.concatenate(
+                    [flux_ref[GROUP * c + i, 3 * (first + f) + q] for i in range(GROUP)], 1
+                )
+                density = density + area[q : q + 1, :] * flux
+            dense[c, f : f + 1, :] = density
+            top = jnp.maximum(top, jnp.abs(density))
+    top = largest(top)
+    scale = TOP / top
+
+    def add_group(c, _):
         patch = slot_row(patch_ref, c)
         u, v = lax.shift_right_logical(patch, 8), lax.bitwise_and(patch, 255)
         hot = onehot(256, v)
         mine = iota((256, GROUP * 128), 0).astype(bf16) == u.astype(bf16)
         heads, rests = [], []
-        for f in range(first, first + freqs):
-            density = jnp.zeros((1, GROUP * 128), f32)
-            for q in range(3):
-                flux = jnp.concatenate(
-                    [flux_ref[GROUP * c + i, 3 * f + q] for i in range(GROUP)], 1
-                )
-                density = density + area[q : q + 1, :] * flux
+        for f in range(freqs):
+            density = dense[c, f : f + 1, :] * scale
             head = density.astype(bf16)
             rest = (density - head.astype(f32)).astype(bf16)
             heads.append(jnp.where(mine, head, jnp.zeros((), bf16)))
-            rests.append(jnp.where(mine, rest, jnp.zeros((), bf16)))
-        left = jnp.concatenate([jnp.concatenate(heads, 0), jnp.concatenate(rests, 0)], 1)
-        right = jnp.concatenate([hot, hot], 1)
-        out_ref[...] += lax.dot_general(
-            left, right, (((1,), (1,)), ((), ())), preferred_element_type=f32
-        ).reshape(freqs, 256, 256)
-
-    half = area_a_ref.shape[0]
-
-    def first_part(c, _):
-        add_group(c, area_a_ref[c])
+            rests.append(jnp.where(mine, rest, jnp.zeros((), bf16)).astype(f8))
+        dims = (((1,), (1,)), ((), ()))
+        total = lax.dot_general(jnp.concatenate(heads, 0), hot, dims, preferred_element_type=f32)
+        total = total + lax.dot_general(
+            jnp.concatenate(rests, 0), hot.astype(f8), dims, preferred_element_type=f32
+        )
+        out_ref[...] += total.reshape(freqs, 256, 256)
         return 0
 
-    def second_part(c, _):
-        add_group(c + half, area_b_ref[c])
-        return 0
-
-    lax.fori_loop(0, half, first_part, 0, unroll=4)
-    lax.fori_loop(0, area_b_ref.shape[0], second_part, 0, unroll=4)
+    lax.fori_loop(0, groups, add_group, 0, unroll=8)
+    out_ref[...] = out_ref[...] * (top * (1.0 / TOP)).reshape(1, 1, 1)
     for f in range(freqs):
         head = jnp.transpose(out_ref[f, :, :128])[:EDGE]
         tail = jnp.transpose(out_ref[f, :, 128:])[128 - EDGE :]
@@ -390,6 +418,7 @@
         out_shape=block_and_edges(freqs),
         in_specs=[VMEM] * 5,
         out_specs=(VMEM,) * 3,
+        scratch_shapes=[pltpu.VMEM((128 // GROUP, 8, GROUP * 128), f32)],
         compiler_params=pltpu.CompilerParams(vmem_limit_bytes=36 << 20),
         cost_estimate=pl.CostEstimate(
             flops=2 * freqs * 65536 * 2 * 16384, bytes_accessed=2000000, transcendentals=0
@@ -478,14 +507,14 @@
     cols_left = shifted(jnp.stack([magnet_x[:, :, -1], magnet_z[:, :, -1]]), "gx", 1)
     odd = jnp.stack([lax.axis_index("gx") % 2, lax.axis_index("gy") % 2])
     odd = jnp.broadcast_to(odd[:, None], (2, 128))
-    area_a, packed, offsets = gather_area_and_pack(counts, skin_cell, patch_slot, area, 4)
+    area_a, packed, offsets = gather_area_and_pack(counts, skin_cell, patch_slot, area, 2)
     rows_below, cols_left, area_a = lax.optimization_barrier((rows_below, cols_left, area_a))
-    e_next, j_next, dft_e_next, dft_h_next, table = field_step(
+    e_next, j_next, dft_e_next, dft_h_next, flux = field_step(
         e_field, h_field, j_field, material, material_table, dft_e, dft_h, rows_below, cols_left
     )
-    rows = gather_flux(counts, offsets, packed, table.reshape(9, 128, 512))
+    rows = gather_flux(offsets, packed, flux)
     arrived = lax.all_to_all(rows, ("gy", "gx"), split_axis=0, concat_axis=0, tiled=True)
-    area_b = gather_area(patch_slot, area, 4, 12)
+    area_b = gather_area(patch_slot, area, 2, 14)
 
     blocks, pieces = [], []
     for first, freqs in PIECES:

time: 95.4 us -> 89.4 us (0.937)
  Pallas kernels: 47.6 us -> 40.2 us
  waiting for transfers between devices: 12.2 us -> 15.8 us
  starting transfers between devices: 29.9 us -> 28.3 us
    pallas_call x2, Pallas kernels: 15 us -> 12.5 us  [scatter_density(): pl.pallas_call(functools.partial(scatter_kernel, first=first), out_shape=...]
    pallas_call x1, Pallas kernels: 5.37 us -> 3.11 us  [gather_area_and_pack(): pl.pallas_call(functools.partial(first_area_kernel, groups=groups), out_s...]
    ppermute x2, waiting for transfers between devices: 0.01 us -> 2.01 us  [shifted(): lax.ppermute(value, axis, [(source, source + steps) for source in range(l...]
    pallas_call x1, Pallas kernels: 11.3 us -> 10 us  [gather_area(): pl.pallas_call(functools.partial(area_kernel, first=first), out_shape=jax...]
    all_to_all x1, waiting for transfers between devices: 0.44 us -> 1.68 us  [shards(): lax.all_to_all(rows, ('gy', 'gx'), split_axis=0, concat_axis=0, tiled=True)]
    pallas_call x1, Pallas kernels: 9.66 us -> 8.49 us  [gather_flux(): pl.pallas_call(gather_kernel, out_shape=jax.ShapeDtypeStruct((128, 9, 1,...]
    all_to_all x1, starting transfers between devices: 11.1 us -> 10.1 us  [shards(): lax.all_to_all(rows, ('gy', 'gx'), split_axis=0, concat_axis=0, tiled=True)]
  transfers between devices with their start and end apart: 9 -> 9, of which waited for: 3 -> 4; matrix products, arithmetic and copies ran while one was open for 2% -> 2% of each run, Pallas kernels for 23% -> 20%
where the time goes in v7:
time: 89.4 us; the launch traced here: 88.3 us
  Pallas kernels  40.2 us (45%)
  starting transfers between devices  28.3 us (32%)
  waiting for transfers between devices  15.8 us (18%)
  local copies, waits for them, and re-layouts  1.98 us (2%)
  other arithmetic  1.02 us (1%)
  between operations  0.97 us (1%)
    ppermute x6, starting transfers between devices, exchange(): swaps.append(lax.ppermute(value, axis, pairs))  12.6 us
    pallas_call x2, Pallas kernels, scatter_density(): pl.pallas_call(functools.partial(scatter_kernel, first=first), out_shape=...  12.5 us
    ppermute x6, waiting for transfers between devices, exchange(): swaps.append(lax.ppermute(value, axis, pairs))  12.1 us
    all_to_all x1, starting transfers between devices, shards(): lax.all_to_all(rows, ('gy', 'gx'), split_axis=0, concat_axis=0, tiled=True)  10.1 us
    pallas_call x1, Pallas kernels, gather_area(): pl.pallas_call(functools.partial(area_kernel, first=first), out_shape=jax...  10 us
    pallas_call x1, Pallas kernels, gather_flux(): pl.pallas_call(gather_kernel, out_shape=jax.ShapeDtypeStruct((128, 9, 1,...  8.49 us
    ppermute x2, starting transfers between devices, shifted(): lax.ppermute(value, axis, [(source, source + steps) for source in range(l...  5.61 us
    pallas_call x1, Pallas kernels, field_step(): pl.pallas_call(field_kernel, grid=(planes,), out_shape=(jax.ShapeDtypeStr...  3.96 us
  transfers between devices with their start and end apart: 9, of which 4 were waited for; matrix products, arithmetic and copies ran while one was open for 2% of the time, Pallas kernels for 20%

profile of v7, /device:TPU:26, one launch (start us, length us, event | category | flops | bytes accessed | tf_op | source)
XLA Modules:
  0.0 88.3 jit_solution(4819307247540042122)
XLA Ops:
  0.7 1.1 %fusion = (f32[1,4,64,128]{3,2,1,0:T(8,128)S(1)}, f32[1,4,64,128]{3,2,1,0:T(8,128)S(1)}, f32[1,4,64,128]{3,2,1,0:T(8,128)S(1)}) fusion(f32[3,4,64,128]{3,2,1,0:T(8,128)} %h_ref.1), kind=kLoop, calls=%fused_computation.8 | loop fusion | bytes 786432 | tf_op jit(solution)/shard_map/slice | solution.py:505
  1.8 0.1 copy.26
  2.0 0.1 copy.27
  2.1 3.7 %collective-permute-start.1 = (f32[2,4,64]{2,1,0:T(4,128)S(1)}, f32[2,4,64]{2,1,0:T(4,128)S(1)}, u32[]{:S(2)}, u32[]{:S(2)}) collective-permute-start(f32[2,4,64]{2,1,0:T(4,128)S(1)} %pad_maximum_fusion.2), channel_id=1, source_target_pairs={{0,1},{1,2},{2,3},{3,4},{4,5},{5,6},{6,7},{8,9},{9,10},{10,11},{11... | collective-permute-start | bytes 6152 | tf_op jit(solution)/shard_map/ppermute | solution.py:35
  5.8 0.2 slice.29
  6.3 1.9 %collective-permute-start = (f32[2,4,128]{2,1,0:T(4,128)S(1)}, f32[2,4,128]{2,1,0:T(4,128)S(1)}, u32[]{:S(2)}, u32[]{:S(2)}) collective-permute-start(f32[2,4,128]{2,1,0:T(4,128)S(1)} %pad_maximum_fusion.1), channel_id=1, source_target_pairs={{0,8},{8,16},{16,24},{24,32},{32,40},{40,48},{48,56},{56,64},{64,7... | collective-permute-start | bytes 12296 | tf_op jit(solution)/shard_map/ppermute | solution.py:35
  8.4 3.1 %area_and_pack.1 = (f32[2,8,1024]{2,1,0:T(8,128)S(1)}, s32[136,128]{1,0:T(8,128)S(1)}, s32[1,136]{1,0:T(1,128)S(1)}) custom-call(s32[1,128]{1,0:T(1,128)S(1)} %copy-done.10, s32[1,128,128]{2,1,0:T(8,128)S(1)} %copy-done.8, s32[1,128,128]{2,1,0:T(8,128)S(1)} %copy-done.9, f32[3,256,256]{2,1,0:T(8,128)S(1)} %copy-done.7), custom_call_target="tpu_custom_call" | custom-call | flops 1610612736 | bytes 2000000 | tf_op jit(solution)/shard_map/area_and_pack/pallas_call | solution.py:324
  11.6 2.0 %collective-permute-done.row_ref = f32[2,4,128]{2,1,0:T(4,128)S(1)} collective-permute-done((f32[2,4,128]{2,1,0:T(4,128)S(1)}, f32[2,4,128]{2,1,0:T(4,128)S(1)}, u32[]{:S(2)}, u32[]{:S(2)}) %collective-permute-start) | collective-permute-done | bytes 4128 | tf_op jit(solution)/shard_map/ppermute | solution.py:35
  13.6 4.0 %field_step.1 = (f32[3,4,64,128]{3,2,1,0:T(8,128)}, f32[3,4,64,128]{3,2,1,0:T(8,128)}, f32[3,2,3,4,64,128]{5,4,3,2,1,0:T(8,128)}, f32[3,2,3,4,64,128]{5,4,3,2,1,0:T(8,128)}, f32[9,4,64,128]{3,2,1,0:T(8,128)S(1)}) custom-call(f32[3,4,64,128]{3,2,1,0:T(8,128)S(1)} %copy-done.3, f32[3,4,64,128]{3,2,1,0:T(8,128)S(1)} %copy-done.2, ...), custom_call_target="tpu_custom_call" | custom-call | tf_op jit(solution)/shard_map/field_step/pallas_call | solution.py:163
  17.6 8.5 %gather_flux.1 = f32[128,9,1,128]{3,2,1,0:T(1,128)} custom-call(s32[1,136]{1,0:T(1,128)S(1)} %get-tuple-element.34.offset_ref, s32[136,128]{1,0:T(8,128)S(1)} %get-tuple-element.35.packed, f32[9,4,64,128]{3,2,1,0:T(8,128)S(1)} %get-tuple-element.36.flux_ref), custom_call_target="tpu_custom_call" | custom-call | tf_op jit(solution)/shard_map/gather_flux/pallas_call | solution.py:232
  26.1 10.1 %all-to-all-start = ((f32[128,9,1,128]{3,2,1,0:T(1,128)}), f32[128,9,1,128]{3,2,1,0:T(1,128)S(1)}, u32[]{:S(2)}, u32[]{:S(2)}) async-start(f32[128,9,1,128]{3,2,1,0:T(1,128)} %gather_flux.1), calls=%async_computation | async-start | bytes 1179648 | tf_op jit(solution)/shard_map/all_to_all | solution.py:516
  36.1 10.0 %gather_area.1.area_b_ref = f32[14,8,1024]{2,1,0:T(8,128)S(1)} custom-call(s32[1,128,128]{2,1,0:T(8,128)S(1)} %copy-done.9, f32[3,256,256]{2,1,0:T(8,128)S(1)} %copy-done.7), custom_call_target="tpu_custom_call" | custom-call | flops 11274289152 | bytes 2000000 | tf_op jit(solution)/shard_map/gather_area/pallas_call | solution.py:341
  46.2 1.7 %all-to-all-done.flux_ref = f32[128,9,1,128]{3,2,1,0:T(1,128)S(1)} async-done(((f32[128,9,1,128]{3,2,1,0:T(1,128)}), f32[128,9,1,128]{3,2,1,0:T(1,128)S(1)}, u32[]{:S(2)}, u32[]{:S(2)}) %all-to-all-start) | async-done | bytes 589856 | tf_op jit(solution)/shard_map/all_to_all | solution.py:516
  47.9 7.9 %scatter_density.2 = (f32[2,256,256]{2,1,0:T(8,128)S(1)}, f32[2,104,256]{2,1,0:T(8,128)S(1)}, f32[2,104,256]{2,1,0:T(8,128)S(1)}) custom-call(s32[2,128]{1,0:T(2,128)S(1)} %broadcast_in_dim.2.odd_ref, s32[1,128,128]{2,1,0:T(8,128)S(1)} %copy-done.9, f32[2,8,1024]{2,1,0:T(8,128)S(1)} %get-tuple-element.33.area_a_ref, ...), custom_call_target="tpu_custom_call" | custom-call | flops 8589934592 | bytes 2000000 | tf_op jit(solution)/shard_map/scatter_density/pallas_call | solution.py:416
  55.8 4.7 %collective-permute-start.2 = (f32[2,104,256]{2,1,0:T(8,128)S(1)}, f32[2,104,256]{2,1,0:T(8,128)S(1)}, u32[]{:S(2)}, u32[]{:S(2)}) collective-permute-start(f32[2,104,256]{2,1,0:T(8,128)S(1)} %get-tuple-element.39), channel_id=1, source_target_pairs={{1,2},{3,4},{5,6},{2,1},{4,3},{6,5},{9,10},{11,12},{13,14},{10,9},... | collective-permute-start | bytes 638984 | tf_op jit(solution)/shard_map/ppermute | solution.py:44
  60.6 4.6 %scatter_density.3 = (f32[1,256,256]{2,1,0:T(8,128)S(1)}, f32[1,104,256]{2,1,0:T(8,128)S(1)}, f32[1,104,256]{2,1,0:T(8,128)S(1)}) custom-call(s32[2,128]{1,0:T(2,128)S(1)} %broadcast_in_dim.2.odd_ref, s32[1,128,128]{2,1,0:T(8,128)S(1)} %copy-done.9, f32[2,8,1024]{2,1,0:T(8,128)S(1)} %get-tuple-element.33.area_a_ref, ...), custom_call_target="tpu_custom_call" | custom-call | flops 4294967296 | bytes 2000000 | tf_op jit(solution)/shard_map/scatter_density/pallas_call | solution.py:416
  65.3 4.7 %collective-permute-start.4 = (f32[1,104,256]{2,1,0:T(8,128)S(1)}, f32[1,104,256]{2,1,0:T(8,128)S(1)}, u32[]{:S(2)}, u32[]{:S(2)}) collective-permute-start(f32[1,104,256]{2,1,0:T(8,128)S(1)} %get-tuple-element.41), channel_id=1, source_target_pairs={{1,2},{3,4},{5,6},{2,1},{4,3},{6,5},{9,10},{11,12},{13,14},{10,9},... | collective-permute-start | bytes 319496 | tf_op jit(solution)/shard_map/ppermute | solution.py:44
  70.1 5.6 %collective-permute-done.4.refs_4_ = f32[1,104,256]{2,1,0:T(8,128)S(1)} collective-permute-done((f32[1,104,256]{2,1,0:T(8,128)S(1)}, f32[1,104,256]{2,1,0:T(8,128)S(1)}, u32[]{:S(2)}, u32[]{:S(2)}) %collective-permute-start.4) | collective-permute-done | bytes 106528 | tf_op jit(solution)/shard_map/ppermute | solution.py:44
  75.7 0.6 column_sum.1
  76.4 2.1 %collective-permute-start.6 = (f32[3,104,256]{2,1,0:T(8,128)S(1)}, f32[3,104,256]{2,1,0:T(8,128)S(1)}, u32[]{:S(2)}, u32[]{:S(2)}) collective-permute-start(f32[3,104,256]{2,1,0:T(8,128)S(1)} %get-tuple-element.44), channel_id=1, source_target_pairs={{8,16},{24,32},{40,48},{56,64},{72,80},{88,96},{104,112},{16,8},{3... | collective-permute-start | bytes 958472 | tf_op jit(solution)/shard_map/ppermute | solution.py:44
  78.4 0.9 %collective-permute-start.7 = (f32[3,104,256]{2,1,0:T(8,128)S(1)}, f32[3,104,256]{2,1,0:T(8,128)S(1)}, u32[]{:S(2)}, u32[]{:S(2)}) collective-permute-start(f32[3,104,256]{2,1,0:T(8,128)S(1)} %get-tuple-element.45), channel_id=1, source_target_pairs={{0,8},{16,24},{32,40},{48,56},{64,72},{80,88},{96,104},{112,120},{... | collective-permute-start | bytes 958472 | tf_op jit(solution)/shard_map/ppermute | solution.py:44
  79.4 0.9 %pad_maximum_fusion = f32[3,256,256]{2,1,0:T(8,128)} fusion(f32[1,256,256]{2,1,0:T(8,128)S(1)} %get-tuple-element.38.refs_3_, f32[2,256,256]{2,1,0:T(8,128)S(1)} %get-tuple-element.37.refs_0_), kind=kLoop, calls=%fused_computation | loop fusion | flops 196608 | bytes 1572864 | tf_op jit(solution)/shard_map/concatenate | solution.py:526
  80.3 6.5 %collective-permute-done.6.one_ref = f32[3,104,256]{2,1,0:T(8,128)S(1)} collective-permute-done((f32[3,104,256]{2,1,0:T(8,128)S(1)}, f32[3,104,256]{2,1,0:T(8,128)S(1)}, u32[]{:S(2)}, u32[]{:S(2)}) %collective-permute-start.6) | collective-permute-done | bytes 319520 | tf_op jit(solution)/shard_map/ppermute | solution.py:44
  86.8 1.5 %row_sum.1 = f32[3,256,256]{2,1,0:T(8,128)} custom-call(s32[2,128]{1,0:T(2,128)S(1)} %broadcast_in_dim.2.odd_ref, f32[3,256,256]{2,1,0:T(8,128)S(1)} %get-tuple-element.43.block_ref, f32[3,104,256]{2,1,0:T(8,128)S(1)} %collective-permute-done.6.one_ref, f32[3,104,256]{2,1,0:T(8,128)S(1)} %collective-permute-done.7.two_ref), custom_call_target="tpu_custom_call" | custom-call | tf_op jit(solution)/shard_map/row_sum/pallas_call | solution.py:491
  (37 shorter events, 0.6 us)
Async XLA Ops:
  0.6 7.6 %copy-start.8 = (s32[1,128,128]{2,1,0:T(8,128)S(1)}, s32[1,128,128]{2,1,0:T(8,128)}, u32[]{:S(2)}) copy-start(s32[1,128,128]{2,1,0:T(8,128)} %cell_ref.1) | copy-start | bytes 196612
  0.6 7.6 %copy-start.10 = (s32[1,128]{1,0:T(1,128)S(1)}, s32[1,128]{1,0:T(1,128)}, u32[]{:S(2)}) copy-start(s32[1,128]{1,0:T(1,128)} %count_ref.1) | copy-start | bytes 1540
  0.7 7.6 %copy-start.9 = (s32[1,128,128]{2,1,0:T(8,128)S(1)}, s32[1,128,128]{2,1,0:T(8,128)}, u32[]{:S(2)}) copy-start(s32[1,128,128]{2,1,0:T(8,128)} %patch_ref.7) | copy-start | bytes 196612
  0.7 7.6 %copy-start.7 = (f32[3,256,256]{2,1,0:T(8,128)S(1)}, f32[3,256,256]{2,1,0:T(8,128)}, u32[]{:S(2)}) copy-start(f32[3,256,256]{2,1,0:T(8,128)} %area_ref.3) | copy-start | bytes 2359300
  2.1 9.4 %collective-permute-start.1 = (f32[2,4,64]{2,1,0:T(4,128)S(1)}, f32[2,4,64]{2,1,0:T(4,128)S(1)}, u32[]{:S(2)}, u32[]{:S(2)}) collective-permute-start(f32[2,4,64]{2,1,0:T(4,128)S(1)} %pad_maximum_fusion.2), channel_id=1, source_target_pairs={{0,1},{1,2},{2,3},{3,4},{4,5},{5,6},{6,7},{8,9},{9,10},{10,11},{11... | collective-permute-start | bytes 6152 | tf_op jit(solution)/shard_map/ppermute | solution.py:35
  6.2 7.4 %copy-start.5 = (s32[4,64,128]{2,1,0:T(8,128)S(1)}, s32[4,64,128]{2,1,0:T(8,128)}, u32[]{:S(2)}) copy-start(s32[4,64,128]{2,1,0:T(8,128)} %kind_ref.1) | copy-start | bytes 393220
  6.3 7.3 %collective-permute-start = (f32[2,4,128]{2,1,0:T(4,128)S(1)}, f32[2,4,128]{2,1,0:T(4,128)S(1)}, u32[]{:S(2)}, u32[]{:S(2)}) collective-permute-start(f32[2,4,128]{2,1,0:T(4,128)S(1)} %pad_maximum_fusion.1), channel_id=1, source_target_pairs={{0,8},{8,16},{16,24},{24,32},{32,40},{40,48},{48,56},{56,64},{64,7... | collective-permute-start | bytes 12296 | tf_op jit(solution)/shard_map/ppermute | solution.py:35
  8.3 5.3 %copy-start = (f32[3,2,3,4,64,128]{5,4,3,2,1,0:T(8,128)S(1)}, f32[3,2,3,4,64,128]{5,4,3,2,1,0:T(8,128)}, u32[]{:S(2)}) copy-start(f32[3,2,3,4,64,128]{5,4,3,2,1,0:T(8,128)} %dft_e_ref.1) | copy-start | bytes 7077892
  8.3 5.3 %copy-start.1 = (f32[3,2,3,4,64,128]{5,4,3,2,1,0:T(8,128)S(1)}, f32[3,2,3,4,64,128]{5,4,3,2,1,0:T(8,128)}, u32[]{:S(2)}) copy-start(f32[3,2,3,4,64,128]{5,4,3,2,1,0:T(8,128)} %dft_h_ref.1) | copy-start | bytes 7077892
  8.3 5.3 %copy-start.2 = (f32[3,4,64,128]{3,2,1,0:T(8,128)S(1)}, f32[3,4,64,128]{3,2,1,0:T(8,128)}, u32[]{:S(2)}) copy-start(f32[3,4,64,128]{3,2,1,0:T(8,128)} %h_ref.1) | copy-start | bytes 1179652
  8.3 5.3 %copy-start.3 = (f32[3,4,64,128]{3,2,1,0:T(8,128)S(1)}, f32[3,4,64,128]{3,2,1,0:T(8,128)}, u32[]{:S(2)}) copy-start(f32[3,4,64,128]{3,2,1,0:T(8,128)} %e_ref.1) | copy-start | bytes 1179652
  8.3 5.3 %copy-start.4 = (f32[3,4,64,128]{3,2,1,0:T(8,128)S(1)}, f32[3,4,64,128]{3,2,1,0:T(8,128)}, u32[]{:S(2)}) copy-start(f32[3,4,64,128]{3,2,1,0:T(8,128)} %j_ref.1) | copy-start | bytes 1179652
  8.3 5.3 %copy-start.6 = (f32[4,32]{1,0:T(4,128)S(1)}, f32[4,32]{1,0:T(4,128)}, u32[]{:S(2)}) copy-start(f32[4,32]{1,0:T(4,128)} %table_ref.1) | copy-start | bytes 1540
  26.1 21.8 %all-to-all-start = ((f32[128,9,1,128]{3,2,1,0:T(1,128)}), f32[128,9,1,128]{3,2,1,0:T(1,128)S(1)}, u32[]{:S(2)}, u32[]{:S(2)}) async-start(f32[128,9,1,128]{3,2,1,0:T(1,128)} %gather_flux.1), calls=%async_computation | async-start | bytes 1179648 | tf_op jit(solution)/shard_map/all_to_all | solution.py:516
  55.8 19.9 %collective-permute-start.2 = (f32[2,104,256]{2,1,0:T(8,128)S(1)}, f32[2,104,256]{2,1,0:T(8,128)S(1)}, u32[]{:S(2)}, u32[]{:S(2)}) collective-permute-start(f32[2,104,256]{2,1,0:T(8,128)S(1)} %get-tuple-element.39), channel_id=1, source_target_pairs={{1,2},{3,4},{5,6},{2,1},{4,3},{6,5},{9,10},{11,12},{13,14},{10,9},... | collective-permute-start | bytes 638984 | tf_op jit(solution)/shard_map/ppermute | solution.py:44
  60.6 15.2 %collective-permute-start.3 = (f32[2,104,256]{2,1,0:T(8,128)S(1)}, f32[2,104,256]{2,1,0:T(8,128)S(1)}, u32[]{:S(2)}, u32[]{:S(2)}) collective-permute-start(f32[2,104,256]{2,1,0:T(8,128)S(1)} %get-tuple-element.40), channel_id=1, source_target_pairs={{0,1},{2,3},{4,5},{6,7},{1,0},{3,2},{5,4},{7,6},{8,9},{10,11},{12,... | collective-permute-start | bytes 638984 | tf_op jit(solution)/shard_map/ppermute | solution.py:44
  65.3 10.4 %collective-permute-start.4 = (f32[1,104,256]{2,1,0:T(8,128)S(1)}, f32[1,104,256]{2,1,0:T(8,128)S(1)}, u32[]{:S(2)}, u32[]{:S(2)}) collective-permute-start(f32[1,104,256]{2,1,0:T(8,128)S(1)} %get-tuple-element.41), channel_id=1, source_target_pairs={{1,2},{3,4},{5,6},{2,1},{4,3},{6,5},{9,10},{11,12},{13,14},{10,9},... | collective-permute-start | bytes 319496 | tf_op jit(solution)/shard_map/ppermute | solution.py:44
  70.0 5.7 %collective-permute-start.5 = (f32[1,104,256]{2,1,0:T(8,128)S(1)}, f32[1,104,256]{2,1,0:T(8,128)S(1)}, u32[]{:S(2)}, u32[]{:S(2)}) collective-permute-start(f32[1,104,256]{2,1,0:T(8,128)S(1)} %get-tuple-element.42), channel_id=1, source_target_pairs={{0,1},{2,3},{4,5},{6,7},{1,0},{3,2},{5,4},{7,6},{8,9},{10,11},{12,... | collective-permute-start | bytes 319496 | tf_op jit(solution)/shard_map/ppermute | solution.py:44
  76.4 10.4 %collective-permute-start.6 = (f32[3,104,256]{2,1,0:T(8,128)S(1)}, f32[3,104,256]{2,1,0:T(8,128)S(1)}, u32[]{:S(2)}, u32[]{:S(2)}) collective-permute-start(f32[3,104,256]{2,1,0:T(8,128)S(1)} %get-tuple-element.44), channel_id=1, source_target_pairs={{8,16},{24,32},{40,48},{56,64},{72,80},{88,96},{104,112},{16,8},{3... | collective-permute-start | bytes 958472 | tf_op jit(solution)/shard_map/ppermute | solution.py:44
  78.4 8.3 %collective-permute-start.7 = (f32[3,104,256]{2,1,0:T(8,128)S(1)}, f32[3,104,256]{2,1,0:T(8,128)S(1)}, u32[]{:S(2)}, u32[]{:S(2)}) collective-permute-start(f32[3,104,256]{2,1,0:T(8,128)S(1)} %get-tuple-element.45), channel_id=1, source_target_pairs={{0,8},{16,24},{32,40},{48,56},{64,72},{80,88},{96,104},{112,120},{... | collective-permute-start | bytes 958472 | tf_op jit(solution)/shard_map/ppermute | solution.py:44

commit v8 on v7

--- a/solution.py
+++ b/solution.py
@@ -79,39 +79,61 @@
     return top * (1.0 / TOP)
 
 
-def field_kernel(
-    e_ref, h_ref, j_ref, kind_ref, table_ref, dft_e_ref, dft_h_ref, row_ref, col_ref,
-    e_out, j_out, dft_e_out, dft_h_out, flux_out, below_ref, wide_ref,
+def edge_kernel(h_ref, row_out, col_out):
+    planes, rows, cols = h_ref.shape[1:]
+    diagonal = iota((rows, rows), 0) == iota((rows, rows), 1)
+    for z in range(planes):
+        for part, c in enumerate((1, 2)):
+            row_out[part, z : z + 1, :] = h_ref[c, z, rows - 1 : rows, :]
+        for part, c in enumerate((0, 2)):
+            last = jnp.broadcast_to(h_ref[c, z, :, cols - 1 : cols], (rows, rows))
+            col_out[part, z : z + 1, :] = jnp.sum(
+                jnp.where(diagonal, last, 0.0), axis=0, keepdims=True
+            )
+
+
+def field_edges(h):
+    planes, rows, cols = h.shape[1:]
+    return pl.pallas_call(
+        edge_kernel,
+        out_shape=(
+            jax.ShapeDtypeStruct((2, planes, cols), f32),
+            jax.ShapeDtypeStruct((2, planes, rows), f32),
+        ),
+        in_specs=[VMEM],
+        out_specs=(VMEM, VMEM),
+        compiler_params=pltpu.CompilerParams(vmem_limit_bytes=8 << 20),
+        name="field_edges",
+    )(h)
+
+
+def field_plane(
+    z, e_ref, h_ref, j_ref, kind_ref, wide_ref, dft_e_ref, dft_h_ref, row_ref, col_ref,
+    e_out, j_out, dft_e_out, dft_h_out, flux_out,
 ):
-    z = pl.program_id(0)
-
-    @pl.when(z == 0)
-    def _():
-        below_ref[...] = jnp.zeros_like(below_ref)
-        wide_ref[...] = jnp.zeros_like(wide_ref)
-        wide_ref[0:4, 0:32] = table_ref[...]
-
     rows, cols = kind_ref.shape[1:]
-    hx, hy, hz = h_ref[0, 0], h_ref[1, 0], h_ref[2, 0]
+    hx, hy, hz = h_ref[0, z], h_ref[1, z], h_ref[2, z]
     first_row = iota((rows, cols), 0) == 0
     first_col = iota((rows, cols), 1) == 0
     diagonal = iota((rows, rows), 0) == iota((rows, rows), 1)
 
     def below_x(field, part):
-        halo = row_ref[part, pl.ds(z, 1), :]
+        halo = row_ref[part, z : z + 1, :]
         return jnp.where(first_row, halo, pltpu.roll(field, 1, 0))
 
     def below_y(field, part):
-        halo = col_ref[part, pl.ds(z, 1), :]
+        halo = col_ref[part, z : z + 1, :]
         halo = jnp.sum(jnp.where(diagonal, halo, 0.0), axis=1, keepdims=True)
         return jnp.where(first_col, halo, pltpu.roll(field, 1, 1))
 
+    zero = jnp.zeros((rows, cols), f32)
+    below_z = (h_ref[0, z - 1], h_ref[1, z - 1]) if z else (zero, zero)
     curl = (
-        (hz - below_y(hz, 1)) - (hy - below_ref[1]),
-        (hx - below_ref[0]) - (hz - below_x(hz, 1)),
+        (hz - below_y(hz, 1)) - (hy - below_z[1]),
+        (hx - below_z[0]) - (hz - below_x(hz, 1)),
         (hy - below_x(hy, 0)) - (hx - below_y(hx, 0)),
     )
-    kinds = kind_ref[0]
+    kinds = kind_ref[z]
     coeffs = [
         jnp.take_along_axis(
             jnp.broadcast_to(wide_ref[r : r + 1, :], (rows, cols)), kinds, axis=1
@@ -120,10 +142,10 @@
     ]
     e_next = []
     for c in range(3):
-        old_e, old_j = e_ref[c, 0], j_ref[c, 0]
+        old_e, old_j = e_ref[c, z], j_ref[c, z]
         new_e = coeffs[0] * old_e + coeffs[1] * (curl[c] - old_j)
-        e_out[c, 0] = new_e
-        j_out[c, 0] = coeffs[2] * old_j + coeffs[3] * (new_e - old_e)
+        e_out[c, z] = new_e
+        j_out[c, z] = coeffs[2] * old_j + coeffs[3] * (new_e - old_e)
         e_next.append(new_e)
     field_h = (hx, hy, hz)
     phase_e, phase_h = phase_list(0.0), phase_list(0.5)
@@ -132,58 +154,22 @@
         for part in range(2):
             factor_e = math.cos(phase_e[f]) if part == 0 else -math.sin(phase_e[f])
             factor_h = math.cos(phase_h[f]) if part == 0 else -math.sin(phase_h[f])
-            now_e = [dft_e_ref[f, part, c, 0] + e_next[c] * factor_e for c in range(3)]
-            now_h = [dft_h_ref[f, part, c, 0] + field_h[c] * factor_h for c in range(3)]
+            now_e = [dft_e_ref[f, part, c, z] + e_next[c] * factor_e for c in range(3)]
+            now_h = [dft_h_ref[f, part, c, z] + field_h[c] * factor_h for c in range(3)]
             for c in range(3):
-                dft_e_out[f, part, c, 0] = now_e[c]
-                dft_h_out[f, part, c, 0] = now_h[c]
+                dft_e_out[f, part, c, z] = now_e[c]
+                dft_h_out[f, part, c, z] = now_h[c]
             spec_e.append(now_e)
             spec_h.append(now_h)
         for c in range(3):
             a, b = (c + 1) % 3, (c + 2) % 3
-            flux = 0.5 * (
+            flux_out[3 * f + c, z] = 0.5 * (
                 (spec_e[0][a] * spec_h[0][b] - spec_e[0][b] * spec_h[0][a])
                 + (spec_e[1][a] * spec_h[1][b] - spec_e[1][b] * spec_h[1][a])
             )
-            flux_out[3 * f + c, 0] = flux
-    below_ref[0] = hx
-    below_ref[1] = hy
-
-
-def field_step(e, h, j, kinds, table, dft_e, dft_h, rows_below, cols_left):
-    planes, rows, cols = kinds.shape
-    plane3 = pl.BlockSpec((3, 1, rows, cols), lambda z: (0, z, 0, 0))
-    spectra = pl.BlockSpec((3, 2, 3, 1, rows, cols), lambda z: (0, 0, 0, z, 0, 0))
-
-    flux = pl.BlockSpec((9, 1, rows, cols), lambda z: (0, z, 0, 0))
-
-    def whole(shape):
-        return pl.BlockSpec(shape, lambda z: (0,) * len(shape))
-
-    return pl.pallas_call(
-        field_kernel,
-        grid=(planes,),
-        out_shape=(
-            jax.ShapeDtypeStruct(e.shape, f32),
-            jax.ShapeDtypeStruct(e.shape, f32),
-            jax.ShapeDtypeStruct(dft_e.shape, f32),
-            jax.ShapeDtypeStruct(dft_h.shape, f32),
-            jax.ShapeDtypeStruct((9, planes, rows, cols), f32),
-        ),
-        in_specs=[
-            plane3, plane3, plane3,
-            pl.BlockSpec((1, rows, cols), lambda z: (z, 0, 0)),
-            whole(table.shape), spectra, spectra,
-            whole(rows_below.shape), whole(cols_left.shape),
-        ],
-        out_specs=(plane3, plane3, spectra, spectra, flux),
-        scratch_shapes=[pltpu.VMEM((2, rows, cols), f32), pltpu.VMEM((8, cols), f32)],
-        compiler_params=pltpu.CompilerParams(vmem_limit_bytes=20 << 20),
-        name="field_step",
-    )(e, h, j, kinds, table, dft_e, dft_h, rows_below, cols_left)
-
-
-def gather_kernel(offset_ref, packed, flux_ref, out_ref, found, head_ref, rest_ref):
+
+
+def lookup_flux(offset_ref, packed, flux_ref, out_ref, found, head_ref, rest_ref):
     planes = [flux_ref[:, z].reshape(576, 128) for z in range(4)]
     back = split_scaled(jnp.concatenate(planes, 1), head_ref, rest_ref)
 
@@ -225,23 +211,55 @@
             out_ref[d, q] = value[q : q + 1, :]
         return 0
 
-    lax.fori_loop(0, 128, unpack, 0, unroll=16)
-
-
-def gather_flux(offsets, packed, flux):
-    return pl.pallas_call(
-        gather_kernel,
-        out_shape=jax.ShapeDtypeStruct((128, 9, 1, 128), f32),
-        in_specs=[SMEM, VMEM, VMEM],
-        out_specs=VMEM,
-        scratch_shapes=[
+    lax.fori_loop(0, 128, unpack, 0, unroll=32)
+
+
+def field_kernel(
+    offset_ref, packed, e_ref, h_ref, j_ref, kind_ref, table_ref, dft_e_ref, dft_h_ref, row_ref,
+    col_ref, e_hbm, j_hbm, dft_e_hbm, dft_h_hbm, out_ref, e_new, j_new, dft_e_new, dft_h_new,
+    flux_ref, wide_ref, found, head_ref, rest_ref, sems,
+):
+    wide_ref[...] = jnp.zeros_like(wide_ref)
+    wide_ref[0:4, 0:32] = table_ref[...]
+    planes = kind_ref.shape[0]
+    copies = []
+    for z in range(planes):
+        field_plane(
+            z, e_ref, h_ref, j_ref, kind_ref, wide_ref, dft_e_ref, dft_h_ref, row_ref, col_ref,
+            e_new, j_new, dft_e_new, dft_h_new, flux_ref,
+        )
+    for i, (new, hbm) in enumerate(
+        ((dft_e_new, dft_e_hbm), (dft_h_new, dft_h_hbm), (e_new, e_hbm), (j_new, j_hbm))
+    ):
+        copy = pltpu.make_async_copy(new, hbm, sems.at[i])
+        copy.start()
+        copies.append(copy)
+    lookup_flux(offset_ref, packed, flux_ref, out_ref, found, head_ref, rest_ref)
+    for copy in copies:
+        copy.wait()
+
+
+def field_and_flux(offsets, packed, e, h, j, kinds, table, dft_e, dft_h, rows_below, cols_left):
+    planes, rows, cols = kinds.shape
+    fields = [e.shape, e.shape, dft_e.shape, dft_h.shape]
+    return pl.pallas_call(
+        field_kernel,
+        out_shape=tuple(jax.ShapeDtypeStruct(shape, f32) for shape in fields)
+        + (jax.ShapeDtypeStruct((128, 9, 1, 128), f32),),
+        in_specs=[SMEM] + [VMEM] * 10,
+        out_specs=(pl.BlockSpec(memory_space=pl.ANY),) * 4 + (VMEM,),
+        scratch_shapes=[pltpu.VMEM(shape, f32) for shape in fields]
+        + [
+            pltpu.VMEM((9, planes, rows, cols), f32),
+            pltpu.VMEM((8, cols), f32),
             pltpu.VMEM((136, 16, 128), f32),
             pltpu.VMEM((576, 512), bf16),
             pltpu.VMEM((576, 512), f8),
+            pltpu.SemaphoreType.DMA((4,)),
         ],
-        compiler_params=pltpu.CompilerParams(vmem_limit_bytes=28 << 20),
-        name="gather_flux",
-    )(offsets, packed, flux)
+        compiler_params=pltpu.CompilerParams(vmem_limit_bytes=30 << 20),
+        name="field_and_flux",
+    )(offsets, packed, e, h, j, kinds, table, dft_e, dft_h, rows_below, cols_left)
 
 
 GROUP = 8
@@ -502,17 +520,17 @@
     e_field, h_field, j_field, material, material_table, dft_e, dft_h, skin_cell, counts,
     patch_slot, area,
 ):
-    magnet_x, magnet_y, magnet_z = (h_field[0], h_field[1], h_field[2])
-    rows_below = shifted(jnp.stack([magnet_y[:, -1, :], magnet_z[:, -1, :]]), "gy", 1)
-    cols_left = shifted(jnp.stack([magnet_x[:, :, -1], magnet_z[:, :, -1]]), "gx", 1)
+    last_rows, last_cols = field_edges(h_field)
+    rows_below = shifted(last_rows, "gy", 1)
+    cols_left = shifted(last_cols, "gx", 1)
     odd = jnp.stack([lax.axis_index("gx") % 2, lax.axis_index("gy") % 2])
     odd = jnp.broadcast_to(odd[:, None], (2, 128))
     area_a, packed, offsets = gather_area_and_pack(counts, skin_cell, patch_slot, area, 2)
     rows_below, cols_left, area_a = lax.optimization_barrier((rows_below, cols_left, area_a))
-    e_next, j_next, dft_e_next, dft_h_next, flux = field_step(
-        e_field, h_field, j_field, material, material_table, dft_e, dft_h, rows_below, cols_left
-    )
-    rows = gather_flux(offsets, packed, flux)
+    e_next, j_next, dft_e_next, dft_h_next, rows = field_and_flux(
+        offsets, packed, e_field, h_field, j_field, material, material_table, dft_e, dft_h,
+        rows_below, cols_left,
+    )
     arrived = lax.all_to_all(rows, ("gy", "gx"), split_axis=0, concat_axis=0, tiled=True)
     area_b = gather_area(patch_slot, area, 2, 14)
 

time: 89.4 us -> 89 us (level)
  local copies, waits for them, and re-layouts: 1.98 us -> 4.56 us
  waiting for transfers between devices: 15.8 us -> 13.8 us
  Pallas kernels: 40.2 us -> 38.6 us
    unnamed x25 -> x28, local copies, waits for them, and re-layouts: 0.47 us -> 4.5 us
    ppermute x2, waiting for transfers between devices: 2.01 us -> 0.01 us  [shifted(): lax.ppermute(value, axis, [(source, source + steps) for source in range(l...]
    pallas_call x2, Pallas kernels: 12.4 us -> 10.8 us  [the longest x1 10.7 us: field_and_flux(): pl.pallas_call(field_kernel, out_shape=tuple((jax.ShapeDtypeStruct(shape,...]
    slice x3 -> x0, local copies, waits for them, and re-layouts: 1.44 us -> none  [the longest x1 1.14 us: shards(): magnet_x, magnet_y, magnet_z = (h_field[0], h_field[1], h_field[2])]
  transfers between devices with their start and end apart: 9 -> 9, of which waited for: 4 -> 3; matrix products, arithmetic and copies ran while one was open for 2% -> 1% of each run, Pallas kernels for 20% -> 20%
where the time goes in v8:
time: 89 us; the launch traced here: 87.8 us
  Pallas kernels  38.6 us (43%)
  starting transfers between devices  28.9 us (32%)
  waiting for transfers between devices  13.8 us (16%)
  local copies, waits for them, and re-layouts  4.56 us (5%)
  other arithmetic  1.01 us (1%)
  between operations  0.9 us (1%)
    ppermute x6, starting transfers between devices, exchange(): swaps.append(lax.ppermute(value, axis, pairs))  12.6 us
    pallas_call x2, Pallas kernels, scatter_density(): pl.pallas_call(functools.partial(scatter_kernel, first=first), out_shape=...  12.5 us
    ppermute x6, waiting for transfers between devices, exchange(): swaps.append(lax.ppermute(value, axis, pairs))  12.1 us
    pallas_call x1, Pallas kernels, field_and_flux(): pl.pallas_call(field_kernel, out_shape=tuple((jax.ShapeDtypeStruct(shape,...  10.7 us
    all_to_all x1, starting transfers between devices, shards(): lax.all_to_all(rows, ('gy', 'gx'), split_axis=0, concat_axis=0, tiled=True)  10.7 us
    pallas_call x1, Pallas kernels, gather_area(): pl.pallas_call(functools.partial(area_kernel, first=first), out_shape=jax...  10 us
    ppermute x2, starting transfers between devices, shifted(): lax.ppermute(value, axis, [(source, source + steps) for source in range(l...  5.61 us
    unnamed x28, local copies, waits for them, and re-layouts  4.5 us
  transfers between devices with their start and end apart: 9, of which 3 were waited for; matrix products, arithmetic and copies ran while one was open for 1% of the time, Pallas kernels for 20%

profile of v8, /device:TPU:26, one launch (start us, length us, event | category | flops | bytes accessed | tf_op | source)
XLA Modules:
  0.0 87.8 jit_solution(11937090669355411773)
XLA Ops:
  0.6 1.0 %copy-done.2 = f32[3,4,64,128]{3,2,1,0:T(8,128)S(1)} copy-done((f32[3,4,64,128]{3,2,1,0:T(8,128)S(1)}, f32[3,4,64,128]{3,2,1,0:T(8,128)}, u32[]{:S(2)}) %copy-start.2) | copy-done | bytes 393240
  1.6 0.1 field_edges.1
  1.8 1.9 %collective-permute-start = (f32[2,4,128]{2,1,0:T(4,128)S(1)}, f32[2,4,128]{2,1,0:T(4,128)S(1)}, u32[]{:S(2)}, u32[]{:S(2)}) collective-permute-start(f32[2,4,128]{2,1,0:T(4,128)S(1)} %get-tuple-element.30), channel_id=1, source_target_pairs={{0,8},{8,16},{16,24},{24,32},{32,40},{40,48},{48,56},{56,64},{64,7... | collective-permute-start | bytes 12296 | tf_op jit(solution)/shard_map/ppermute | solution.py:35
  3.7 3.7 %collective-permute-start.1 = (f32[2,4,64]{2,1,0:T(4,128)S(1)}, f32[2,4,64]{2,1,0:T(4,128)S(1)}, u32[]{:S(2)}, u32[]{:S(2)}) collective-permute-start(f32[2,4,64]{2,1,0:T(4,128)S(1)} %get-tuple-element.31), channel_id=1, source_target_pairs={{0,1},{1,2},{2,3},{3,4},{4,5},{5,6},{6,7},{8,9},{9,10},{10,11},{11... | collective-permute-start | bytes 6152 | tf_op jit(solution)/shard_map/ppermute | solution.py:35
  7.4 1.1 %copy-done.8 = f32[3,256,256]{2,1,0:T(8,128)S(1)} copy-done((f32[3,256,256]{2,1,0:T(8,128)S(1)}, f32[3,256,256]{2,1,0:T(8,128)}, u32[]{:S(2)}) %copy-start.8) | copy-done | bytes 786456
  8.6 0.8 copy-done.10
  9.4 0.8 copy-done.11
  10.2 0.7 copy-done.13
  10.9 3.1 %area_and_pack.1 = (f32[2,8,1024]{2,1,0:T(8,128)S(1)}, s32[136,128]{1,0:T(8,128)S(1)}, s32[1,136]{1,0:T(1,128)S(1)}) custom-call(s32[1,128]{1,0:T(1,128)S(1)} %copy-done.13, s32[1,128,128]{2,1,0:T(8,128)S(1)} %copy-done.10, s32[1,128,128]{2,1,0:T(8,128)S(1)} %copy-done.11, f32[3,256,256]{2,1,0:T(8,128)S(1)} %copy-done.8), custom_call_target="tpu_custom_call" | custom-call | flops 1610612736 | bytes 2000000 | tf_op jit(solution)/shard_map/area_and_pack/pallas_call | solution.py:342
  14.2 10.7 %field_and_flux.1 = (f32[3,4,64,128]{3,2,1,0:T(8,128)}, f32[3,4,64,128]{3,2,1,0:T(8,128)}, f32[3,2,3,4,64,128]{5,4,3,2,1,0:T(8,128)}, f32[3,2,3,4,64,128]{5,4,3,2,1,0:T(8,128)}, f32[128,9,1,128]{3,2,1,0:T(1,128)}) custom-call(s32[1,136]{1,0:T(1,128)S(1)} %get-tuple-element.28.offset_ref, s32[136,128]{1,0:T(8,128)S(1)} %get-tuple-element.29.packed, ...), custom_call_target="tpu_custom_call" | custom-call | tf_op jit(solution)/shard_map/field_and_flux/pallas_call | solution.py:245
  24.9 10.7 %all-to-all-start = ((f32[128,9,1,128]{3,2,1,0:T(1,128)}), f32[128,9,1,128]{3,2,1,0:T(1,128)S(1)}, u32[]{:S(2)}, u32[]{:S(2)}) async-start(f32[128,9,1,128]{3,2,1,0:T(1,128)} %get-tuple-element.40), calls=%async_computation | async-start | bytes 1179648 | tf_op jit(solution)/shard_map/all_to_all | solution.py:534
  35.6 10.0 %gather_area.1.area_b_ref = f32[14,8,1024]{2,1,0:T(8,128)S(1)} custom-call(s32[1,128,128]{2,1,0:T(8,128)S(1)} %copy-done.12, f32[3,256,256]{2,1,0:T(8,128)S(1)} %copy-done.9), custom_call_target="tpu_custom_call" | custom-call | flops 11274289152 | bytes 2000000 | tf_op jit(solution)/shard_map/gather_area/pallas_call | solution.py:359
  45.7 1.6 %all-to-all-done.flux_ref = f32[128,9,1,128]{3,2,1,0:T(1,128)S(1)} async-done(((f32[128,9,1,128]{3,2,1,0:T(1,128)}), f32[128,9,1,128]{3,2,1,0:T(1,128)S(1)}, u32[]{:S(2)}, u32[]{:S(2)}) %all-to-all-start) | async-done | bytes 589856 | tf_op jit(solution)/shard_map/all_to_all | solution.py:534
  47.4 7.9 %scatter_density.2 = (f32[2,256,256]{2,1,0:T(8,128)S(1)}, f32[2,104,256]{2,1,0:T(8,128)S(1)}, f32[2,104,256]{2,1,0:T(8,128)S(1)}) custom-call(s32[2,128]{1,0:T(2,128)S(1)} %broadcast_in_dim.2.odd_ref, s32[1,128,128]{2,1,0:T(8,128)S(1)} %copy-done.12, f32[2,8,1024]{2,1,0:T(8,128)S(1)} %get-tuple-element.39.area_a_ref, ...), custom_call_target="tpu_custom_call" | custom-call | flops 8589934592 | bytes 2000000 | tf_op jit(solution)/shard_map/scatter_density/pallas_call | solution.py:434
  55.3 4.7 %collective-permute-start.2 = (f32[2,104,256]{2,1,0:T(8,128)S(1)}, f32[2,104,256]{2,1,0:T(8,128)S(1)}, u32[]{:S(2)}, u32[]{:S(2)}) collective-permute-start(f32[2,104,256]{2,1,0:T(8,128)S(1)} %get-tuple-element.43), channel_id=1, source_target_pairs={{1,2},{3,4},{5,6},{2,1},{4,3},{6,5},{9,10},{11,12},{13,14},{10,9},... | collective-permute-start | bytes 638984 | tf_op jit(solution)/shard_map/ppermute | solution.py:44
  60.1 4.6 %scatter_density.3 = (f32[1,256,256]{2,1,0:T(8,128)S(1)}, f32[1,104,256]{2,1,0:T(8,128)S(1)}, f32[1,104,256]{2,1,0:T(8,128)S(1)}) custom-call(s32[2,128]{1,0:T(2,128)S(1)} %broadcast_in_dim.2.odd_ref, s32[1,128,128]{2,1,0:T(8,128)S(1)} %copy-done.12, f32[2,8,1024]{2,1,0:T(8,128)S(1)} %get-tuple-element.39.area_a_ref, ...), custom_call_target="tpu_custom_call" | custom-call | flops 4294967296 | bytes 2000000 | tf_op jit(solution)/shard_map/scatter_density/pallas_call | solution.py:434
  64.8 4.7 %collective-permute-start.4 = (f32[1,104,256]{2,1,0:T(8,128)S(1)}, f32[1,104,256]{2,1,0:T(8,128)S(1)}, u32[]{:S(2)}, u32[]{:S(2)}) collective-permute-start(f32[1,104,256]{2,1,0:T(8,128)S(1)} %get-tuple-element.45), channel_id=1, source_target_pairs={{1,2},{3,4},{5,6},{2,1},{4,3},{6,5},{9,10},{11,12},{13,14},{10,9},... | collective-permute-start | bytes 319496 | tf_op jit(solution)/shard_map/ppermute | solution.py:44
  69.6 5.6 %collective-permute-done.4.refs_4_ = f32[1,104,256]{2,1,0:T(8,128)S(1)} collective-permute-done((f32[1,104,256]{2,1,0:T(8,128)S(1)}, f32[1,104,256]{2,1,0:T(8,128)S(1)}, u32[]{:S(2)}, u32[]{:S(2)}) %collective-permute-start.4) | collective-permute-done | bytes 106528 | tf_op jit(solution)/shard_map/ppermute | solution.py:44
  75.2 0.6 column_sum.1
  75.8 2.1 %collective-permute-start.6 = (f32[3,104,256]{2,1,0:T(8,128)S(1)}, f32[3,104,256]{2,1,0:T(8,128)S(1)}, u32[]{:S(2)}, u32[]{:S(2)}) collective-permute-start(f32[3,104,256]{2,1,0:T(8,128)S(1)} %get-tuple-element.48), channel_id=1, source_target_pairs={{8,16},{24,32},{40,48},{56,64},{72,80},{88,96},{104,112},{16,8},{3... | collective-permute-start | bytes 958472 | tf_op jit(solution)/shard_map/ppermute | solution.py:44
  78.0 0.9 %collective-permute-start.7 = (f32[3,104,256]{2,1,0:T(8,128)S(1)}, f32[3,104,256]{2,1,0:T(8,128)S(1)}, u32[]{:S(2)}, u32[]{:S(2)}) collective-permute-start(f32[3,104,256]{2,1,0:T(8,128)S(1)} %get-tuple-element.49), channel_id=1, source_target_pairs={{0,8},{16,24},{32,40},{48,56},{64,72},{80,88},{96,104},{112,120},{... | collective-permute-start | bytes 958472 | tf_op jit(solution)/shard_map/ppermute | solution.py:44
  78.8 0.9 %pad_maximum_fusion = f32[3,256,256]{2,1,0:T(8,128)} fusion(f32[1,256,256]{2,1,0:T(8,128)S(1)} %get-tuple-element.42.refs_3_, f32[2,256,256]{2,1,0:T(8,128)S(1)} %get-tuple-element.41.refs_0_), kind=kLoop, calls=%fused_computation | loop fusion | flops 196608 | bytes 1572864 | tf_op jit(solution)/shard_map/concatenate | solution.py:544
  79.8 6.5 %collective-permute-done.6.one_ref = f32[3,104,256]{2,1,0:T(8,128)S(1)} collective-permute-done((f32[3,104,256]{2,1,0:T(8,128)S(1)}, f32[3,104,256]{2,1,0:T(8,128)S(1)}, u32[]{:S(2)}, u32[]{:S(2)}) %collective-permute-start.6) | collective-permute-done | bytes 319520 | tf_op jit(solution)/shard_map/ppermute | solution.py:44
  86.3 1.5 %row_sum.1 = f32[3,256,256]{2,1,0:T(8,128)} custom-call(s32[2,128]{1,0:T(2,128)S(1)} %broadcast_in_dim.2.odd_ref, f32[3,256,256]{2,1,0:T(8,128)S(1)} %get-tuple-element.47.block_ref, f32[3,104,256]{2,1,0:T(8,128)S(1)} %collective-permute-done.6.one_ref, f32[3,104,256]{2,1,0:T(8,128)S(1)} %collective-permute-done.7.two_ref), custom_call_target="tpu_custom_call" | custom-call | tf_op jit(solution)/shard_map/row_sum/pallas_call | solution.py:509
  (33 shorter events, 0.4 us)
Async XLA Ops:
  0.6 1.0 %copy-start.2 = (f32[3,4,64,128]{3,2,1,0:T(8,128)S(1)}, f32[3,4,64,128]{3,2,1,0:T(8,128)}, u32[]{:S(2)}) copy-start(f32[3,4,64,128]{3,2,1,0:T(8,128)} %h_ref.3) | copy-start | bytes 1179652
  1.6 12.5 %copy-start.6 = (s32[4,64,128]{2,1,0:T(8,128)S(1)}, s32[4,64,128]{2,1,0:T(8,128)}, u32[]{:S(2)}) copy-start(s32[4,64,128]{2,1,0:T(8,128)} %kind_ref.1) | copy-start | bytes 393220
  1.8 12.4 %collective-permute-start = (f32[2,4,128]{2,1,0:T(4,128)S(1)}, f32[2,4,128]{2,1,0:T(4,128)S(1)}, u32[]{:S(2)}, u32[]{:S(2)}) collective-permute-start(f32[2,4,128]{2,1,0:T(4,128)S(1)} %get-tuple-element.30), channel_id=1, source_target_pairs={{0,8},{8,16},{16,24},{24,32},{32,40},{40,48},{48,56},{56,64},{64,7... | collective-permute-start | bytes 12296 | tf_op jit(solution)/shard_map/ppermute | solution.py:35
  3.7 10.4 %collective-permute-start.1 = (f32[2,4,64]{2,1,0:T(4,128)S(1)}, f32[2,4,64]{2,1,0:T(4,128)S(1)}, u32[]{:S(2)}, u32[]{:S(2)}) collective-permute-start(f32[2,4,64]{2,1,0:T(4,128)S(1)} %get-tuple-element.31), channel_id=1, source_target_pairs={{0,1},{1,2},{2,3},{3,4},{4,5},{5,6},{6,7},{8,9},{9,10},{10,11},{11... | collective-permute-start | bytes 6152 | tf_op jit(solution)/shard_map/ppermute | solution.py:35
  7.4 1.1 %copy-start.8 = (f32[3,256,256]{2,1,0:T(8,128)S(1)}, f32[3,256,256]{2,1,0:T(8,128)}, u32[]{:S(2)}) copy-start(f32[3,256,256]{2,1,0:T(8,128)} %area_ref.3) | copy-start | bytes 2359300
  8.6 0.8 copy-start.10
  9.4 0.8 copy-start.11
  10.2 0.7 copy-start.13
  10.9 3.2 %copy-start = (f32[3,2,3,4,64,128]{5,4,3,2,1,0:T(8,128)S(1)}, f32[3,2,3,4,64,128]{5,4,3,2,1,0:T(8,128)}, u32[]{:S(2)}) copy-start(f32[3,2,3,4,64,128]{5,4,3,2,1,0:T(8,128)} %dft_e_ref.1) | copy-start | bytes 7077892
  10.9 3.3 %copy-start.1 = (f32[3,2,3,4,64,128]{5,4,3,2,1,0:T(8,128)S(1)}, f32[3,2,3,4,64,128]{5,4,3,2,1,0:T(8,128)}, u32[]{:S(2)}) copy-start(f32[3,2,3,4,64,128]{5,4,3,2,1,0:T(8,128)} %dft_h_ref.1) | copy-start | bytes 7077892
  10.9 3.3 %copy-start.3 = (f32[3,4,64,128]{3,2,1,0:T(8,128)S(1)}, f32[3,4,64,128]{3,2,1,0:T(8,128)}, u32[]{:S(2)}) copy-start(f32[3,4,64,128]{3,2,1,0:T(8,128)} %h_ref.3) | copy-start | bytes 1179652
  10.9 3.3 %copy-start.4 = (f32[3,4,64,128]{3,2,1,0:T(8,128)S(1)}, f32[3,4,64,128]{3,2,1,0:T(8,128)}, u32[]{:S(2)}) copy-start(f32[3,4,64,128]{3,2,1,0:T(8,128)} %e_ref.1) | copy-start | bytes 1179652
  10.9 3.3 %copy-start.5 = (f32[3,4,64,128]{3,2,1,0:T(8,128)S(1)}, f32[3,4,64,128]{3,2,1,0:T(8,128)}, u32[]{:S(2)}) copy-start(f32[3,4,64,128]{3,2,1,0:T(8,128)} %j_ref.1) | copy-start | bytes 1179652
  10.9 3.3 %copy-start.7 = (f32[4,32]{1,0:T(4,128)S(1)}, f32[4,32]{1,0:T(4,128)}, u32[]{:S(2)}) copy-start(f32[4,32]{1,0:T(4,128)} %table_ref.1) | copy-start | bytes 1540
  14.2 21.4 %copy-start.9 = (f32[3,256,256]{2,1,0:T(8,128)S(1)}, f32[3,256,256]{2,1,0:T(8,128)}, u32[]{:S(2)}) copy-start(f32[3,256,256]{2,1,0:T(8,128)} %area_ref.3) | copy-start | bytes 2359300
  14.2 21.4 %copy-start.12 = (s32[1,128,128]{2,1,0:T(8,128)S(1)}, s32[1,128,128]{2,1,0:T(8,128)}, u32[]{:S(2)}) copy-start(s32[1,128,128]{2,1,0:T(8,128)} %patch_ref.7) | copy-start | bytes 196612
  24.9 22.4 %all-to-all-start = ((f32[128,9,1,128]{3,2,1,0:T(1,128)}), f32[128,9,1,128]{3,2,1,0:T(1,128)S(1)}, u32[]{:S(2)}, u32[]{:S(2)}) async-start(f32[128,9,1,128]{3,2,1,0:T(1,128)} %get-tuple-element.40), calls=%async_computation | async-start | bytes 1179648 | tf_op jit(solution)/shard_map/all_to_all | solution.py:534
  55.3 19.9 %collective-permute-start.2 = (f32[2,104,256]{2,1,0:T(8,128)S(1)}, f32[2,104,256]{2,1,0:T(8,128)S(1)}, u32[]{:S(2)}, u32[]{:S(2)}) collective-permute-start(f32[2,104,256]{2,1,0:T(8,128)S(1)} %get-tuple-element.43), channel_id=1, source_target_pairs={{1,2},{3,4},{5,6},{2,1},{4,3},{6,5},{9,10},{11,12},{13,14},{10,9},... | collective-permute-start | bytes 638984 | tf_op jit(solution)/shard_map/ppermute | solution.py:44
  60.0 15.2 %collective-permute-start.3 = (f32[2,104,256]{2,1,0:T(8,128)S(1)}, f32[2,104,256]{2,1,0:T(8,128)S(1)}, u32[]{:S(2)}, u32[]{:S(2)}) collective-permute-start(f32[2,104,256]{2,1,0:T(8,128)S(1)} %get-tuple-element.44), channel_id=1, source_target_pairs={{0,1},{2,3},{4,5},{6,7},{1,0},{3,2},{5,4},{7,6},{8,9},{10,11},{12,... | collective-permute-start | bytes 638984 | tf_op jit(solution)/shard_map/ppermute | solution.py:44
  64.8 10.4 %collective-permute-start.4 = (f32[1,104,256]{2,1,0:T(8,128)S(1)}, f32[1,104,256]{2,1,0:T(8,128)S(1)}, u32[]{:S(2)}, u32[]{:S(2)}) collective-permute-start(f32[1,104,256]{2,1,0:T(8,128)S(1)} %get-tuple-element.45), channel_id=1, source_target_pairs={{1,2},{3,4},{5,6},{2,1},{4,3},{6,5},{9,10},{11,12},{13,14},{10,9},... | collective-permute-start | bytes 319496 | tf_op jit(solution)/shard_map/ppermute | solution.py:44
  69.5 5.7 %collective-permute-start.5 = (f32[1,104,256]{2,1,0:T(8,128)S(1)}, f32[1,104,256]{2,1,0:T(8,128)S(1)}, u32[]{:S(2)}, u32[]{:S(2)}) collective-permute-start(f32[1,104,256]{2,1,0:T(8,128)S(1)} %get-tuple-element.46), channel_id=1, source_target_pairs={{0,1},{2,3},{4,5},{6,7},{1,0},{3,2},{5,4},{7,6},{8,9},{10,11},{12,... | collective-permute-start | bytes 319496 | tf_op jit(solution)/shard_map/ppermute | solution.py:44
  75.8 10.4 %collective-permute-start.6 = (f32[3,104,256]{2,1,0:T(8,128)S(1)}, f32[3,104,256]{2,1,0:T(8,128)S(1)}, u32[]{:S(2)}, u32[]{:S(2)}) collective-permute-start(f32[3,104,256]{2,1,0:T(8,128)S(1)} %get-tuple-element.48), channel_id=1, source_target_pairs={{8,16},{24,32},{40,48},{56,64},{72,80},{88,96},{104,112},{16,8},{3... | collective-permute-start | bytes 958472 | tf_op jit(solution)/shard_map/ppermute | solution.py:44
  78.0 8.3 %collective-permute-start.7 = (f32[3,104,256]{2,1,0:T(8,128)S(1)}, f32[3,104,256]{2,1,0:T(8,128)S(1)}, u32[]{:S(2)}, u32[]{:S(2)}) collective-permute-start(f32[3,104,256]{2,1,0:T(8,128)S(1)} %get-tuple-element.49), channel_id=1, source_target_pairs={{0,8},{16,24},{32,40},{48,56},{64,72},{80,88},{96,104},{112,120},{... | collective-permute-start | bytes 958472 | tf_op jit(solution)/shard_map/ppermute | solution.py:44

commit v9 on v8

--- a/solution.py
+++ b/solution.py
@@ -103,6 +103,7 @@
         in_specs=[VMEM],
         out_specs=(VMEM, VMEM),
         compiler_params=pltpu.CompilerParams(vmem_limit_bytes=8 << 20),
+        cost_estimate=pl.CostEstimate(flops=3000000000, bytes_accessed=1000000, transcendentals=0),
         name="field_edges",
     )(h)
 
@@ -329,7 +330,7 @@
         area_group(patch_ref, head_ref, rest_ref, back, out_ref, c, first)
         return 0
 
-    lax.fori_loop(0, out_ref.shape[0], chunk, 0, unroll=7)
+    lax.fori_loop(0, out_ref.shape[0], chunk, 0, unroll=5)
 
 
 def area_cost(groups):
@@ -525,14 +526,14 @@
     cols_left = shifted(last_cols, "gx", 1)
     odd = jnp.stack([lax.axis_index("gx") % 2, lax.axis_index("gy") % 2])
     odd = jnp.broadcast_to(odd[:, None], (2, 128))
-    area_a, packed, offsets = gather_area_and_pack(counts, skin_cell, patch_slot, area, 2)
+    area_a, packed, offsets = gather_area_and_pack(counts, skin_cell, patch_slot, area, 1)
     rows_below, cols_left, area_a = lax.optimization_barrier((rows_below, cols_left, area_a))
     e_next, j_next, dft_e_next, dft_h_next, rows = field_and_flux(
         offsets, packed, e_field, h_field, j_field, material, material_table, dft_e, dft_h,
         rows_below, cols_left,
     )
     arrived = lax.all_to_all(rows, ("gy", "gx"), split_axis=0, concat_axis=0, tiled=True)
-    area_b = gather_area(patch_slot, area, 2, 14)
+    area_b = gather_area(patch_slot, area, 1, 15)
 
     blocks, pieces = [], []
     for first, freqs in PIECES:

time: 89 us -> 85 us (0.955)
  local copies, waits for them, and re-layouts: 4.56 us -> 1.11 us
  waiting for transfers between devices: 13.8 us -> 12.8 us
    unnamed x28 -> x24, local copies, waits for them, and re-layouts: 4.5 us -> 1.04 us
    all_to_all x1, waiting for transfers between devices: 1.65 us -> 0.75 us  [shards(): lax.all_to_all(rows, ('gy', 'gx'), split_axis=0, concat_axis=0, tiled=True)]
  transfers between devices with their start and end apart: 9 -> 9, of which waited for: 3 -> 3; matrix products, arithmetic and copies ran while one was open for 1% -> 1% of each run, Pallas kernels for 20% -> 21%
where the time goes in v9:
time: 85 us; the launch traced here: 83.9 us
  Pallas kernels  38.8 us (46%)
  starting transfers between devices  29.3 us (34%)
  waiting for transfers between devices  12.8 us (15%)
  local copies, waits for them, and re-layouts  1.11 us (1%)
  other arithmetic  1.01 us (1%)
  between operations  0.95 us (1%)
    ppermute x6, starting transfers between devices, exchange(): swaps.append(lax.ppermute(value, axis, pairs))  12.7 us
    pallas_call x2, Pallas kernels, scatter_density(): pl.pallas_call(functools.partial(scatter_kernel, first=first), out_shape=...  12.5 us
    ppermute x6, waiting for transfers between devices, exchange(): swaps.append(lax.ppermute(value, axis, pairs))  12 us
    pallas_call x1, Pallas kernels, gather_area(): pl.pallas_call(functools.partial(area_kernel, first=first), out_shape=jax...  10.9 us
    pallas_call x1, Pallas kernels, field_and_flux(): pl.pallas_call(field_kernel, out_shape=tuple((jax.ShapeDtypeStruct(shape,...  10.7 us
    all_to_all x1, starting transfers between devices, shards(): lax.all_to_all(rows, ('gy', 'gx'), split_axis=0, concat_axis=0, tiled=True)  10.5 us
    ppermute x2, starting transfers between devices, shifted(): lax.ppermute(value, axis, [(source, source + steps) for source in range(l...  6.01 us
    pallas_call x1, Pallas kernels, gather_area_and_pack(): pl.pallas_call(functools.partial(first_area_kernel, groups=groups), out_s...  2.43 us
  transfers between devices with their start and end apart: 9, of which 3 were waited for; matrix products, arithmetic and copies ran while one was open for 1% of the time, Pallas kernels for 21%

profile of v9, /device:TPU:26, one launch (start us, length us, event | category | flops | bytes accessed | tf_op | source)
XLA Modules:
  0.0 83.9 jit_solution(11666519592784350452)
XLA Ops:
  0.6 1.0 %copy-done.3 = f32[3,4,64,128]{3,2,1,0:T(8,128)S(1)} copy-done((f32[3,4,64,128]{3,2,1,0:T(8,128)S(1)}, f32[3,4,64,128]{3,2,1,0:T(8,128)}, u32[]{:S(2)}) %copy-start.3) | copy-done | bytes 393240
  1.7 0.1 field_edges.1
  1.9 2.3 %collective-permute-start = (f32[2,4,128]{2,1,0:T(4,128)S(1)}, f32[2,4,128]{2,1,0:T(4,128)S(1)}, u32[]{:S(2)}, u32[]{:S(2)}) collective-permute-start(f32[2,4,128]{2,1,0:T(4,128)S(1)} %get-tuple-element.30), channel_id=1, source_target_pairs={{0,8},{8,16},{16,24},{24,32},{32,40},{40,48},{48,56},{56,64},{64,7... | collective-permute-start | bytes 12296 | tf_op jit(solution)/shard_map/ppermute | solution.py:35
  4.2 3.7 %collective-permute-start.1 = (f32[2,4,64]{2,1,0:T(4,128)S(1)}, f32[2,4,64]{2,1,0:T(4,128)S(1)}, u32[]{:S(2)}, u32[]{:S(2)}) collective-permute-start(f32[2,4,64]{2,1,0:T(4,128)S(1)} %get-tuple-element.31), channel_id=1, source_target_pairs={{0,1},{1,2},{2,3},{3,4},{4,5},{5,6},{6,7},{8,9},{9,10},{10,11},{11... | collective-permute-start | bytes 6152 | tf_op jit(solution)/shard_map/ppermute | solution.py:35
  7.9 2.4 %area_and_pack.1 = (f32[1,8,1024]{2,1,0:T(8,128)S(1)}, s32[136,128]{1,0:T(8,128)S(1)}, s32[1,136]{1,0:T(1,128)S(1)}) custom-call(s32[1,128]{1,0:T(1,128)S(1)} %copy-done.11, s32[1,128,128]{2,1,0:T(8,128)S(1)} %copy-done.9, s32[1,128,128]{2,1,0:T(8,128)S(1)} %copy-done.10, f32[3,256,256]{2,1,0:T(8,128)S(1)} %copy-done.8), custom_call_target="tpu_custom_call" | custom-call | flops 805306368 | bytes 2000000 | tf_op jit(solution)/shard_map/area_and_pack/pallas_call | solution.py:343
  10.5 10.7 %field_and_flux.1 = (f32[3,4,64,128]{3,2,1,0:T(8,128)}, f32[3,4,64,128]{3,2,1,0:T(8,128)}, f32[3,2,3,4,64,128]{5,4,3,2,1,0:T(8,128)}, f32[3,2,3,4,64,128]{5,4,3,2,1,0:T(8,128)}, f32[128,9,1,128]{3,2,1,0:T(1,128)}) custom-call(s32[1,136]{1,0:T(1,128)S(1)} %get-tuple-element.28.offset_ref, s32[136,128]{1,0:T(8,128)S(1)} %get-tuple-element.29.packed, ...), custom_call_target="tpu_custom_call" | custom-call | tf_op jit(solution)/shard_map/field_and_flux/pallas_call | solution.py:246
  21.2 10.5 %all-to-all-start = ((f32[128,9,1,128]{3,2,1,0:T(1,128)}), f32[128,9,1,128]{3,2,1,0:T(1,128)S(1)}, u32[]{:S(2)}, u32[]{:S(2)}) async-start(f32[128,9,1,128]{3,2,1,0:T(1,128)} %get-tuple-element.40), calls=%async_computation | async-start | bytes 1179648 | tf_op jit(solution)/shard_map/all_to_all | solution.py:535
  31.7 10.9 %gather_area.1.area_b_ref = f32[15,8,1024]{2,1,0:T(8,128)S(1)} custom-call(s32[1,128,128]{2,1,0:T(8,128)S(1)} %copy-done.10, f32[3,256,256]{2,1,0:T(8,128)S(1)} %copy-done.8), custom_call_target="tpu_custom_call" | custom-call | flops 12079595520 | bytes 2000000 | tf_op jit(solution)/shard_map/gather_area/pallas_call | solution.py:360
  42.6 0.1 pad_add_fusion
  42.7 0.7 all-to-all-done.flux_ref
  43.4 0.1 broadcast_in_dim.2.odd_ref
  43.5 7.9 %scatter_density.2 = (f32[2,256,256]{2,1,0:T(8,128)S(1)}, f32[2,104,256]{2,1,0:T(8,128)S(1)}, f32[2,104,256]{2,1,0:T(8,128)S(1)}) custom-call(s32[2,128]{1,0:T(2,128)S(1)} %broadcast_in_dim.2.odd_ref, s32[1,128,128]{2,1,0:T(8,128)S(1)} %copy-done.10, f32[1,8,1024]{2,1,0:T(8,128)S(1)} %get-tuple-element.39.area_a_ref, ...), custom_call_target="tpu_custom_call" | custom-call | flops 8589934592 | bytes 2000000 | tf_op jit(solution)/shard_map/scatter_density/pallas_call | solution.py:435
  51.4 4.7 %collective-permute-start.2 = (f32[2,104,256]{2,1,0:T(8,128)S(1)}, f32[2,104,256]{2,1,0:T(8,128)S(1)}, u32[]{:S(2)}, u32[]{:S(2)}) collective-permute-start(f32[2,104,256]{2,1,0:T(8,128)S(1)} %get-tuple-element.43), channel_id=1, source_target_pairs={{1,2},{3,4},{5,6},{2,1},{4,3},{6,5},{9,10},{11,12},{13,14},{10,9},... | collective-permute-start | bytes 638984 | tf_op jit(solution)/shard_map/ppermute | solution.py:44
  56.2 0.1 collective-permute-start.3
  56.2 4.6 %scatter_density.3 = (f32[1,256,256]{2,1,0:T(8,128)S(1)}, f32[1,104,256]{2,1,0:T(8,128)S(1)}, f32[1,104,256]{2,1,0:T(8,128)S(1)}) custom-call(s32[2,128]{1,0:T(2,128)S(1)} %broadcast_in_dim.2.odd_ref, s32[1,128,128]{2,1,0:T(8,128)S(1)} %copy-done.10, f32[1,8,1024]{2,1,0:T(8,128)S(1)} %get-tuple-element.39.area_a_ref, ...), custom_call_target="tpu_custom_call" | custom-call | flops 4294967296 | bytes 2000000 | tf_op jit(solution)/shard_map/scatter_density/pallas_call | solution.py:435
  60.9 4.7 %collective-permute-start.4 = (f32[1,104,256]{2,1,0:T(8,128)S(1)}, f32[1,104,256]{2,1,0:T(8,128)S(1)}, u32[]{:S(2)}, u32[]{:S(2)}) collective-permute-start(f32[1,104,256]{2,1,0:T(8,128)S(1)} %get-tuple-element.45), channel_id=1, source_target_pairs={{1,2},{3,4},{5,6},{2,1},{4,3},{6,5},{9,10},{11,12},{13,14},{10,9},... | collective-permute-start | bytes 319496 | tf_op jit(solution)/shard_map/ppermute | solution.py:44
  65.6 0.1 collective-permute-start.5
  65.7 5.6 %collective-permute-done.4.refs_4_ = f32[1,104,256]{2,1,0:T(8,128)S(1)} collective-permute-done((f32[1,104,256]{2,1,0:T(8,128)S(1)}, f32[1,104,256]{2,1,0:T(8,128)S(1)}, u32[]{:S(2)}, u32[]{:S(2)}) %collective-permute-start.4) | collective-permute-done | bytes 106528 | tf_op jit(solution)/shard_map/ppermute | solution.py:44
  71.3 0.6 column_sum.1
  72.0 3.0 %collective-permute-start.6 = (f32[3,104,256]{2,1,0:T(8,128)S(1)}, f32[3,104,256]{2,1,0:T(8,128)S(1)}, u32[]{:S(2)}, u32[]{:S(2)}) collective-permute-start(f32[3,104,256]{2,1,0:T(8,128)S(1)} %get-tuple-element.48), channel_id=1, source_target_pairs={{8,16},{24,32},{40,48},{56,64},{72,80},{88,96},{104,112},{16,8},{3... | collective-permute-start | bytes 958472 | tf_op jit(solution)/shard_map/ppermute | solution.py:44
  75.0 0.1 collective-permute-start.7
  75.1 0.9 %pad_maximum_fusion = f32[3,256,256]{2,1,0:T(8,128)} fusion(f32[1,256,256]{2,1,0:T(8,128)S(1)} %get-tuple-element.42.refs_3_, f32[2,256,256]{2,1,0:T(8,128)S(1)} %get-tuple-element.41.refs_0_), kind=kLoop, calls=%fused_computation | loop fusion | flops 196608 | bytes 1572864 | tf_op jit(solution)/shard_map/concatenate | solution.py:545
  76.0 6.4 %collective-permute-done.6.one_ref = f32[3,104,256]{2,1,0:T(8,128)S(1)} collective-permute-done((f32[3,104,256]{2,1,0:T(8,128)S(1)}, f32[3,104,256]{2,1,0:T(8,128)S(1)}, u32[]{:S(2)}, u32[]{:S(2)}) %collective-permute-start.6) | collective-permute-done | bytes 319520 | tf_op jit(solution)/shard_map/ppermute | solution.py:44
  82.4 1.5 %row_sum.1 = f32[3,256,256]{2,1,0:T(8,128)} custom-call(s32[2,128]{1,0:T(2,128)S(1)} %broadcast_in_dim.2.odd_ref, f32[3,256,256]{2,1,0:T(8,128)S(1)} %get-tuple-element.47.block_ref, f32[3,104,256]{2,1,0:T(8,128)S(1)} %collective-permute-done.6.one_ref, f32[3,104,256]{2,1,0:T(8,128)S(1)} %collective-permute-done.7.two_ref), custom_call_target="tpu_custom_call" | custom-call | tf_op jit(solution)/shard_map/row_sum/pallas_call | solution.py:510
  (29 shorter events, 0.1 us)
Async XLA Ops:
  0.6 1.0 %copy-start.3 = (f32[3,4,64,128]{3,2,1,0:T(8,128)S(1)}, f32[3,4,64,128]{3,2,1,0:T(8,128)}, u32[]{:S(2)}) copy-start(f32[3,4,64,128]{3,2,1,0:T(8,128)} %h_ref.3) | copy-start | bytes 1179652
  1.6 6.3 %copy-start.8 = (f32[3,256,256]{2,1,0:T(8,128)S(1)}, f32[3,256,256]{2,1,0:T(8,128)}, u32[]{:S(2)}) copy-start(f32[3,256,256]{2,1,0:T(8,128)} %area_ref.3) | copy-start | bytes 2359300
  1.6 6.3 %copy-start.9 = (s32[1,128,128]{2,1,0:T(8,128)S(1)}, s32[1,128,128]{2,1,0:T(8,128)}, u32[]{:S(2)}) copy-start(s32[1,128,128]{2,1,0:T(8,128)} %cell_ref.1) | copy-start | bytes 196612
  1.6 6.3 %copy-start.10 = (s32[1,128,128]{2,1,0:T(8,128)S(1)}, s32[1,128,128]{2,1,0:T(8,128)}, u32[]{:S(2)}) copy-start(s32[1,128,128]{2,1,0:T(8,128)} %patch_ref.7) | copy-start | bytes 196612
  1.6 6.3 %copy-start.11 = (s32[1,128]{1,0:T(1,128)S(1)}, s32[1,128]{1,0:T(1,128)}, u32[]{:S(2)}) copy-start(s32[1,128]{1,0:T(1,128)} %count_ref.1) | copy-start | bytes 1540
  1.6 8.7 %copy-start.1 = (f32[3,2,3,4,64,128]{5,4,3,2,1,0:T(8,128)S(1)}, f32[3,2,3,4,64,128]{5,4,3,2,1,0:T(8,128)}, u32[]{:S(2)}) copy-start(f32[3,2,3,4,64,128]{5,4,3,2,1,0:T(8,128)} %dft_h_ref.1) | copy-start | bytes 7077892
  1.7 8.7 %copy-start.4 = (f32[3,4,64,128]{3,2,1,0:T(8,128)S(1)}, f32[3,4,64,128]{3,2,1,0:T(8,128)}, u32[]{:S(2)}) copy-start(f32[3,4,64,128]{3,2,1,0:T(8,128)} %h_ref.3) | copy-start | bytes 1179652
  1.7 8.7 %copy-start.5 = (f32[3,4,64,128]{3,2,1,0:T(8,128)S(1)}, f32[3,4,64,128]{3,2,1,0:T(8,128)}, u32[]{:S(2)}) copy-start(f32[3,4,64,128]{3,2,1,0:T(8,128)} %j_ref.1) | copy-start | bytes 1179652
  1.8 8.6 %copy-start = (f32[3,2,3,4,64,128]{5,4,3,2,1,0:T(8,128)S(1)}, f32[3,2,3,4,64,128]{5,4,3,2,1,0:T(8,128)}, u32[]{:S(2)}) copy-start(f32[3,2,3,4,64,128]{5,4,3,2,1,0:T(8,128)} %dft_e_ref.1) | copy-start | bytes 7077892
  1.8 8.6 %copy-start.2 = (f32[3,4,64,128]{3,2,1,0:T(8,128)S(1)}, f32[3,4,64,128]{3,2,1,0:T(8,128)}, u32[]{:S(2)}) copy-start(f32[3,4,64,128]{3,2,1,0:T(8,128)} %e_ref.1) | copy-start | bytes 1179652
  1.8 8.6 %copy-start.6 = (s32[4,64,128]{2,1,0:T(8,128)S(1)}, s32[4,64,128]{2,1,0:T(8,128)}, u32[]{:S(2)}) copy-start(s32[4,64,128]{2,1,0:T(8,128)} %kind_ref.1) | copy-start | bytes 393220
  1.9 8.6 %copy-start.7 = (f32[4,32]{1,0:T(4,128)S(1)}, f32[4,32]{1,0:T(4,128)}, u32[]{:S(2)}) copy-start(f32[4,32]{1,0:T(4,128)} %table_ref.1) | copy-start | bytes 1540
  1.9 8.5 %collective-permute-start = (f32[2,4,128]{2,1,0:T(4,128)S(1)}, f32[2,4,128]{2,1,0:T(4,128)S(1)}, u32[]{:S(2)}, u32[]{:S(2)}) collective-permute-start(f32[2,4,128]{2,1,0:T(4,128)S(1)} %get-tuple-element.30), channel_id=1, source_target_pairs={{0,8},{8,16},{16,24},{24,32},{32,40},{40,48},{48,56},{56,64},{64,7... | collective-permute-start | bytes 12296 | tf_op jit(solution)/shard_map/ppermute | solution.py:35
  4.2 6.2 %collective-permute-start.1 = (f32[2,4,64]{2,1,0:T(4,128)S(1)}, f32[2,4,64]{2,1,0:T(4,128)S(1)}, u32[]{:S(2)}, u32[]{:S(2)}) collective-permute-start(f32[2,4,64]{2,1,0:T(4,128)S(1)} %get-tuple-element.31), channel_id=1, source_target_pairs={{0,1},{1,2},{2,3},{3,4},{4,5},{5,6},{6,7},{8,9},{9,10},{10,11},{11... | collective-permute-start | bytes 6152 | tf_op jit(solution)/shard_map/ppermute | solution.py:35
  21.2 22.3 %all-to-all-start = ((f32[128,9,1,128]{3,2,1,0:T(1,128)}), f32[128,9,1,128]{3,2,1,0:T(1,128)S(1)}, u32[]{:S(2)}, u32[]{:S(2)}) async-start(f32[128,9,1,128]{3,2,1,0:T(1,128)} %get-tuple-element.40), calls=%async_computation | async-start | bytes 1179648 | tf_op jit(solution)/shard_map/all_to_all | solution.py:535
  51.4 19.9 %collective-permute-start.2 = (f32[2,104,256]{2,1,0:T(8,128)S(1)}, f32[2,104,256]{2,1,0:T(8,128)S(1)}, u32[]{:S(2)}, u32[]{:S(2)}) collective-permute-start(f32[2,104,256]{2,1,0:T(8,128)S(1)} %get-tuple-element.43), channel_id=1, source_target_pairs={{1,2},{3,4},{5,6},{2,1},{4,3},{6,5},{9,10},{11,12},{13,14},{10,9},... | collective-permute-start | bytes 638984 | tf_op jit(solution)/shard_map/ppermute | solution.py:44
  56.2 15.2 %collective-permute-start.3 = (f32[2,104,256]{2,1,0:T(8,128)S(1)}, f32[2,104,256]{2,1,0:T(8,128)S(1)}, u32[]{:S(2)}, u32[]{:S(2)}) collective-permute-start(f32[2,104,256]{2,1,0:T(8,128)S(1)} %get-tuple-element.44), channel_id=1, source_target_pairs={{0,1},{2,3},{4,5},{6,7},{1,0},{3,2},{5,4},{7,6},{8,9},{10,11},{12,... | collective-permute-start | bytes 638984 | tf_op jit(solution)/shard_map/ppermute | solution.py:44
  60.9 10.4 %collective-permute-start.4 = (f32[1,104,256]{2,1,0:T(8,128)S(1)}, f32[1,104,256]{2,1,0:T(8,128)S(1)}, u32[]{:S(2)}, u32[]{:S(2)}) collective-permute-start(f32[1,104,256]{2,1,0:T(8,128)S(1)} %get-tuple-element.45), channel_id=1, source_target_pairs={{1,2},{3,4},{5,6},{2,1},{4,3},{6,5},{9,10},{11,12},{13,14},{10,9},... | collective-permute-start | bytes 319496 | tf_op jit(solution)/shard_map/ppermute | solution.py:44
  65.6 5.7 %collective-permute-start.5 = (f32[1,104,256]{2,1,0:T(8,128)S(1)}, f32[1,104,256]{2,1,0:T(8,128)S(1)}, u32[]{:S(2)}, u32[]{:S(2)}) collective-permute-start(f32[1,104,256]{2,1,0:T(8,128)S(1)} %get-tuple-element.46), channel_id=1, source_target_pairs={{0,1},{2,3},{4,5},{6,7},{1,0},{3,2},{5,4},{7,6},{8,9},{10,11},{12,... | collective-permute-start | bytes 319496 | tf_op jit(solution)/shard_map/ppermute | solution.py:44
  72.0 10.4 %collective-permute-start.6 = (f32[3,104,256]{2,1,0:T(8,128)S(1)}, f32[3,104,256]{2,1,0:T(8,128)S(1)}, u32[]{:S(2)}, u32[]{:S(2)}) collective-permute-start(f32[3,104,256]{2,1,0:T(8,128)S(1)} %get-tuple-element.48), channel_id=1, source_target_pairs={{8,16},{24,32},{40,48},{56,64},{72,80},{88,96},{104,112},{16,8},{3... | collective-permute-start | bytes 958472 | tf_op jit(solution)/shard_map/ppermute | solution.py:44
  75.0 7.4 %collective-permute-start.7 = (f32[3,104,256]{2,1,0:T(8,128)S(1)}, f32[3,104,256]{2,1,0:T(8,128)S(1)}, u32[]{:S(2)}, u32[]{:S(2)}) collective-permute-start(f32[3,104,256]{2,1,0:T(8,128)S(1)} %get-tuple-element.49), channel_id=1, source_target_pairs={{0,8},{16,24},{32,40},{48,56},{64,72},{80,88},{96,104},{112,120},{... | collective-permute-start | bytes 958472 | tf_op jit(solution)/shard_map/ppermute | solution.py:44

commit v10 on v9

--- a/solution.py
+++ b/solution.py
@@ -455,8 +455,7 @@
     return head, (cells - head.astype(f32)).astype(bf16)
 
 
-def column_kernel(odd_ref, *refs):
-    refs, (out_ref, first_ref, second_ref) = refs[:-3], refs[-3:]
+def column_kernel(odd_ref, block_ref, one_ref, two_ref, out_ref, first_ref, second_ref):
     inner = in_window(iota((256, 256), 0) - iota((256, 256), 1))
     place, column = iota((EDGE, 256), 0), iota((EDGE, 256), 1)
     outer = jnp.concatenate(
@@ -464,57 +463,58 @@
     )
     inner = jnp.concatenate([inner, inner], 0)
     outer = jnp.concatenate([outer, outer], 0)
+    for f in range(block_ref.shape[0]):
+        total = jnp.dot(
+            jnp.concatenate(two_parts(block_ref[f]), 1), inner, preferred_element_type=f32
+        )
+        edges = jnp.concatenate(got_edges(is_odd(odd_ref, 0), one_ref, two_ref, f), 0)
+        total = total + lax.dot_general(
+            jnp.concatenate(two_parts(edges), 0),
+            outer,
+            (((0,), (0,)), ((), ())),
+            preferred_element_type=f32,
+        )
+        out_ref[f] = total
+        put_edges(is_odd(odd_ref, 1), total[:EDGE], total[256 - EDGE :], first_ref, second_ref, f)
+
+
+def column_sum(odd, block, first, second):
+    return pl.pallas_call(
+        column_kernel,
+        out_shape=block_and_edges(block.shape[0]),
+        in_specs=[VMEM] * 4,
+        out_specs=(VMEM,) * 3,
+        compiler_params=pltpu.CompilerParams(vmem_limit_bytes=16 << 20),
+        name="column_sum",
+    )(odd, block, first, second)
+
+
+def row_kernel(odd_ref, *refs):
+    refs, out_ref = refs[:-1], refs[-1]
+    length = 256 + 2 * EDGE
+    band = in_window(iota((256, length), 1) - EDGE - iota((256, length), 0))
+    band = jnp.concatenate([band, band], 1)
     done = 0
     for block_ref, one_ref, two_ref in zip(refs[0::3], refs[1::3], refs[2::3]):
         for f in range(block_ref.shape[0]):
+            before, after = got_edges(is_odd(odd_ref, 1), one_ref, two_ref, f)
+            cells = jnp.concatenate([before, block_ref[f], after], 0)
             total = jnp.dot(
-                jnp.concatenate(two_parts(block_ref[f]), 1), inner, preferred_element_type=f32
+                band, jnp.concatenate(two_parts(cells), 0), preferred_element_type=f32
             )
-            edges = jnp.concatenate(got_edges(is_odd(odd_ref, 0), one_ref, two_ref, f), 0)
-            total = total + lax.dot_general(
-                jnp.concatenate(two_parts(edges), 0),
-                outer,
-                (((0,), (0,)), ((), ())),
-                preferred_element_type=f32,
-            )
-            out_ref[done] = total
-            put_edges(
-                is_odd(odd_ref, 1), total[:EDGE], total[256 - EDGE :], first_ref, second_ref, done
-            )
+            out_ref[done] = total * (1.0 / (4.0 * HALF * HALF))
             done += 1
 
 
-def column_sum(odd, *pieces):
-    return pl.pallas_call(
-        column_kernel,
-        out_shape=block_and_edges(3),
-        in_specs=[VMEM] * (1 + len(pieces)),
-        out_specs=(VMEM,) * 3,
-        compiler_params=pltpu.CompilerParams(vmem_limit_bytes=16 << 20),
-        name="column_sum",
-    )(odd, *pieces)
-
-
-def row_kernel(odd_ref, block_ref, one_ref, two_ref, out_ref):
-    length = 256 + 2 * EDGE
-    band = in_window(iota((256, length), 1) - EDGE - iota((256, length), 0))
-    band = jnp.concatenate([band, band], 1)
-    for f in range(3):
-        before, after = got_edges(is_odd(odd_ref, 1), one_ref, two_ref, f)
-        cells = jnp.concatenate([before, block_ref[f], after], 0)
-        total = jnp.dot(band, jnp.concatenate(two_parts(cells), 0), preferred_element_type=f32)
-        out_ref[f] = total * (1.0 / (4.0 * HALF * HALF))
-
-
-def row_sum(odd, block, first, second):
+def row_sum(odd, *pieces):
     return pl.pallas_call(
         row_kernel,
         out_shape=jax.ShapeDtypeStruct((3, 256, 256), f32),
-        in_specs=[VMEM] * 4,
+        in_specs=[VMEM] * (1 + len(pieces)),
         out_specs=VMEM,
         compiler_params=pltpu.CompilerParams(vmem_limit_bytes=16 << 20),
         name="row_sum",
-    )(odd, block, first, second)
+    )(odd, *pieces)
 
 
 def shards(
@@ -535,15 +535,16 @@
     arrived = lax.all_to_all(rows, ("gy", "gx"), split_axis=0, concat_axis=0, tiled=True)
     area_b = gather_area(patch_slot, area, 1, 15)
 
-    blocks, pieces = [], []
+    blocks, swaps, pieces = [], [], []
     for first, freqs in PIECES:
         block, *edges = scatter_density(odd, patch_slot, area_a, area_b, arrived, first, freqs)
         blocks.append(block)
-        pieces += [block, *exchange(*edges, "gx")]
-    strip, *edges = column_sum(odd, *pieces)
-    edges = exchange(*edges, "gy")
+        swaps.append(exchange(*edges, "gx"))
+    for block, swap in zip(blocks, swaps):
+        strip, *edges = column_sum(odd, block, *swap)
+        pieces += [strip, *exchange(*edges, "gy")]
     point_density = jnp.concatenate(blocks, 0)
-    avg_density = row_sum(odd, strip, *edges)
+    avg_density = row_sum(odd, *pieces)
     return (e_next, j_next, dft_e_next, dft_h_next, point_density, avg_density)
 
 

time: 85 us -> 82.4 us (0.969)
  waiting for transfers between devices: 12.8 us -> 6.02 us
  starting transfers between devices: 29.3 us -> 33.2 us
    ppermute x6 -> x8, waiting for transfers between devices: 12 us -> 5.27 us  [exchange(): swaps.append(lax.ppermute(value, axis, pairs))]
    ppermute x6 -> x8, starting transfers between devices: 12.7 us -> 16.6 us  [exchange(): swaps.append(lax.ppermute(value, axis, pairs))]
  transfers between devices with their start and end apart: 9 -> 11, of which waited for: 3 -> 3; matrix products, arithmetic and copies ran while one was open for 1% -> 1% of each run, Pallas kernels for 21% -> 23%
where the time goes in v10:
time: 82.4 us; the launch traced here: 81.3 us
  Pallas kernels  39 us (47%)
  starting transfers between devices  33.2 us (40%)
  waiting for transfers between devices  6.02 us (7%)
  local copies, waits for them, and re-layouts  1.11 us (1%)
  other arithmetic  1.01 us (1%)
  between operations  0.99 us (1%)
    ppermute x8, starting transfers between devices, exchange(): swaps.append(lax.ppermute(value, axis, pairs))  16.6 us
    pallas_call x2, Pallas kernels, scatter_density(): pl.pallas_call(functools.partial(scatter_kernel, first=first), out_shape=...  12.5 us
    pallas_call x1, Pallas kernels, gather_area(): pl.pallas_call(functools.partial(area_kernel, first=first), out_shape=jax...  10.9 us
    pallas_call x1, Pallas kernels, field_and_flux(): pl.pallas_call(field_kernel, out_shape=tuple((jax.ShapeDtypeStruct(shape,...  10.7 us
    all_to_all x1, starting transfers between devices, shards(): lax.all_to_all(rows, ('gy', 'gx'), split_axis=0, concat_axis=0, tiled=True)  10.5 us
    ppermute x2, starting transfers between devices, shifted(): lax.ppermute(value, axis, [(source, source + steps) for source in range(l...  6.01 us
    ppermute x8, waiting for transfers between devices, exchange(): swaps.append(lax.ppermute(value, axis, pairs))  5.27 us
    pallas_call x1, Pallas kernels, gather_area_and_pack(): pl.pallas_call(functools.partial(first_area_kernel, groups=groups), out_s...  2.43 us
  transfers between devices with their start and end apart: 11, of which 3 were waited for; matrix products, arithmetic and copies ran while one was open for 1% of the time, Pallas kernels for 23%

profile of v10, /device:TPU:26, one launch (start us, length us, event | category | flops | bytes accessed | tf_op | source)
XLA Modules:
  0.0 81.3 jit_solution(12432222783208382344)
XLA Ops:
  0.6 1.0 %copy-done.3 = f32[3,4,64,128]{3,2,1,0:T(8,128)S(1)} copy-done((f32[3,4,64,128]{3,2,1,0:T(8,128)S(1)}, f32[3,4,64,128]{3,2,1,0:T(8,128)}, u32[]{:S(2)}) %copy-start.3) | copy-done | bytes 393240
  1.7 0.1 field_edges.1
  1.9 2.3 %collective-permute-start = (f32[2,4,128]{2,1,0:T(4,128)S(1)}, f32[2,4,128]{2,1,0:T(4,128)S(1)}, u32[]{:S(2)}, u32[]{:S(2)}) collective-permute-start(f32[2,4,128]{2,1,0:T(4,128)S(1)} %get-tuple-element.33), channel_id=1, source_target_pairs={{0,8},{8,16},{16,24},{24,32},{32,40},{40,48},{48,56},{56,64},{64,7... | collective-permute-start | bytes 12296 | tf_op jit(solution)/shard_map/ppermute | solution.py:35
  4.2 3.7 %collective-permute-start.1 = (f32[2,4,64]{2,1,0:T(4,128)S(1)}, f32[2,4,64]{2,1,0:T(4,128)S(1)}, u32[]{:S(2)}, u32[]{:S(2)}) collective-permute-start(f32[2,4,64]{2,1,0:T(4,128)S(1)} %get-tuple-element.34), channel_id=1, source_target_pairs={{0,1},{1,2},{2,3},{3,4},{4,5},{5,6},{6,7},{8,9},{9,10},{10,11},{11... | collective-permute-start | bytes 6152 | tf_op jit(solution)/shard_map/ppermute | solution.py:35
  7.9 2.4 %area_and_pack.1 = (f32[1,8,1024]{2,1,0:T(8,128)S(1)}, s32[136,128]{1,0:T(8,128)S(1)}, s32[1,136]{1,0:T(1,128)S(1)}) custom-call(s32[1,128]{1,0:T(1,128)S(1)} %copy-done.11, s32[1,128,128]{2,1,0:T(8,128)S(1)} %copy-done.9, s32[1,128,128]{2,1,0:T(8,128)S(1)} %copy-done.10, f32[3,256,256]{2,1,0:T(8,128)S(1)} %copy-done.8), custom_call_target="tpu_custom_call" | custom-call | flops 805306368 | bytes 2000000 | tf_op jit(solution)/shard_map/area_and_pack/pallas_call | solution.py:343
  10.5 10.7 %field_and_flux.1 = (f32[3,4,64,128]{3,2,1,0:T(8,128)}, f32[3,4,64,128]{3,2,1,0:T(8,128)}, f32[3,2,3,4,64,128]{5,4,3,2,1,0:T(8,128)}, f32[3,2,3,4,64,128]{5,4,3,2,1,0:T(8,128)}, f32[128,9,1,128]{3,2,1,0:T(1,128)}) custom-call(s32[1,136]{1,0:T(1,128)S(1)} %get-tuple-element.31.offset_ref, s32[136,128]{1,0:T(8,128)S(1)} %get-tuple-element.32.packed, ...), custom_call_target="tpu_custom_call" | custom-call | tf_op jit(solution)/shard_map/field_and_flux/pallas_call | solution.py:246
  21.2 10.5 %all-to-all-start = ((f32[128,9,1,128]{3,2,1,0:T(1,128)}), f32[128,9,1,128]{3,2,1,0:T(1,128)S(1)}, u32[]{:S(2)}, u32[]{:S(2)}) async-start(f32[128,9,1,128]{3,2,1,0:T(1,128)} %get-tuple-element.43), calls=%async_computation | async-start | bytes 1179648 | tf_op jit(solution)/shard_map/all_to_all | solution.py:535
  31.7 10.9 %gather_area.1.area_b_ref = f32[15,8,1024]{2,1,0:T(8,128)S(1)} custom-call(s32[1,128,128]{2,1,0:T(8,128)S(1)} %copy-done.10, f32[3,256,256]{2,1,0:T(8,128)S(1)} %copy-done.8), custom_call_target="tpu_custom_call" | custom-call | flops 12079595520 | bytes 2000000 | tf_op jit(solution)/shard_map/gather_area/pallas_call | solution.py:360
  42.7 0.7 all-to-all-done.flux_ref
  43.5 7.9 %scatter_density.2 = (f32[2,256,256]{2,1,0:T(8,128)S(1)}, f32[2,104,256]{2,1,0:T(8,128)S(1)}, f32[2,104,256]{2,1,0:T(8,128)S(1)}) custom-call(s32[2,128]{1,0:T(2,128)S(1)} %broadcast_in_dim.2.odd_ref, s32[1,128,128]{2,1,0:T(8,128)S(1)} %copy-done.10, f32[1,8,1024]{2,1,0:T(8,128)S(1)} %get-tuple-element.42.area_a_ref, ...), custom_call_target="tpu_custom_call" | custom-call | flops 8589934592 | bytes 2000000 | tf_op jit(solution)/shard_map/scatter_density/pallas_call | solution.py:435
  51.4 4.7 %collective-permute-start.2 = (f32[2,104,256]{2,1,0:T(8,128)S(1)}, f32[2,104,256]{2,1,0:T(8,128)S(1)}, u32[]{:S(2)}, u32[]{:S(2)}) collective-permute-start(f32[2,104,256]{2,1,0:T(8,128)S(1)} %get-tuple-element.46), channel_id=1, source_target_pairs={{1,2},{3,4},{5,6},{2,1},{4,3},{6,5},{9,10},{11,12},{13,14},{10,9},... | collective-permute-start | bytes 638984 | tf_op jit(solution)/shard_map/ppermute | solution.py:44
  56.2 0.1 collective-permute-start.3
  56.2 4.6 %scatter_density.3 = (f32[1,256,256]{2,1,0:T(8,128)S(1)}, f32[1,104,256]{2,1,0:T(8,128)S(1)}, f32[1,104,256]{2,1,0:T(8,128)S(1)}) custom-call(s32[2,128]{1,0:T(2,128)S(1)} %broadcast_in_dim.2.odd_ref, s32[1,128,128]{2,1,0:T(8,128)S(1)} %copy-done.10, f32[1,8,1024]{2,1,0:T(8,128)S(1)} %get-tuple-element.42.area_a_ref, ...), custom_call_target="tpu_custom_call" | custom-call | flops 4294967296 | bytes 2000000 | tf_op jit(solution)/shard_map/scatter_density/pallas_call | solution.py:435
  60.9 4.7 %collective-permute-start.6 = (f32[1,104,256]{2,1,0:T(8,128)S(1)}, f32[1,104,256]{2,1,0:T(8,128)S(1)}, u32[]{:S(2)}, u32[]{:S(2)}) collective-permute-start(f32[1,104,256]{2,1,0:T(8,128)S(1)} %get-tuple-element.51), channel_id=1, source_target_pairs={{1,2},{3,4},{5,6},{2,1},{4,3},{6,5},{9,10},{11,12},{13,14},{10,9},... | collective-permute-start | bytes 319496 | tf_op jit(solution)/shard_map/ppermute | solution.py:44
  65.6 0.1 collective-permute-start.7
  65.7 0.5 column_sum.2
  66.2 3.8 %collective-permute-start.4 = (f32[2,104,256]{2,1,0:T(8,128)S(1)}, f32[2,104,256]{2,1,0:T(8,128)S(1)}, u32[]{:S(2)}, u32[]{:S(2)}) collective-permute-start(f32[2,104,256]{2,1,0:T(8,128)S(1)} %get-tuple-element.49), channel_id=1, source_target_pairs={{8,16},{24,32},{40,48},{56,64},{72,80},{88,96},{104,112},{16,8},{3... | collective-permute-start | bytes 638984 | tf_op jit(solution)/shard_map/ppermute | solution.py:44
  70.1 0.1 collective-permute-start.5
  70.2 1.2 %collective-permute-done.6.one_ref = f32[1,104,256]{2,1,0:T(8,128)S(1)} collective-permute-done((f32[1,104,256]{2,1,0:T(8,128)S(1)}, f32[1,104,256]{2,1,0:T(8,128)S(1)}, u32[]{:S(2)}, u32[]{:S(2)}) %collective-permute-start.6) | collective-permute-done | bytes 106528 | tf_op jit(solution)/shard_map/ppermute | solution.py:44
  71.3 0.3 column_sum.3
  71.7 3.0 %collective-permute-start.8 = (f32[1,104,256]{2,1,0:T(8,128)S(1)}, f32[1,104,256]{2,1,0:T(8,128)S(1)}, u32[]{:S(2)}, u32[]{:S(2)}) collective-permute-start(f32[1,104,256]{2,1,0:T(8,128)S(1)} %get-tuple-element.54), channel_id=1, source_target_pairs={{8,16},{24,32},{40,48},{56,64},{72,80},{88,96},{104,112},{16,8},{3... | collective-permute-start | bytes 319496 | tf_op jit(solution)/shard_map/ppermute | solution.py:44
  74.8 0.9 %pad_maximum_fusion = f32[3,256,256]{2,1,0:T(8,128)} fusion(f32[1,256,256]{2,1,0:T(8,128)S(1)} %get-tuple-element.45.block_ref, f32[2,256,256]{2,1,0:T(8,128)S(1)} %get-tuple-element.44.block_ref), kind=kLoop, calls=%fused_computation | loop fusion | flops 196608 | bytes 1572864 | tf_op jit(solution)/shard_map/concatenate | solution.py:546
  75.7 4.1 %collective-permute-done.8.refs_4_ = f32[1,104,256]{2,1,0:T(8,128)S(1)} collective-permute-done((f32[1,104,256]{2,1,0:T(8,128)S(1)}, f32[1,104,256]{2,1,0:T(8,128)S(1)}, u32[]{:S(2)}, u32[]{:S(2)}) %collective-permute-start.8) | collective-permute-done | bytes 106528 | tf_op jit(solution)/shard_map/ppermute | solution.py:44
  79.8 1.5 %row_sum.1 = f32[3,256,256]{2,1,0:T(8,128)} custom-call(s32[2,128]{1,0:T(2,128)S(1)} %broadcast_in_dim.2.odd_ref, f32[2,256,256]{2,1,0:T(8,128)S(1)} %get-tuple-element.48.refs_0_, f32[2,104,256]{2,1,0:T(8,128)S(1)} %collective-permute-done.4.refs_1_, f32[2,104,256]{2,1,0:T(8,128)S(1)} %collective-permute-done.5.refs_2_, ...), custom_call_target="tpu_custom_call" | custom-call | tf_op jit(solution)/shard_map/row_sum/pallas_call | solution.py:510
  (34 shorter events, 0.3 us)
Async XLA Ops:
  0.6 1.0 %copy-start.3 = (f32[3,4,64,128]{3,2,1,0:T(8,128)S(1)}, f32[3,4,64,128]{3,2,1,0:T(8,128)}, u32[]{:S(2)}) copy-start(f32[3,4,64,128]{3,2,1,0:T(8,128)} %h_ref.3) | copy-start | bytes 1179652
  1.6 6.3 %copy-start.8 = (f32[3,256,256]{2,1,0:T(8,128)S(1)}, f32[3,256,256]{2,1,0:T(8,128)}, u32[]{:S(2)}) copy-start(f32[3,256,256]{2,1,0:T(8,128)} %area_ref.3) | copy-start | bytes 2359300
  1.6 6.3 %copy-start.9 = (s32[1,128,128]{2,1,0:T(8,128)S(1)}, s32[1,128,128]{2,1,0:T(8,128)}, u32[]{:S(2)}) copy-start(s32[1,128,128]{2,1,0:T(8,128)} %cell_ref.1) | copy-start | bytes 196612
  1.6 6.3 %copy-start.10 = (s32[1,128,128]{2,1,0:T(8,128)S(1)}, s32[1,128,128]{2,1,0:T(8,128)}, u32[]{:S(2)}) copy-start(s32[1,128,128]{2,1,0:T(8,128)} %patch_ref.7) | copy-start | bytes 196612
  1.6 6.3 %copy-start.11 = (s32[1,128]{1,0:T(1,128)S(1)}, s32[1,128]{1,0:T(1,128)}, u32[]{:S(2)}) copy-start(s32[1,128]{1,0:T(1,128)} %count_ref.1) | copy-start | bytes 1540
  1.6 8.7 %copy-start.1 = (f32[3,2,3,4,64,128]{5,4,3,2,1,0:T(8,128)S(1)}, f32[3,2,3,4,64,128]{5,4,3,2,1,0:T(8,128)}, u32[]{:S(2)}) copy-start(f32[3,2,3,4,64,128]{5,4,3,2,1,0:T(8,128)} %dft_h_ref.1) | copy-start | bytes 7077892
  1.7 8.7 %copy-start.4 = (f32[3,4,64,128]{3,2,1,0:T(8,128)S(1)}, f32[3,4,64,128]{3,2,1,0:T(8,128)}, u32[]{:S(2)}) copy-start(f32[3,4,64,128]{3,2,1,0:T(8,128)} %h_ref.3) | copy-start | bytes 1179652
  1.7 8.7 %copy-start.5 = (f32[3,4,64,128]{3,2,1,0:T(8,128)S(1)}, f32[3,4,64,128]{3,2,1,0:T(8,128)}, u32[]{:S(2)}) copy-start(f32[3,4,64,128]{3,2,1,0:T(8,128)} %j_ref.1) | copy-start | bytes 1179652
  1.8 8.6 %copy-start = (f32[3,2,3,4,64,128]{5,4,3,2,1,0:T(8,128)S(1)}, f32[3,2,3,4,64,128]{5,4,3,2,1,0:T(8,128)}, u32[]{:S(2)}) copy-start(f32[3,2,3,4,64,128]{5,4,3,2,1,0:T(8,128)} %dft_e_ref.1) | copy-start | bytes 7077892
  1.8 8.6 %copy-start.2 = (f32[3,4,64,128]{3,2,1,0:T(8,128)S(1)}, f32[3,4,64,128]{3,2,1,0:T(8,128)}, u32[]{:S(2)}) copy-start(f32[3,4,64,128]{3,2,1,0:T(8,128)} %e_ref.1) | copy-start | bytes 1179652
  1.8 8.6 %copy-start.6 = (s32[4,64,128]{2,1,0:T(8,128)S(1)}, s32[4,64,128]{2,1,0:T(8,128)}, u32[]{:S(2)}) copy-start(s32[4,64,128]{2,1,0:T(8,128)} %kind_ref.1) | copy-start | bytes 393220
  1.9 8.6 %copy-start.7 = (f32[4,32]{1,0:T(4,128)S(1)}, f32[4,32]{1,0:T(4,128)}, u32[]{:S(2)}) copy-start(f32[4,32]{1,0:T(4,128)} %table_ref.1) | copy-start | bytes 1540
  1.9 8.5 %collective-permute-start = (f32[2,4,128]{2,1,0:T(4,128)S(1)}, f32[2,4,128]{2,1,0:T(4,128)S(1)}, u32[]{:S(2)}, u32[]{:S(2)}) collective-permute-start(f32[2,4,128]{2,1,0:T(4,128)S(1)} %get-tuple-element.33), channel_id=1, source_target_pairs={{0,8},{8,16},{16,24},{24,32},{32,40},{40,48},{48,56},{56,64},{64,7... | collective-permute-start | bytes 12296 | tf_op jit(solution)/shard_map/ppermute | solution.py:35
  4.2 6.2 %collective-permute-start.1 = (f32[2,4,64]{2,1,0:T(4,128)S(1)}, f32[2,4,64]{2,1,0:T(4,128)S(1)}, u32[]{:S(2)}, u32[]{:S(2)}) collective-permute-start(f32[2,4,64]{2,1,0:T(4,128)S(1)} %get-tuple-element.34), channel_id=1, source_target_pairs={{0,1},{1,2},{2,3},{3,4},{4,5},{5,6},{6,7},{8,9},{9,10},{10,11},{11... | collective-permute-start | bytes 6152 | tf_op jit(solution)/shard_map/ppermute | solution.py:35
  21.2 22.3 %all-to-all-start = ((f32[128,9,1,128]{3,2,1,0:T(1,128)}), f32[128,9,1,128]{3,2,1,0:T(1,128)S(1)}, u32[]{:S(2)}, u32[]{:S(2)}) async-start(f32[128,9,1,128]{3,2,1,0:T(1,128)} %get-tuple-element.43), calls=%async_computation | async-start | bytes 1179648 | tf_op jit(solution)/shard_map/all_to_all | solution.py:535
  51.4 14.3 %collective-permute-start.2 = (f32[2,104,256]{2,1,0:T(8,128)S(1)}, f32[2,104,256]{2,1,0:T(8,128)S(1)}, u32[]{:S(2)}, u32[]{:S(2)}) collective-permute-start(f32[2,104,256]{2,1,0:T(8,128)S(1)} %get-tuple-element.46), channel_id=1, source_target_pairs={{1,2},{3,4},{5,6},{2,1},{4,3},{6,5},{9,10},{11,12},{13,14},{10,9},... | collective-permute-start | bytes 638984 | tf_op jit(solution)/shard_map/ppermute | solution.py:44
  56.2 9.5 %collective-permute-start.3 = (f32[2,104,256]{2,1,0:T(8,128)S(1)}, f32[2,104,256]{2,1,0:T(8,128)S(1)}, u32[]{:S(2)}, u32[]{:S(2)}) collective-permute-start(f32[2,104,256]{2,1,0:T(8,128)S(1)} %get-tuple-element.47), channel_id=1, source_target_pairs={{0,1},{2,3},{4,5},{6,7},{1,0},{3,2},{5,4},{7,6},{8,9},{10,11},{12,... | collective-permute-start | bytes 638984 | tf_op jit(solution)/shard_map/ppermute | solution.py:44
  60.9 10.4 %collective-permute-start.6 = (f32[1,104,256]{2,1,0:T(8,128)S(1)}, f32[1,104,256]{2,1,0:T(8,128)S(1)}, u32[]{:S(2)}, u32[]{:S(2)}) collective-permute-start(f32[1,104,256]{2,1,0:T(8,128)S(1)} %get-tuple-element.51), channel_id=1, source_target_pairs={{1,2},{3,4},{5,6},{2,1},{4,3},{6,5},{9,10},{11,12},{13,14},{10,9},... | collective-permute-start | bytes 319496 | tf_op jit(solution)/shard_map/ppermute | solution.py:44
  65.6 5.7 %collective-permute-start.7 = (f32[1,104,256]{2,1,0:T(8,128)S(1)}, f32[1,104,256]{2,1,0:T(8,128)S(1)}, u32[]{:S(2)}, u32[]{:S(2)}) collective-permute-start(f32[1,104,256]{2,1,0:T(8,128)S(1)} %get-tuple-element.52), channel_id=1, source_target_pairs={{0,1},{2,3},{4,5},{6,7},{1,0},{3,2},{5,4},{7,6},{8,9},{10,11},{12,... | collective-permute-start | bytes 319496 | tf_op jit(solution)/shard_map/ppermute | solution.py:44
  66.2 13.6 %collective-permute-start.4 = (f32[2,104,256]{2,1,0:T(8,128)S(1)}, f32[2,104,256]{2,1,0:T(8,128)S(1)}, u32[]{:S(2)}, u32[]{:S(2)}) collective-permute-start(f32[2,104,256]{2,1,0:T(8,128)S(1)} %get-tuple-element.49), channel_id=1, source_target_pairs={{8,16},{24,32},{40,48},{56,64},{72,80},{88,96},{104,112},{16,8},{3... | collective-permute-start | bytes 638984 | tf_op jit(solution)/shard_map/ppermute | solution.py:44
  70.1 9.7 %collective-permute-start.5 = (f32[2,104,256]{2,1,0:T(8,128)S(1)}, f32[2,104,256]{2,1,0:T(8,128)S(1)}, u32[]{:S(2)}, u32[]{:S(2)}) collective-permute-start(f32[2,104,256]{2,1,0:T(8,128)S(1)} %get-tuple-element.50), channel_id=1, source_target_pairs={{0,8},{16,24},{32,40},{48,56},{64,72},{80,88},{96,104},{112,120},{... | collective-permute-start | bytes 638984 | tf_op jit(solution)/shard_map/ppermute | solution.py:44
  71.7 8.1 %collective-permute-start.8 = (f32[1,104,256]{2,1,0:T(8,128)S(1)}, f32[1,104,256]{2,1,0:T(8,128)S(1)}, u32[]{:S(2)}, u32[]{:S(2)}) collective-permute-start(f32[1,104,256]{2,1,0:T(8,128)S(1)} %get-tuple-element.54), channel_id=1, source_target_pairs={{8,16},{24,32},{40,48},{56,64},{72,80},{88,96},{104,112},{16,8},{3... | collective-permute-start | bytes 319496 | tf_op jit(solution)/shard_map/ppermute | solution.py:44
  74.7 5.1 %collective-permute-start.9 = (f32[1,104,256]{2,1,0:T(8,128)S(1)}, f32[1,104,256]{2,1,0:T(8,128)S(1)}, u32[]{:S(2)}, u32[]{:S(2)}) collective-permute-start(f32[1,104,256]{2,1,0:T(8,128)S(1)} %get-tuple-element.55), channel_id=1, source_target_pairs={{0,8},{16,24},{32,40},{48,56},{64,72},{80,88},{96,104},{112,120},{... | collective-permute-start | bytes 319496 | tf_op jit(solution)/shard_map/ppermute | solution.py:44

commit v11 on v10

--- a/solution.py
+++ b/solution.py
@@ -79,7 +79,7 @@
     return top * (1.0 / TOP)
 
 
-def edge_kernel(h_ref, row_out, col_out):
+def edge_kernel(h_ref, col_out, row_out):
     planes, rows, cols = h_ref.shape[1:]
     diagonal = iota((rows, rows), 0) == iota((rows, rows), 1)
     for z in range(planes):
@@ -97,8 +97,8 @@
     return pl.pallas_call(
         edge_kernel,
         out_shape=(
+            jax.ShapeDtypeStruct((2, planes, rows), f32),
             jax.ShapeDtypeStruct((2, planes, cols), f32),
-            jax.ShapeDtypeStruct((2, planes, rows), f32),
         ),
         in_specs=[VMEM],
         out_specs=(VMEM, VMEM),
@@ -196,7 +196,15 @@
             lookup(4 * c + part)
         return 0
 
-    lax.fori_loop(0, lax.shift_right_logical(offset_ref[0, 128] + 1023, 10), chunk, 0)
+    total = offset_ref[0, 128]
+    whole = lax.shift_right_logical(total, 10)
+    lax.fori_loop(0, whole, chunk, 0)
+
+    def last(c, _):
+        lookup(4 * whole + c)
+        return 0
+
+    lax.fori_loop(0, lax.shift_right_logical(lax.bitwise_and(total, 1023) + 255, 8), last, 0)
     lanes = iota((16, 128), 1)
 
     def unpack(d, _):
@@ -216,8 +224,8 @@
 
 
 def field_kernel(
-    offset_ref, packed, e_ref, h_ref, j_ref, kind_ref, table_ref, dft_e_ref, dft_h_ref, row_ref,
-    col_ref, e_hbm, j_hbm, dft_e_hbm, dft_h_hbm, out_ref, e_new, j_new, dft_e_new, dft_h_new,
+    offset_ref, packed, e_ref, h_ref, j_ref, kind_ref, table_ref, dft_e_ref, dft_h_ref, col_ref,
+    row_ref, e_hbm, j_hbm, dft_e_hbm, dft_h_hbm, out_ref, e_new, j_new, dft_e_new, dft_h_new,
     flux_ref, wide_ref, found, head_ref, rest_ref, sems,
 ):
     wide_ref[...] = jnp.zeros_like(wide_ref)
@@ -240,7 +248,7 @@
         copy.wait()
 
 
-def field_and_flux(offsets, packed, e, h, j, kinds, table, dft_e, dft_h, rows_below, cols_left):
+def field_and_flux(offsets, packed, e, h, j, kinds, table, dft_e, dft_h, cols_left, rows_below):
     planes, rows, cols = kinds.shape
     fields = [e.shape, e.shape, dft_e.shape, dft_h.shape]
     return pl.pallas_call(
@@ -260,7 +268,7 @@
         ],
         compiler_params=pltpu.CompilerParams(vmem_limit_bytes=30 << 20),
         name="field_and_flux",
-    )(offsets, packed, e, h, j, kinds, table, dft_e, dft_h, rows_below, cols_left)
+    )(offsets, packed, e, h, j, kinds, table, dft_e, dft_h, cols_left, rows_below)
 
 
 GROUP = 8
@@ -521,16 +529,16 @@
     e_field, h_field, j_field, material, material_table, dft_e, dft_h, skin_cell, counts,
     patch_slot, area,
 ):
-    last_rows, last_cols = field_edges(h_field)
+    last_cols, last_rows = field_edges(h_field)
+    cols_left = shifted(last_cols, "gx", 1)
     rows_below = shifted(last_rows, "gy", 1)
-    cols_left = shifted(last_cols, "gx", 1)
     odd = jnp.stack([lax.axis_index("gx") % 2, lax.axis_index("gy") % 2])
     odd = jnp.broadcast_to(odd[:, None], (2, 128))
     area_a, packed, offsets = gather_area_and_pack(counts, skin_cell, patch_slot, area, 1)
-    rows_below, cols_left, area_a = lax.optimization_barrier((rows_below, cols_left, area_a))
+    cols_left, rows_below, area_a = lax.optimization_barrier((cols_left, rows_below, area_a))
     e_next, j_next, dft_e_next, dft_h_next, rows = field_and_flux(
         offsets, packed, e_field, h_field, j_field, material, material_table, dft_e, dft_h,
-        rows_below, cols_left,
+        cols_left, rows_below,
     )
     arrived = lax.all_to_all(rows, ("gy", "gx"), split_axis=0, concat_axis=0, tiled=True)
     area_b = gather_area(patch_slot, area, 1, 15)

time: 82.4 us -> 82.6 us (level)
  waiting for transfers between devices: 6.02 us -> 8.84 us
  starting transfers between devices: 33.2 us -> 31.6 us
    ppermute x2, waiting for transfers between devices: 0.01 us -> 2.84 us  [shifted(): lax.ppermute(value, axis, [(source, source + steps) for source in range(l...]
    all_to_all x1, starting transfers between devices: 10.5 us -> 9.13 us  [shards(): lax.all_to_all(rows, ('gy', 'gx'), split_axis=0, concat_axis=0, tiled=True)]
  transfers between devices with their start and end apart: 11 -> 11, of which waited for: 3 -> 4; matrix products, arithmetic and copies ran while one was open for 1% -> 1% of each run, Pallas kernels for 23% -> 23%
where the time goes in v11:
time: 82.6 us; the launch traced here: 82 us
  Pallas kernels  38.4 us (46%)
  starting transfers between devices  31.6 us (38%)
  waiting for transfers between devices  8.84 us (11%)
  local copies, waits for them, and re-layouts  1.11 us (1%)
  other arithmetic  1.01 us (1%)
  between operations  0.97 us (1%)
    ppermute x8, starting transfers between devices, exchange(): swaps.append(lax.ppermute(value, axis, pairs))  16.6 us
    pallas_call x2, Pallas kernels, scatter_density(): pl.pallas_call(functools.partial(scatter_kernel, first=first), out_shape=...  12.5 us
    pallas_call x1, Pallas kernels, gather_area(): pl.pallas_call(functools.partial(area_kernel, first=first), out_shape=jax...  10.9 us
    pallas_call x1, Pallas kernels, field_and_flux(): pl.pallas_call(field_kernel, out_shape=tuple((jax.ShapeDtypeStruct(shape,...  10.1 us
    all_to_all x1, starting transfers between devices, shards(): lax.all_to_all(rows, ('gy', 'gx'), split_axis=0, concat_axis=0, tiled=True)  9.13 us
    ppermute x2, starting transfers between devices, shifted(): lax.ppermute(value, axis, [(source, source + steps) for source in range(l...  5.88 us
    ppermute x8, waiting for transfers between devices, exchange(): swaps.append(lax.ppermute(value, axis, pairs))  5.26 us
    ppermute x2, waiting for transfers between devices, shifted(): lax.ppermute(value, axis, [(source, source + steps) for source in range(l...  2.84 us
  transfers between devices with their start and end apart: 11, of which 4 were waited for; matrix products, arithmetic and copies ran while one was open for 1% of the time, Pallas kernels for 23%

profile of v11, /device:TPU:26, one launch (start us, length us, event | category | flops | bytes accessed | tf_op | source)
XLA Modules:
  0.0 82.0 jit_solution(10937055784669517984)
XLA Ops:
  0.6 1.0 %copy-done.3 = f32[3,4,64,128]{3,2,1,0:T(8,128)S(1)} copy-done((f32[3,4,64,128]{3,2,1,0:T(8,128)S(1)}, f32[3,4,64,128]{3,2,1,0:T(8,128)}, u32[]{:S(2)}) %copy-start.3) | copy-done | bytes 393240
  1.7 0.1 field_edges.1
  1.9 4.0 %collective-permute-start = (f32[2,4,64]{2,1,0:T(4,128)S(1)}, f32[2,4,64]{2,1,0:T(4,128)S(1)}, u32[]{:S(2)}, u32[]{:S(2)}) collective-permute-start(f32[2,4,64]{2,1,0:T(4,128)S(1)} %get-tuple-element.33), channel_id=1, source_target_pairs={{0,1},{1,2},{2,3},{3,4},{4,5},{5,6},{6,7},{8,9},{9,10},{10,11},{11... | collective-permute-start | bytes 6152 | tf_op jit(solution)/shard_map/ppermute | solution.py:35
  5.8 1.9 %collective-permute-start.1 = (f32[2,4,128]{2,1,0:T(4,128)S(1)}, f32[2,4,128]{2,1,0:T(4,128)S(1)}, u32[]{:S(2)}, u32[]{:S(2)}) collective-permute-start(f32[2,4,128]{2,1,0:T(4,128)S(1)} %get-tuple-element.34), channel_id=1, source_target_pairs={{0,8},{8,16},{16,24},{24,32},{32,40},{40,48},{48,56},{56,64},{64,7... | collective-permute-start | bytes 12296 | tf_op jit(solution)/shard_map/ppermute | solution.py:35
  7.8 2.4 %area_and_pack.1 = (f32[1,8,1024]{2,1,0:T(8,128)S(1)}, s32[136,128]{1,0:T(8,128)S(1)}, s32[1,136]{1,0:T(1,128)S(1)}) custom-call(s32[1,128]{1,0:T(1,128)S(1)} %copy-done.11, s32[1,128,128]{2,1,0:T(8,128)S(1)} %copy-done.9, s32[1,128,128]{2,1,0:T(8,128)S(1)} %copy-done.10, f32[3,256,256]{2,1,0:T(8,128)S(1)} %copy-done.8), custom_call_target="tpu_custom_call" | custom-call | flops 805306368 | bytes 2000000 | tf_op jit(solution)/shard_map/area_and_pack/pallas_call | solution.py:351
  10.3 2.8 %collective-permute-done.1.row_ref = f32[2,4,128]{2,1,0:T(4,128)S(1)} collective-permute-done((f32[2,4,128]{2,1,0:T(4,128)S(1)}, f32[2,4,128]{2,1,0:T(4,128)S(1)}, u32[]{:S(2)}, u32[]{:S(2)}) %collective-permute-start.1) | collective-permute-done | bytes 4128 | tf_op jit(solution)/shard_map/ppermute | solution.py:35
  13.1 10.1 %field_and_flux.1 = (f32[3,4,64,128]{3,2,1,0:T(8,128)}, f32[3,4,64,128]{3,2,1,0:T(8,128)}, f32[3,2,3,4,64,128]{5,4,3,2,1,0:T(8,128)}, f32[3,2,3,4,64,128]{5,4,3,2,1,0:T(8,128)}, f32[128,9,1,128]{3,2,1,0:T(1,128)}) custom-call(s32[1,136]{1,0:T(1,128)S(1)} %get-tuple-element.31.offset_ref, s32[136,128]{1,0:T(8,128)S(1)} %get-tuple-element.32.packed, ...), custom_call_target="tpu_custom_call" | custom-call | tf_op jit(solution)/shard_map/field_and_flux/pallas_call | solution.py:254
  23.3 9.1 %all-to-all-start = ((f32[128,9,1,128]{3,2,1,0:T(1,128)}), f32[128,9,1,128]{3,2,1,0:T(1,128)S(1)}, u32[]{:S(2)}, u32[]{:S(2)}) async-start(f32[128,9,1,128]{3,2,1,0:T(1,128)} %get-tuple-element.43), calls=%async_computation | async-start | bytes 1179648 | tf_op jit(solution)/shard_map/all_to_all | solution.py:543
  32.4 10.9 %gather_area.1.area_b_ref = f32[15,8,1024]{2,1,0:T(8,128)S(1)} custom-call(s32[1,128,128]{2,1,0:T(8,128)S(1)} %copy-done.10, f32[3,256,256]{2,1,0:T(8,128)S(1)} %copy-done.8), custom_call_target="tpu_custom_call" | custom-call | flops 12079595520 | bytes 2000000 | tf_op jit(solution)/shard_map/gather_area/pallas_call | solution.py:368
  43.4 0.7 all-to-all-done.flux_ref
  44.2 7.9 %scatter_density.2 = (f32[2,256,256]{2,1,0:T(8,128)S(1)}, f32[2,104,256]{2,1,0:T(8,128)S(1)}, f32[2,104,256]{2,1,0:T(8,128)S(1)}) custom-call(s32[2,128]{1,0:T(2,128)S(1)} %broadcast_in_dim.2.odd_ref, s32[1,128,128]{2,1,0:T(8,128)S(1)} %copy-done.10, f32[1,8,1024]{2,1,0:T(8,128)S(1)} %get-tuple-element.42.area_a_ref, ...), custom_call_target="tpu_custom_call" | custom-call | flops 8589934592 | bytes 2000000 | tf_op jit(solution)/shard_map/scatter_density/pallas_call | solution.py:443
  52.1 4.8 %collective-permute-start.2 = (f32[2,104,256]{2,1,0:T(8,128)S(1)}, f32[2,104,256]{2,1,0:T(8,128)S(1)}, u32[]{:S(2)}, u32[]{:S(2)}) collective-permute-start(f32[2,104,256]{2,1,0:T(8,128)S(1)} %get-tuple-element.46), channel_id=1, source_target_pairs={{1,2},{3,4},{5,6},{2,1},{4,3},{6,5},{9,10},{11,12},{13,14},{10,9},... | collective-permute-start | bytes 638984 | tf_op jit(solution)/shard_map/ppermute | solution.py:44
  56.8 0.1 collective-permute-start.3
  56.9 4.6 %scatter_density.3 = (f32[1,256,256]{2,1,0:T(8,128)S(1)}, f32[1,104,256]{2,1,0:T(8,128)S(1)}, f32[1,104,256]{2,1,0:T(8,128)S(1)}) custom-call(s32[2,128]{1,0:T(2,128)S(1)} %broadcast_in_dim.2.odd_ref, s32[1,128,128]{2,1,0:T(8,128)S(1)} %copy-done.10, f32[1,8,1024]{2,1,0:T(8,128)S(1)} %get-tuple-element.42.area_a_ref, ...), custom_call_target="tpu_custom_call" | custom-call | flops 4294967296 | bytes 2000000 | tf_op jit(solution)/shard_map/scatter_density/pallas_call | solution.py:443
  61.5 4.7 %collective-permute-start.6 = (f32[1,104,256]{2,1,0:T(8,128)S(1)}, f32[1,104,256]{2,1,0:T(8,128)S(1)}, u32[]{:S(2)}, u32[]{:S(2)}) collective-permute-start(f32[1,104,256]{2,1,0:T(8,128)S(1)} %get-tuple-element.51), channel_id=1, source_target_pairs={{1,2},{3,4},{5,6},{2,1},{4,3},{6,5},{9,10},{11,12},{13,14},{10,9},... | collective-permute-start | bytes 319496 | tf_op jit(solution)/shard_map/ppermute | solution.py:44
  66.3 0.1 collective-permute-start.7
  66.4 0.5 column_sum.2
  66.9 3.8 %collective-permute-start.4 = (f32[2,104,256]{2,1,0:T(8,128)S(1)}, f32[2,104,256]{2,1,0:T(8,128)S(1)}, u32[]{:S(2)}, u32[]{:S(2)}) collective-permute-start(f32[2,104,256]{2,1,0:T(8,128)S(1)} %get-tuple-element.49), channel_id=1, source_target_pairs={{8,16},{24,32},{40,48},{56,64},{72,80},{88,96},{104,112},{16,8},{3... | collective-permute-start | bytes 638984 | tf_op jit(solution)/shard_map/ppermute | solution.py:44
  70.8 1.2 %collective-permute-done.6.one_ref = f32[1,104,256]{2,1,0:T(8,128)S(1)} collective-permute-done((f32[1,104,256]{2,1,0:T(8,128)S(1)}, f32[1,104,256]{2,1,0:T(8,128)S(1)}, u32[]{:S(2)}, u32[]{:S(2)}) %collective-permute-start.6) | collective-permute-done | bytes 106528 | tf_op jit(solution)/shard_map/ppermute | solution.py:44
  72.0 0.3 column_sum.3
  72.3 3.0 %collective-permute-start.8 = (f32[1,104,256]{2,1,0:T(8,128)S(1)}, f32[1,104,256]{2,1,0:T(8,128)S(1)}, u32[]{:S(2)}, u32[]{:S(2)}) collective-permute-start(f32[1,104,256]{2,1,0:T(8,128)S(1)} %get-tuple-element.54), channel_id=1, source_target_pairs={{8,16},{24,32},{40,48},{56,64},{72,80},{88,96},{104,112},{16,8},{3... | collective-permute-start | bytes 319496 | tf_op jit(solution)/shard_map/ppermute | solution.py:44
  75.5 0.9 %pad_maximum_fusion = f32[3,256,256]{2,1,0:T(8,128)} fusion(f32[1,256,256]{2,1,0:T(8,128)S(1)} %get-tuple-element.45.block_ref, f32[2,256,256]{2,1,0:T(8,128)S(1)} %get-tuple-element.44.block_ref), kind=kLoop, calls=%fused_computation | loop fusion | flops 196608 | bytes 1572864 | tf_op jit(solution)/shard_map/concatenate | solution.py:554
  76.4 4.1 %collective-permute-done.8.refs_4_ = f32[1,104,256]{2,1,0:T(8,128)S(1)} collective-permute-done((f32[1,104,256]{2,1,0:T(8,128)S(1)}, f32[1,104,256]{2,1,0:T(8,128)S(1)}, u32[]{:S(2)}, u32[]{:S(2)}) %collective-permute-start.8) | collective-permute-done | bytes 106528 | tf_op jit(solution)/shard_map/ppermute | solution.py:44
  80.5 1.5 %row_sum.1 = f32[3,256,256]{2,1,0:T(8,128)} custom-call(s32[2,128]{1,0:T(2,128)S(1)} %broadcast_in_dim.2.odd_ref, f32[2,256,256]{2,1,0:T(8,128)S(1)} %get-tuple-element.48.refs_0_, f32[2,104,256]{2,1,0:T(8,128)S(1)} %collective-permute-done.4.refs_1_, f32[2,104,256]{2,1,0:T(8,128)S(1)} %collective-permute-done.5.refs_2_, ...), custom_call_target="tpu_custom_call" | custom-call | tf_op jit(solution)/shard_map/row_sum/pallas_call | solution.py:518
  (34 shorter events, 0.4 us)
Async XLA Ops:
  0.6 1.0 %copy-start.3 = (f32[3,4,64,128]{3,2,1,0:T(8,128)S(1)}, f32[3,4,64,128]{3,2,1,0:T(8,128)}, u32[]{:S(2)}) copy-start(f32[3,4,64,128]{3,2,1,0:T(8,128)} %h_ref.3) | copy-start | bytes 1179652
  1.6 6.1 %copy-start.8 = (f32[3,256,256]{2,1,0:T(8,128)S(1)}, f32[3,256,256]{2,1,0:T(8,128)}, u32[]{:S(2)}) copy-start(f32[3,256,256]{2,1,0:T(8,128)} %area_ref.3) | copy-start | bytes 2359300
  1.6 6.1 %copy-start.9 = (s32[1,128,128]{2,1,0:T(8,128)S(1)}, s32[1,128,128]{2,1,0:T(8,128)}, u32[]{:S(2)}) copy-start(s32[1,128,128]{2,1,0:T(8,128)} %cell_ref.1) | copy-start | bytes 196612
  1.6 6.1 %copy-start.10 = (s32[1,128,128]{2,1,0:T(8,128)S(1)}, s32[1,128,128]{2,1,0:T(8,128)}, u32[]{:S(2)}) copy-start(s32[1,128,128]{2,1,0:T(8,128)} %patch_ref.7) | copy-start | bytes 196612
  1.6 6.2 %copy-start.11 = (s32[1,128]{1,0:T(1,128)S(1)}, s32[1,128]{1,0:T(1,128)}, u32[]{:S(2)}) copy-start(s32[1,128]{1,0:T(1,128)} %count_ref.1) | copy-start | bytes 1540
  1.6 11.4 %copy-start.1 = (f32[3,2,3,4,64,128]{5,4,3,2,1,0:T(8,128)S(1)}, f32[3,2,3,4,64,128]{5,4,3,2,1,0:T(8,128)}, u32[]{:S(2)}) copy-start(f32[3,2,3,4,64,128]{5,4,3,2,1,0:T(8,128)} %dft_h_ref.1) | copy-start | bytes 7077892
  1.7 11.4 %copy-start.4 = (f32[3,4,64,128]{3,2,1,0:T(8,128)S(1)}, f32[3,4,64,128]{3,2,1,0:T(8,128)}, u32[]{:S(2)}) copy-start(f32[3,4,64,128]{3,2,1,0:T(8,128)} %h_ref.3) | copy-start | bytes 1179652
  1.7 11.4 %copy-start.5 = (f32[3,4,64,128]{3,2,1,0:T(8,128)S(1)}, f32[3,4,64,128]{3,2,1,0:T(8,128)}, u32[]{:S(2)}) copy-start(f32[3,4,64,128]{3,2,1,0:T(8,128)} %j_ref.1) | copy-start | bytes 1179652
  1.8 11.3 %copy-start = (f32[3,2,3,4,64,128]{5,4,3,2,1,0:T(8,128)S(1)}, f32[3,2,3,4,64,128]{5,4,3,2,1,0:T(8,128)}, u32[]{:S(2)}) copy-start(f32[3,2,3,4,64,128]{5,4,3,2,1,0:T(8,128)} %dft_e_ref.1) | copy-start | bytes 7077892
  1.8 11.3 %copy-start.2 = (f32[3,4,64,128]{3,2,1,0:T(8,128)S(1)}, f32[3,4,64,128]{3,2,1,0:T(8,128)}, u32[]{:S(2)}) copy-start(f32[3,4,64,128]{3,2,1,0:T(8,128)} %e_ref.1) | copy-start | bytes 1179652
  1.8 11.3 %copy-start.6 = (s32[4,64,128]{2,1,0:T(8,128)S(1)}, s32[4,64,128]{2,1,0:T(8,128)}, u32[]{:S(2)}) copy-start(s32[4,64,128]{2,1,0:T(8,128)} %kind_ref.1) | copy-start | bytes 393220
  1.9 11.3 %copy-start.7 = (f32[4,32]{1,0:T(4,128)S(1)}, f32[4,32]{1,0:T(4,128)}, u32[]{:S(2)}) copy-start(f32[4,32]{1,0:T(4,128)} %table_ref.1) | copy-start | bytes 1540
  1.9 8.4 %collective-permute-start = (f32[2,4,64]{2,1,0:T(4,128)S(1)}, f32[2,4,64]{2,1,0:T(4,128)S(1)}, u32[]{:S(2)}, u32[]{:S(2)}) collective-permute-start(f32[2,4,64]{2,1,0:T(4,128)S(1)} %get-tuple-element.33), channel_id=1, source_target_pairs={{0,1},{1,2},{2,3},{3,4},{4,5},{5,6},{6,7},{8,9},{9,10},{10,11},{11... | collective-permute-start | bytes 6152 | tf_op jit(solution)/shard_map/ppermute | solution.py:35
  5.8 7.3 %collective-permute-start.1 = (f32[2,4,128]{2,1,0:T(4,128)S(1)}, f32[2,4,128]{2,1,0:T(4,128)S(1)}, u32[]{:S(2)}, u32[]{:S(2)}) collective-permute-start(f32[2,4,128]{2,1,0:T(4,128)S(1)} %get-tuple-element.34), channel_id=1, source_target_pairs={{0,8},{8,16},{16,24},{24,32},{32,40},{40,48},{48,56},{56,64},{64,7... | collective-permute-start | bytes 12296 | tf_op jit(solution)/shard_map/ppermute | solution.py:35
  23.3 20.9 %all-to-all-start = ((f32[128,9,1,128]{3,2,1,0:T(1,128)}), f32[128,9,1,128]{3,2,1,0:T(1,128)S(1)}, u32[]{:S(2)}, u32[]{:S(2)}) async-start(f32[128,9,1,128]{3,2,1,0:T(1,128)} %get-tuple-element.43), calls=%async_computation | async-start | bytes 1179648 | tf_op jit(solution)/shard_map/all_to_all | solution.py:543
  52.1 14.3 %collective-permute-start.2 = (f32[2,104,256]{2,1,0:T(8,128)S(1)}, f32[2,104,256]{2,1,0:T(8,128)S(1)}, u32[]{:S(2)}, u32[]{:S(2)}) collective-permute-start(f32[2,104,256]{2,1,0:T(8,128)S(1)} %get-tuple-element.46), channel_id=1, source_target_pairs={{1,2},{3,4},{5,6},{2,1},{4,3},{6,5},{9,10},{11,12},{13,14},{10,9},... | collective-permute-start | bytes 638984 | tf_op jit(solution)/shard_map/ppermute | solution.py:44
  56.8 9.5 %collective-permute-start.3 = (f32[2,104,256]{2,1,0:T(8,128)S(1)}, f32[2,104,256]{2,1,0:T(8,128)S(1)}, u32[]{:S(2)}, u32[]{:S(2)}) collective-permute-start(f32[2,104,256]{2,1,0:T(8,128)S(1)} %get-tuple-element.47), channel_id=1, source_target_pairs={{0,1},{2,3},{4,5},{6,7},{1,0},{3,2},{5,4},{7,6},{8,9},{10,11},{12,... | collective-permute-start | bytes 638984 | tf_op jit(solution)/shard_map/ppermute | solution.py:44
  61.5 10.4 %collective-permute-start.6 = (f32[1,104,256]{2,1,0:T(8,128)S(1)}, f32[1,104,256]{2,1,0:T(8,128)S(1)}, u32[]{:S(2)}, u32[]{:S(2)}) collective-permute-start(f32[1,104,256]{2,1,0:T(8,128)S(1)} %get-tuple-element.51), channel_id=1, source_target_pairs={{1,2},{3,4},{5,6},{2,1},{4,3},{6,5},{9,10},{11,12},{13,14},{10,9},... | collective-permute-start | bytes 319496 | tf_op jit(solution)/shard_map/ppermute | solution.py:44
  66.3 5.7 %collective-permute-start.7 = (f32[1,104,256]{2,1,0:T(8,128)S(1)}, f32[1,104,256]{2,1,0:T(8,128)S(1)}, u32[]{:S(2)}, u32[]{:S(2)}) collective-permute-start(f32[1,104,256]{2,1,0:T(8,128)S(1)} %get-tuple-element.52), channel_id=1, source_target_pairs={{0,1},{2,3},{4,5},{6,7},{1,0},{3,2},{5,4},{7,6},{8,9},{10,11},{12,... | collective-permute-start | bytes 319496 | tf_op jit(solution)/shard_map/ppermute | solution.py:44
  66.9 13.6 %collective-permute-start.4 = (f32[2,104,256]{2,1,0:T(8,128)S(1)}, f32[2,104,256]{2,1,0:T(8,128)S(1)}, u32[]{:S(2)}, u32[]{:S(2)}) collective-permute-start(f32[2,104,256]{2,1,0:T(8,128)S(1)} %get-tuple-element.49), channel_id=1, source_target_pairs={{8,16},{24,32},{40,48},{56,64},{72,80},{88,96},{104,112},{16,8},{3... | collective-permute-start | bytes 638984 | tf_op jit(solution)/shard_map/ppermute | solution.py:44
  70.7 9.7 %collective-permute-start.5 = (f32[2,104,256]{2,1,0:T(8,128)S(1)}, f32[2,104,256]{2,1,0:T(8,128)S(1)}, u32[]{:S(2)}, u32[]{:S(2)}) collective-permute-start(f32[2,104,256]{2,1,0:T(8,128)S(1)} %get-tuple-element.50), channel_id=1, source_target_pairs={{0,8},{16,24},{32,40},{48,56},{64,72},{80,88},{96,104},{112,120},{... | collective-permute-start | bytes 638984 | tf_op jit(solution)/shard_map/ppermute | solution.py:44
  72.3 8.1 %collective-permute-start.8 = (f32[1,104,256]{2,1,0:T(8,128)S(1)}, f32[1,104,256]{2,1,0:T(8,128)S(1)}, u32[]{:S(2)}, u32[]{:S(2)}) collective-permute-start(f32[1,104,256]{2,1,0:T(8,128)S(1)} %get-tuple-element.54), channel_id=1, source_target_pairs={{8,16},{24,32},{40,48},{56,64},{72,80},{88,96},{104,112},{16,8},{3... | collective-permute-start | bytes 319496 | tf_op jit(solution)/shard_map/ppermute | solution.py:44
  75.4 5.1 %collective-permute-start.9 = (f32[1,104,256]{2,1,0:T(8,128)S(1)}, f32[1,104,256]{2,1,0:T(8,128)S(1)}, u32[]{:S(2)}, u32[]{:S(2)}) collective-permute-start(f32[1,104,256]{2,1,0:T(8,128)S(1)} %get-tuple-element.55), channel_id=1, source_target_pairs={{0,8},{16,24},{32,40},{48,56},{64,72},{80,88},{96,104},{112,120},{... | collective-permute-start | bytes 319496 | tf_op jit(solution)/shard_map/ppermute | solution.py:44

commit v12 on v11

--- a/solution.py
+++ b/solution.py
@@ -286,8 +286,8 @@
     return split_scaled(jnp.concatenate(halves, 1), head_ref, rest_ref)
 
 
-def area_group(patch_ref, head_ref, rest_ref, back, out_ref, c, first):
-    patch = slot_row(patch_ref, c + first)
+def area_group(patch_ref, head_ref, rest_ref, back, out_ref, c):
+    patch = slot_row(patch_ref, c)
     u, v = lax.shift_right_logical(patch, 8), lax.bitwise_and(patch, 255)
     hot = jnp.concatenate(
         [onehot(256, jnp.where(u < 128, v, 512)), onehot(256, jnp.where(u < 128, 512, v))], 0
@@ -301,44 +301,34 @@
         out_ref[c, q : q + 1, :] = found * back
 
 
-def first_area_kernel(
-    count_ref, cell_ref, patch_ref, area_ref, out_ref, packed, offset_ref, head_ref, rest_ref,
-    *, groups
-):
-    back = split_area(area_ref, head_ref, rest_ref)
+def pack_kernel(count_ref, cell_ref, packed, offset_ref):
     lane = iota((1, 128), 1)
-    share = 128 // groups
-
-    def chunk(c, carry):
+
+    def pack(d, carry):
         offset, current = carry
-        for i in range(share):
-            d = c * share + i
-            row, start = lax.shift_right_logical(offset, 7), lax.bitwise_and(offset, 127)
-            live = count_ref[0, d]
-            offset_ref[0, d] = offset
-            rolled = pltpu.roll(cell_ref[0, pl.ds(d, 1), :], start, 1)
-            merged = jnp.where(lane >= start, rolled, current)
-            packed[pl.ds(row, 1), :] = merged
-            current = jnp.where(start + live >= 128, rolled, merged)
-            offset = offset + live
-        area_group(patch_ref, head_ref, rest_ref, back, out_ref, c, 0)
-        return offset, current
+        row, start = lax.shift_right_logical(offset, 7), lax.bitwise_and(offset, 127)
+        live = count_ref[0, d]
+        offset_ref[0, d] = offset
+        rolled = pltpu.roll(cell_ref[0, pl.ds(d, 1), :], start, 1)
+        merged = jnp.where(lane >= start, rolled, current)
+        packed[pl.ds(row, 1), :] = merged
+        return offset + live, jnp.where(start + live >= 128, rolled, merged)
 
     offset, current = lax.fori_loop(
-        0, groups, chunk, (jnp.int32(0), jnp.zeros((1, 128), jnp.int32)), unroll=2
+        0, 128, pack, (jnp.int32(0), jnp.zeros((1, 128), jnp.int32)), unroll=64
     )
     packed[pl.ds(lax.shift_right_logical(offset, 7), 1), :] = current
     offset_ref[0, 128] = offset
 
 
-def area_kernel(patch_ref, area_ref, out_ref, head_ref, rest_ref, *, first):
+def area_kernel(patch_ref, area_ref, out_ref, head_ref, rest_ref):
     back = split_area(area_ref, head_ref, rest_ref)
 
     def chunk(c, _):
-        area_group(patch_ref, head_ref, rest_ref, back, out_ref, c, first)
+        area_group(patch_ref, head_ref, rest_ref, back, out_ref, c)
         return 0
 
-    lax.fori_loop(0, out_ref.shape[0], chunk, 0, unroll=5)
+    lax.fori_loop(0, out_ref.shape[0], chunk, 0, unroll=8)
 
 
 def area_cost(groups):
@@ -347,26 +337,25 @@
     )
 
 
-def gather_area_and_pack(counts, cells, patch, area, groups):
-    return pl.pallas_call(
-        functools.partial(first_area_kernel, groups=groups),
+def pack_slots(counts, cells):
+    return pl.pallas_call(
+        pack_kernel,
         out_shape=(
-            jax.ShapeDtypeStruct((groups, 8, GROUP * 128), f32),
             jax.ShapeDtypeStruct((136, 128), jnp.int32),
             jax.ShapeDtypeStruct((1, 136), jnp.int32),
         ),
-        in_specs=[SMEM, VMEM, VMEM, VMEM],
-        out_specs=(VMEM, VMEM, SMEM),
-        scratch_shapes=AREA_SCRATCH,
-        compiler_params=pltpu.CompilerParams(vmem_limit_bytes=32 << 20),
-        cost_estimate=area_cost(groups),
-        name="area_and_pack",
-    )(counts, cells, patch, area)
-
-
-def gather_area(patch, area, first, groups):
-    return pl.pallas_call(
-        functools.partial(area_kernel, first=first),
+        in_specs=[SMEM, VMEM],
+        out_specs=(VMEM, SMEM),
+        compiler_params=pltpu.CompilerParams(vmem_limit_bytes=8 << 20),
+        cost_estimate=area_cost(3),
+        name="pack_slots",
+    )(counts, cells)
+
+
+def gather_area(patch, area):
+    groups = 128 // GROUP
+    return pl.pallas_call(
+        area_kernel,
         out_shape=jax.ShapeDtypeStruct((groups, 8, GROUP * 128), f32),
         in_specs=[VMEM, VMEM],
         out_specs=VMEM,
@@ -382,15 +371,15 @@
 
 
 def scatter_kernel(
-    odd_ref, patch_ref, area_a_ref, area_b_ref, flux_ref, out_ref, first_ref, second_ref, dense,
+    odd_ref, patch_ref, area_ref, flux_ref, out_ref, first_ref, second_ref, dense,
     *, first
 ):
     freqs = out_ref.shape[0]
-    half, groups = area_a_ref.shape[0], dense.shape[0]
+    groups = dense.shape[0]
     out_ref[...] = jnp.zeros_like(out_ref)
     top = jnp.zeros((1, GROUP * 128), f32)
     for c in range(groups):
-        area = area_a_ref[c] if c < half else area_b_ref[c - half]
+        area = area_ref[c]
         for f in range(freqs):
             density = jnp.zeros((1, GROUP * 128), f32)
             for q in range(3):
@@ -439,11 +428,11 @@
     )
 
 
-def scatter_density(odd, patch, area_a, area_b, flux, first, freqs):
+def scatter_density(odd, patch, area_rows, flux, first, freqs):
     return pl.pallas_call(
         functools.partial(scatter_kernel, first=first),
         out_shape=block_and_edges(freqs),
-        in_specs=[VMEM] * 5,
+        in_specs=[VMEM] * 4,
         out_specs=(VMEM,) * 3,
         scratch_shapes=[pltpu.VMEM((128 // GROUP, 8, GROUP * 128), f32)],
         compiler_params=pltpu.CompilerParams(vmem_limit_bytes=36 << 20),
@@ -451,7 +440,7 @@
             flops=2 * freqs * 65536 * 2 * 16384, bytes_accessed=2000000, transcendentals=0
         ),
         name="scatter_density",
-    )(odd, patch, area_a, area_b, flux)
+    )(odd, patch, area_rows, flux)
 
 
 def in_window(place):
@@ -498,7 +487,8 @@
 
 
 def row_kernel(odd_ref, *refs):
-    refs, out_ref = refs[:-1], refs[-1]
+    refs, (out_hbm, out_ref, sems) = refs[:-3], refs[-3:]
+    copies = []
     length = 256 + 2 * EDGE
     band = in_window(iota((256, length), 1) - EDGE - iota((256, length), 0))
     band = jnp.concatenate([band, band], 1)
@@ -511,7 +501,12 @@
                 band, jnp.concatenate(two_parts(cells), 0), preferred_element_type=f32
             )
             out_ref[done] = total * (1.0 / (4.0 * HALF * HALF))
+            copy = pltpu.make_async_copy(out_ref.at[done], out_hbm.at[done], sems.at[done])
+            copy.start()
+            copies.append(copy)
             done += 1
+    for copy in copies:
+        copy.wait()
 
 
 def row_sum(odd, *pieces):
@@ -519,7 +514,8 @@
         row_kernel,
         out_shape=jax.ShapeDtypeStruct((3, 256, 256), f32),
         in_specs=[VMEM] * (1 + len(pieces)),
-        out_specs=VMEM,
+        out_specs=pl.BlockSpec(memory_space=pl.ANY),
+        scratch_shapes=[pltpu.VMEM((3, 256, 256), f32), pltpu.SemaphoreType.DMA((3,))],
         compiler_params=pltpu.CompilerParams(vmem_limit_bytes=16 << 20),
         name="row_sum",
     )(odd, *pieces)
@@ -534,18 +530,19 @@
     rows_below = shifted(last_rows, "gy", 1)
     odd = jnp.stack([lax.axis_index("gx") % 2, lax.axis_index("gy") % 2])
     odd = jnp.broadcast_to(odd[:, None], (2, 128))
-    area_a, packed, offsets = gather_area_and_pack(counts, skin_cell, patch_slot, area, 1)
-    cols_left, rows_below, area_a = lax.optimization_barrier((cols_left, rows_below, area_a))
+    packed, offsets = pack_slots(counts, skin_cell)
+    cols_left, rows_below, packed = lax.optimization_barrier((cols_left, rows_below, packed))
     e_next, j_next, dft_e_next, dft_h_next, rows = field_and_flux(
         offsets, packed, e_field, h_field, j_field, material, material_table, dft_e, dft_h,
         cols_left, rows_below,
     )
+    rows, patch, area_here = lax.optimization_barrier((rows, patch_slot, area))
     arrived = lax.all_to_all(rows, ("gy", "gx"), split_axis=0, concat_axis=0, tiled=True)
-    area_b = gather_area(patch_slot, area, 1, 15)
+    area_rows = gather_area(patch, area_here)
 
     blocks, swaps, pieces = [], [], []
     for first, freqs in PIECES:
-        block, *edges = scatter_density(odd, patch_slot, area_a, area_b, arrived, first, freqs)
+        block, *edges = scatter_density(odd, patch, area_rows, arrived, first, freqs)
         blocks.append(block)
         swaps.append(exchange(*edges, "gx"))
     for block, swap in zip(blocks, swaps):

time: 82.6 us -> 82.6 us (level)
  the two profiles are of different devices: /device:TPU:26 before, /device:TPU:6 now
where the time goes in v12:
time: 82.6 us; the launch traced here: 81.5 us
  Pallas kernels  37.8 us (46%)
  starting transfers between devices  31.4 us (38%)
  waiting for transfers between devices  9.03 us (11%)
  between operations  1.14 us (1%)
  local copies, waits for them, and re-layouts  1.12 us (1%)
  other arithmetic  1.01 us (1%)
    ppermute x8, starting transfers between devices, exchange(): swaps.append(lax.ppermute(value, axis, pairs))  17.1 us
    pallas_call x2, Pallas kernels, scatter_density(): pl.pallas_call(functools.partial(scatter_kernel, first=first), out_shape=...  12.5 us
    pallas_call x1, Pallas kernels, gather_area(): pl.pallas_call(area_kernel, out_shape=jax.ShapeDtypeStruct((groups, 8, GR...  11.4 us
    pallas_call x1, Pallas kernels, field_and_flux(): pl.pallas_call(field_kernel, out_shape=tuple((jax.ShapeDtypeStruct(shape,...  9.73 us
    all_to_all x1, starting transfers between devices, shards(): lax.all_to_all(rows, ('gy', 'gx'), split_axis=0, concat_axis=0, tiled=True)  8.89 us
    ppermute x2, starting transfers between devices, shifted(): lax.ppermute(value, axis, [(source, source + steps) for source in range(l...  5.41 us
    ppermute x8, waiting for transfers between devices, exchange(): swaps.append(lax.ppermute(value, axis, pairs))  4.73 us
    ppermute x2, waiting for transfers between devices, shifted(): lax.ppermute(value, axis, [(source, source + steps) for source in range(l...  3.15 us
  transfers between devices with their start and end apart: 11, of which 5 were waited for; matrix products, arithmetic and copies ran while one was open for 1% of the time, Pallas kernels for 23%

profile of v12, /device:TPU:6, one launch (start us, length us, event | category | flops | bytes accessed | tf_op | source)
XLA Modules:
  0.0 81.5 jit_solution(10497973296314745163)
XLA Ops:
  0.6 1.0 %copy-done.3 = f32[3,4,64,128]{3,2,1,0:T(8,128)S(1)} copy-done((f32[3,4,64,128]{3,2,1,0:T(8,128)S(1)}, f32[3,4,64,128]{3,2,1,0:T(8,128)}, u32[]{:S(2)}) %copy-start.3) | copy-done | bytes 393240
  1.8 3.5 %collective-permute-start = (f32[2,4,64]{2,1,0:T(4,128)S(1)}, f32[2,4,64]{2,1,0:T(4,128)S(1)}, u32[]{:S(2)}, u32[]{:S(2)}) collective-permute-start(f32[2,4,64]{2,1,0:T(4,128)S(1)} %get-tuple-element.34), channel_id=1, source_target_pairs={{0,1},{1,2},{2,3},{3,4},{4,5},{5,6},{6,7},{8,9},{9,10},{10,11},{11... | collective-permute-start | bytes 6152 | tf_op jit(solution)/shard_map/ppermute | solution.py:35
  5.3 1.9 %collective-permute-start.1 = (f32[2,4,128]{2,1,0:T(4,128)S(1)}, f32[2,4,128]{2,1,0:T(4,128)S(1)}, u32[]{:S(2)}, u32[]{:S(2)}) collective-permute-start(f32[2,4,128]{2,1,0:T(4,128)S(1)} %get-tuple-element.35), channel_id=1, source_target_pairs={{0,8},{8,16},{16,24},{24,32},{32,40},{40,48},{48,56},{56,64},{64,7... | collective-permute-start | bytes 12296 | tf_op jit(solution)/shard_map/ppermute | solution.py:35
  7.3 1.8 %pack_slots.1 = (s32[136,128]{1,0:T(8,128)S(1)}, s32[1,136]{1,0:T(1,128)S(1)}) custom-call(s32[1,128]{1,0:T(1,128)S(1)} %copy-done.11, s32[1,128,128]{2,1,0:T(8,128)S(1)} %copy-done.9), custom_call_target="tpu_custom_call" | custom-call | flops 2415919104 | bytes 2000000 | tf_op jit(solution)/shard_map/pack_slots/pallas_call | solution.py:341
  9.2 1.7 %collective-permute-done.col_ref = f32[2,4,64]{2,1,0:T(4,128)S(1)} collective-permute-done((f32[2,4,64]{2,1,0:T(4,128)S(1)}, f32[2,4,64]{2,1,0:T(4,128)S(1)}, u32[]{:S(2)}, u32[]{:S(2)}) %collective-permute-start) | collective-permute-done | bytes 2080 | tf_op jit(solution)/shard_map/ppermute | solution.py:35
  10.9 1.4 %collective-permute-done.1.row_ref = f32[2,4,128]{2,1,0:T(4,128)S(1)} collective-permute-done((f32[2,4,128]{2,1,0:T(4,128)S(1)}, f32[2,4,128]{2,1,0:T(4,128)S(1)}, u32[]{:S(2)}, u32[]{:S(2)}) %collective-permute-start.1) | collective-permute-done | bytes 4128 | tf_op jit(solution)/shard_map/ppermute | solution.py:35
  12.4 9.7 %field_and_flux.1 = (f32[3,4,64,128]{3,2,1,0:T(8,128)}, f32[3,4,64,128]{3,2,1,0:T(8,128)}, f32[3,2,3,4,64,128]{5,4,3,2,1,0:T(8,128)}, f32[3,2,3,4,64,128]{5,4,3,2,1,0:T(8,128)}, f32[128,9,1,128]{3,2,1,0:T(1,128)}) custom-call(s32[1,136]{1,0:T(1,128)S(1)} %get-tuple-element.33.offset_ref, s32[136,128]{1,0:T(8,128)S(1)} %get-tuple-element.37.packed, ...), custom_call_target="tpu_custom_call" | custom-call | tf_op jit(solution)/shard_map/field_and_flux/pallas_call | solution.py:254
  22.1 8.9 %all-to-all-start = ((f32[128,9,1,128]{3,2,1,0:T(1,128)}), f32[128,9,1,128]{3,2,1,0:T(1,128)S(1)}, u32[]{:S(2)}, u32[]{:S(2)}) async-start(f32[128,9,1,128]{3,2,1,0:T(1,128)} %get-tuple-element.47), calls=%async_computation | async-start | bytes 1179648 | tf_op jit(solution)/shard_map/all_to_all | solution.py:540
  31.0 11.4 %gather_area.1.area_ref = f32[16,8,1024]{2,1,0:T(8,128)S(1)} custom-call(s32[1,128,128]{2,1,0:T(8,128)S(1)} %copy-done.10, f32[3,256,256]{2,1,0:T(8,128)S(1)} %copy-done.8), custom_call_target="tpu_custom_call" | custom-call | flops 12884901888 | bytes 2000000 | tf_op jit(solution)/shard_map/gather_area/pallas_call | solution.py:357
  42.4 1.1 %all-to-all-done.flux_ref = f32[128,9,1,128]{3,2,1,0:T(1,128)S(1)} async-done(((f32[128,9,1,128]{3,2,1,0:T(1,128)}), f32[128,9,1,128]{3,2,1,0:T(1,128)S(1)}, u32[]{:S(2)}, u32[]{:S(2)}) %all-to-all-start) | async-done | bytes 589856 | tf_op jit(solution)/shard_map/all_to_all | solution.py:540
  43.7 7.9 %scatter_density.2 = (f32[2,256,256]{2,1,0:T(8,128)S(1)}, f32[2,104,256]{2,1,0:T(8,128)S(1)}, f32[2,104,256]{2,1,0:T(8,128)S(1)}) custom-call(s32[2,128]{1,0:T(2,128)S(1)} %broadcast_in_dim.2.odd_ref, s32[1,128,128]{2,1,0:T(8,128)S(1)} %copy-done.10, f32[16,8,1024]{2,1,0:T(8,128)S(1)} %gather_area.1.area_ref, f32[128,9,1,128]{3,2,1,0:T(1,128)S(1)} %all-to-all-done.flux_ref), custom_call_target="tpu_custom_call" | custom-call | flops 8589934592 | bytes 2000000 | tf_op jit(solution)/shard_map/scatter_density/pallas_call | solution.py:432
  51.5 4.7 %collective-permute-start.2 = (f32[2,104,256]{2,1,0:T(8,128)S(1)}, f32[2,104,256]{2,1,0:T(8,128)S(1)}, u32[]{:S(2)}, u32[]{:S(2)}) collective-permute-start(f32[2,104,256]{2,1,0:T(8,128)S(1)} %get-tuple-element.50), channel_id=1, source_target_pairs={{1,2},{3,4},{5,6},{2,1},{4,3},{6,5},{9,10},{11,12},{13,14},{10,9},... | collective-permute-start | bytes 638984 | tf_op jit(solution)/shard_map/ppermute | solution.py:44
  56.3 0.3 collective-permute-start.3
  56.6 4.6 %scatter_density.3 = (f32[1,256,256]{2,1,0:T(8,128)S(1)}, f32[1,104,256]{2,1,0:T(8,128)S(1)}, f32[1,104,256]{2,1,0:T(8,128)S(1)}) custom-call(s32[2,128]{1,0:T(2,128)S(1)} %broadcast_in_dim.2.odd_ref, s32[1,128,128]{2,1,0:T(8,128)S(1)} %copy-done.10, f32[16,8,1024]{2,1,0:T(8,128)S(1)} %gather_area.1.area_ref, f32[128,9,1,128]{3,2,1,0:T(1,128)S(1)} %all-to-all-done.flux_ref), custom_call_target="tpu_custom_call" | custom-call | flops 4294967296 | bytes 2000000 | tf_op jit(solution)/shard_map/scatter_density/pallas_call | solution.py:432
  61.2 4.7 %collective-permute-start.6 = (f32[1,104,256]{2,1,0:T(8,128)S(1)}, f32[1,104,256]{2,1,0:T(8,128)S(1)}, u32[]{:S(2)}, u32[]{:S(2)}) collective-permute-start(f32[1,104,256]{2,1,0:T(8,128)S(1)} %get-tuple-element.55), channel_id=1, source_target_pairs={{1,2},{3,4},{5,6},{2,1},{4,3},{6,5},{9,10},{11,12},{13,14},{10,9},... | collective-permute-start | bytes 319496 | tf_op jit(solution)/shard_map/ppermute | solution.py:44
  66.1 0.5 column_sum.2
  66.6 3.6 %collective-permute-start.4 = (f32[2,104,256]{2,1,0:T(8,128)S(1)}, f32[2,104,256]{2,1,0:T(8,128)S(1)}, u32[]{:S(2)}, u32[]{:S(2)}) collective-permute-start(f32[2,104,256]{2,1,0:T(8,128)S(1)} %get-tuple-element.53), channel_id=1, source_target_pairs={{8,16},{24,32},{40,48},{56,64},{72,80},{88,96},{104,112},{16,8},{3... | collective-permute-start | bytes 638984 | tf_op jit(solution)/shard_map/ppermute | solution.py:44
  70.3 1.1 %collective-permute-done.6.one_ref = f32[1,104,256]{2,1,0:T(8,128)S(1)} collective-permute-done((f32[1,104,256]{2,1,0:T(8,128)S(1)}, f32[1,104,256]{2,1,0:T(8,128)S(1)}, u32[]{:S(2)}, u32[]{:S(2)}) %collective-permute-start.6) | collective-permute-done | bytes 106528 | tf_op jit(solution)/shard_map/ppermute | solution.py:44
  71.4 0.3 column_sum.3
  71.8 3.0 %collective-permute-start.8 = (f32[1,104,256]{2,1,0:T(8,128)S(1)}, f32[1,104,256]{2,1,0:T(8,128)S(1)}, u32[]{:S(2)}, u32[]{:S(2)}) collective-permute-start(f32[1,104,256]{2,1,0:T(8,128)S(1)} %get-tuple-element.58), channel_id=1, source_target_pairs={{8,16},{24,32},{40,48},{56,64},{72,80},{88,96},{104,112},{16,8},{3... | collective-permute-start | bytes 319496 | tf_op jit(solution)/shard_map/ppermute | solution.py:44
  74.7 0.6 collective-permute-start.9
  75.3 0.9 %pad_maximum_fusion = f32[3,256,256]{2,1,0:T(8,128)} fusion(f32[1,256,256]{2,1,0:T(8,128)S(1)} %get-tuple-element.49.block_ref, f32[2,256,256]{2,1,0:T(8,128)S(1)} %get-tuple-element.48.block_ref), kind=kLoop, calls=%fused_computation | loop fusion | flops 196608 | bytes 1572864 | tf_op jit(solution)/shard_map/concatenate | solution.py:551
  76.3 3.6 %collective-permute-done.8.refs_4_ = f32[1,104,256]{2,1,0:T(8,128)S(1)} collective-permute-done((f32[1,104,256]{2,1,0:T(8,128)S(1)}, f32[1,104,256]{2,1,0:T(8,128)S(1)}, u32[]{:S(2)}, u32[]{:S(2)}) %collective-permute-start.8) | collective-permute-done | bytes 106528 | tf_op jit(solution)/shard_map/ppermute | solution.py:44
  79.9 1.4 %row_sum.1 = f32[3,256,256]{2,1,0:T(8,128)} custom-call(s32[2,128]{1,0:T(2,128)S(1)} %broadcast_in_dim.2.odd_ref, f32[2,256,256]{2,1,0:T(8,128)S(1)} %get-tuple-element.52.refs_0_, f32[2,104,256]{2,1,0:T(8,128)S(1)} %collective-permute-done.4.refs_1_, f32[2,104,256]{2,1,0:T(8,128)S(1)} %collective-permute-done.5.refs_2_, ...), custom_call_target="tpu_custom_call" | custom-call | tf_op jit(solution)/shard_map/row_sum/pallas_call | solution.py:513
  (34 shorter events, 0.5 us)
Async XLA Ops:
  0.6 1.0 %copy-start.3 = (f32[3,4,64,128]{3,2,1,0:T(8,128)S(1)}, f32[3,4,64,128]{3,2,1,0:T(8,128)}, u32[]{:S(2)}) copy-start(f32[3,4,64,128]{3,2,1,0:T(8,128)} %h_ref.3) | copy-start | bytes 1179652
  1.6 5.6 %copy-start.9 = (s32[1,128,128]{2,1,0:T(8,128)S(1)}, s32[1,128,128]{2,1,0:T(8,128)}, u32[]{:S(2)}) copy-start(s32[1,128,128]{2,1,0:T(8,128)} %cell_ref.1) | copy-start | bytes 196612
  1.6 5.6 %copy-start.11 = (s32[1,128]{1,0:T(1,128)S(1)}, s32[1,128]{1,0:T(1,128)}, u32[]{:S(2)}) copy-start(s32[1,128]{1,0:T(1,128)} %count_ref.1) | copy-start | bytes 1540
  1.8 9.1 %collective-permute-start = (f32[2,4,64]{2,1,0:T(4,128)S(1)}, f32[2,4,64]{2,1,0:T(4,128)S(1)}, u32[]{:S(2)}, u32[]{:S(2)}) collective-permute-start(f32[2,4,64]{2,1,0:T(4,128)S(1)} %get-tuple-element.34), channel_id=1, source_target_pairs={{0,1},{1,2},{2,3},{3,4},{4,5},{5,6},{6,7},{8,9},{9,10},{10,11},{11... | collective-permute-start | bytes 6152 | tf_op jit(solution)/shard_map/ppermute | solution.py:35
  5.3 7.0 %collective-permute-start.1 = (f32[2,4,128]{2,1,0:T(4,128)S(1)}, f32[2,4,128]{2,1,0:T(4,128)S(1)}, u32[]{:S(2)}, u32[]{:S(2)}) collective-permute-start(f32[2,4,128]{2,1,0:T(4,128)S(1)} %get-tuple-element.35), channel_id=1, source_target_pairs={{0,8},{8,16},{16,24},{24,32},{32,40},{40,48},{48,56},{56,64},{64,7... | collective-permute-start | bytes 12296 | tf_op jit(solution)/shard_map/ppermute | solution.py:35
  7.2 5.1 %copy-start = (f32[3,2,3,4,64,128]{5,4,3,2,1,0:T(8,128)S(1)}, f32[3,2,3,4,64,128]{5,4,3,2,1,0:T(8,128)}, u32[]{:S(2)}) copy-start(f32[3,2,3,4,64,128]{5,4,3,2,1,0:T(8,128)} %dft_e_ref.1) | copy-start | bytes 7077892
  7.2 5.1 %copy-start.1 = (f32[3,2,3,4,64,128]{5,4,3,2,1,0:T(8,128)S(1)}, f32[3,2,3,4,64,128]{5,4,3,2,1,0:T(8,128)}, u32[]{:S(2)}) copy-start(f32[3,2,3,4,64,128]{5,4,3,2,1,0:T(8,128)} %dft_h_ref.1) | copy-start | bytes 7077892
  7.3 5.1 %copy-start.2 = (f32[3,4,64,128]{3,2,1,0:T(8,128)S(1)}, f32[3,4,64,128]{3,2,1,0:T(8,128)}, u32[]{:S(2)}) copy-start(f32[3,4,64,128]{3,2,1,0:T(8,128)} %e_ref.1) | copy-start | bytes 1179652
  7.3 5.0 %copy-start.4 = (f32[3,4,64,128]{3,2,1,0:T(8,128)S(1)}, f32[3,4,64,128]{3,2,1,0:T(8,128)}, u32[]{:S(2)}) copy-start(f32[3,4,64,128]{3,2,1,0:T(8,128)} %h_ref.3) | copy-start | bytes 1179652
  7.3 5.0 %copy-start.5 = (f32[3,4,64,128]{3,2,1,0:T(8,128)S(1)}, f32[3,4,64,128]{3,2,1,0:T(8,128)}, u32[]{:S(2)}) copy-start(f32[3,4,64,128]{3,2,1,0:T(8,128)} %j_ref.1) | copy-start | bytes 1179652
  7.3 5.0 %copy-start.6 = (s32[4,64,128]{2,1,0:T(8,128)S(1)}, s32[4,64,128]{2,1,0:T(8,128)}, u32[]{:S(2)}) copy-start(s32[4,64,128]{2,1,0:T(8,128)} %kind_ref.1) | copy-start | bytes 393220
  7.3 5.0 %copy-start.7 = (f32[4,32]{1,0:T(4,128)S(1)}, f32[4,32]{1,0:T(4,128)}, u32[]{:S(2)}) copy-start(f32[4,32]{1,0:T(4,128)} %table_ref.1) | copy-start | bytes 1540
  12.4 18.7 %copy-start.8 = (f32[3,256,256]{2,1,0:T(8,128)S(1)}, f32[3,256,256]{2,1,0:T(8,128)}, u32[]{:S(2)}) copy-start(f32[3,256,256]{2,1,0:T(8,128)} %area_ref) | copy-start | bytes 2359300
  12.4 18.7 %copy-start.10 = (s32[1,128,128]{2,1,0:T(8,128)S(1)}, s32[1,128,128]{2,1,0:T(8,128)}, u32[]{:S(2)}) copy-start(s32[1,128,128]{2,1,0:T(8,128)} %patch_ref.2) | copy-start | bytes 196612
  22.1 21.5 %all-to-all-start = ((f32[128,9,1,128]{3,2,1,0:T(1,128)}), f32[128,9,1,128]{3,2,1,0:T(1,128)S(1)}, u32[]{:S(2)}, u32[]{:S(2)}) async-start(f32[128,9,1,128]{3,2,1,0:T(1,128)} %get-tuple-element.47), calls=%async_computation | async-start | bytes 1179648 | tf_op jit(solution)/shard_map/all_to_all | solution.py:540
  51.5 14.5 %collective-permute-start.2 = (f32[2,104,256]{2,1,0:T(8,128)S(1)}, f32[2,104,256]{2,1,0:T(8,128)S(1)}, u32[]{:S(2)}, u32[]{:S(2)}) collective-permute-start(f32[2,104,256]{2,1,0:T(8,128)S(1)} %get-tuple-element.50), channel_id=1, source_target_pairs={{1,2},{3,4},{5,6},{2,1},{4,3},{6,5},{9,10},{11,12},{13,14},{10,9},... | collective-permute-start | bytes 638984 | tf_op jit(solution)/shard_map/ppermute | solution.py:44
  56.3 9.8 %collective-permute-start.3 = (f32[2,104,256]{2,1,0:T(8,128)S(1)}, f32[2,104,256]{2,1,0:T(8,128)S(1)}, u32[]{:S(2)}, u32[]{:S(2)}) collective-permute-start(f32[2,104,256]{2,1,0:T(8,128)S(1)} %get-tuple-element.51), channel_id=1, source_target_pairs={{0,1},{2,3},{4,5},{6,7},{1,0},{3,2},{5,4},{7,6},{8,9},{10,11},{12,... | collective-permute-start | bytes 638984 | tf_op jit(solution)/shard_map/ppermute | solution.py:44
  61.2 10.2 %collective-permute-start.6 = (f32[1,104,256]{2,1,0:T(8,128)S(1)}, f32[1,104,256]{2,1,0:T(8,128)S(1)}, u32[]{:S(2)}, u32[]{:S(2)}) collective-permute-start(f32[1,104,256]{2,1,0:T(8,128)S(1)} %get-tuple-element.55), channel_id=1, source_target_pairs={{1,2},{3,4},{5,6},{2,1},{4,3},{6,5},{9,10},{11,12},{13,14},{10,9},... | collective-permute-start | bytes 319496 | tf_op jit(solution)/shard_map/ppermute | solution.py:44
  65.9 5.5 %collective-permute-start.7 = (f32[1,104,256]{2,1,0:T(8,128)S(1)}, f32[1,104,256]{2,1,0:T(8,128)S(1)}, u32[]{:S(2)}, u32[]{:S(2)}) collective-permute-start(f32[1,104,256]{2,1,0:T(8,128)S(1)} %get-tuple-element.56), channel_id=1, source_target_pairs={{0,1},{2,3},{4,5},{6,7},{1,0},{3,2},{5,4},{7,6},{8,9},{10,11},{12,... | collective-permute-start | bytes 319496 | tf_op jit(solution)/shard_map/ppermute | solution.py:44
  66.6 13.3 %collective-permute-start.4 = (f32[2,104,256]{2,1,0:T(8,128)S(1)}, f32[2,104,256]{2,1,0:T(8,128)S(1)}, u32[]{:S(2)}, u32[]{:S(2)}) collective-permute-start(f32[2,104,256]{2,1,0:T(8,128)S(1)} %get-tuple-element.53), channel_id=1, source_target_pairs={{8,16},{24,32},{40,48},{56,64},{72,80},{88,96},{104,112},{16,8},{3... | collective-permute-start | bytes 638984 | tf_op jit(solution)/shard_map/ppermute | solution.py:44
  70.2 9.7 %collective-permute-start.5 = (f32[2,104,256]{2,1,0:T(8,128)S(1)}, f32[2,104,256]{2,1,0:T(8,128)S(1)}, u32[]{:S(2)}, u32[]{:S(2)}) collective-permute-start(f32[2,104,256]{2,1,0:T(8,128)S(1)} %get-tuple-element.54), channel_id=1, source_target_pairs={{0,8},{16,24},{32,40},{48,56},{64,72},{80,88},{96,104},{112,120},{... | collective-permute-start | bytes 638984 | tf_op jit(solution)/shard_map/ppermute | solution.py:44
  71.8 8.1 %collective-permute-start.8 = (f32[1,104,256]{2,1,0:T(8,128)S(1)}, f32[1,104,256]{2,1,0:T(8,128)S(1)}, u32[]{:S(2)}, u32[]{:S(2)}) collective-permute-start(f32[1,104,256]{2,1,0:T(8,128)S(1)} %get-tuple-element.58), channel_id=1, source_target_pairs={{8,16},{24,32},{40,48},{56,64},{72,80},{88,96},{104,112},{16,8},{3... | collective-permute-start | bytes 319496 | tf_op jit(solution)/shard_map/ppermute | solution.py:44
  74.7 5.2 %collective-permute-start.9 = (f32[1,104,256]{2,1,0:T(8,128)S(1)}, f32[1,104,256]{2,1,0:T(8,128)S(1)}, u32[]{:S(2)}, u32[]{:S(2)}) collective-permute-start(f32[1,104,256]{2,1,0:T(8,128)S(1)} %get-tuple-element.59), channel_id=1, source_target_pairs={{0,8},{16,24},{32,40},{48,56},{64,72},{80,88},{96,104},{112,120},{... | collective-permute-start | bytes 319496 | tf_op jit(solution)/shard_map/ppermute | solution.py:44
